TPU v7x, 32 devices: a whole 2x2x4 slice. The times are simulated.
32 devices in a mesh: dp: 8 (over y, x, core), tensor: 4 (over z).
Axes of the slice: x: 2, y: 2, z: 4, core: 2. Of those that a mesh axis runs over, the one named last changes fastest.
Arguments:
- inputs: bfloat16 [16384, 1024], P(('dp', 'tensor')), may hold values from -6 to 6
- teacher: bfloat16 [16384, 1024], P(('dp', 'tensor')), may hold values from -6 to 6
- lengths: int32 [8], replicated, may hold values from 512 to 2048, as said below
- w_qkv: bfloat16 [1024, 3, 1024], P('dp', None, 'tensor'), may hold values from -0.1875 to 0.1875
- w_out_t: bfloat16 [1024, 1024], P('dp', 'tensor'), may hold values from -0.5 to 0.5
- w_gate_up: bfloat16 [1024, 2, 4096], P('dp', None, 'tensor'), may hold values from -0.1875 to 0.1875
- w_down_t: bfloat16 [1024, 4096], P('dp', 'tensor'), may hold values from -0.09375 to 0.09375
- gains: bfloat16 [1024, 2], P('dp'), may hold values from 0.25 to 1.75
Outputs:
- output: bfloat16 [16384, 1024], P(('dp', 'tensor'))
- grad_inputs: float32 [16384, 1024], P(('dp', 'tensor'))
- grad_qkv: float32 [1024, 3, 1024], P('dp', None, 'tensor')
- grad_out_t: float32 [1024, 1024], P('dp', 'tensor')
- grad_gate_up: float32 [1024, 2, 4096], P('dp', None, 'tensor')
- grad_down_t: float32 [1024, 4096], P('dp', 'tensor')
- grad_gains: float32 [1024, 2], P(('dp', 'tensor'))
Inputs may be any that keep to these rules, and one draw needn't show every extreme that they name: `lengths`: the longest slot is full, with 2048 valid rows.
All inputs are finite; a program needn't handle non-finite values.
Results may differ from a plain program's by a relative error of at most 0.017.
Values may be sent and summed in bfloat16 or wider, within the bound.
No kernel may reach another device: no remote copies, remote signals or barrier semaphores. Data moves between devices by JAX's collectives and lax.ppermute only.
A program may use at most 192 MiB of HBM per device.

v0:
```python
import math

import jax
import jax.numpy as jnp
from jax import lax
from jax.sharding import PartitionSpec as P

HEAD = 64


negative = -1e30


def norm_forward(values):
    inverse = lax.rsqrt(jnp.mean(values * values, axis=-1, keepdims=True) + 1e-05)
    return (values * inverse, inverse)


def norm_backward(grad_normed, scaled, inverse, gain):
    grad_scaled = grad_normed * gain
    grad_values = inverse * (
        grad_scaled - scaled * jnp.mean(grad_scaled * scaled, axis=-1, keepdims=True)
    )
    return (grad_values, jnp.sum(grad_normed * scaled, axis=0))


def key_limit(query_index):
    return query_index + 1


def score_block(query_block, keys_all, query_start, key_start, length):
    block = query_block.shape[0]
    key_block = lax.dynamic_slice_in_dim(keys_all, key_start, block, 0)
    scores = jnp.einsum("qhe,khe->hqk", query_block, key_block, preferred_element_type=jnp.float32)
    query_pos = query_start + jnp.arange(block, dtype=jnp.int32)
    key_pos = key_start + jnp.arange(block, dtype=jnp.int32)
    allowed = (key_pos[None, :] <= query_pos[:, None]) & (key_pos[None, :] < length)
    return jnp.where(allowed[None], scores, negative)


def attention_forward(queries, keys_all, values_all, length):
    slot, heads, head = queries.shape
    block = min(512, slot)
    block_count = slot // block

    def query_step(index, carry):
        mixed, maxima, totals = carry
        query_start = index * block
        query_block = lax.dynamic_slice_in_dim(queries, query_start, block, 0)
        upper = key_limit(index)

        def stats_step(inner, state):
            maximum, total = state
            scores = score_block(query_block, keys_all, query_start, inner * block, length)
            larger = jnp.maximum(maximum, jnp.max(scores, axis=-1))
            total = total * jnp.exp(maximum - larger) + jnp.sum(
                jnp.exp(scores - larger[..., None]), axis=-1
            )
            return (larger, total)

        start_state = (
            jnp.full((heads, block), negative, jnp.float32),
            jnp.zeros((heads, block), jnp.float32),
        )
        maximum, total = lax.fori_loop(0, upper, stats_step, start_state)

        def mix_step(inner, accum):
            key_start = inner * block
            scores = score_block(query_block, keys_all, query_start, key_start, length)
            weights = (jnp.exp(scores - maximum[..., None]) / total[..., None]).astype(jnp.bfloat16)
            value_block = lax.dynamic_slice_in_dim(values_all, key_start, block, 0)
            return accum + jnp.einsum(
                "hqk,khe->qhe", weights, value_block, preferred_element_type=jnp.float32
            )

        accum = lax.fori_loop(0, upper, mix_step, jnp.zeros((block, heads, head), jnp.float32))
        mixed = lax.dynamic_update_slice_in_dim(mixed, accum, query_start, 0)
        maxima = lax.dynamic_update_index_in_dim(maxima, maximum, index, 0)
        totals = lax.dynamic_update_index_in_dim(totals, total, index, 0)
        return (mixed, maxima, totals)

    start = (
        jnp.zeros((slot, heads, head), jnp.float32),
        jnp.zeros((block_count, heads, block), jnp.float32),
        jnp.zeros((block_count, heads, block), jnp.float32),
    )
    return lax.fori_loop(0, block_count, query_step, start)


def attention_backward(queries, keys_all, values_all, grad_mixed, maxima, totals, length):
    slot, heads, head = queries.shape
    block = min(512, slot)
    block_count = slot // block

    def query_step(index, carry):
        grad_queries, grad_keys, grad_values = carry
        query_start = index * block
        query_block = lax.dynamic_slice_in_dim(queries, query_start, block, 0)
        grad_block = lax.dynamic_slice_in_dim(grad_mixed, query_start, block, 0)
        maximum = lax.dynamic_index_in_dim(maxima, index, 0, keepdims=False)
        total = lax.dynamic_index_in_dim(totals, index, 0, keepdims=False)
        upper = key_limit(index)

        def probs_of(inner):
            key_start = inner * block
            scores = score_block(query_block, keys_all, query_start, key_start, length)
            probs = jnp.exp(scores - maximum[..., None]) / total[..., None]
            value_block = lax.dynamic_slice_in_dim(values_all, key_start, block, 0)
            grad_probs = jnp.einsum(
                "qhe,khe->hqk", grad_block, value_block, preferred_element_type=jnp.float32
            )
            return (probs, grad_probs, key_start)

        def delta_step(inner, delta):
            probs, grad_probs, key_start = probs_of(inner)
            return delta + jnp.sum(probs * grad_probs, axis=-1)

        delta = lax.fori_loop(0, upper, delta_step, jnp.zeros((heads, block), jnp.float32))

        def grad_step(inner, state):
            grad_query, grad_keys, grad_values = state
            probs, grad_probs, key_start = probs_of(inner)
            grad_scores = (probs * (grad_probs - delta[..., None])).astype(jnp.bfloat16)
            key_block = lax.dynamic_slice_in_dim(keys_all, key_start, block, 0)
            grad_query = grad_query + jnp.einsum(
                "hqk,khe->qhe", grad_scores, key_block, preferred_element_type=jnp.float32
            )
            key_part = jnp.einsum(
                "hqk,qhe->khe", grad_scores, query_block, preferred_element_type=jnp.float32
            )
            value_part = jnp.einsum(
                "hqk,qhe->khe",
                probs.astype(jnp.bfloat16),
                grad_block,
                preferred_element_type=jnp.float32,
            )
            old_keys = lax.dynamic_slice_in_dim(grad_keys, key_start, block, 0)
            old_values = lax.dynamic_slice_in_dim(grad_values, key_start, block, 0)
            grad_keys = lax.dynamic_update_slice_in_dim(
                grad_keys, old_keys + key_part, key_start, 0
            )
            grad_values = lax.dynamic_update_slice_in_dim(
                grad_values, old_values + value_part, key_start, 0
            )
            return (grad_query, grad_keys, grad_values)

        start_state = (jnp.zeros((block, heads, head), jnp.float32), grad_keys, grad_values)
        grad_query, grad_keys, grad_values = lax.fori_loop(0, upper, grad_step, start_state)
        grad_queries = lax.dynamic_update_slice_in_dim(grad_queries, grad_query, query_start, 0)
        return (grad_queries, grad_keys, grad_values)

    empty = jnp.zeros((slot, heads, head), jnp.float32)
    return lax.fori_loop(0, block_count, query_step, (empty, empty, empty))


def on_device(inputs, teacher, lengths, w_qkv, w_out_t, w_gate_up, w_down_t, gains):
    own_rows = inputs.shape[0]
    slot = own_rows * lax.axis_size("tensor")
    total_rows = slot * lax.axis_size("dp")
    local_width = w_qkv.shape[2]
    local_heads = local_width // HEAD
    scale = 1.0 / math.sqrt(HEAD)
    length = lax.dynamic_index_in_dim(lengths, lax.axis_index("dp"), 0, keepdims=False)
    count = jnp.sum(lengths).astype(jnp.float32)
    own_start = lax.axis_index("tensor") * own_rows
    row_pos = own_start + jnp.arange(own_rows, dtype=jnp.int32)
    valid = (row_pos < length)[:, None]
    qkv_all, out_all, gains_all = (
        lax.all_gather(w_qkv, "dp", axis=0, tiled=True),
        lax.all_gather(w_out_t, "dp", axis=0, tiled=True),
        lax.all_gather(gains, "dp", axis=0, tiled=True),
    )
    gate_up_all, down_all = (
        lax.all_gather(w_gate_up, "dp", axis=0, tiled=True),
        lax.all_gather(w_down_t, "dp", axis=0, tiled=True),
    )
    gain_one = gains_all[:, 0].astype(jnp.float32)
    gain_two = gains_all[:, 1].astype(jnp.float32)
    rows = inputs.astype(jnp.float32)
    scaled_one, inverse_one = norm_forward(rows)
    normed_one = (scaled_one * gain_one).astype(jnp.bfloat16)
    gathered_one = lax.all_gather(normed_one, "tensor", axis=0, tiled=True)
    qkv = jnp.einsum("rd,dcf->rcf", gathered_one, qkv_all, preferred_element_type=jnp.float32)
    queries = (qkv[:, 0] * scale).astype(jnp.bfloat16).reshape(slot, local_heads, HEAD)
    keys_all = qkv[:, 1].astype(jnp.bfloat16).reshape(slot, local_heads, HEAD)
    values_all = qkv[:, 2].astype(jnp.bfloat16).reshape(slot, local_heads, HEAD)
    mixed, maxima, totals = attention_forward(queries, keys_all, values_all, length)
    mixed = mixed.reshape(slot, local_width).astype(jnp.bfloat16)
    piece = mixed
    middle = rows + lax.psum_scatter(
        jnp.einsum("rk,dk->rd", piece, out_all, preferred_element_type=jnp.float32).astype(
            jnp.bfloat16
        ),
        "tensor",
        scatter_dimension=0,
        tiled=True,
    ).astype(jnp.float32)
    scaled_two, inverse_two = norm_forward(middle)
    normed_two = (scaled_two * gain_two).astype(jnp.bfloat16)
    gathered_two = lax.all_gather(normed_two, "tensor", axis=0, tiled=True)
    rows_two = None
    gate_up = jnp.einsum(
        "rd,dcf->rcf", gathered_two, gate_up_all, preferred_element_type=jnp.float32
    )
    gate = gate_up[:, 0]
    upper = gate_up[:, 1]
    sigmoid = jax.nn.sigmoid(gate)
    hidden = (gate * sigmoid * upper).astype(jnp.bfloat16)
    piece = hidden
    final = middle + lax.psum_scatter(
        jnp.einsum("rf,df->rd", piece, down_all, preferred_element_type=jnp.float32).astype(
            jnp.bfloat16
        ),
        "tensor",
        scatter_dimension=0,
        tiled=True,
    ).astype(jnp.float32)
    output = final.astype(jnp.bfloat16)
    grad_final = jnp.where(valid, final - teacher.astype(jnp.float32), 0.0) * (total_rows / count)
    grad_feed = lax.all_gather(grad_final.astype(jnp.bfloat16), "tensor", axis=0, tiled=True)
    grad_down = jnp.einsum("rd,rf->df", grad_feed, hidden, preferred_element_type=jnp.float32)
    grad_hidden = jnp.einsum("rd,df->rf", grad_feed, down_all, preferred_element_type=jnp.float32)
    grad_gate = grad_hidden * upper * (sigmoid * (1.0 + gate * (1.0 - sigmoid)))
    grad_upper = grad_hidden * (gate * sigmoid)
    grad_gu = jnp.stack([grad_gate, grad_upper], axis=1).astype(jnp.bfloat16)
    rows_two = lax.all_gather(normed_two, "tensor", axis=0, tiled=True)
    grad_gate_up = jnp.einsum("rd,rcf->dcf", rows_two, grad_gu, preferred_element_type=jnp.float32)
    piece = grad_gu
    grad_normed_two = lax.psum_scatter(
        jnp.einsum("rcf,dcf->rd", piece, gate_up_all, preferred_element_type=jnp.float32).astype(
            jnp.bfloat16
        ),
        "tensor",
        scatter_dimension=0,
        tiled=True,
    ).astype(jnp.float32)
    grad_norm_two, grad_gain_two = norm_backward(grad_normed_two, scaled_two, inverse_two, gain_two)
    grad_middle = grad_final + grad_norm_two
    grad_branch = lax.all_gather(grad_middle.astype(jnp.bfloat16), "tensor", axis=0, tiled=True)
    grad_out = jnp.einsum("rd,rk->dk", grad_branch, mixed, preferred_element_type=jnp.float32)
    grad_mixed = jnp.einsum("rd,dk->rk", grad_branch, out_all, preferred_element_type=jnp.float32)
    grad_mixed = grad_mixed.astype(jnp.bfloat16).reshape(slot, local_heads, HEAD)
    grad_queries, grad_keys, grad_values = attention_backward(
        queries, keys_all, values_all, grad_mixed, maxima, totals, length
    )
    grad_rows_qkv = jnp.stack(
        [
            grad_queries.reshape(slot, local_width).astype(jnp.bfloat16) * scale,
            grad_keys.reshape(slot, local_width).astype(jnp.bfloat16),
            grad_values.reshape(slot, local_width).astype(jnp.bfloat16),
        ],
        axis=1,
    )
    rows_one = lax.all_gather(normed_one, "tensor", axis=0, tiled=True)
    grad_qkv = jnp.einsum(
        "rd,rcf->dcf", rows_one, grad_rows_qkv, preferred_element_type=jnp.float32
    )
    piece = grad_rows_qkv
    grad_normed_one = lax.psum_scatter(
        jnp.einsum("rcf,dcf->rd", piece, qkv_all, preferred_element_type=jnp.float32).astype(
            jnp.bfloat16
        ),
        "tensor",
        scatter_dimension=0,
        tiled=True,
    ).astype(jnp.float32)
    grad_norm_one, grad_gain_one = norm_backward(grad_normed_one, scaled_one, inverse_one, gain_one)
    grad_inputs = grad_middle + grad_norm_one
    grad_qkv, grad_out, grad_gate_up, grad_down = (
        lax.psum_scatter(
            grad_qkv.astype(jnp.bfloat16), "dp", scatter_dimension=0, tiled=True
        ).astype(jnp.float32),
        lax.psum_scatter(
            grad_out.astype(jnp.bfloat16), "dp", scatter_dimension=0, tiled=True
        ).astype(jnp.float32),
        lax.psum_scatter(
            grad_gate_up.astype(jnp.bfloat16), "dp", scatter_dimension=0, tiled=True
        ).astype(jnp.float32),
        lax.psum_scatter(
            grad_down.astype(jnp.bfloat16), "dp", scatter_dimension=0, tiled=True
        ).astype(jnp.float32),
    )
    grad_gains = lax.psum_scatter(
        jnp.stack([grad_gain_one, grad_gain_two], axis=1),
        ("dp", "tensor"),
        scatter_dimension=0,
        tiled=True,
    )
    return (output, grad_inputs, grad_qkv, grad_out, grad_gate_up, grad_down, grad_gains)


def solution(mesh):
    return jax.shard_map(
        on_device,
        mesh=mesh,
        in_specs=(
            P(("dp", "tensor"), None),
            P(("dp", "tensor"), None),
            P(),
            P("dp", None, "tensor"),
            P("dp", "tensor"),
            P("dp", None, "tensor"),
            P("dp", "tensor"),
            P("dp", None),
        ),
        out_specs=(
            P(("dp", "tensor"), None),
            P(("dp", "tensor"), None),
            P("dp", None, "tensor"),
            P("dp", "tensor"),
            P("dp", None, "tensor"),
            P("dp", "tensor"),
            P(("dp", "tensor"), None),
        ),
        check_vma=False,
    )
```

profile of v0, /device:TPU:0, one launch (start us, length us, event | category | flops | bytes accessed | tf_op | source)
XLA Modules:
  0.0 1232.7 jit_solution(13212471489866110778)
XLA Ops:
  9.1 10.3 all_gather.29
  25.9 12.1 all_gather.32
  40.5 82.9 %all-gather.8.cloned.1.call-done = bf16[2048,1024]{1,0:T(8,128)(2,1)} async-done(((bf16[512,1024]{1,0:T(8,128)(2,1)}), bf16[2048,1024]{1,0:T(8,128)(2,1)}) %all-gather.8.cloned.1.call-update) | async-done | bytes 4194320 | tf_op jit(solution)/shard_map/all_gather | solution.py:182
  123.4 5.7 fusion.97
  130.5 59.0 %while.138 = (s32[]{:T(128)}, bf16[2048,4,64]{0,2,1:T(8,128)(2,1)}, f32[4,4,512]{2,1,0:T(4,128)S(1)}, f32[4,4,512]{2,1,0:T(4,128)S(1)}, bf16[2048,4,64]{0,2,1:T(...) while((s32[]{:T(128)}, bf16[2048,4,64]{0,2,1:T(8,128)(2,1)}, ...), condition=%wide.region_8.9_spmd, body=%wide.region_1.8_spmd.sunk | while | flops 413278208 | bytes 14348141 | solution.py:87
  131.5 2.7 while.142
  138.5 5.3 while.142
  143.9 5.0 while.143
  150.6 8.0 while.142
  158.7 7.5 while.143
  168.0 10.6 while.142
  178.7 10.0 while.143
  190.5 4.7 convolution_convert_fusion
  197.3 73.4 %reduce-scatter.12.cloned.1.call-done = bf16[512,1024]{1,0:T(8,128)(2,1)} async-done(((bf16[2048,1024]{1,0:T(8,128)(2,1)}), bf16[512,1024]{1,0:T(8,128)(2,1)}) %reduce-scatter.12.cloned.1.call-update) | async-done | bytes 1048592 | tf_op jit(solution)/shard_map/reduce_scatter | solution.py:190
  275.8 34.7 %all-gather.14.cloned.1.call-done = bf16[1024,2,1024]{2,0,1:T(8,128)(2,1)} async-done(((bf16[128,2,1024]{2,0,1:T(8,128)(2,1)}), bf16[1024,2,1024]{2,0,1:T(8,128)(2,1)}) %all-gather.14.cloned.1.call-update) | async-done | bytes 4194320 | tf_op jit(solution)/shard_map/all_gather | solution.py:174
  310.5 82.9 %all-gather.12.cloned.1.call-done = bf16[2048,1024]{1,0:T(8,128)(2,1)} async-done(((bf16[512,1024]{1,0:T(8,128)(2,1)}), bf16[2048,1024]{1,0:T(8,128)(2,1)}) %all-gather.12.cloned.1.call-update) | async-done | bytes 4194320 | tf_op jit(solution)/shard_map/all_gather | solution.py:200
  393.3 14.8 %fusion.55 = f32[2048,2,1024]{2,0,1:T(8,128)S(1)} fusion(bf16[1024,2,1024]{2,0,1:T(8,128)(2,1)} %all-gather.14.cloned.1.call-done, bf16[2048,1024]{1,0:T(8,128)(2,1)} %all-gather.12.cloned.1.call-done), kind=kOutput, calls=%fused_computation.91 | convolution fusion | flops 8589934592 | bytes 25165824 | tf_op jit(solution)/shard_map/rd,dcf->rcf/dot_general | solution.py:202
  408.2 5.9 copy-done.6
  414.0 4.2 multiply_convert_fusion.2
  418.2 3.4 all-gather.16.cloned.1.call-done
  421.7 9.4 convolution_convert_fusion.1
  433.7 74.3 %reduce-scatter.14.cloned.1.call-done = bf16[512,1024]{1,0:T(8,128)(2,1)} async-done(((bf16[2048,1024]{1,0:T(8,128)(2,1)}), bf16[512,1024]{1,0:T(8,128)(2,1)}) %reduce-scatter.14.cloned.1.call-update) | async-done | bytes 1048592 | tf_op jit(solution)/shard_map/reduce_scatter | solution.py:210
  508.0 3.2 fusion.88
  511.5 81.2 %all-gather.18.cloned.1.call-done = bf16[2048,1024]{1,0:T(8,128)(2,1)} async-done(((bf16[512,1024]{1,0:T(8,128)(2,1)}), bf16[2048,1024]{1,0:T(8,128)(2,1)}) %all-gather.18.cloned.1.call-update) | async-done | bytes 4194320 | tf_op jit(solution)/shard_map/all_gather | solution.py:220
  592.7 13.4 %fusion.61 = (bf16[2048,1,1024]{2,0,1:T(8,128)(2,1)S(1)}, bf16[2048,1,1024]{2,0,1:T(8,128)(2,1)S(1)}) fusion(f32[2048,2,1024]{2,0,1:T(8,128)} %copy-done.6, bf16[2048,1024]{1,0:T(8,128)(2,1)} %all-gather.18.cloned.1.call-done, bf16[1024,1024]{1,0:T(8,128)(2,1)} %all-gather.16.cloned.1.call-done), kind=kOutput, calls=%fused_computation.97 | convolution fusion | flops 4322230272 | bytes 31457280 | tf_op jit(solution)/shard_map/rd,df->rf/dot_general | solution.py:222
  609.3 10.7 bitcast_convert_fusion.1
  620.1 75.4 %reduce-scatter.16.cloned.1.call-done = bf16[512,1024]{1,0:T(8,128)(2,1)} async-done(((bf16[2048,1024]{1,0:T(8,128)(2,1)}), bf16[512,1024]{1,0:T(8,128)(2,1)}) %reduce-scatter.16.cloned.1.call-update) | async-done | bytes 1048592 | tf_op jit(solution)/shard_map/reduce_scatter | solution.py:229
  695.5 2.7 fusion.77
  698.3 4.1 fusion.93
  702.9 9.3 convolution_convert_fusion.3
  712.3 14.3 %fusion.66 = bf16[1024,2,1024]{2,0,1:T(8,128)(2,1)} fusion(bf16[2048,1,1024]{2,0,1:T(8,128)(2,1)} %copy-done.25, bf16[2048,1,1024]{2,0,1:T(8,128)(2,1)} %copy-done.24, bf16[2048,1024]{1,0:T(8,128)(2,1)} %all-gather.12.cloned.1.call-done), kind=kOutput, calls=%fused_computation.108 | convolution fusion | flops 8608808960 | bytes 16777216 | tf_op jit(solution)/shard_map/rd,rcf->dcf/dot_general | solution.py:227
  726.8 57.1 %all-gather.20.cloned.1.call-done = bf16[2048,1024]{1,0:T(8,128)(2,1)} async-done(((bf16[512,1024]{1,0:T(8,128)(2,1)}), bf16[2048,1024]{1,0:T(8,128)(2,1)}) %all-gather.20.cloned.1.call-update) | async-done | bytes 4194320 | tf_op jit(solution)/shard_map/all_gather | solution.py:239
  783.9 4.5 convolution_convert_fusion.2
  791.6 128.7 %while.141 = (s32[]{:T(128)}, bf16[2048,4,64]{0,2,1:T(8,128)(2,1)}, f32[2048,4,64]{0,2,1:T(8,128)}, f32[2048,4,64]{0,2,1:T(8,128)}, bf16[2048,4,64]{0,2,1:T(8,12...) while((s32[]{:T(128)}, bf16[2048,4,64]{0,2,1:T(8,128)(2,1)}, ...), condition=%wide.region_21.22_spmd, body=%wide.region_15.21_spmd.sunk | while | flops 953552896 | bytes 37096448 | solution.py:153
  792.7 3.3 while.144
  796.0 8.8 while.145
  799.1 2.6 fusion.170
  802.2 2.6 fusion.171
  806.7 6.6 while.144
  813.4 17.6 %while.145 = (s32[]{:T(128)}, f32[512,4,64]{0,2,1:T(8,128)S(1)}, f32[2048,4,64]{0,2,1:T(8,128)}, f32[2048,4,64]{0,2,1:T(8,128)}, s32[]{:T(128)}, /*index=5*/bf16...) while((s32[]{:T(128)}, f32[512,4,64]{0,2,1:T(8,128)S(1)}, ...), condition=%wide.region_20.20_spmd, body=%wide.region_19.19_spmd.sunk | while | flops 679348224 | bytes 24413432 | solution.py:148
  819.6 2.6 fusion.171
  825.2 2.6 fusion.170
  828.3 2.7 fusion.171
  832.9 9.9 while.144
  842.8 26.4 %while.145 = (s32[]{:T(128)}, f32[512,4,64]{0,2,1:T(8,128)S(1)}, f32[2048,4,64]{0,2,1:T(8,128)}, f32[2048,4,64]{0,2,1:T(8,128)}, s32[]{:T(128)}, /*index=5*/bf16...) while((s32[]{:T(128)}, f32[512,4,64]{0,2,1:T(8,128)S(1)}, ...), condition=%wide.region_20.20_spmd, body=%wide.region_19.19_spmd.sunk | while | flops 679348224 | bytes 24413432 | solution.py:148
  849.0 2.6 fusion.171
  854.6 2.6 fusion.170
  857.7 2.7 fusion.171
  866.6 2.7 fusion.171
  871.1 13.1 %while.144 = (s32[]{:T(128)}, f32[4,512]{1,0:T(4,128)S(1)}, s32[]{:T(128)}, s32[]{:T(128)}, s32[]{:T(128)}, /*index=5*/bf16[2048,4,64]{0,2,1:T(8,128)(2,1)S(1)},...) while((s32[]{:T(128)}, f32[4,512]{1,0:T(4,128)S(1)}, ...), condition=%wide.region_18.18_spmd, body=%wide.region_16.17_spmd.sunk | while | flops 274204672 | bytes 10020051 | solution.py:118
  884.3 35.2 %while.145 = (s32[]{:T(128)}, f32[512,4,64]{0,2,1:T(8,128)S(1)}, f32[2048,4,64]{0,2,1:T(8,128)}, f32[2048,4,64]{0,2,1:T(8,128)}, s32[]{:T(128)}, /*index=5*/bf16...) while((s32[]{:T(128)}, f32[512,4,64]{0,2,1:T(8,128)S(1)}, ...), condition=%wide.region_20.20_spmd, body=%wide.region_19.19_spmd.sunk | while | flops 679348224 | bytes 24413432 | solution.py:148
  890.5 2.6 fusion.171
  896.1 2.6 fusion.170
  899.3 2.7 fusion.171
  908.1 2.7 fusion.171
  916.9 2.6 fusion.171
  928.9 4.4 convolution_convert_fusion.4
  933.6 7.2 fusion.84
  940.9 6.4 bitcast_convert_fusion
  951.9 14.3 %reduce-scatter.22.cloned.1.call-done = bf16[128,256]{1,0:T(8,128)(2,1)} async-done(((bf16[1024,256]{1,0:T(8,128)(2,1)}), bf16[128,256]{1,0:T(8,128)(2,1)}) %reduce-scatter.22.cloned.1.call-update) | async-done | bytes 65552 | tf_op jit(solution)/shard_map/reduce_scatter | solution.py:273
  967.7 40.1 %reduce-scatter.20.cloned.1.call-done = bf16[128,3,256]{2,0,1:T(8,128)(2,1)} async-done(((bf16[1024,3,256]{2,0,1:T(8,128)(2,1)}), bf16[128,3,256]{2,0,1:T(8,128)(2,1)}) %reduce-scatter.20.cloned.1.call-update) | async-done | bytes 196624 | tf_op jit(solution)/shard_map/reduce_scatter | solution.py:270
  1009.5 77.2 %reduce-scatter.18.cloned.1.call-done = bf16[512,1024]{1,0:T(8,128)(2,1)} async-done(((bf16[2048,1024]{1,0:T(8,128)(2,1)}), bf16[512,1024]{1,0:T(8,128)(2,1)}) %reduce-scatter.18.cloned.1.call-update) | async-done | bytes 1048592 | tf_op jit(solution)/shard_map/reduce_scatter | solution.py:259
  1089.9 3.1 fusion.73
  1093.0 131.5 %reduce-scatter.28.cloned.1.call-done = f32[32,2]{1,0:T(8,128)} async-done(((f32[1024,2]{1,0:T(8,128)}), f32[32,2]{1,0:T(8,128)}) %reduce-scatter.28.cloned.1.call-update) | async-done | bytes 272
  (413 shorter events, 201.2 us)
Async XLA Ops:
  7.2 18.1 %copy-start.22 = (s32[8]{0:T(128)S(1)}, s32[8]{0:T(128)}, u32[]{:S(2)}) copy-start(s32[8]{0:T(128)} %param.22) | copy-start | bytes 100
  7.2 18.8 %copy-start.17 = (bf16[128,256]{1,0:T(8,128)(2,1)S(1)}, bf16[128,256]{1,0:T(8,128)(2,1)}, u32[]{:S(2)}) copy-start(bf16[128,256]{1,0:T(8,128)(2,1)} %param.24) | copy-start | bytes 196612
  7.2 33.3 %all-gather.10.cloned.1.call-start = ((), (), s32[]{:S(2)}) async-start(), calls=%async_computation.10 | async-start | bytes 1769472 | tf_op jit(solution)/shard_map/all_gather | solution.py:169
  9.0 114.4 %all-gather.8.cloned.1.call-start = ((), (), s32[]{:S(2)}) async-start(), calls=%async_computation.9 | async-start | bytes 5242880 | tf_op jit(solution)/shard_map/all_gather | solution.py:182
  20.9 3.2 copy-start.18
  21.5 2.6 copy-start.14
  24.0 246.6 %reduce-scatter.12.cloned.1.call-start = ((), (), s32[]{:S(2)}) async-start(), calls=%async_computation.11 | async-start | bytes 5242880 | tf_op jit(solution)/shard_map/reduce_scatter | solution.py:190
  24.3 104.9 %copy-start.7 = (bf16[2048,4,64]{0,2,1:T(8,128)(2,1)}, bf16[2048,4,64]{0,2,1:T(8,128)(2,1)S(1)}, u32[]{:S(2)}) copy-start(bf16[2048,4,64]{0,2,1:T(8,128)(2,1)S(1)} %fusion.96) | copy-start | bytes 3145732
  189.5 1.0 copy-start.3
  195.2 1.0 copy-start.13
  195.2 75.5 %copy-start.1 = (bf16[512,1024]{1,0:T(8,128)(2,1)S(1)}, bf16[512,1024]{1,0:T(8,128)(2,1)}, u32[]{:S(2)}) copy-start(bf16[512,1024]{1,0:T(8,128)(2,1)} %param.20) | copy-start | bytes 3145732
  195.2 77.1 %copy-start.16 = (f32[1024,1]{0,1:T(1,128)S(1)}, f32[1024,1]{0,1:T(1,128)}, u32[]{:S(2)}) copy-start(f32[1024,1]{0,1:T(1,128)} %get-tuple-element.780) | copy-start | bytes 12292
  195.3 115.2 %all-gather.14.cloned.1.call-start = ((), (), s32[]{:S(2)}) async-start(), calls=%async_computation.13 | async-start | bytes 4718592 | tf_op jit(solution)/shard_map/all_gather | solution.py:174
  197.2 196.1 %all-gather.12.cloned.1.call-start = ((), (), s32[]{:S(2)}) async-start(), calls=%async_computation.12 | async-start | bytes 5242880 | tf_op jit(solution)/shard_map/all_gather | solution.py:200
  275.0 146.7 %all-gather.16.cloned.1.call-start = ((), (), s32[]{:S(2)}) async-start(), calls=%async_computation.14 | async-start | bytes 2359296 | tf_op jit(solution)/shard_map/all_gather | solution.py:175
  275.5 232.5 %reduce-scatter.14.cloned.1.call-start = ((), (), s32[]{:S(2)}) async-start(), calls=%async_computation.15 | async-start | bytes 5242880 | tf_op jit(solution)/shard_map/reduce_scatter | solution.py:210
  408.1 5.9 copy-start.6
  431.1 0.7 copy-start.23
  431.1 76.9 %copy-start.5 = (bf16[512,1024]{1,0:T(8,128)(2,1)S(1)}, bf16[512,1024]{1,0:T(8,128)(2,1)}, u32[]{:S(2)}) copy-start(bf16[512,1024]{1,0:T(8,128)(2,1)} %reduce-scatter.12.cloned.1.call-done) | copy-start | bytes 3145732
  431.1 161.5 %all-gather.18.cloned.1.call-start = ((), (), s32[]{:S(2)}) async-start(), calls=%async_computation.16 | async-start | bytes 5242880 | tf_op jit(solution)/shard_map/all_gather | solution.py:220
  511.2 184.3 %reduce-scatter.16.cloned.1.call-start = ((), (), s32[]{:S(2)}) async-start(), calls=%async_computation.17 | async-start | bytes 5242880 | tf_op jit(solution)/shard_map/reduce_scatter | solution.py:229
  592.7 16.7 %copy-start.21 = (bf16[1024,2,1024]{2,0,1:T(8,128)(2,1)S(1)}, bf16[1024,2,1024]{2,0,1:T(8,128)(2,1)}, u32[]{:S(2)}) copy-start(bf16[1024,2,1024]{2,0,1:T(8,128)(2,1)} %all-gather.14.cloned.1.call-done) | copy-start | bytes 12582916
  606.1 1.9 copy-start.24
  606.1 3.2 copy-start.25
  620.1 163.8 %all-gather.20.cloned.1.call-start = ((), (), s32[]{:S(2)}) async-start(), calls=%async_computation.18 | async-start | bytes 5242880 | tf_op jit(solution)/shard_map/all_gather | solution.py:239
  702.4 245.0 %reduce-scatter.26.cloned.1.call-start = ((), (), s32[]{:S(2)}) async-start(), calls=%async_computation.23 | async-start | bytes 2359296 | tf_op jit(solution)/shard_map/reduce_scatter | solution.py:279
  712.3 237.1 %reduce-scatter.24.cloned.1.call-start = ((), (), s32[]{:S(2)}) async-start(), calls=%async_computation.22 | async-start | bytes 4718592 | tf_op jit(solution)/shard_map/reduce_scatter | solution.py:276
  726.6 57.3 %copy-start.10 = (bf16[1024,256]{1,0:T(8,128)(2,1)S(1)}, bf16[1024,256]{1,0:T(8,128)(2,1)}, u32[]{:S(2)}) copy-start(bf16[1024,256]{1,0:T(8,128)(2,1)} %all_gather.32) | copy-start | bytes 1572868
  726.6 239.6 %reduce-scatter.22.cloned.1.call-start = ((), (), s32[]{:S(2)}) async-start(), calls=%async_computation.21 | async-start | bytes 589824 | tf_op jit(solution)/shard_map/reduce_scatter | solution.py:273
  788.3 3.2 copy-start.4
  920.3 2.8 copy-start
  924.2 4.7 copy-start.9
  928.9 4.7 copy-start.11
  933.3 7.6 copy-start.12
  933.3 74.5 %reduce-scatter.20.cloned.1.call-start = ((), (), s32[]{:S(2)}) async-start(), calls=%async_computation.20 | async-start | bytes 1769472 | tf_op jit(solution)/shard_map/reduce_scatter | solution.py:270
  940.8 146.0 %reduce-scatter.18.cloned.1.call-start = ((), (), s32[]{:S(2)}) async-start(), calls=%async_computation.19 | async-start | bytes 5242880 | tf_op jit(solution)/shard_map/reduce_scatter | solution.py:259
  947.3 139.5 %copy-start.2 = (bf16[512,1024]{1,0:T(8,128)(2,1)S(1)}, bf16[512,1024]{1,0:T(8,128)(2,1)}, u32[]{:S(2)}) copy-start(bf16[512,1024]{1,0:T(8,128)(2,1)} %param.20) | copy-start | bytes 3145732
  947.3 139.5 %copy-start.15 = (f32[1024,1]{0,1:T(1,128)S(1)}, f32[1024,1]{0,1:T(1,128)}, u32[]{:S(2)}) copy-start(f32[1024,1]{0,1:T(1,128)} %copy-done.14) | copy-start | bytes 12292
  947.3 139.5 %copy-start.19 = (f32[512]{0:T(512)S(1)}, f32[512]{0:T(512)}, u32[]{:S(2)}) copy-start(f32[512]{0:T(512)} %copy-done.18) | copy-start | bytes 6148
  947.3 141.5 %copy-start.20 = (f32[1024]{0:T(1024)S(1)}, f32[1024]{0:T(1024)}, u32[]{:S(2)}) copy-start(f32[1024]{0:T(1024)} %get-tuple-element.627) | copy-start | bytes 12292
  947.3 142.6 %copy-start.8 = (f32[512,1024]{1,0:T(8,128)S(1)}, f32[512,1024]{1,0:T(8,128)}, u32[]{:S(2)}) copy-start(f32[512,1024]{1,0:T(8,128)} %get-tuple-element.756) | copy-start | bytes 6291460
  947.4 277.2 %reduce-scatter.28.cloned.1.call-start = ((), (), s32[]{:S(2)}) async-start(), calls=%async_computation.24 | async-start | bytes 540672
Sparse Core Ops, SparseCore 0:
  10.5 29.9 all-gather.9
  42.6 80.7 all-gather.7
  195.4 75.2 reduce-scatter.11
  273.2 37.2 all-gather.13
  312.5 80.7 all-gather.11
  395.2 26.4 all-gather.15
  431.2 76.7 reduce-scatter.13
  511.3 81.2 all-gather.17
  620.2 75.2 reduce-scatter.15
  702.5 81.2 all-gather.19
  787.5 39.7 reduce-scatter.25
  830.5 51.2 reduce-scatter.23
  933.4 32.7 reduce-scatter.21
  969.4 38.4 reduce-scatter.19
  1010.0 76.7 reduce-scatter.17
  1090.0 134.5 reduce-scatter.27
where the time goes:
time: 1240 us; the launch traced here: 1230 us
  waiting for transfers between devices  832 us (67%)
  matrix products  230 us (19%)
  other arithmetic  85.5 us (7%)
  local copies, waits for them, and re-layouts  43.4 us (4%)
  blocking collectives  22.4 us (2%)
  between operations  15.2 us (1%)
    unnamed x17, waiting for transfers between devices  132 us
    all_gather x1, waiting for transfers between devices, on_device(): gathered_one = lax.all_gather(normed_one, 'tensor', axis=0, tiled=True)  82.9 us
    all_gather x1, waiting for transfers between devices, on_device(): gathered_two = lax.all_gather(normed_two, 'tensor', axis=0, tiled=True)  82.9 us
    all_gather x1, waiting for transfers between devices, on_device(): lax.all_gather(grad_final.astype(jnp.bfloat16), 'tensor', axis=0, tiled=T...  81.2 us
    reduce_scatter x1, waiting for transfers between devices, on_device(): lax.psum_scatter(jnp.einsum('rcf,dcf->rd', piece, qkv_all, preferred_elem...  77.2 us
    reduce_scatter x1, waiting for transfers between devices, on_device(): lax.psum_scatter(jnp.einsum('rcf,dcf->rd', piece, gate_up_all, preferred_...  75.4 us
    reduce_scatter x1, waiting for transfers between devices, on_device(): lax.psum_scatter(jnp.einsum('rf,df->rd', piece, down_all, preferred_eleme...  74.3 us
    reduce_scatter x1, waiting for transfers between devices, on_device(): lax.psum_scatter(jnp.einsum('rk,dk->rd', piece, out_all, preferred_elemen...  73.4 us
  transfers between devices with their start and end apart: 16, of which 14 were waited for; matrix products, arithmetic and copies ran while one was open for 18% of the time, Pallas kernels for 0%

commit v1 on v0

--- a/solution.py
+++ b/solution.py
@@ -3,6 +3,8 @@
 import jax
 import jax.numpy as jnp
 from jax import lax
+from jax.experimental import pallas as pl
+from jax.experimental.pallas import tpu as pltpu
 from jax.sharding import PartitionSpec as P
 
 HEAD = 64
@@ -289,9 +291,457 @@
     return (output, grad_inputs, grad_qkv, grad_out, grad_gate_up, grad_down, grad_gains)
 
 
+BF = jnp.bfloat16
+F32 = jnp.float32
+AXES = ("dp", "tensor")
+
+
+def shift(value, where):
+    pairs = []
+    for y in range(2):
+        for x in range(2):
+            for c in range(2):
+                for z in range(4):
+                    to = where(y, x, c, z)
+                    if to is not None:
+                        ty, tx, tc, tz = to
+                        pairs.append((((y * 2 + x) * 2 + c) * 4 + z, ((ty * 2 + tx) * 2 + tc) * 4 + tz))
+    return lax.ppermute(value, AXES, pairs)
+
+
+def core_swap(value):
+    return shift(value, lambda y, x, c, z: (y, x, 1 - c, z))
+
+
+def x_swap(value):
+    return shift(value, lambda y, x, c, z: (y, 1 - x, c, z))
+
+
+def y_swap(value):
+    return shift(value, lambda y, x, c, z: (1 - y, x, c, z))
+
+
+def z_swap(value, bits):
+    return shift(value, lambda y, x, c, z: (y, x, c, z ^ bits))
+
+
+def home_of(y, x, c, z):
+    if (c == 1 and z < 2) or (c == 0 and z >= 2):
+        return (y, x, 1 - c, 3 - z)
+    return (y, x, c, z)
+
+
+def home_swap(value):
+    return shift(value, home_of)
+
+
+def partner_of_home(y, x, c, z):
+    y, x, c, z = home_of(y, x, c, z)
+    z ^= 1
+    if c == 1 and z in (1, 2):
+        return None
+    return (y, x, c, z)
+
+
+def head_masks(rows):
+    lanes = lax.broadcasted_iota(jnp.int32, (rows, 2 * HEAD), 1)
+    return (lanes < HEAD, lanes >= HEAD)
+
+
+def dot_nt(a, b):
+    return lax.dot_general(a, b, (((1,), (1,)), ((), ())), preferred_element_type=F32)
+
+
+def dot_nn(a, b):
+    return lax.dot_general(a, b, (((1,), (0,)), ((), ())), preferred_element_type=F32)
+
+
+def dot_tn(a, b):
+    return lax.dot_general(a, b, (((0,), (0,)), ((), ())), preferred_element_type=F32)
+
+
+def attend_forward_kernel(sc_ref, q_ref, k_ref, v_ref, o_ref, lse_ref, m_ref, l_ref, acc_ref):
+    chunk = q_ref.shape[0] // 2
+    tile = chunk // 2
+    role = sc_ref[0]
+    masks = head_masks(tile)
+
+    def update(state, head, row, key, width, count, diagonal):
+        query = jnp.where(masks[head], q_ref[pl.ds(row, tile), :], 0)
+        scores = dot_nt(query, k_ref[pl.ds(key, width), :])
+        cols = lax.broadcasted_iota(jnp.int32, (tile, width), 1)
+        allowed = cols < count
+        if diagonal is not None:
+            allowed = allowed & (cols <= lax.broadcasted_iota(jnp.int32, (tile, width), 0) + diagonal)
+        scores = jnp.where(allowed, scores, negative)
+        top = jnp.max(scores, axis=1, keepdims=True)
+        if state is None:
+            larger = top
+        else:
+            maximum, total, accum = state
+            larger = jnp.maximum(maximum, top)
+        weights = jnp.exp(scores - larger)
+        part = jnp.sum(weights, axis=1, keepdims=True)
+        mix = dot_nn(weights.astype(BF), v_ref[pl.ds(key, width), :])
+        if state is None:
+            return (larger, part, mix)
+        decay = jnp.exp(maximum - larger)
+        return (larger, total * decay + part, accum * decay + mix)
+
+    for head in range(2):
+        for high in range(2):
+            for half in range(2):
+                row = high * chunk + half * tile
+                state = None
+                if high:
+                    state = update(state, head, row, 0, chunk, sc_ref[1], None)
+                    state = update(state, head, row, 2 * chunk, chunk, sc_ref[3], None)
+                own = high * chunk
+                state = update(state, head, row, own, (half + 1) * tile, sc_ref[1 + high], half * tile)
+                m_ref[head, pl.ds(row, tile), :] = state[0]
+                l_ref[head, pl.ds(row, tile), :] = state[1]
+                acc_ref[head, pl.ds(row, tile), :] = state[2]
+        extra_row = (1 - role) * chunk
+        extra_key = (3 - role) * chunk
+        for half in range(2):
+            row = pl.multiple_of(extra_row + half * tile, tile)
+            key = pl.multiple_of(extra_key, tile)
+            state = (m_ref[head, pl.ds(row, tile), :], l_ref[head, pl.ds(row, tile), :], acc_ref[head, pl.ds(row, tile), :])
+            state = update(state, head, row, key, chunk, sc_ref[5], None)
+            m_ref[head, pl.ds(row, tile), :] = state[0]
+            l_ref[head, pl.ds(row, tile), :] = state[1]
+            acc_ref[head, pl.ds(row, tile), :] = state[2]
+    for part in range(4):
+        rows = pl.ds(part * tile, tile)
+        mixed = [acc_ref[h, rows, :] / l_ref[h, rows, :] for h in range(2)]
+        o_ref[rows, :] = jnp.where(masks[0], mixed[0], mixed[1]).astype(BF)
+        lse = [m_ref[h, rows, :] + jnp.log(l_ref[h, rows, :]) for h in range(2)]
+        turned = jnp.transpose(jnp.where(masks[0], lse[0], lse[1]))
+        lse_ref[0, 0:1, rows] = turned[0:1]
+        lse_ref[0, 1:2, rows] = turned[HEAD : HEAD + 1]
+
+
+def attend_forward(scalars, queries, keys_all, values_all):
+    rows, width = queries.shape
+    slot = keys_all.shape[0]
+    pairs = width // (2 * HEAD)
+    column = lambda i, sc: (0, i)
+    return pl.pallas_call(
+        attend_forward_kernel,
+        out_shape=(
+            jax.ShapeDtypeStruct((rows, width), BF),
+            jax.ShapeDtypeStruct((pairs, 8, rows), F32),
+        ),
+        grid_spec=pltpu.PrefetchScalarGridSpec(
+            num_scalar_prefetch=1,
+            grid=(pairs,),
+            in_specs=[
+                pl.BlockSpec((rows, 2 * HEAD), column),
+                pl.BlockSpec((slot, 2 * HEAD), column),
+                pl.BlockSpec((slot, 2 * HEAD), column),
+            ],
+            out_specs=(
+                pl.BlockSpec((rows, 2 * HEAD), column),
+                pl.BlockSpec((1, 8, rows), lambda i, sc: (i, 0, 0)),
+            ),
+            scratch_shapes=[
+                pltpu.VMEM((2, rows, 1), F32),
+                pltpu.VMEM((2, rows, 1), F32),
+                pltpu.VMEM((2, rows, 2 * HEAD), F32),
+            ],
+        ),
+        compiler_params=pltpu.CompilerParams(vmem_limit_bytes=40 << 20),
+        cost_estimate=pl.CostEstimate(
+            flops=pairs * 2 * 5 * 4 * (rows // 2) ** 2 * HEAD * 2,
+            bytes_accessed=2 * width * (2 * rows + 2 * slot),
+            transcendentals=pairs * 2 * 5 * (rows // 2) ** 2,
+        ),
+    )(scalars, queries, keys_all, values_all)
+
+
+def attend_backward_kernel(sc_ref, q_ref, k_ref, v_ref, o_ref, g_ref, lse_ref, dq_ref, dk_ref, dv_ref, dq_acc, dk_acc, dv_acc, delta_ref):
+    chunk = q_ref.shape[0] // 2
+    tile = chunk // 2
+    role = sc_ref[0]
+    dq_acc[...] = jnp.zeros_like(dq_acc)
+    dk_acc[...] = jnp.zeros_like(dk_acc)
+    dv_acc[...] = jnp.zeros_like(dv_acc)
+    for part in range(4):
+        rows = pl.ds(part * tile, tile)
+        product = jnp.transpose(o_ref[rows, :].astype(F32) * g_ref[rows, :].astype(F32))
+        delta_ref[0:1, rows] = jnp.sum(product[:HEAD], axis=0, keepdims=True)
+        delta_ref[1:2, rows] = jnp.sum(product[HEAD:], axis=0, keepdims=True)
+
+    def step(head, row, width, key, count, shift_rows):
+        rows = pl.ds(row, width)
+        keys = pl.ds(key, tile)
+        query = jnp.where(head_masks(width)[head], q_ref[rows, :], 0)
+        grad = jnp.where(head_masks(width)[head], g_ref[rows, :], 0)
+        key_block = k_ref[keys, :]
+        scores = dot_nt(key_block, query)
+        index = lax.broadcasted_iota(jnp.int32, (tile, width), 0)
+        allowed = index < count
+        if shift_rows is not None:
+            allowed = allowed & (index <= lax.broadcasted_iota(jnp.int32, (tile, width), 1) + shift_rows)
+        probs = jnp.exp(jnp.where(allowed, scores, negative) - lse_ref[0, head : head + 1, rows])
+        grad_probs = dot_nt(v_ref[keys, :], grad)
+        grad_scores = (probs * (grad_probs - delta_ref[head : head + 1, rows])).astype(BF)
+        dv_acc[keys, :] += dot_nn(probs.astype(BF), grad)
+        dk_acc[keys, :] += dot_nn(grad_scores, query)
+        key_masked = jnp.where(head_masks(tile)[head], key_block, 0)
+        dq_acc[rows, :] += dot_tn(grad_scores, key_masked)
+
+    for head in range(2):
+        for half in range(2):
+            low = half * tile
+            for high in range(2):
+                own = high * chunk
+                count = sc_ref[1 + high] - low
+                step(head, own + low, chunk - low, own + low, count, 0)
+            step(head, chunk, chunk, low, sc_ref[1] - low, None)
+            step(head, chunk, chunk, 2 * chunk + low, sc_ref[3] - low, None)
+            extra_row = pl.multiple_of((1 - role) * chunk, chunk)
+            extra_key = pl.multiple_of((3 - role) * chunk + low, tile)
+            step(head, extra_row, chunk, extra_key, sc_ref[5] - low, None)
+    dq_ref[...] = (dq_acc[...] * (1.0 / math.sqrt(HEAD))).astype(BF)
+    dk_ref[...] = dk_acc[...].astype(BF)
+    dv_ref[...] = dv_acc[...].astype(BF)
+
+
+def attend_backward(scalars, queries, keys_all, values_all, mixed, grad_mixed, lse):
+    rows, width = queries.shape
+    slot = keys_all.shape[0]
+    pairs = width // (2 * HEAD)
+    column = lambda i, sc: (0, i)
+    row_spec = pl.BlockSpec((rows, 2 * HEAD), column)
+    slot_spec = pl.BlockSpec((slot, 2 * HEAD), column)
+    return pl.pallas_call(
+        attend_backward_kernel,
+        out_shape=(
+            jax.ShapeDtypeStruct((rows, width), BF),
+            jax.ShapeDtypeStruct((slot, width), BF),
+            jax.ShapeDtypeStruct((slot, width), BF),
+        ),
+        grid_spec=pltpu.PrefetchScalarGridSpec(
+            num_scalar_prefetch=1,
+            grid=(pairs,),
+            in_specs=[row_spec, slot_spec, slot_spec, row_spec, row_spec, pl.BlockSpec((1, 8, rows), lambda i, sc: (i, 0, 0))],
+            out_specs=(row_spec, slot_spec, slot_spec),
+            scratch_shapes=[
+                pltpu.VMEM((rows, 2 * HEAD), F32),
+                pltpu.VMEM((slot, 2 * HEAD), F32),
+                pltpu.VMEM((slot, 2 * HEAD), F32),
+                pltpu.VMEM((8, rows), F32),
+            ],
+        ),
+        compiler_params=pltpu.CompilerParams(vmem_limit_bytes=40 << 20),
+        cost_estimate=pl.CostEstimate(
+            flops=pairs * 2 * 5 * 10 * (rows // 2) ** 2 * HEAD * 2,
+            bytes_accessed=2 * width * (4 * rows + 4 * slot),
+            transcendentals=pairs * 2 * 5 * (rows // 2) ** 2,
+        ),
+    )(scalars, queries, keys_all, values_all, mixed, grad_mixed, lse)
+
+
+def gather_pieces(piece):
+    out = []
+    for k in range(4):
+        own = piece if k == 0 else z_swap(piece, k)
+        x = x_swap(own)
+        y = y_swap(own)
+        diagonal = y_swap(x) if k % 2 == 0 else x_swap(y)
+        out.append(jnp.concatenate([own, x, y, diagonal], axis=1))
+    return out
+
+
+def scatter_pieces(grads):
+    total = None
+    for k in range(4):
+        own, x, y, diagonal = jnp.split(grads[k], 4, axis=1)
+        if k % 2 == 0:
+            x = (x.astype(F32) + y_swap(diagonal.astype(BF)).astype(F32)).astype(BF)
+        else:
+            y = (y.astype(F32) + x_swap(diagonal.astype(BF)).astype(F32)).astype(BF)
+        part = own.astype(F32) + x_swap(x.astype(BF)).astype(F32) + y_swap(y.astype(BF)).astype(F32)
+        total = part if k == 0 else total + z_swap(part.astype(BF), k).astype(F32)
+    return total
+
+
+def on_square(inputs, teacher, lengths, w_qkv, w_out_t, w_gate_up, w_down_t, gains):
+    chunk, model = inputs.shape
+    slot = chunk * 4
+    total_rows = slot * 8
+    dp = lax.axis_index("dp")
+    z = lax.axis_index("tensor")
+    core = dp % 2
+    first = core == 0
+    odd_x = (dp // 2) % 2 == 1
+    odd_y = dp // 4 == 1
+    inner = jnp.where((z == 1) | (z == 2), 1, 0)
+    chunk_low, chunk_high = inner, 3 - inner
+    length = lax.dynamic_index_in_dim(lengths, (dp // 2) * 2 + z // 2, 0, keepdims=False)
+    count = jnp.sum(lengths).astype(F32)
+    places = jnp.stack([chunk_low, chunk_high, 1 - chunk_low, 5 - chunk_high]) * chunk
+    places = places.at[3].set((2 + inner) * chunk)
+    counts = jnp.clip(length - places, 0, chunk)
+    scalars = jnp.concatenate([jnp.stack([inner]), counts, jnp.stack([jnp.where(inner == 0, counts[3], counts[2])])]).astype(jnp.int32)
+
+    def turn(value):
+        a, b, c, d = jnp.split(value, 4, axis=-1)
+        a, b, c, d = jnp.where(odd_x, b, a), jnp.where(odd_x, a, b), jnp.where(odd_x, d, c), jnp.where(odd_x, c, d)
+        return jnp.concatenate([jnp.where(odd_y, c, a), jnp.where(odd_y, d, b), jnp.where(odd_y, a, c), jnp.where(odd_y, b, d)], axis=-1)
+
+    def sort_cores(own, other, axis):
+        return jnp.where(first, jnp.concatenate([own, other], axis=axis), jnp.concatenate([other, own], axis=axis))
+
+    def pick(pair):
+        return jnp.where(first, pair[0], pair[1]), jnp.where(first, pair[1], pair[0])
+
+    def join_rows(partial):
+        return partial[:chunk] + core_swap(partial[chunk:].astype(BF)).astype(F32)
+
+    def core_piece(stacked):
+        keep, give = pick(jnp.split(stacked, 2, axis=2))
+        return sort_cores(keep, core_swap(give), 1)
+
+    attention_piece = core_piece(jnp.concatenate([jnp.swapaxes(w_qkv, 0, 1), w_out_t[None]], axis=0))
+    feed_piece = core_piece(jnp.concatenate([jnp.swapaxes(w_gate_up, 0, 1), w_down_t[None]], axis=0))
+    gains_pair = sort_cores(gains, core_swap(gains), 0)
+    gains_x = x_swap(gains_pair)
+    gains_all = jnp.concatenate([gains_pair, gains_x, y_swap(gains_pair), y_swap(gains_x)], axis=0)
+    gain_one = gains_all[:, 0].astype(F32)
+    gain_two = gains_all[:, 1].astype(F32)
+
+    inputs_rel = turn(inputs)
+    own_rows = home_swap(inputs_rel)
+    partner_rows = shift(inputs_rel, partner_of_home)
+    other_rows = core_swap(own_rows)
+    other_partner = core_swap(partner_rows)
+    attention_w = jnp.concatenate(gather_pieces(attention_piece), axis=2)
+    feed_w = jnp.concatenate(gather_pieces(feed_piece), axis=2)
+    w_queries, w_keys, w_values, w_out = attention_w[0], attention_w[1], attention_w[2], attention_w[3]
+    w_gate, w_up, w_down = feed_w[0], feed_w[1], feed_w[2]
+
+    low, high = pick((own_rows, other_rows))
+    low_partner, high_partner = pick((partner_rows, other_partner))
+    rows_all = jnp.concatenate([low, high, low_partner, high_partner], axis=0).astype(F32)
+    scaled_all, _ = norm_forward(rows_all)
+    normed_all = (scaled_all * gain_one).astype(BF)
+    normed_own = normed_all[: 2 * chunk]
+    rows = own_rows.astype(F32)
+
+    def matmul(a, b):
+        return jnp.einsum("ab,bc->ac", a, b, preferred_element_type=F32)
+
+    def matmul_nt(a, b):
+        return jnp.einsum("ab,cb->ac", a, b, preferred_element_type=F32)
+
+    def matmul_tn(a, b):
+        return jnp.einsum("ba,bc->ac", a, b, preferred_element_type=F32)
+
+    queries = (matmul(normed_own, w_queries) * (1.0 / math.sqrt(HEAD))).astype(BF)
+    keys_all = matmul(normed_all, w_keys).astype(BF)
+    values_all = matmul(normed_all, w_values).astype(BF)
+    mixed, lse = attend_forward(scalars, queries, keys_all, values_all)
+    branch = matmul_nt(mixed, w_out)
+    keep, give = pick((branch[:chunk], branch[chunk:]))
+    middle = rows + keep + core_swap(give.astype(BF)).astype(F32)
+
+    scaled_two, inverse_two = norm_forward(middle)
+    normed_two = (scaled_two * gain_two).astype(BF)
+    normed_two_all = jnp.concatenate([normed_two, core_swap(normed_two)], axis=0)
+    gate = matmul(normed_two_all, w_gate)
+    upper = matmul(normed_two_all, w_up)
+    sigmoid = jax.nn.sigmoid(gate)
+    hidden = (gate * sigmoid * upper).astype(BF)
+    final = middle + join_rows(matmul_nt(hidden, w_down))
+    output = home_swap(turn(final.astype(BF)))
+
+    teacher_rows = home_swap(turn(teacher)).astype(F32)
+    own_place = jnp.where(first, chunk_low, chunk_high) * chunk
+    valid = (own_place + jnp.arange(chunk, dtype=jnp.int32) < length)[:, None]
+    grad_final = jnp.where(valid, final - teacher_rows, 0.0) * (total_rows / count)
+    grad_feed = grad_final.astype(BF)
+    grad_feed_all = jnp.concatenate([grad_feed, core_swap(grad_feed)], axis=0)
+    grad_hidden = matmul(grad_feed_all, w_down)
+    grad_gate = (grad_hidden * upper * (sigmoid * (1.0 + gate * (1.0 - sigmoid)))).astype(BF)
+    grad_upper = (grad_hidden * (gate * sigmoid)).astype(BF)
+    grad_normed_two = join_rows(matmul_nt(grad_gate, w_gate) + matmul_nt(grad_upper, w_up))
+    grad_down = matmul_tn(grad_feed_all, hidden).astype(BF)
+    grad_w_gate = matmul_tn(normed_two_all, grad_gate).astype(BF)
+    grad_w_up = matmul_tn(normed_two_all, grad_upper).astype(BF)
+    feed_grads = [
+        jnp.stack([g[:, k * (g.shape[1] // 4) : (k + 1) * (g.shape[1] // 4)] for g in (grad_w_gate, grad_w_up, grad_down)])
+        for k in range(4)
+    ]
+    feed_total = scatter_pieces(feed_grads)
+
+    grad_norm_two, grad_gain_two = norm_backward(grad_normed_two, scaled_two, inverse_two, gain_two)
+    grad_middle = grad_final + grad_norm_two
+    grad_branch = grad_middle.astype(BF)
+    grad_branch_both = sort_cores(grad_branch, core_swap(grad_branch), 0)
+    grad_mixed = matmul(grad_branch_both, w_out).astype(BF)
+    grad_out = matmul_tn(grad_branch_both, mixed).astype(BF)
+    grad_queries, grad_keys, grad_values = attend_backward(scalars, queries, keys_all, values_all, mixed, grad_mixed, lse)
+
+    part_all = matmul_nt(grad_keys, w_keys) + matmul_nt(grad_values, w_values)
+    part_own = part_all[: 2 * chunk] + matmul_nt(grad_queries, w_queries)
+    part_partner = part_all[2 * chunk :]
+    keep_own, give_own = pick((part_own[:chunk], part_own[chunk:]))
+    keep_partner, give_partner = pick((part_partner[:chunk], part_partner[chunk:]))
+    for_partner = keep_partner + core_swap(give_partner.astype(BF)).astype(F32)
+    grad_normed_one = (
+        keep_own + core_swap(give_own.astype(BF)).astype(F32) + z_swap(for_partner.astype(BF), 1).astype(F32)
+    )
+    scaled_one, inverse_one = norm_forward(rows)
+    grad_norm_one, grad_gain_one = norm_backward(grad_normed_one, scaled_one, inverse_one, gain_one)
+    grad_inputs = home_swap(turn((grad_middle + grad_norm_one).astype(BF))).astype(F32)
+
+    grad_w_queries = matmul_tn(normed_own, grad_queries).astype(BF)
+    grad_w_keys = matmul_tn(normed_all, grad_keys).astype(BF)
+    grad_w_values = matmul_tn(normed_all, grad_values).astype(BF)
+    attention_grads = [
+        jnp.stack([g[:, k * (g.shape[1] // 4) : (k + 1) * (g.shape[1] // 4)] for g in (grad_w_queries, grad_w_keys, grad_w_values, grad_out)])
+        for k in range(4)
+    ]
+    attention_total = scatter_pieces(attention_grads)
+
+    def to_home(total):
+        keep, give = pick(jnp.split(total, 2, axis=1))
+        return sort_cores(keep, core_swap(give.astype(BF)).astype(F32), 2)
+
+    attention_out = to_home(attention_total)
+    feed_out = to_home(feed_total)
+
+    both = jnp.stack([grad_gain_one, grad_gain_two], axis=0)
+    quarter = model // 4
+    a, b, c, d = jnp.split(both, 4, axis=1)
+    sent = x_swap(jnp.concatenate([b, d], axis=1))
+    a, c = a + sent[:, :quarter], c + sent[:, quarter:]
+    a = a + y_swap(c)
+    keep, give = pick(jnp.split(a, 2, axis=1))
+    a = keep + core_swap(give)
+    size = a.shape[1] // 4
+    total = lax.dynamic_slice_in_dim(a, z * size, size, 1)
+    for k in range(1, 4):
+        total = total + z_swap(lax.dynamic_slice_in_dim(a, (z ^ k) * size, size, 1), k)
+    grad_gains = jnp.swapaxes(total, 0, 1)
+
+    return (
+        output,
+        grad_inputs,
+        jnp.swapaxes(attention_out[:3], 0, 1),
+        attention_out[3],
+        jnp.swapaxes(feed_out[:2], 0, 1),
+        feed_out[2],
+        grad_gains,
+    )
+
+
 def solution(mesh):
+    square = dict(mesh.shape) == {"dp": 8, "tensor": 4}
     return jax.shard_map(
-        on_device,
+        on_square if square else on_device,
         mesh=mesh,
         in_specs=(
             P(("dp", "tensor"), None),

time: 1240 us -> 716 us (0.58)
  waiting for transfers between devices: 832 us -> 271 us
  starting transfers between devices: 1.83 us -> 166 us
  matrix products: 230 us -> 99.7 us
  Pallas kernels: 0 us -> 63.7 us
  blocking collectives: 22.4 us -> 0 us
  local copies, waits for them, and re-layouts: 43.4 us -> 23.3 us
    reduce_scatter x8 -> x0, waiting for transfers between devices: 355 us -> none  [the longest x1 77.2 us: on_device(): lax.psum_scatter(jnp.einsum('rcf,dcf->rd', piece, qkv_all, preferred_elem...]
    all_gather x7 -> x0, waiting for transfers between devices: 345 us -> none  [the longest x1 82.9 us: on_device(): gathered_one = lax.all_gather(normed_one, 'tensor', axis=0, tiled=True)]
    ppermute x0 -> x90, waiting for transfers between devices: none -> 271 us  [shift(): return lax.ppermute(value, AXES, pairs)]
    ppermute x0 -> x90, starting transfers between devices: none -> 166 us  [shift(): return lax.ppermute(value, AXES, pairs)]
    unnamed x17 -> x0, waiting for transfers between devices: 132 us -> none
    dot_general x102 -> x21, matrix products: 230 us -> 99.7 us  [the longest x7 42.8 us: matmul(): return jnp.einsum('ab,bc->ac', a, b, preferred_element_type=F32)]
    pallas_call x0 -> x2, Pallas kernels: none -> 63.7 us  [the longest x1 32.5 us: attend_backward(): pl.pallas_call(attend_backward_kernel, out_shape=(jax.ShapeDtypeStruct((r...]
    concatenate x0 -> x9, other arithmetic: none -> 39.3 us  [the longest x1 33.8 us: on_square(): feed_w = jnp.concatenate(gather_pieces(feed_piece), axis=2)]
  transfers between devices with their start and end apart: 16 -> 90, of which waited for: 14 -> 38; matrix products, arithmetic and copies ran while one was open for 18% -> 23% of each run, Pallas kernels for 0% -> 9%
where the time goes in v1:
time: 716 us; the launch traced here: 712 us
  waiting for transfers between devices  271 us (38%)
  starting transfers between devices  166 us (23%)
  matrix products  99.7 us (14%)
  other arithmetic  84.3 us (12%)
  Pallas kernels  63.7 us (9%)
  local copies, waits for them, and re-layouts  23.3 us (3%)
    ppermute x90, waiting for transfers between devices, shift(): return lax.ppermute(value, AXES, pairs)  271 us
    ppermute x90, starting transfers between devices, shift(): return lax.ppermute(value, AXES, pairs)  166 us
    dot_general x7, matrix products, matmul(): return jnp.einsum('ab,bc->ac', a, b, preferred_element_type=F32)  42.8 us
    concatenate x1, other arithmetic, on_square(): feed_w = jnp.concatenate(gather_pieces(feed_piece), axis=2)  33.8 us
    pallas_call x1, Pallas kernels, attend_backward(): pl.pallas_call(attend_backward_kernel, out_shape=(jax.ShapeDtypeStruct((r...  32.5 us
    pallas_call x1, Pallas kernels, attend_forward(): pl.pallas_call(attend_forward_kernel, out_shape=(jax.ShapeDtypeStruct((ro...  31.2 us
    dot_general x7, matrix products, matmul_tn(): return jnp.einsum('ba,bc->ac', a, b, preferred_element_type=F32)  30.6 us
    dot_general x7, matrix products, matmul_nt(): return jnp.einsum('ab,cb->ac', a, b, preferred_element_type=F32)  26.3 us
  transfers between devices with their start and end apart: 90, of which 38 were waited for; matrix products, arithmetic and copies ran while one was open for 23% of the time, Pallas kernels for 9%

profile of v1, /device:TPU:0, one launch (start us, length us, event | category | flops | bytes accessed | tf_op | source)
XLA Modules:
  0.0 712.2 jit_solution(12607571428499310045)
XLA Ops:
  4.5 3.0 collective-permute-start.12
  7.4 2.6 collective-permute-start.16
  24.9 4.0 collective-permute-done.20
  31.5 7.0 collective-permute-start.2
  44.1 3.8 collective-permute-done.17
  51.1 4.1 collective-permute-done.11
  62.3 2.3 collective-permute-done.21
  65.6 4.6 collective-permute-done.15
  70.2 4.8 collective-permute-done.23
  75.6 3.0 maximum_maximum_fusion.1
  79.1 23.1 %collective-permute-done.30 = bf16[3,256,512]{2,1,0:T(8,128)(2,1)S(1)} collective-permute-done((bf16[3,256,512]{2,1,0:T(8,128)(2,1)S(1)}, bf16[3,256,512]{2,1,0:T(8,128)(2,1)S(1)}, u32[]{:S(2)}, u32[]{:S(2)}) %collective-permute-start.30) | collective-permute-done | bytes 786464 | tf_op jit(solution)/shard_map/ppermute | solution.py:309
  105.4 11.2 %fusion.2 = bf16[2048,1024]{1,0:T(8,128)(2,1)S(1)} fusion(f32[1024]{0:T(1024)S(1)} %bitcast.141, f32[2048]{0:T(1024)S(1)} %add_rsqrt_fusion, bf16[512,1024]{1,0:T(8,128)(2,1)S(1)} %get-tuple-element.71, bf16[512,1024]{1,0:T(8,128)(2,1)S(1)} %get-tuple-element.70, bf16[512,1024]{1,0:T(8,128)(2,1)S(1)} %get-tuple-element.69, ...), kind=kLoop, calls=%fused_computation.5 | loop fusion | flops 23068672 | bytes 8400896 | tf_op jit(solution)/shard_map/convert_element_type | solution.py:629
  116.6 2.5 convolution_convert_fusion.3.v_ref
  119.1 2.5 convolution_convert_fusion.4.k_ref
  122.9 31.2 %shard_map.135 = (bf16[1024,512]{1,0:T(8,128)(2,1)S(1)}, f32[4,8,1024]{2,1,0:T(8,128)S(1)}) custom-call(s32[6]{0:T(128)S(1)} %pad_add_fusion.sc_ref, bf16[1024,512]{1,0:T(8,128)(2,1)S(1)} %multiply_convert_fusion.4.q_ref, bf16[2048,512]{1,0:T(8,128)(2,1)S(1)} %convolution_convert_fusion.4.k_ref, bf16[2048,512]{1,0:T(8,128)(2,1)S(1)} %convolution_convert_fusion.3.v_ref), custom_call_target="tpu_custom_call" | custom-call | flops 5368709120 | bytes 6291456 | tf_op jit(solution)/shard_map/pallas_call | solution.py:429
  155.8 2.8 collective-permute-start.35
  161.9 15.0 %collective-permute-done.35 = bf16[3,256,512]{2,1,0:T(8,128)(2,1)S(1)} collective-permute-done((bf16[3,256,512]{2,1,0:T(8,128)(2,1)S(1)}, bf16[3,256,512]{2,1,0:T(8,128)(2,1)S(1)}, u32[]{:S(2)}, u32[]{:S(2)}) %collective-permute-start.35) | collective-permute-done | bytes 786464 | tf_op jit(solution)/shard_map/ppermute | solution.py:309
  179.0 16.8 %collective-permute-done.29 = bf16[3,256,512]{2,1,0:T(8,128)(2,1)S(1)} collective-permute-done((bf16[3,256,512]{2,1,0:T(8,128)(2,1)S(1)}, bf16[3,256,512]{2,1,0:T(8,128)(2,1)S(1)}, u32[]{:S(2)}, u32[]{:S(2)}) %collective-permute-start.29) | collective-permute-done | bytes 786464 | tf_op jit(solution)/shard_map/ppermute | solution.py:309
  200.0 12.7 %collective-permute-done.36 = bf16[3,256,512]{2,1,0:T(8,128)(2,1)S(1)} collective-permute-done((bf16[3,256,512]{2,1,0:T(8,128)(2,1)S(1)}, bf16[3,256,512]{2,1,0:T(8,128)(2,1)S(1)}, u32[]{:S(2)}, u32[]{:S(2)}) %collective-permute-start.36) | collective-permute-done | bytes 786464 | tf_op jit(solution)/shard_map/ppermute | solution.py:309
  214.5 30.2 %collective-permute-start.25 = (bf16[512,1024]{1,0:T(8,128)(2,1)}, bf16[512,1024]{1,0:T(8,128)(2,1)}, u32[]{:S(2)}, u32[]{:S(2)}) collective-permute-start(bf16[512,1024]{1,0:T(8,128)(2,1)} %multiply_convert_fusion.3), channel_id=1, source_target_pairs={{0,4},{1,5},{2,6},{3,7},{4,0},{5,1},{6,2},{7,3},{8,12},{9,13},{10,... | collective-permute-start | bytes 3145736 | tf_op jit(solution)/shard_map/ppermute | solution.py:309
  246.5 33.8 %maximum_maximum_fusion = bf16[3,1024,2048]{2,1,0:T(8,128)(2,1)S(1)} fusion(bf16[3,256,512]{2,1,0:T(8,128)(2,1)} %collective-permute-done.41, bf16[3,256,512]{2,1,0:T(8,128)(2,1)} %copy-done.37, bf16[3,256,512]{2,1,0:T(8,128)(2,1)} %copy-done.41, bf16[3,256,512]{2,1,0:T(8,128)(2,1)} %copy-done.32, bf16[3,256,512]{2,1,0:T(8,128)(2,1)} %copy-done.43, ...), kind=kLoop, calls=%fused_computation | loop fusion | flops 201326592 | bytes 25165824 | tf_op jit(solution)/shard_map/concatenate | solution.py:621
  280.3 9.9 %fusion.5 = f32[1024,2048]{1,0:T(8,128)} fusion(bf16[3,1024,2048]{2,1,0:T(8,128)(2,1)S(1)} %maximum_maximum_fusion, bf16[512,1024]{1,0:T(8,128)(2,1)} %collective-permute-done.25, bf16[512,1024]{1,0:T(8,128)(2,1)} %multiply_convert_fusion.3), kind=kOutput, calls=%fused_computation.22 | convolution fusion | flops 4299161600 | bytes 14680064 | tf_op jit(solution)/shard_map/ab,bc->ac/dot_general | solution.py:634
  290.2 10.3 %multiply_convert_fusion.2 = (bf16[1024,2048]{1,0:T(8,128)(2,1)S(1)}, f32[1024,2048]{1,0:T(8,128)}) fusion(f32[1024,2048]{1,0:T(8,128)} %fusion.5, bf16[3,1024,2048]{2,1,0:T(8,128)(2,1)S(1)} %maximum_maximum_fusion, bf16[512,1024]{1,0:T(8,128)(2,1)} %collective-permute-done.25, bf16[512,1024]{1,0:T(8,128)(2,1)} %multiply_convert_fusion.3), kind=kOutput, calls=%fused_computation.8 | convolution fusion | flops 4311744512 | bytes 27262976 | tf_op jit(solution)/shard_map/ab,bc->ac/dot_general | solution.py:634
  300.6 4.5 fusion.9
  311.3 3.4 fusion.32
  315.4 2.3 collective-permute-done.45
  317.7 13.4 %multiply_convert_fusion.1 = (bf16[1024,2048]{1,0:T(8,128)(2,1)}, bf16[1024,2048]{1,0:T(8,128)(2,1)S(1)}) fusion(f32[1024,2048]{1,0:T(8,128)} %fusion.5, f32[1024,2048]{1,0:T(8,128)} %get-tuple-element.127, bf16[3,1024,2048]{2,1,0:T(8,128)(2,1)} %copy-done.12, bf16[512,1024]{1,0:T(8,128)(2,1)} %collective-permute-done.45, bf16[512,1024]{1,0:T(8,128)(2,1)} %fusion.32), kind=kOutput, calls=%fused_computation.7 | convolution fusion | flops 4326424576 | bytes 31457280 | tf_op jit(solution)/shard_map/ab,bc->ac/dot_general | solution.py:634
  331.1 6.6 fusion.6
  337.6 6.6 fusion.22
  344.7 6.4 convolution_convert_fusion.2
  351.4 6.4 convolution_convert_fusion.1
  360.0 6.6 convolution_convert_fusion
  374.1 14.7 %collective-permute-done.68 = bf16[3,256,512]{2,1,0:T(8,128)(2,1)S(1)} collective-permute-done((bf16[3,256,512]{2,1,0:T(8,128)(2,1)S(1)}, bf16[3,256,512]{2,1,0:T(8,128)(2,1)S(1)}, u32[]{:S(2)}, u32[]{:S(2)}) %collective-permute-start.68) | collective-permute-done | bytes 786464 | tf_op jit(solution)/shard_map/ppermute | solution.py:309
  392.1 13.5 %collective-permute-done.75 = bf16[3,256,512]{2,1,0:T(8,128)(2,1)S(1)} collective-permute-done((bf16[3,256,512]{2,1,0:T(8,128)(2,1)S(1)}, bf16[3,256,512]{2,1,0:T(8,128)(2,1)S(1)}, u32[]{:S(2)}, u32[]{:S(2)}) %collective-permute-start.75) | collective-permute-done | bytes 786464 | tf_op jit(solution)/shard_map/ppermute | solution.py:309
  407.9 15.3 %collective-permute-done.80 = bf16[3,256,512]{2,1,0:T(8,128)(2,1)S(1)} collective-permute-done((bf16[3,256,512]{2,1,0:T(8,128)(2,1)S(1)}, bf16[3,256,512]{2,1,0:T(8,128)(2,1)S(1)}, u32[]{:S(2)}, u32[]{:S(2)}) %collective-permute-start.80) | collective-permute-done | bytes 786464 | tf_op jit(solution)/shard_map/ppermute | solution.py:309
  428.1 3.5 fusion.47
  431.8 11.8 %collective-permute-done.73 = bf16[3,256,512]{2,1,0:T(8,128)(2,1)S(1)} collective-permute-done((bf16[3,256,512]{2,1,0:T(8,128)(2,1)S(1)}, bf16[3,256,512]{2,1,0:T(8,128)(2,1)S(1)}, u32[]{:S(2)}, u32[]{:S(2)}) %collective-permute-start.73) | collective-permute-done | bytes 786464 | tf_op jit(solution)/shard_map/ppermute | solution.py:309
  446.9 9.5 %collective-permute-done.76 = bf16[3,256,512]{2,1,0:T(8,128)(2,1)S(1)} collective-permute-done((bf16[3,256,512]{2,1,0:T(8,128)(2,1)S(1)}, bf16[3,256,512]{2,1,0:T(8,128)(2,1)S(1)}, u32[]{:S(2)}, u32[]{:S(2)}) %collective-permute-start.76) | collective-permute-done | bytes 786464 | tf_op jit(solution)/shard_map/ppermute | solution.py:309
  458.3 2.1 collective-permute-done.81
  461.7 3.0 convolution_convert_fusion.6.g_ref
  465.2 32.5 %shard_map.136 = (bf16[1024,512]{1,0:T(8,128)(2,1)S(1)}, bf16[2048,512]{1,0:T(8,128)(2,1)S(1)}, bf16[2048,512]{1,0:T(8,128)(2,1)S(1)}) custom-call(s32[6]{0:T(128)S(1)} %copy-done.1, bf16[1024,512]{1,0:T(8,128)(2,1)S(1)} %copy-done.9, bf16[2048,512]{1,0:T(8,128)(2,1)S(1)} %copy-done.7, bf16[2048,512]{1,0:T(8,128)(2,1)S(1)} %copy-done.5, ...), custom_call_target="tpu_custom_call" | custom-call | flops 13421772800 | bytes 12582912 | tf_op jit(solution)/shard_map/pallas_call | solution.py:518
  497.7 3.7 fusion.33
  501.4 3.4 convolution_convert_fusion.7
  504.8 3.4 convolution_convert_fusion.8
  508.3 2.3 convolution_add_fusion
  510.6 2.9 convolution_convert_fusion.5
  524.4 29.5 %collective-permute-start.74 = (bf16[3,256,512]{2,1,0:T(8,128)(2,1)S(1)}, bf16[3,256,512]{2,1,0:T(8,128)(2,1)S(1)}, u32[]{:S(2)}, u32[]{:S(2)}) collective-permute-start(bf16[3,256,512]{2,1,0:T(8,128)(2,1)S(1)} %copy-done.45), channel_id=1, source_target_pairs={{0,1},{1,0},{2,3},{3,2},{4,5},{5,4},{6,7},{7,6},{8,9},{9,8},{10,11... | collective-permute-start | bytes 2359304 | tf_op jit(solution)/shard_map/ppermute | solution.py:309
  553.8 3.2 collective-permute-start.78
  557.0 5.0 collective-permute-start.82
  562.7 25.0 %collective-permute-done.74 = bf16[3,256,512]{2,1,0:T(8,128)(2,1)S(1)} collective-permute-done((bf16[3,256,512]{2,1,0:T(8,128)(2,1)S(1)}, bf16[3,256,512]{2,1,0:T(8,128)(2,1)S(1)}, u32[]{:S(2)}, u32[]{:S(2)}) %collective-permute-start.74) | collective-permute-done | bytes 786464 | tf_op jit(solution)/shard_map/ppermute | solution.py:309
  587.7 21.4 %collective-permute-done.78 = bf16[3,256,512]{2,1,0:T(8,128)(2,1)S(1)} collective-permute-done((bf16[3,256,512]{2,1,0:T(8,128)(2,1)S(1)}, bf16[3,256,512]{2,1,0:T(8,128)(2,1)S(1)}, u32[]{:S(2)}, u32[]{:S(2)}) %collective-permute-start.78) | collective-permute-done | bytes 786464 | tf_op jit(solution)/shard_map/ppermute | solution.py:309
  613.5 4.9 collective-permute-done.57
  618.5 2.1 collective-permute-start.54
  621.4 3.3 collective-permute-done.65
  624.7 12.3 %collective-permute-start.58 = (bf16[4,256,128]{1,2,0:T(8,128)(2,1)S(1)}, bf16[4,256,128]{1,2,0:T(8,128)(2,1)S(1)}, u32[]{:S(2)}, u32[]{:S(2)}) collective-permute-start(bf16[4,256,128]{1,2,0:T(8,128)(2,1)S(1)} %add_convert_fusion.12), channel_id=1, source_target_pairs={{0,1},{1,0},{2,3},{3,2},{4,5},{5,4},{6,7},{7,6},{8,9},{9,8},{10,11... | collective-permute-start | bytes 786440 | tf_op jit(solution)/shard_map/ppermute | solution.py:309
  639.5 2.4 collective-permute-start.66
  644.7 2.9 collective-permute-done.58
  647.6 7.9 %collective-permute-done.62 = bf16[4,256,128]{1,2,0:T(8,128)(2,1)S(1)} collective-permute-done((bf16[4,256,128]{1,2,0:T(8,128)(2,1)S(1)}, bf16[4,256,128]{1,2,0:T(8,128)(2,1)S(1)}, u32[]{:S(2)}, u32[]{:S(2)}) %collective-permute-start.62) | collective-permute-done | bytes 262176 | tf_op jit(solution)/shard_map/ppermute | solution.py:309
  657.7 16.9 %collective-permute-done.50 = bf16[512,1024]{1,0:T(8,128)(2,1)S(1)} collective-permute-done((bf16[512,1024]{1,0:T(8,128)(2,1)S(1)}, bf16[512,1024]{1,0:T(8,128)(2,1)S(1)}, u32[]{:S(2)}, u32[]{:S(2)}) %collective-permute-start.50) | collective-permute-done | bytes 1048608 | tf_op jit(solution)/shard_map/ppermute | solution.py:309
  677.1 2.2 collective-permute-done.84
  679.3 2.2 collective-permute-start.85
  683.1 2.2 collective-permute-start.86
  687.3 3.3 collective-permute-start.89
  693.8 14.3 %collective-permute-done.88 = f32[2,32]{1,0:T(2,128)} collective-permute-done((f32[2,32]{1,0:T(2,128)S(1)}, f32[2,32]{1,0:T(2,128)}, u32[]{:S(2)}, u32[]{:S(2)}) %collective-permute-start.88) | collective-permute-done | bytes 288 | tf_op jit(solution)/shard_map/ppermute | solution.py:309
  (368 shorter events, 128.0 us)
Async XLA Ops:
  4.5 16.8 %collective-permute-start.12 = (bf16[4,256,128]{1,2,0:T(8,128)(2,1)S(1)}, bf16[4,256,128]{1,2,0:T(8,128)(2,1)S(1)}, u32[]{:S(2)}, u32[]{:S(2)}) collective-permute-start(bf16[4,256,128]{1,2,0:T(8,128)(2,1)S(1)} %maximum_select_fusion.6), channel_id=1, source_target_pairs={{0,1},{1,0},{2,3},{3,2},{4,5},{5,4},{6,7},{7,6},{8,9},{9,8},{10,11... | collective-permute-start | bytes 786440 | tf_op jit(solution)/shard_map/ppermute | solution.py:309
  7.4 14.7 %collective-permute-start.16 = (bf16[4,256,128]{1,2,0:T(8,128)(2,1)S(1)}, bf16[4,256,128]{1,2,0:T(8,128)(2,1)S(1)}, u32[]{:S(2)}, u32[]{:S(2)}) collective-permute-start(bf16[4,256,128]{1,2,0:T(8,128)(2,1)S(1)} %maximum_select_fusion.6), channel_id=1, source_target_pairs={{0,2},{1,3},{2,0},{3,1},{4,6},{5,7},{6,4},{7,5},{8,10},{9,11},{10,... | collective-permute-start | bytes 786440 | tf_op jit(solution)/shard_map/ppermute | solution.py:309
  15.4 24.6 %collective-permute-start.26 = (bf16[3,128,512]{2,1,0:T(8,128)(2,1)}, bf16[3,128,512]{2,1,0:T(8,128)(2,1)S(1)}, u32[]{:S(2)}, u32[]{:S(2)}) collective-permute-start(bf16[3,128,512]{2,1,0:T(8,128)(2,1)} %get-tuple-element.114), channel_id=1, source_target_pairs={{0,4},{1,5},{2,6},{3,7},{4,0},{5,1},{6,2},{7,3},{8,12},{9,13},{10,... | collective-permute-start | bytes 1179656 | tf_op jit(solution)/shard_map/ppermute | solution.py:309
  21.2 17.3 %collective-permute-start.10 = (bf16[4,256,128]{1,2,0:T(8,128)(2,1)S(1)}, bf16[4,256,128]{1,2,0:T(8,128)(2,1)}, u32[]{:S(2)}, u32[]{:S(2)}) collective-permute-start(bf16[4,256,128]{1,2,0:T(8,128)(2,1)S(1)} %maximum_select_fusion.6), channel_id=1, source_target_pairs={{0,16},{1,17},{2,18},{3,19},{4,20},{5,21},{6,22},{7,23},{8,24},{9,... | collective-permute-start | bytes 786440 | tf_op jit(solution)/shard_map/ppermute | solution.py:309
  22.2 19.4 %collective-permute-start.14 = (bf16[4,256,128]{1,2,0:T(8,128)(2,1)S(1)}, bf16[4,256,128]{1,2,0:T(8,128)(2,1)}, u32[]{:S(2)}, u32[]{:S(2)}) collective-permute-start(bf16[4,256,128]{1,2,0:T(8,128)(2,1)S(1)} %collective-permute-done.12), channel_id=1, source_target_pairs={{0,16},{1,17},{2,18},{3,19},{4,20},{5,21},{6,22},{7,23},{8,24},{9,... | collective-permute-start | bytes 786440 | tf_op jit(solution)/shard_map/ppermute | solution.py:309
  28.9 46.1 %collective-permute-start = (bf16[512,1024]{1,0:T(8,128)(2,1)}, bf16[512,1024]{1,0:T(8,128)(2,1)S(1)}, u32[]{:S(2)}, u32[]{:S(2)}) collective-permute-start(bf16[512,1024]{1,0:T(8,128)(2,1)} %pad_maximum_fusion.9), channel_id=1, source_target_pairs={{0,0},{1,1},{2,5},{3,4},{4,3},{5,2},{6,6},{7,7},{8,8},{9,9},{10,13... | collective-permute-start | bytes 3145736 | tf_op jit(solution)/shard_map/ppermute | solution.py:309
  31.5 43.6 %collective-permute-start.2 = (bf16[512,1024]{1,0:T(8,128)(2,1)}, bf16[512,1024]{1,0:T(8,128)(2,1)S(1)}, u32[]{:S(2)}, u32[]{:S(2)}) collective-permute-start(bf16[512,1024]{1,0:T(8,128)(2,1)} %pad_maximum_fusion.9), channel_id=1, source_target_pairs={{0,1},{1,0},{2,4},{4,2},{5,3},{6,7},{8,9},{9,8},{10,12},{12,10},{1... | collective-permute-start | bytes 3145736 | tf_op jit(solution)/shard_map/ppermute | solution.py:309
  41.6 13.6 %collective-permute-start.11 = (bf16[4,256,128]{1,2,0:T(8,128)(2,1)}, bf16[4,256,128]{1,2,0:T(8,128)(2,1)}, u32[]{:S(2)}, u32[]{:S(2)}) collective-permute-start(bf16[4,256,128]{1,2,0:T(8,128)(2,1)} %copy-done.49), channel_id=1, source_target_pairs={{0,16},{1,17},{2,18},{3,19},{4,20},{5,21},{6,22},{7,23},{8,24},{9,... | collective-permute-start | bytes 786440 | tf_op jit(solution)/shard_map/ppermute | solution.py:309
  49.5 11.2 %collective-permute-start.18 = (bf16[4,256,128]{1,2,0:T(8,128)(2,1)}, bf16[4,256,128]{1,2,0:T(8,128)(2,1)}, u32[]{:S(2)}, u32[]{:S(2)}) collective-permute-start(bf16[4,256,128]{1,2,0:T(8,128)(2,1)} %copy-done.48), channel_id=1, source_target_pairs={{0,16},{1,17},{2,18},{3,19},{4,20},{5,21},{6,22},{7,23},{8,24},{9,... | collective-permute-start | bytes 786440 | tf_op jit(solution)/shard_map/ppermute | solution.py:309
  57.7 12.4 %collective-permute-start.15 = (bf16[4,256,128]{1,2,0:T(8,128)(2,1)}, bf16[4,256,128]{1,2,0:T(8,128)(2,1)S(1)}, u32[]{:S(2)}, u32[]{:S(2)}) collective-permute-start(bf16[4,256,128]{1,2,0:T(8,128)(2,1)} %collective-permute-done.14), channel_id=1, source_target_pairs={{0,8},{1,9},{2,10},{3,11},{4,12},{5,13},{6,14},{7,15},{8,0},{9,1},... | collective-permute-start | bytes 786440 | tf_op jit(solution)/shard_map/ppermute | solution.py:309
  70.1 32.1 %collective-permute-start.30 = (bf16[3,256,512]{2,1,0:T(8,128)(2,1)S(1)}, bf16[3,256,512]{2,1,0:T(8,128)(2,1)S(1)}, u32[]{:S(2)}, u32[]{:S(2)}) collective-permute-start(bf16[3,256,512]{2,1,0:T(8,128)(2,1)S(1)} %maximum_select_fusion.2), channel_id=1, source_target_pairs={{0,1},{1,0},{2,3},{3,2},{4,5},{5,4},{6,7},{7,6},{8,9},{9,8},{10,11... | collective-permute-start | bytes 2359304 | tf_op jit(solution)/shard_map/ppermute | solution.py:309
  70.2 85.4 %collective-permute-start.34 = (bf16[3,256,512]{2,1,0:T(8,128)(2,1)S(1)}, bf16[3,256,512]{2,1,0:T(8,128)(2,1)S(1)}, u32[]{:S(2)}, u32[]{:S(2)}) collective-permute-start(bf16[3,256,512]{2,1,0:T(8,128)(2,1)S(1)} %maximum_select_fusion.2), channel_id=1, source_target_pairs={{0,2},{1,3},{2,0},{3,1},{4,6},{5,7},{6,4},{7,5},{8,10},{9,11},{10,... | collective-permute-start | bytes 2359304 | tf_op jit(solution)/shard_map/ppermute | solution.py:309
  75.0 80.8 %collective-permute-start.38 = (bf16[3,256,512]{2,1,0:T(8,128)(2,1)S(1)}, bf16[3,256,512]{2,1,0:T(8,128)(2,1)S(1)}, u32[]{:S(2)}, u32[]{:S(2)}) collective-permute-start(bf16[3,256,512]{2,1,0:T(8,128)(2,1)S(1)} %maximum_select_fusion.2), channel_id=1, source_target_pairs={{0,3},{1,2},{2,1},{3,0},{4,7},{5,6},{6,5},{7,4},{8,11},{9,10},{10,... | collective-permute-start | bytes 2359304 | tf_op jit(solution)/shard_map/ppermute | solution.py:309
  75.1 27.2 %collective-permute-start.3 = (bf16[512,1024]{1,0:T(8,128)(2,1)S(1)}, bf16[512,1024]{1,0:T(8,128)(2,1)S(1)}, u32[]{:S(2)}, u32[]{:S(2)}) collective-permute-start(bf16[512,1024]{1,0:T(8,128)(2,1)S(1)} %collective-permute-done.2), channel_id=1, source_target_pairs={{0,4},{1,5},{2,6},{3,7},{4,0},{5,1},{6,2},{7,3},{8,12},{9,13},{10,... | collective-permute-start | bytes 3145736 | tf_op jit(solution)/shard_map/ppermute | solution.py:309
  78.6 80.0 %collective-permute-start.27 = (bf16[3,256,512]{2,1,0:T(8,128)(2,1)S(1)}, bf16[3,256,512]{2,1,0:T(8,128)(2,1)S(1)}, u32[]{:S(2)}, u32[]{:S(2)}) collective-permute-start(bf16[3,256,512]{2,1,0:T(8,128)(2,1)S(1)} %maximum_select_fusion.2), channel_id=1, source_target_pairs={{0,8},{1,9},{2,10},{3,11},{4,12},{5,13},{6,14},{7,15},{8,0},{9,1},... | collective-permute-start | bytes 2359304 | tf_op jit(solution)/shard_map/ppermute | solution.py:309
  102.2 56.4 %collective-permute-start.28 = (bf16[3,256,512]{2,1,0:T(8,128)(2,1)S(1)}, bf16[3,256,512]{2,1,0:T(8,128)(2,1)S(1)}, u32[]{:S(2)}, u32[]{:S(2)}) collective-permute-start(bf16[3,256,512]{2,1,0:T(8,128)(2,1)S(1)} %maximum_select_fusion.2), channel_id=1, source_target_pairs={{0,16},{1,17},{2,18},{3,19},{4,20},{5,21},{6,22},{7,23},{8,24},{9,... | collective-permute-start | bytes 2359304 | tf_op jit(solution)/shard_map/ppermute | solution.py:309
  102.2 58.3 %collective-permute-start.32 = (bf16[3,256,512]{2,1,0:T(8,128)(2,1)S(1)}, bf16[3,256,512]{2,1,0:T(8,128)(2,1)S(1)}, u32[]{:S(2)}, u32[]{:S(2)}) collective-permute-start(bf16[3,256,512]{2,1,0:T(8,128)(2,1)S(1)} %collective-permute-done.30), channel_id=1, source_target_pairs={{0,16},{1,17},{2,18},{3,19},{4,20},{5,21},{6,22},{7,23},{8,24},{9,... | collective-permute-start | bytes 2359304 | tf_op jit(solution)/shard_map/ppermute | solution.py:309
  155.7 40.3 %collective-permute-start.24 = (bf16[512,1024]{1,0:T(8,128)(2,1)S(1)}, bf16[512,1024]{1,0:T(8,128)(2,1)S(1)}, u32[]{:S(2)}, u32[]{:S(2)}) collective-permute-start(bf16[512,1024]{1,0:T(8,128)(2,1)S(1)} %select_convert_fusion.2), channel_id=1, source_target_pairs={{0,4},{1,5},{2,6},{3,7},{4,0},{5,1},{6,2},{7,3},{8,12},{9,13},{10,... | collective-permute-start | bytes 3145736 | tf_op jit(solution)/shard_map/ppermute | solution.py:309
  155.8 21.2 %collective-permute-start.35 = (bf16[3,256,512]{2,1,0:T(8,128)(2,1)S(1)}, bf16[3,256,512]{2,1,0:T(8,128)(2,1)S(1)}, u32[]{:S(2)}, u32[]{:S(2)}) collective-permute-start(bf16[3,256,512]{2,1,0:T(8,128)(2,1)S(1)} %collective-permute-done.34), channel_id=1, source_target_pairs={{0,8},{1,9},{2,10},{3,11},{4,12},{5,13},{6,14},{7,15},{8,0},{9,1},... | collective-permute-start | bytes 2359304 | tf_op jit(solution)/shard_map/ppermute | solution.py:309
  158.5 20.4 %collective-permute-start.40 = (bf16[3,256,512]{2,1,0:T(8,128)(2,1)S(1)}, bf16[3,256,512]{2,1,0:T(8,128)(2,1)S(1)}, u32[]{:S(2)}, u32[]{:S(2)}) collective-permute-start(bf16[3,256,512]{2,1,0:T(8,128)(2,1)S(1)} %collective-permute-done.38), channel_id=1, source_target_pairs={{0,16},{1,17},{2,18},{3,19},{4,20},{5,21},{6,22},{7,23},{8,24},{9,... | collective-permute-start | bytes 2359304 | tf_op jit(solution)/shard_map/ppermute | solution.py:309
  158.7 37.1 %collective-permute-start.29 = (bf16[3,256,512]{2,1,0:T(8,128)(2,1)S(1)}, bf16[3,256,512]{2,1,0:T(8,128)(2,1)S(1)}, u32[]{:S(2)}, u32[]{:S(2)}) collective-permute-start(bf16[3,256,512]{2,1,0:T(8,128)(2,1)S(1)} %collective-permute-done.27), channel_id=1, source_target_pairs={{0,16},{1,17},{2,18},{3,19},{4,20},{5,21},{6,22},{7,23},{8,24},{9,... | collective-permute-start | bytes 2359304 | tf_op jit(solution)/shard_map/ppermute | solution.py:309
  160.6 35.3 %collective-permute-start.31 = (bf16[3,256,512]{2,1,0:T(8,128)(2,1)S(1)}, bf16[3,256,512]{2,1,0:T(8,128)(2,1)S(1)}, u32[]{:S(2)}, u32[]{:S(2)}) collective-permute-start(bf16[3,256,512]{2,1,0:T(8,128)(2,1)S(1)} %collective-permute-done.30), channel_id=1, source_target_pairs={{0,8},{1,9},{2,10},{3,11},{4,12},{5,13},{6,14},{7,15},{8,0},{9,1},... | collective-permute-start | bytes 2359304 | tf_op jit(solution)/shard_map/ppermute | solution.py:309
  176.9 35.7 %collective-permute-start.36 = (bf16[3,256,512]{2,1,0:T(8,128)(2,1)S(1)}, bf16[3,256,512]{2,1,0:T(8,128)(2,1)S(1)}, u32[]{:S(2)}, u32[]{:S(2)}) collective-permute-start(bf16[3,256,512]{2,1,0:T(8,128)(2,1)S(1)} %collective-permute-done.34), channel_id=1, source_target_pairs={{0,16},{1,17},{2,18},{3,19},{4,20},{5,21},{6,22},{7,23},{8,24},{9,... | collective-permute-start | bytes 2359304 | tf_op jit(solution)/shard_map/ppermute | solution.py:309
  178.9 35.6 %collective-permute-start.39 = (bf16[3,256,512]{2,1,0:T(8,128)(2,1)S(1)}, bf16[3,256,512]{2,1,0:T(8,128)(2,1)S(1)}, u32[]{:S(2)}, u32[]{:S(2)}) collective-permute-start(bf16[3,256,512]{2,1,0:T(8,128)(2,1)S(1)} %collective-permute-done.38), channel_id=1, source_target_pairs={{0,8},{1,9},{2,10},{3,11},{4,12},{5,13},{6,14},{7,15},{8,0},{9,1},... | collective-permute-start | bytes 2359304 | tf_op jit(solution)/shard_map/ppermute | solution.py:309
  195.8 49.0 %collective-permute-start.33 = (bf16[3,256,512]{2,1,0:T(8,128)(2,1)S(1)}, bf16[3,256,512]{2,1,0:T(8,128)(2,1)S(1)}, u32[]{:S(2)}, u32[]{:S(2)}) collective-permute-start(bf16[3,256,512]{2,1,0:T(8,128)(2,1)S(1)} %collective-permute-done.32), channel_id=1, source_target_pairs={{0,8},{1,9},{2,10},{3,11},{4,12},{5,13},{6,14},{7,15},{8,0},{9,1},... | collective-permute-start | bytes 2359304 | tf_op jit(solution)/shard_map/ppermute | solution.py:309
  195.8 48.9 %collective-permute-start.37 = (bf16[3,256,512]{2,1,0:T(8,128)(2,1)S(1)}, bf16[3,256,512]{2,1,0:T(8,128)(2,1)S(1)}, u32[]{:S(2)}, u32[]{:S(2)}) collective-permute-start(bf16[3,256,512]{2,1,0:T(8,128)(2,1)S(1)} %collective-permute-done.35), channel_id=1, source_target_pairs={{0,16},{1,17},{2,18},{3,19},{4,20},{5,21},{6,22},{7,23},{8,24},{9,... | collective-permute-start | bytes 2359304 | tf_op jit(solution)/shard_map/ppermute | solution.py:309
  195.9 50.6 %collective-permute-start.41 = (bf16[3,256,512]{2,1,0:T(8,128)(2,1)S(1)}, bf16[3,256,512]{2,1,0:T(8,128)(2,1)}, u32[]{:S(2)}, u32[]{:S(2)}) collective-permute-start(bf16[3,256,512]{2,1,0:T(8,128)(2,1)S(1)} %collective-permute-done.40), channel_id=1, source_target_pairs={{0,8},{1,9},{2,10},{3,11},{4,12},{5,13},{6,14},{7,15},{8,0},{9,1},... | collective-permute-start | bytes 2359304 | tf_op jit(solution)/shard_map/ppermute | solution.py:309
  212.6 97.8 %collective-permute-start.44 = (bf16[512,1024]{1,0:T(8,128)(2,1)}, bf16[512,1024]{1,0:T(8,128)(2,1)S(1)}, u32[]{:S(2)}, u32[]{:S(2)}) collective-permute-start(bf16[512,1024]{1,0:T(8,128)(2,1)} %pad_maximum_fusion.11), channel_id=1, source_target_pairs={{0,0},{1,1},{2,5},{3,4},{4,3},{5,2},{6,6},{7,7},{8,8},{9,9},{10,13... | collective-permute-start | bytes 3145736 | tf_op jit(solution)/shard_map/ppermute | solution.py:309
  214.5 65.8 %collective-permute-start.25 = (bf16[512,1024]{1,0:T(8,128)(2,1)}, bf16[512,1024]{1,0:T(8,128)(2,1)}, u32[]{:S(2)}, u32[]{:S(2)}) collective-permute-start(bf16[512,1024]{1,0:T(8,128)(2,1)} %multiply_convert_fusion.3), channel_id=1, source_target_pairs={{0,4},{1,5},{2,6},{3,7},{4,0},{5,1},{6,2},{7,3},{8,12},{9,13},{10,... | collective-permute-start | bytes 3145736 | tf_op jit(solution)/shard_map/ppermute | solution.py:309
  344.5 80.8 %collective-permute-start.46 = (bf16[512,1024]{1,0:T(8,128)(2,1)S(1)}, bf16[512,1024]{1,0:T(8,128)(2,1)S(1)}, u32[]{:S(2)}, u32[]{:S(2)}) collective-permute-start(bf16[512,1024]{1,0:T(8,128)(2,1)S(1)} %slice.398), channel_id=1, source_target_pairs={{0,4},{1,5},{2,6},{3,7},{4,0},{5,1},{6,2},{7,3},{8,12},{9,13},{10,... | collective-permute-start | bytes 3145736 | tf_op jit(solution)/shard_map/ppermute | solution.py:309
  368.4 20.4 %collective-permute-start.68 = (bf16[3,256,512]{2,1,0:T(8,128)(2,1)S(1)}, bf16[3,256,512]{2,1,0:T(8,128)(2,1)S(1)}, u32[]{:S(2)}, u32[]{:S(2)}) collective-permute-start(bf16[3,256,512]{2,1,0:T(8,128)(2,1)S(1)} %get-tuple-element.60), channel_id=1, source_target_pairs={{0,16},{1,17},{2,18},{3,19},{4,20},{5,21},{6,22},{7,23},{8,24},{9,... | collective-permute-start | bytes 2359304 | tf_op jit(solution)/shard_map/ppermute | solution.py:309
  369.0 22.9 %collective-permute-start.72 = (bf16[3,256,512]{2,1,0:T(8,128)(2,1)S(1)}, bf16[3,256,512]{2,1,0:T(8,128)(2,1)S(1)}, u32[]{:S(2)}, u32[]{:S(2)}) collective-permute-start(bf16[3,256,512]{2,1,0:T(8,128)(2,1)S(1)} %get-tuple-element.63), channel_id=1, source_target_pairs={{0,8},{1,9},{2,10},{3,11},{4,12},{5,13},{6,14},{7,15},{8,0},{9,1},... | collective-permute-start | bytes 2359304 | tf_op jit(solution)/shard_map/ppermute | solution.py:309
  371.0 60.7 %collective-permute-start.71 = (bf16[3,256,512]{2,1,0:T(8,128)(2,1)S(1)}, bf16[3,256,512]{2,1,0:T(8,128)(2,1)S(1)}, u32[]{:S(2)}, u32[]{:S(2)}) collective-permute-start(bf16[3,256,512]{2,1,0:T(8,128)(2,1)S(1)} %get-tuple-element.62), channel_id=1, source_target_pairs={{0,8},{1,9},{2,10},{3,11},{4,12},{5,13},{6,14},{7,15},{8,0},{9,1},... | collective-permute-start | bytes 2359304 | tf_op jit(solution)/shard_map/ppermute | solution.py:309
  371.6 34.1 %collective-permute-start.75 = (bf16[3,256,512]{2,1,0:T(8,128)(2,1)S(1)}, bf16[3,256,512]{2,1,0:T(8,128)(2,1)S(1)}, u32[]{:S(2)}, u32[]{:S(2)}) collective-permute-start(bf16[3,256,512]{2,1,0:T(8,128)(2,1)S(1)} %get-tuple-element.64), channel_id=1, source_target_pairs={{0,16},{1,17},{2,18},{3,19},{4,20},{5,21},{6,22},{7,23},{8,24},{9,... | collective-permute-start | bytes 2359304 | tf_op jit(solution)/shard_map/ppermute | solution.py:309
  388.8 34.3 %collective-permute-start.80 = (bf16[3,256,512]{2,1,0:T(8,128)(2,1)S(1)}, bf16[3,256,512]{2,1,0:T(8,128)(2,1)S(1)}, u32[]{:S(2)}, u32[]{:S(2)}) collective-permute-start(bf16[3,256,512]{2,1,0:T(8,128)(2,1)S(1)} %get-tuple-element.67), channel_id=1, source_target_pairs={{0,8},{1,9},{2,10},{3,11},{4,12},{5,13},{6,14},{7,15},{8,0},{9,1},... | collective-permute-start | bytes 2359304 | tf_op jit(solution)/shard_map/ppermute | solution.py:309
  391.9 53.1 %collective-permute-start.77 = (bf16[3,256,512]{2,1,0:T(8,128)(2,1)S(1)}, bf16[3,256,512]{2,1,0:T(8,128)(2,1)S(1)}, u32[]{:S(2)}, u32[]{:S(2)}) collective-permute-start(bf16[3,256,512]{2,1,0:T(8,128)(2,1)S(1)} %get-tuple-element.65), channel_id=1, source_target_pairs={{0,16},{1,17},{2,18},{3,19},{4,20},{5,21},{6,22},{7,23},{8,24},{9,... | collective-permute-start | bytes 2359304 | tf_op jit(solution)/shard_map/ppermute | solution.py:309
  405.6 52.7 %collective-permute-start.79 = (bf16[3,256,512]{2,1,0:T(8,128)(2,1)S(1)}, bf16[3,256,512]{2,1,0:T(8,128)(2,1)S(1)}, u32[]{:S(2)}, u32[]{:S(2)}) collective-permute-start(bf16[3,256,512]{2,1,0:T(8,128)(2,1)S(1)} %get-tuple-element.66), channel_id=1, source_target_pairs={{0,8},{1,9},{2,10},{3,11},{4,12},{5,13},{6,14},{7,15},{8,0},{9,1},... | collective-permute-start | bytes 2359304 | tf_op jit(solution)/shard_map/ppermute | solution.py:309
  423.1 20.5 %collective-permute-start.73 = (bf16[3,256,512]{2,1,0:T(8,128)(2,1)S(1)}, bf16[3,256,512]{2,1,0:T(8,128)(2,1)S(1)}, u32[]{:S(2)}, u32[]{:S(2)}) collective-permute-start(bf16[3,256,512]{2,1,0:T(8,128)(2,1)S(1)} %add_convert_fusion.6), channel_id=1, source_target_pairs={{0,16},{1,17},{2,18},{3,19},{4,20},{5,21},{6,22},{7,23},{8,24},{9,... | collective-permute-start | bytes 2359304 | tf_op jit(solution)/shard_map/ppermute | solution.py:309
  425.3 31.1 %collective-permute-start.76 = (bf16[3,256,512]{2,1,0:T(8,128)(2,1)S(1)}, bf16[3,256,512]{2,1,0:T(8,128)(2,1)S(1)}, u32[]{:S(2)}, u32[]{:S(2)}) collective-permute-start(bf16[3,256,512]{2,1,0:T(8,128)(2,1)S(1)} %add_convert_fusion.4), channel_id=1, source_target_pairs={{0,8},{1,9},{2,10},{3,11},{4,12},{5,13},{6,14},{7,15},{8,0},{9,1},... | collective-permute-start | bytes 2359304 | tf_op jit(solution)/shard_map/ppermute | solution.py:309
  431.7 28.8 %collective-permute-start.81 = (bf16[3,256,512]{2,1,0:T(8,128)(2,1)S(1)}, bf16[3,256,512]{2,1,0:T(8,128)(2,1)S(1)}, u32[]{:S(2)}, u32[]{:S(2)}) collective-permute-start(bf16[3,256,512]{2,1,0:T(8,128)(2,1)S(1)} %add_convert_fusion.2), channel_id=1, source_target_pairs={{0,16},{1,17},{2,18},{3,19},{4,20},{5,21},{6,22},{7,23},{8,24},{9,... | collective-permute-start | bytes 2359304 | tf_op jit(solution)/shard_map/ppermute | solution.py:309
  443.6 18.1 %collective-permute-start.47 = (bf16[512,1024]{1,0:T(8,128)(2,1)S(1)}, bf16[512,1024]{1,0:T(8,128)(2,1)S(1)}, u32[]{:S(2)}, u32[]{:S(2)}) collective-permute-start(bf16[512,1024]{1,0:T(8,128)(2,1)S(1)} %get-tuple-element.41), channel_id=1, source_target_pairs={{0,4},{1,5},{2,6},{3,7},{4,0},{5,1},{6,2},{7,3},{8,12},{9,13},{10,... | collective-permute-start | bytes 3145736 | tf_op jit(solution)/shard_map/ppermute | solution.py:309
  445.0 117.4 %collective-permute-start.70 = (bf16[3,256,512]{2,1,0:T(8,128)(2,1)}, bf16[3,256,512]{2,1,0:T(8,128)(2,1)}, u32[]{:S(2)}, u32[]{:S(2)}) collective-permute-start(bf16[3,256,512]{2,1,0:T(8,128)(2,1)} %get-tuple-element.61), channel_id=1, source_target_pairs={{0,16},{1,17},{2,18},{3,19},{4,20},{5,21},{6,22},{7,23},{8,24},{9,... | collective-permute-start | bytes 2359304 | tf_op jit(solution)/shard_map/ppermute | solution.py:309
  456.4 65.6 %collective-permute-start.43 = (bf16[512,1024]{1,0:T(8,128)(2,1)S(1)}, bf16[512,1024]{1,0:T(8,128)(2,1)S(1)}, u32[]{:S(2)}, u32[]{:S(2)}) collective-permute-start(bf16[512,1024]{1,0:T(8,128)(2,1)S(1)} %pad_maximum_fusion.10), channel_id=1, source_target_pairs={{0,0},{1,1},{2,5},{3,4},{4,3},{5,2},{6,6},{7,7},{8,8},{9,9},{10,13... | collective-permute-start | bytes 3145736 | tf_op jit(solution)/shard_map/ppermute | solution.py:309
  520.0 33.8 %collective-permute-start.59 = (bf16[4,256,128]{1,2,0:T(8,128)(2,1)S(1)}, bf16[4,256,128]{1,2,0:T(8,128)(2,1)S(1)}, u32[]{:S(2)}, u32[]{:S(2)}) collective-permute-start(bf16[4,256,128]{1,2,0:T(8,128)(2,1)S(1)} %get-tuple-element.92), channel_id=1, source_target_pairs={{0,16},{1,17},{2,18},{3,19},{4,20},{5,21},{6,22},{7,23},{8,24},{9,... | collective-permute-start | bytes 786440 | tf_op jit(solution)/shard_map/ppermute | solution.py:309
  522.0 35.0 %collective-permute-start.64 = (bf16[4,256,128]{1,2,0:T(8,128)(2,1)S(1)}, bf16[4,256,128]{1,2,0:T(8,128)(2,1)S(1)}, u32[]{:S(2)}, u32[]{:S(2)}) collective-permute-start(bf16[4,256,128]{1,2,0:T(8,128)(2,1)S(1)} %get-tuple-element.95), channel_id=1, source_target_pairs={{0,8},{1,9},{2,10},{3,11},{4,12},{5,13},{6,14},{7,15},{8,0},{9,1},... | collective-permute-start | bytes 786440 | tf_op jit(solution)/shard_map/ppermute | solution.py:309
  522.3 40.2 %collective-permute-start.69 = (bf16[3,256,512]{2,1,0:T(8,128)(2,1)S(1)}, bf16[3,256,512]{2,1,0:T(8,128)(2,1)S(1)}, u32[]{:S(2)}, u32[]{:S(2)}) collective-permute-start(bf16[3,256,512]{2,1,0:T(8,128)(2,1)S(1)} %copy-done.44), channel_id=1, source_target_pairs={{0,8},{1,9},{2,10},{3,11},{4,12},{5,13},{6,14},{7,15},{8,0},{9,1},... | collective-permute-start | bytes 2359304 | tf_op jit(solution)/shard_map/ppermute | solution.py:309
  524.4 63.4 %collective-permute-start.74 = (bf16[3,256,512]{2,1,0:T(8,128)(2,1)S(1)}, bf16[3,256,512]{2,1,0:T(8,128)(2,1)S(1)}, u32[]{:S(2)}, u32[]{:S(2)}) collective-permute-start(bf16[3,256,512]{2,1,0:T(8,128)(2,1)S(1)} %copy-done.45), channel_id=1, source_target_pairs={{0,1},{1,0},{2,3},{3,2},{4,5},{5,4},{6,7},{7,6},{8,9},{9,8},{10,11... | collective-permute-start | bytes 2359304 | tf_op jit(solution)/shard_map/ppermute | solution.py:309
  553.8 55.3 %collective-permute-start.78 = (bf16[3,256,512]{2,1,0:T(8,128)(2,1)S(1)}, bf16[3,256,512]{2,1,0:T(8,128)(2,1)S(1)}, u32[]{:S(2)}, u32[]{:S(2)}) collective-permute-start(bf16[3,256,512]{2,1,0:T(8,128)(2,1)S(1)} %copy-done.46), channel_id=1, source_target_pairs={{0,2},{1,3},{2,0},{3,1},{4,6},{5,7},{6,4},{7,5},{8,10},{9,11},{10,... | collective-permute-start | bytes 2359304 | tf_op jit(solution)/shard_map/ppermute | solution.py:309
  557.0 52.2 %collective-permute-start.82 = (bf16[3,256,512]{2,1,0:T(8,128)(2,1)S(1)}, bf16[3,256,512]{2,1,0:T(8,128)(2,1)S(1)}, u32[]{:S(2)}, u32[]{:S(2)}) collective-permute-start(bf16[3,256,512]{2,1,0:T(8,128)(2,1)S(1)} %copy-done.47), channel_id=1, source_target_pairs={{0,3},{1,2},{2,1},{3,0},{4,7},{5,6},{6,5},{7,4},{8,11},{9,10},{10,... | collective-permute-start | bytes 2359304 | tf_op jit(solution)/shard_map/ppermute | solution.py:309
  562.4 77.1 %collective-permute-start.49 = (bf16[512,1024]{1,0:T(8,128)(2,1)S(1)}, bf16[512,1024]{1,0:T(8,128)(2,1)S(1)}, u32[]{:S(2)}, u32[]{:S(2)}) collective-permute-start(bf16[512,1024]{1,0:T(8,128)(2,1)S(1)} %select_convert_fusion), channel_id=1, source_target_pairs={{0,4},{1,5},{2,6},{3,7},{4,0},{5,1},{6,2},{7,3},{8,12},{9,13},{10,... | collective-permute-start | bytes 3145736 | tf_op jit(solution)/shard_map/ppermute | solution.py:309
  562.5 50.1 %collective-permute-start.55 = (bf16[4,256,128]{1,2,0:T(8,128)(2,1)S(1)}, bf16[4,256,128]{1,2,0:T(8,128)(2,1)S(1)}, u32[]{:S(2)}, u32[]{:S(2)}) collective-permute-start(bf16[4,256,128]{1,2,0:T(8,128)(2,1)S(1)} %get-tuple-element.90), channel_id=1, source_target_pairs={{0,8},{1,9},{2,10},{3,11},{4,12},{5,13},{6,14},{7,15},{8,0},{9,1},... | collective-permute-start | bytes 786440 | tf_op jit(solution)/shard_map/ppermute | solution.py:309
  587.7 30.7 %collective-permute-start.61 = (bf16[4,256,128]{1,2,0:T(8,128)(2,1)S(1)}, bf16[4,256,128]{1,2,0:T(8,128)(2,1)S(1)}, u32[]{:S(2)}, u32[]{:S(2)}) collective-permute-start(bf16[4,256,128]{1,2,0:T(8,128)(2,1)S(1)} %get-tuple-element.93), channel_id=1, source_target_pairs={{0,16},{1,17},{2,18},{3,19},{4,20},{5,21},{6,22},{7,23},{8,24},{9,... | collective-permute-start | bytes 786440 | tf_op jit(solution)/shard_map/ppermute | solution.py:309
  609.2 11.4 %collective-permute-start.60 = (bf16[4,256,128]{1,2,0:T(8,128)(2,1)S(1)}, bf16[4,256,128]{1,2,0:T(8,128)(2,1)S(1)}, u32[]{:S(2)}, u32[]{:S(2)}) collective-permute-start(bf16[4,256,128]{1,2,0:T(8,128)(2,1)S(1)} %add_convert_fusion.11), channel_id=1, source_target_pairs={{0,8},{1,9},{2,10},{3,11},{4,12},{5,13},{6,14},{7,15},{8,0},{9,1},... | collective-permute-start | bytes 786440 | tf_op jit(solution)/shard_map/ppermute | solution.py:309
  618.5 24.1 %collective-permute-start.54 = (bf16[4,256,128]{1,2,0:T(8,128)(2,1)S(1)}, bf16[4,256,128]{1,2,0:T(8,128)(2,1)S(1)}, u32[]{:S(2)}, u32[]{:S(2)}) collective-permute-start(bf16[4,256,128]{1,2,0:T(8,128)(2,1)S(1)} %get-tuple-element.73), channel_id=1, source_target_pairs={{0,16},{1,17},{2,18},{3,19},{4,20},{5,21},{6,22},{7,23},{8,24},{9,... | collective-permute-start | bytes 786440 | tf_op jit(solution)/shard_map/ppermute | solution.py:309
  620.6 16.6 %collective-permute-start.83 = (bf16[3,128,512]{2,1,0:T(8,128)(2,1)S(1)}, bf16[3,128,512]{2,1,0:T(8,128)(2,1)S(1)}, u32[]{:S(2)}, u32[]{:S(2)}) collective-permute-start(bf16[3,128,512]{2,1,0:T(8,128)(2,1)S(1)} %select_convert_fusion.3), channel_id=1, source_target_pairs={{0,4},{1,5},{2,6},{3,7},{4,0},{5,1},{6,2},{7,3},{8,12},{9,13},{10,... | collective-permute-start | bytes 1179656 | tf_op jit(solution)/shard_map/ppermute | solution.py:309
  620.7 22.0 %collective-permute-start.53 = (bf16[4,256,128]{1,2,0:T(8,128)(2,1)S(1)}, bf16[4,256,128]{1,2,0:T(8,128)(2,1)S(1)}, u32[]{:S(2)}, u32[]{:S(2)}) collective-permute-start(bf16[4,256,128]{1,2,0:T(8,128)(2,1)S(1)} %add_convert_fusion.14), channel_id=1, source_target_pairs={{0,8},{1,9},{2,10},{3,11},{4,12},{5,13},{6,14},{7,15},{8,0},{9,1},... | collective-permute-start | bytes 786440 | tf_op jit(solution)/shard_map/ppermute | solution.py:309
  624.7 22.9 %collective-permute-start.58 = (bf16[4,256,128]{1,2,0:T(8,128)(2,1)S(1)}, bf16[4,256,128]{1,2,0:T(8,128)(2,1)S(1)}, u32[]{:S(2)}, u32[]{:S(2)}) collective-permute-start(bf16[4,256,128]{1,2,0:T(8,128)(2,1)S(1)} %add_convert_fusion.12), channel_id=1, source_target_pairs={{0,1},{1,0},{2,3},{3,2},{4,5},{5,4},{6,7},{7,6},{8,9},{9,8},{10,11... | collective-permute-start | bytes 786440 | tf_op jit(solution)/shard_map/ppermute | solution.py:309
  637.2 18.3 %collective-permute-start.62 = (bf16[4,256,128]{1,2,0:T(8,128)(2,1)S(1)}, bf16[4,256,128]{1,2,0:T(8,128)(2,1)S(1)}, u32[]{:S(2)}, u32[]{:S(2)}) collective-permute-start(bf16[4,256,128]{1,2,0:T(8,128)(2,1)S(1)} %add_convert_fusion.10), channel_id=1, source_target_pairs={{0,2},{1,3},{2,0},{3,1},{4,6},{5,7},{6,4},{7,5},{8,10},{9,11},{10,... | collective-permute-start | bytes 786440 | tf_op jit(solution)/shard_map/ppermute | solution.py:309
  639.5 16.4 %collective-permute-start.66 = (bf16[4,256,128]{1,2,0:T(8,128)(2,1)S(1)}, bf16[4,256,128]{1,2,0:T(8,128)(2,1)S(1)}, u32[]{:S(2)}, u32[]{:S(2)}) collective-permute-start(bf16[4,256,128]{1,2,0:T(8,128)(2,1)S(1)} %add_convert_fusion.8), channel_id=1, source_target_pairs={{0,3},{1,2},{2,1},{3,0},{4,7},{5,6},{6,5},{7,4},{8,11},{9,10},{10,... | collective-permute-start | bytes 786440 | tf_op jit(solution)/shard_map/ppermute | solution.py:309
  642.6 15.1 %collective-permute-start.48 = (bf16[512,1024]{1,0:T(8,128)(2,1)S(1)}, bf16[512,1024]{1,0:T(8,128)(2,1)S(1)}, u32[]{:S(2)}, u32[]{:S(2)}) collective-permute-start(bf16[512,1024]{1,0:T(8,128)(2,1)S(1)} %select_convert_fusion.1), channel_id=1, source_target_pairs={{0,4},{1,5},{2,6},{3,7},{4,0},{5,1},{6,2},{7,3},{8,12},{9,13},{10,... | collective-permute-start | bytes 3145736 | tf_op jit(solution)/shard_map/ppermute | solution.py:309
  642.7 31.9 %collective-permute-start.50 = (bf16[512,1024]{1,0:T(8,128)(2,1)S(1)}, bf16[512,1024]{1,0:T(8,128)(2,1)S(1)}, u32[]{:S(2)}, u32[]{:S(2)}) collective-permute-start(bf16[512,1024]{1,0:T(8,128)(2,1)S(1)} %add_convert_fusion), channel_id=1, source_target_pairs={{0,1},{1,0},{2,3},{3,2},{4,5},{5,4},{6,7},{7,6},{8,9},{9,8},{10,11... | collective-permute-start | bytes 3145736 | tf_op jit(solution)/shard_map/ppermute | solution.py:309
  681.6 27.8 %collective-permute-start.51 = (bf16[512,1024]{1,0:T(8,128)(2,1)S(1)}, bf16[512,1024]{1,0:T(8,128)(2,1)S(1)}, u32[]{:S(2)}, u32[]{:S(2)}) collective-permute-start(bf16[512,1024]{1,0:T(8,128)(2,1)S(1)} %pad_maximum_fusion.12), channel_id=1, source_target_pairs={{0,0},{1,1},{2,5},{3,4},{4,3},{5,2},{6,6},{7,7},{8,8},{9,9},{10,13... | collective-permute-start | bytes 3145736 | tf_op jit(solution)/shard_map/ppermute | solution.py:309
  686.2 21.9 %collective-permute-start.88 = (f32[2,32]{1,0:T(2,128)S(1)}, f32[2,32]{1,0:T(2,128)}, u32[]{:S(2)}, u32[]{:S(2)}) collective-permute-start(f32[2,32]{1,0:T(2,128)S(1)} %get-tuple-element.123), channel_id=1, source_target_pairs={{0,2},{1,3},{2,0},{3,1},{4,6},{5,7},{6,4},{7,5},{8,10},{9,11},{10,... | collective-permute-start | bytes 776 | tf_op jit(solution)/shard_map/ppermute | solution.py:309
  687.3 20.8 %collective-permute-start.89 = (f32[2,32]{1,0:T(2,128)S(1)}, f32[2,32]{1,0:T(2,128)}, u32[]{:S(2)}, u32[]{:S(2)}) collective-permute-start(f32[2,32]{1,0:T(2,128)S(1)} %get-tuple-element.122), channel_id=1, source_target_pairs={{0,3},{1,2},{2,1},{3,0},{4,7},{5,6},{6,5},{7,4},{8,11},{9,10},{10,... | collective-permute-start | bytes 776 | tf_op jit(solution)/shard_map/ppermute | solution.py:309
  (84 other events, 1328.5 us)

commit v2 on v0

--- a/solution.py
+++ b/solution.py
@@ -3,6 +3,8 @@
 import jax
 import jax.numpy as jnp
 from jax import lax
+from jax.experimental import pallas as pl
+from jax.experimental.pallas import tpu as pltpu
 from jax.sharding import PartitionSpec as P
 
 HEAD = 64
@@ -289,9 +291,783 @@
     return (output, grad_inputs, grad_qkv, grad_out, grad_gate_up, grad_down, grad_gains)
 
 
+BF = jnp.bfloat16
+F32 = jnp.float32
+AXES = ("dp", "tensor")
+LIGHT = pl.CostEstimate(flops=1000, bytes_accessed=1000, transcendentals=0)
+
+
+def shift(value, where):
+    pairs = []
+    for y in range(2):
+        for x in range(2):
+            for c in range(2):
+                for z in range(4):
+                    to = where(y, x, c, z)
+                    if to is not None:
+                        ty, tx, tc, tz = to
+                        pairs.append((((y * 2 + x) * 2 + c) * 4 + z, ((ty * 2 + tx) * 2 + tc) * 4 + tz))
+    return lax.ppermute(value, AXES, pairs)
+
+
+def core_swap(value):
+    return shift(value, lambda y, x, c, z: (y, x, 1 - c, z))
+
+
+def core_swap_halves(value):
+    half = value.shape[0] // 2
+    return jnp.concatenate([core_swap(value[:half]), core_swap(value[half:])], axis=0)
+
+
+def x_swap(value):
+    return shift(value, lambda y, x, c, z: (y, 1 - x, c, z))
+
+
+def y_swap(value):
+    return shift(value, lambda y, x, c, z: (1 - y, x, c, z))
+
+
+def square_swap(value):
+    return shift(value, lambda y, x, c, z: (1 - y, 1 - x, c, z))
+
+
+def z_swap(value, bits):
+    return shift(value, lambda y, x, c, z: (y, x, c, z ^ bits))
+
+
+def home_of(y, x, c, z):
+    if (c == 1 and z < 2) or (c == 0 and z >= 2):
+        return (y, x, 1 - c, 3 - z)
+    return (y, x, c, z)
+
+
+def home_swap(value):
+    return shift(value, home_of)
+
+
+def partner_of_home(y, x, c, z):
+    y, x, c, z = home_of(y, x, c, z)
+    z ^= 1
+    if c == 1 and z in (1, 2):
+        return None
+    return (y, x, c, z)
+
+
+def head_masks(rows):
+    lanes = lax.broadcasted_iota(jnp.int32, (rows, 2 * HEAD), 1)
+    return (lanes < HEAD, lanes >= HEAD)
+
+
+def dot_nt(a, b):
+    return lax.dot_general(a, b, (((1,), (1,)), ((), ())), preferred_element_type=F32)
+
+
+def dot_nn(a, b):
+    return lax.dot_general(a, b, (((1,), (0,)), ((), ())), preferred_element_type=F32)
+
+
+def dot_tn(a, b):
+    return lax.dot_general(a, b, (((0,), (0,)), ((), ())), preferred_element_type=F32)
+
+
+def attend_forward_kernel(outer_ref, sc_ref, q_ref, k_ref, v_ref, o_ref, lse_ref):
+    chunk = q_ref.shape[0] // 2
+    tile = chunk // 2
+    lanes = 2 * HEAD
+    head = pl.program_id(0) % 2
+    low, high, low_partner, extra_row, extra_key = [pl.multiple_of(sc_ref[i], chunk) for i in range(5)]
+    mine = lax.broadcasted_iota(jnp.int32, (tile, lanes), 1) // HEAD == head
+
+    def fold(op, parts):
+        parts = [p[:, i * lanes : (i + 1) * lanes] for p in parts for i in range(p.shape[1] // lanes)]
+        while len(parts) > 1:
+            parts = [op(parts[i], parts[i + 1]) if i + 1 < len(parts) else parts[i] for i in range(0, len(parts), 2)]
+        return parts[0]
+
+    def unit(row, own, own_count, half, others):
+        rows = pl.ds(pl.multiple_of(row + half * tile, tile), tile)
+        query = jnp.where(mine, q_ref[rows, :], 0)
+        blocks = [(pl.ds(start, chunk), count, chunk, None) for start, count in others]
+        blocks.append((pl.ds(own, (half + 1) * tile), own_count, (half + 1) * tile, half * tile))
+        scores = []
+        for keys, count, width, diagonal in blocks:
+            s = dot_nt(query, k_ref[keys, :])
+            s = s + jnp.where(lax.broadcasted_iota(jnp.int32, (1, width), 1) < count, 0.0, negative)
+            if diagonal is not None:
+                cols = lax.broadcasted_iota(jnp.int32, (tile, width), 1)
+                s = jnp.where(cols <= lax.broadcasted_iota(jnp.int32, (tile, width), 0) + diagonal, s, negative)
+            scores.append(s)
+        top = jnp.max(fold(jnp.maximum, scores), axis=1, keepdims=True)
+        weights = [jnp.exp(s - top) for s in scores]
+        total = jnp.sum(fold(jnp.add, weights), axis=1, keepdims=True)
+        mixed = None
+        for w, (keys, _, _, _) in zip(weights, blocks):
+            part = dot_nn(w.astype(BF), v_ref[keys, :])
+            mixed = part if mixed is None else mixed + part
+        return rows, mixed / total, top + jnp.log(total)
+
+    def finish(units):
+        for rows, mixed, lse in units:
+            mixed = mixed.astype(BF)
+            o_ref[rows, :] = jnp.where(mine, mixed, o_ref[rows, :])
+            lse_ref[0, pl.ds(head, 1), rows] = jnp.transpose(jnp.broadcast_to(lse, (tile, lanes)))[0:1]
+
+    near = [(low, sc_ref[5]), (low_partner, sc_ref[7])]
+    extra = [(extra_key, sc_ref[8])]
+
+    @pl.when(outer_ref[0] == 1)
+    def _():
+        for half in range(2):
+            finish([unit(high, high, sc_ref[6], half, near + extra), unit(low, low, sc_ref[5], half, [])])
+
+    @pl.when(outer_ref[0] == 0)
+    def _():
+        for half in range(2):
+            finish([unit(high, high, sc_ref[6], half, near), unit(low, low, sc_ref[5], half, extra)])
+
+
+def attend_forward(outer, scalars, queries, keys_all, values_all, start, pairs):
+    rows = queries.shape[0]
+    width = pairs * 2 * HEAD
+    slot = keys_all.shape[0]
+    own = lambda i, *_: (0, i // 2)
+    column = lambda i, *_: (0, i // 2 + start)
+    return pl.pallas_call(
+        attend_forward_kernel,
+        out_shape=(
+            jax.ShapeDtypeStruct((rows, width), BF),
+            jax.ShapeDtypeStruct((pairs, 8, rows), F32),
+        ),
+        grid_spec=pltpu.PrefetchScalarGridSpec(
+            num_scalar_prefetch=2,
+            grid=(2 * pairs,),
+            in_specs=[
+                pl.BlockSpec((rows, 2 * HEAD), column),
+                pl.BlockSpec((slot, 2 * HEAD), column),
+                pl.BlockSpec((slot, 2 * HEAD), column),
+            ],
+            out_specs=(
+                pl.BlockSpec((rows, 2 * HEAD), own),
+                pl.BlockSpec((1, 8, rows), lambda i, *_: (i // 2, 0, 0)),
+            ),
+        ),
+        compiler_params=pltpu.CompilerParams(vmem_limit_bytes=24 << 20),
+        cost_estimate=LIGHT,
+        name="attend_forward",
+    )(outer, scalars, queries, keys_all, values_all)
+
+
+def attend_backward_kernel(sc_ref, q_ref, k_ref, v_ref, o_ref, g_ref, lse_ref, dq_ref, dk_ref, dv_ref, dq_acc, dk_acc, dv_acc, delta_ref):
+    chunk = q_ref.shape[0] // 2
+    tile = chunk // 2
+    low, high_row, low_partner, extra_row, extra_key = [pl.multiple_of(sc_ref[i], chunk) for i in range(5)]
+    dq_acc[...] = jnp.zeros_like(dq_acc)
+    dk_acc[...] = jnp.zeros_like(dk_acc)
+    dv_acc[...] = jnp.zeros_like(dv_acc)
+    for part in range(4):
+        rows = pl.ds(part * tile, tile)
+        product = jnp.transpose(o_ref[rows, :].astype(F32) * g_ref[rows, :].astype(F32))
+        delta_ref[0:1, rows] = jnp.sum(product[:HEAD], axis=0, keepdims=True)
+        delta_ref[1:2, rows] = jnp.sum(product[HEAD:], axis=0, keepdims=True)
+
+    def step(head, row, width, key, count, shift_rows):
+        rows = pl.ds(row, width)
+        keys = pl.ds(key, tile)
+        query = jnp.where(head_masks(width)[head], q_ref[rows, :], 0)
+        grad = jnp.where(head_masks(width)[head], g_ref[rows, :], 0)
+        key_block = k_ref[keys, :]
+        scores = dot_nt(key_block, query)
+        index = lax.broadcasted_iota(jnp.int32, (tile, width), 0)
+        allowed = index < count
+        if shift_rows is not None:
+            allowed = allowed & (index <= lax.broadcasted_iota(jnp.int32, (tile, width), 1) + shift_rows)
+        probs = jnp.exp(jnp.where(allowed, scores, negative) - lse_ref[0, head : head + 1, rows])
+        grad_probs = dot_nt(v_ref[keys, :], grad)
+        grad_scores = (probs * (grad_probs - delta_ref[head : head + 1, rows])).astype(BF)
+        dv_acc[keys, :] += dot_nn(probs.astype(BF), grad)
+        dk_acc[keys, :] += dot_nn(grad_scores, query)
+        key_masked = jnp.where(head_masks(tile)[head], key_block, 0)
+        dq_acc[rows, :] += dot_tn(grad_scores, key_masked)
+
+    for head in range(2):
+        for half in range(2):
+            down = half * tile
+            add = lambda start: pl.multiple_of(start + down, tile)
+            step(head, add(low), chunk - down, add(low), sc_ref[5] - down, 0)
+            step(head, add(high_row), chunk - down, add(high_row), sc_ref[6] - down, 0)
+            step(head, high_row, chunk, add(low), sc_ref[5] - down, None)
+            step(head, high_row, chunk, add(low_partner), sc_ref[7] - down, None)
+            step(head, extra_row, chunk, add(extra_key), sc_ref[8] - down, None)
+    dq_ref[...] = (dq_acc[...] * (1.0 / math.sqrt(HEAD))).astype(BF)
+    dk_ref[...] = dk_acc[...].astype(BF)
+    dv_ref[...] = dv_acc[...].astype(BF)
+
+
+def attend_backward(scalars, queries, keys_all, values_all, mixed, grad_mixed, lse, start):
+    rows, width = mixed.shape
+    pairs = width // (2 * HEAD)
+    slot = keys_all.shape[0]
+    own = lambda i, sc: (0, i)
+    column = lambda i, sc: (0, i + start)
+    own_spec = pl.BlockSpec((rows, 2 * HEAD), own)
+    row_spec = pl.BlockSpec((rows, 2 * HEAD), column)
+    slot_spec = pl.BlockSpec((slot, 2 * HEAD), column)
+    return pl.pallas_call(
+        attend_backward_kernel,
+        out_shape=(
+            jax.ShapeDtypeStruct((rows, width), BF),
+            jax.ShapeDtypeStruct((slot, width), BF),
+            jax.ShapeDtypeStruct((slot, width), BF),
+        ),
+        grid_spec=pltpu.PrefetchScalarGridSpec(
+            num_scalar_prefetch=1,
+            grid=(pairs,),
+            in_specs=[row_spec, slot_spec, slot_spec, own_spec, row_spec, pl.BlockSpec((1, 8, rows), lambda i, sc: (i, 0, 0))],
+            out_specs=(own_spec, pl.BlockSpec((slot, 2 * HEAD), own), pl.BlockSpec((slot, 2 * HEAD), own)),
+            scratch_shapes=[
+                pltpu.VMEM((rows, 2 * HEAD), F32),
+                pltpu.VMEM((slot, 2 * HEAD), F32),
+                pltpu.VMEM((slot, 2 * HEAD), F32),
+                pltpu.VMEM((8, rows), F32),
+            ],
+        ),
+        compiler_params=pltpu.CompilerParams(vmem_limit_bytes=32 << 20),
+        cost_estimate=LIGHT,
+    )(scalars, queries, keys_all, values_all, mixed, grad_mixed, lse)
+
+
+def project_kernel(*refs):
+    rows_refs, gain_ref, (low_ref, low_x_ref, low_yd_ref, high_ref, high_y_ref, high_xd_ref) = refs[:4], refs[4], refs[5:11]
+    normed_ref, q_ref, k_ref, v_ref, wq_ref, wk_ref, wv_ref, wo_ref = refs[11:]
+    step = pl.program_id(0)
+    _, block, width = low_ref.shape
+    part = width // 4
+    tile = rows_refs[0].shape[0] // 2
+
+    @pl.when(step == 0)
+    def _():
+        for k in range(4):
+            if k < 2:
+                blocks = (low_ref.at[k], low_x_ref.at[k], low_yd_ref.at[k], low_yd_ref.at[k + 2])
+            else:
+                blocks = (high_ref.at[k - 2], high_xd_ref.at[k - 2], high_y_ref.at[k - 2], high_xd_ref.at[k])
+            for r in range(4):
+                for n, out in enumerate((wq_ref, wk_ref, wv_ref, wo_ref)):
+                    out[r * block : (r + 1) * block, k * part : (k + 1) * part] = blocks[r][:, n * part : (n + 1) * part]
+
+    for n in range(4):
+
+        @pl.when(step == n)
+        def _():
+            for half in range(2):
+                rows = slice(half * tile, (half + 1) * tile)
+                values = rows_refs[n][rows, :].astype(F32)
+                inverse = lax.rsqrt(jnp.mean(values * values, axis=-1, keepdims=True) + 1e-05)
+                normed = (values * inverse * gain_ref[...]).astype(BF)
+                normed_ref[rows, :] = normed
+                k_ref[rows, :] = dot_nn(normed, wk_ref[...]).astype(BF)
+                v_ref[rows, :] = dot_nn(normed, wv_ref[...]).astype(BF)
+                if n < 2:
+                    q_ref[rows, :] = (dot_nn(normed, wq_ref[...]) * (1.0 / math.sqrt(HEAD))).astype(BF)
+
+
+def project(rows_parts, gain, weights):
+    chunk, model = rows_parts[0].shape
+    _, block, width = weights[0].shape
+    whole = lambda shape: pl.BlockSpec(shape, lambda i: (0,) * len(shape))
+    tiles = lambda cols: pl.BlockSpec((chunk, cols), lambda i: (i, 0))
+    shape = lambda r, c: jax.ShapeDtypeStruct((r, c), BF)
+    return pl.pallas_call(
+        project_kernel,
+        out_shape=(
+            shape(4 * chunk, model),
+            shape(2 * chunk, width),
+            shape(4 * chunk, width),
+            shape(4 * chunk, width),
+            shape(model, width),
+            shape(model, width),
+            shape(model, width),
+            shape(model, width),
+        ),
+        grid=(4,),
+        in_specs=[whole((chunk, model))] * 4 + [whole((1, model))] + [whole(w.shape) for w in weights],
+        out_specs=(
+            tiles(model),
+            pl.BlockSpec((chunk, width), lambda i: (jnp.minimum(i, 1), 0)),
+            tiles(width),
+            tiles(width),
+        )
+        + tuple(whole((model, width)) for _ in range(4)),
+        compiler_params=pltpu.CompilerParams(vmem_limit_bytes=60 << 20),
+        cost_estimate=LIGHT,
+        name="project",
+    )(*rows_parts, gain, *weights)
+
+
+def feed_forward_kernel(first_piece, *refs):
+    x_ref, weight_refs = refs[0], refs[1:5]
+    block = weight_refs[0].shape[1]
+    if not first_piece:
+        y_in_ref = refs[5]
+    silu_ref, slope_ref, hidden_ref, y_ref = refs[-4:]
+    x = x_ref[...]
+    gate = upper = None
+    for r in range(4):
+        part = x[:, r * block : (r + 1) * block]
+        g = dot_nn(part, weight_refs[r][0])
+        u = dot_nn(part, weight_refs[r][1])
+        gate = g if gate is None else gate + g
+        upper = u if upper is None else upper + u
+    sigmoid = jax.nn.sigmoid(gate)
+    silu = gate * sigmoid
+    hidden = (silu * upper).astype(BF)
+    silu_ref[...] = silu.astype(BF)
+    slope_ref[...] = (upper * (sigmoid * (1.0 + gate * (1.0 - sigmoid)))).astype(BF)
+    hidden_ref[...] = hidden
+    for r in range(4):
+        cols = slice(r * block, (r + 1) * block)
+        y = dot_nt(hidden, weight_refs[r][2])
+        y_ref[:, cols] = y if first_piece else y + y_in_ref[:, cols]
+
+
+def alone(piece):
+    return (piece[None], 0)
+
+
+def feed_forward(x, pieces, y):
+    rows, model = x.shape
+    _, _, block, width = pieces[0][0].shape
+    tile = rows // 4
+    tiles = lambda cols: pl.BlockSpec((tile, cols), lambda i: (i, 0))
+    weight_specs = [pl.BlockSpec((None, 3, block, width), lambda i, n=n: (n, 0, 0, 0)) for _, n in pieces]
+    extra = [] if y is None else [y]
+    return pl.pallas_call(
+        lambda *refs: feed_forward_kernel(y is None, *refs),
+        out_shape=tuple(jax.ShapeDtypeStruct((rows, width), BF) for _ in range(3)) + (jax.ShapeDtypeStruct((rows, model), F32),),
+        grid=(4,),
+        in_specs=[tiles(model)] + weight_specs + [tiles(model) for _ in extra],
+        out_specs=(tiles(width), tiles(width), tiles(width), tiles(model)),
+        input_output_aliases={5: 3} if extra else {},
+        compiler_params=pltpu.CompilerParams(vmem_limit_bytes=24 << 20),
+        cost_estimate=LIGHT,
+        name="feed_forward",
+    )(x, *[w for w, _ in pieces], *extra)
+
+
+def feed_backward_kernel(places, has_sum, last, *refs):
+    count = len(places) // 4
+    refs = list(refs)
+    take = lambda n: [refs.pop(0) for _ in range(n)]
+    x_ref, g_ref = take(2)
+    silu_hbm, slope_hbm, hidden_hbm, weight_hbm = take(count), take(count), take(count), take(4 * count)
+    sum_ref = take(1)[0] if has_sum else None
+    dx_ref, dx_other_ref = take(2) if last else take(1) * 2
+    out_hbm = take(4 * count)
+    xt_ref, gt_ref, kept_ref, hidden_ref, gu_ref, down_ref, acc_ref, out_ref, act_sem, weight_sem, out_sem = refs
+    _, _, block, width = weight_hbm[0].shape
+    rows_all = x_ref.shape[0]
+    half = rows_all // 2
+    copies_of, late_copies = [], []
+    for p in range(count):
+        copies = []
+        for n, source in enumerate((slope_hbm[p], silu_hbm[p])):
+            copies.append(pltpu.make_async_copy(source, kept_ref.at[p, :, pl.ds(n * width, width)], act_sem.at[p, n]))
+        for r in range(4):
+            features = pl.ds(r * block, block)
+            source = weight_hbm[p * 4 + r].at[places[p * 4 + r]]
+            for n, target in enumerate((gu_ref.at[p, features, pl.ds(0, width)], gu_ref.at[p, features, pl.ds(width, width)], down_ref.at[p, features, :])):
+                copies.append(pltpu.make_async_copy(source.at[n], target, weight_sem.at[p, r, n]))
+        copies_of.append(copies)
+        late_copies.append(pltpu.make_async_copy(hidden_hbm[p], hidden_ref.at[p], act_sem.at[p, 2]))
+    for copy in copies_of[0]:
+        copy.start()
+    for t in range(4):
+        rows = slice(t * rows_all // 4, (t + 1) * rows_all // 4)
+        xt_ref[:, rows] = jnp.transpose(x_ref[rows, :])
+        gt_ref[:, rows] = jnp.transpose(g_ref[rows, :])
+
+    for p in range(count):
+        for copy in copies_of[p]:
+            copy.wait()
+        for copy in copies_of[p + 1] if p < count - 1 else late_copies:
+            copy.start()
+        for t in range(2):
+            rows = slice(t * half, (t + 1) * half)
+            grad_hidden = dot_nn(g_ref[rows, :], down_ref[p])
+            kept_ref[p, rows, :width] = (grad_hidden * kept_ref[p, rows, :width].astype(F32)).astype(BF)
+            kept_ref[p, rows, width:] = (grad_hidden * kept_ref[p, rows, width:].astype(F32)).astype(BF)
+            part = dot_nt(kept_ref[p, rows, :], gu_ref[p])
+            if p > 0:
+                part = acc_ref[rows, :] + part
+            elif has_sum:
+                part = sum_ref[rows, :] + part
+            if p < count - 1:
+                acc_ref[rows, :] = part
+            elif not last:
+                dx_ref[rows, :] = part
+            elif t == 0:
+                dx_ref[...] = part
+            else:
+                dx_other_ref[...] = part.astype(BF)
+
+    slots = out_ref.shape[0]
+    copies = []
+    for p in range(count):
+        late_copies[p].wait()
+        for r in range(3, -1, -1):
+            features = slice(r * block, (r + 1) * block)
+            slot = len(copies) % slots
+            if len(copies) >= slots:
+                copies[len(copies) - slots].wait()
+            gu = dot_nn(xt_ref[features, :], kept_ref[p]).astype(BF)
+            out_ref[slot, 0] = gu[:, :width]
+            out_ref[slot, 1] = gu[:, width:]
+            out_ref[slot, 2] = dot_nn(gt_ref[features, :], hidden_ref[p]).astype(BF)
+            copies.append(pltpu.make_async_copy(out_ref.at[slot], out_hbm[p * 4 + r], out_sem.at[slot]))
+            copies[-1].start()
+    for copy in copies[-slots:]:
+        copy.wait()
+
+
+def feed_backward(x, g, silus, slopes, hiddens, pieces, total, last):
+    count = len(pieces)
+    extra = [] if total is None else [total]
+    rows, model = x.shape
+    _, _, block, width = pieces[0][0][0].shape
+    places = [n for piece in pieces for _, n in piece]
+    vmem = pl.BlockSpec(memory_space=pltpu.VMEM)
+    hbm = pl.BlockSpec(memory_space=pl.ANY)
+    outs = pl.pallas_call(
+        lambda *refs: feed_backward_kernel(places, total is not None, last, *refs),
+        out_shape=(
+            (jax.ShapeDtypeStruct((rows // 2, model), F32), jax.ShapeDtypeStruct((rows // 2, model), BF))
+            if last
+            else (jax.ShapeDtypeStruct((rows, model), F32),)
+        )
+        + tuple(jax.ShapeDtypeStruct((3, block, width), BF) for _ in range(4 * count)),
+        in_specs=[vmem] * 2 + [hbm] * (7 * count) + [vmem] * len(extra),
+        out_specs=((vmem, vmem) if last else (vmem,)) + (hbm,) * (4 * count),
+        scratch_shapes=[
+            pltpu.VMEM((model, rows), BF),
+            pltpu.VMEM((model, rows), BF),
+            pltpu.VMEM((count, rows, 2 * width), BF),
+            pltpu.VMEM((count, rows, width), BF),
+            pltpu.VMEM((count, model, 2 * width), BF),
+            pltpu.VMEM((count, model, width), BF),
+            pltpu.VMEM((rows, model), F32),
+            pltpu.VMEM((3, 3, block, width), BF),
+            pltpu.SemaphoreType.DMA((count, 3)),
+            pltpu.SemaphoreType.DMA((count, 4, 3)),
+            pltpu.SemaphoreType.DMA((3,)),
+        ],
+        compiler_params=pltpu.CompilerParams(vmem_limit_bytes=60 << 20),
+        cost_estimate=LIGHT,
+        name="feed_backward",
+    )(x, g, *silus, *slopes, *hiddens, *[w for piece in pieces for w, _ in piece], *extra)
+    first = 2 if last else 1
+    return outs[:first], [outs[first + 4 * p : first + 4 + 4 * p] for p in range(count)]
+
+
+class Order:
+    def __init__(self):
+        self.last = ()
+
+    def event(self, *values):
+        out = lax.optimization_barrier((*values, *self.last))[: len(values)]
+        self.last = out
+        return out
+
+
+def on_square(inputs, teacher, lengths, w_qkv, w_out_t, w_gate_up, w_down_t, gains):
+    chunk, model = inputs.shape
+    slot = chunk * 4
+    total_rows = slot * 8
+    dp = lax.axis_index("dp")
+    z = lax.axis_index("tensor")
+    core = dp % 2
+    first = core == 0
+    odd_x = (dp // 2) % 2 == 1
+    odd_y = dp // 4 == 1
+    inner = jnp.where((z == 1) | (z == 2), 1, 0)
+    chunk_low, chunk_high = inner, 3 - inner
+    length = lax.dynamic_index_in_dim(lengths, (dp // 2) * 2 + z // 2, 0, keepdims=False)
+    count = jnp.sum(lengths).astype(F32)
+    places = jnp.stack([chunk_low, chunk_high, 1 - chunk_low, 2 + inner]) * chunk
+    counts = jnp.clip(length - places, 0, chunk)
+    outer = 1 - inner
+    low_row, high_row = core * chunk, (1 - core) * chunk
+    low_partner, high_partner = low_row + 2 * chunk, high_row + 2 * chunk
+    scalars = jnp.stack(
+        [
+            low_row,
+            high_row,
+            low_partner,
+            jnp.where(outer == 1, high_row, low_row),
+            jnp.where(outer == 1, high_partner, low_partner),
+            counts[0],
+            counts[1],
+            counts[2],
+            jnp.where(outer == 1, counts[3], counts[2]),
+        ]
+    ).astype(jnp.int32)
+
+    def turn(value):
+        a, b, c, d = jnp.split(value, 4, axis=-1)
+        a, b, c, d = jnp.where(odd_x, b, a), jnp.where(odd_x, a, b), jnp.where(odd_x, d, c), jnp.where(odd_x, c, d)
+        return jnp.concatenate([jnp.where(odd_y, c, a), jnp.where(odd_y, d, b), jnp.where(odd_y, a, c), jnp.where(odd_y, b, d)], axis=-1)
+
+    def sort_cores(own, other, axis):
+        return jnp.where(first, jnp.concatenate([own, other], axis=axis), jnp.concatenate([other, own], axis=axis))
+
+    def pick(pair):
+        return jnp.where(first, pair[0], pair[1]), jnp.where(first, pair[1], pair[0])
+
+    def join_rows(partial):
+        return partial[:chunk] + core_swap(partial[chunk:].astype(BF)).astype(F32)
+
+    def core_piece(stacked):
+        keep, give = pick(jnp.split(stacked, 2, axis=2))
+        return sort_cores(keep, core_swap(give), 1)
+
+    def matmul(a, b):
+        return jnp.einsum("ab,bc->ac", a, b, preferred_element_type=F32)
+
+    def matmul_nt(a, b):
+        return jnp.einsum("ab,cb->ac", a, b, preferred_element_type=F32)
+
+    def matmul_tn(a, b):
+        return jnp.einsum("ba,bc->ac", a, b, preferred_element_type=F32)
+
+    order = Order()
+    event = order.event
+
+    attention_piece = core_piece(jnp.concatenate([jnp.swapaxes(w_qkv, 0, 1), w_out_t[None]], axis=0))
+    attention_piece = jnp.concatenate([attention_piece[n] for n in range(4)], axis=1)
+    feed_piece = core_piece(jnp.concatenate([jnp.swapaxes(w_gate_up, 0, 1), w_down_t[None]], axis=0))
+    feed_p, feed_x, feed_y, feed_d = [None] * 4, [None] * 4, [None] * 4, [None] * 4
+    (gains_pair,) = event(sort_cores(gains, core_swap(gains), 0))
+    gains_x, gains_y, gains_d = x_swap(gains_pair), y_swap(gains_pair), square_swap(gains_pair)
+    inputs_rel = turn(inputs)
+    gains_x, gains_y, gains_d, attention_piece, feed_p[0] = event(gains_x, gains_y, gains_d, attention_piece, feed_piece)
+    gains_all = jnp.concatenate([gains_pair, gains_x, gains_y, gains_d], axis=0)
+
+    att_1, att_2, att_3 = z_swap(attention_piece, 1), z_swap(attention_piece, 2), z_swap(attention_piece, 3)
+    feed_x[0], feed_y[0] = x_swap(feed_p[0]), y_swap(feed_p[0])
+    att_1, att_2, att_3, inputs_rel = event(att_1, att_2, att_3, inputs_rel)
+    att_low, att_high = jnp.stack([attention_piece, att_1]), jnp.stack([att_2, att_3])
+    own_rows, partner_rows = home_swap(inputs_rel), shift(inputs_rel, partner_of_home)
+    att_low_x, att_high_y = x_swap(att_low), y_swap(att_high)
+    feed_x[0], feed_y[0] = event(feed_x[0], feed_y[0])
+    att_low_x, att_high_y, feed_piece = event(att_low_x, att_high_y, feed_p[0])
+    att_low_yd = y_swap(jnp.concatenate([att_low, att_low_x], axis=0))
+    att_high_xd = x_swap(jnp.concatenate([att_high, att_high_y], axis=0))
+    own_rows, feed_piece = event(own_rows, feed_piece)
+    partner_rows, feed_piece, feed_x[0] = event(partner_rows, feed_piece, feed_x[0])
+    other_rows, other_partner = core_swap(own_rows), core_swap(partner_rows)
+    feed_p[1] = z_swap(feed_piece, 1)
+    feed_d[0] = y_swap(feed_x[0])
+    att_low_yd, att_high_xd = event(att_low_yd, att_high_xd)
+    other_rows, other_partner, feed_piece = event(other_rows, other_partner, feed_piece)
+    feed_p[2] = z_swap(feed_piece, 2)
+    rows = own_rows.astype(F32)
+    gain_one = gains_all[:, 0].astype(F32)
+    gain_two = gains_all[:, 1].astype(F32)
+
+    normed_all, queries, keys_all, values_all, w_queries, w_keys, w_values, w_out = project(
+        (own_rows, other_rows, partner_rows, other_partner), gain_one[None], [att_low, att_low_x, att_low_yd, att_high, att_high_y, att_high_xd]
+    )
+    normed_own = normed_all[: 2 * chunk]
+    outer_only = (1 - inner)[None].astype(jnp.int32)
+    parts = [None] * 4
+
+    def attend(n):
+        return attend_forward(outer_only, scalars, queries, keys_all, values_all, n, 1)
+
+    queries, feed_d[0], feed_p[1] = event(queries, feed_d[0], feed_p[1])
+    feed_x[1], feed_y[1] = x_swap(feed_p[1]), y_swap(feed_p[1])
+    parts[0] = attend(0)
+    parts[1] = attend(1)
+    queries, feed_x[1], feed_y[1], feed_p[2], _, _ = event(queries, feed_x[1], feed_y[1], feed_p[2], parts[0][0], parts[1][0])
+    feed_p[3] = z_swap(feed_p[2], 1)
+    batch_x = x_swap(jnp.stack([feed_y[1], feed_p[2]]))
+    feed_y[2] = y_swap(feed_p[2])
+    parts[2] = attend(2)
+    parts[3] = attend(3)
+    mixed = jnp.concatenate([p[0] for p in parts], axis=1)
+    branch = matmul_nt(mixed, w_out)
+    branch_own, branch_other, feed_p[3], feed_y[2], batch_x, teacher = event(
+        branch[:chunk], branch[chunk:].astype(BF), feed_p[3], feed_y[2], batch_x, teacher
+    )
+    batch_y = y_swap(jnp.stack([feed_p[3], batch_x[1]]))
+    feed_x[3] = x_swap(feed_p[3])
+    teacher_rel = turn(teacher)
+    middle = rows + branch_own + core_swap_halves(branch_other).astype(F32)
+
+    scaled_two, inverse_two = norm_forward(middle)
+    normed_two = (scaled_two * gain_two).astype(BF)
+    normed_two_all = jnp.concatenate([normed_two, core_swap_halves(normed_two)], axis=0)
+    silus, slopes, hiddens, feed = [None] * 4, [None] * 4, [None] * 4, None
+    pieces = [
+        [alone(feed_p[0]), alone(feed_x[0]), alone(feed_y[0]), alone(feed_d[0])],
+        [alone(feed_p[1]), alone(feed_x[1]), alone(feed_y[1]), (batch_x, 0)],
+    ]
+    for k in range(4):
+        if k == 2:
+            feed, batch_y, feed_x[3], teacher_rel = event(feed, batch_y, feed_x[3], teacher_rel)
+            feed_d[3] = x_swap(batch_y[0])
+            teacher_rows = home_swap(teacher_rel)
+            pieces.append([alone(feed_p[2]), (batch_x, 1), alone(feed_y[2]), (batch_y, 1)])
+        if k == 3:
+            feed, feed_d[3] = event(feed, feed_d[3])
+            pieces.append([alone(feed_p[3]), alone(feed_x[3]), (batch_y, 0), alone(feed_d[3])])
+        silus[k], slopes[k], hiddens[k], feed = feed_forward(normed_two_all, pieces[k], feed)
+    feed_own, feed_other, teacher_rows = event(feed[:chunk], feed[chunk:].astype(BF), teacher_rows)
+    final = middle + feed_own + core_swap(feed_other).astype(F32)
+
+    own_place = jnp.where(first, chunk_low, chunk_high) * chunk
+    valid = (own_place + jnp.arange(chunk, dtype=jnp.int32) < length)[:, None]
+    grad_final = jnp.where(valid, final - teacher_rows.astype(F32), 0.0) * (total_rows / count)
+    grad_feed = grad_final.astype(BF)
+    grad_feed_all, output = event(jnp.concatenate([grad_feed, core_swap(grad_feed)], axis=0), turn(final.astype(BF)))
+    output = home_swap(output)
+
+    def add(a, b):
+        return (a.astype(F32) + b.astype(F32)).astype(BF)
+
+    def total_of(own, x, y):
+        return own.astype(F32) + x.astype(F32) + y.astype(F32)
+
+    def feed_back(k, total):
+        pair = slice(k, k + 2)
+        return feed_backward(normed_two_all, grad_feed_all, silus[pair], slopes[pair], hiddens[pair], pieces[pair], total, k == 0)
+
+    (grad_x,), ((own_2, x_2, y_2, d_2), (own_3, x_3, y_3, d_3)) = feed_back(2, None)
+    grad_x, d_2, d_3 = event(grad_x, d_2, d_3)
+    d_2, d_3 = y_swap(d_2), x_swap(d_3)
+    (grad_x, grad_x_other), ((own_0, x_0, y_0, d_0), (own_1, x_1, y_1, d_1)) = feed_back(0, grad_x)
+    grad_x, grad_x_other, output, d_2, d_3, d_0, d_1, y_2, x_3 = event(grad_x, grad_x_other, output, d_2, d_3, d_0, d_1, y_2, x_3)
+    batch_x, batch_y = x_swap(jnp.stack([add(x_2, d_2), x_3])), y_swap(jnp.stack([y_2, add(y_3, d_3)]))
+    grad_normed_two = grad_x + core_swap_halves(grad_x_other).astype(F32)
+
+    grad_norm_two, grad_gain_two = norm_backward(grad_normed_two, scaled_two, inverse_two, gain_two)
+    grad_middle = grad_final + grad_norm_two
+    grad_branch = grad_middle.astype(BF)
+    grad_branch_both = jnp.concatenate([grad_branch, core_swap_halves(grad_branch)], axis=0)
+    grad_mixed = matmul(grad_branch_both, w_out).astype(BF)
+    half_width = mixed.shape[1] // 2
+
+    def attend_back(n):
+        lse = jnp.concatenate([parts[2 * n][1], parts[2 * n + 1][1]], axis=0)
+        return attend_backward(scalars, queries, keys_all, values_all, mixed[:, n * half_width : (n + 1) * half_width], grad_mixed, lse, 2 * n)
+
+    gq_a, gk_a, gv_a = attend_back(0)
+    gq_a, grad_mixed, d_0, d_1 = event(gq_a, grad_mixed, d_0, d_1)
+    d_0, d_1 = y_swap(d_0), x_swap(d_1)
+    gq_b, gk_b, gv_b = attend_back(1)
+
+    gq_b, batch_x, batch_y = event(gq_b, batch_x, batch_y)
+    part_3 = z_swap(total_of(own_3, batch_x[1], batch_y[1]).astype(BF), 1)
+    part_2 = total_of(own_2, batch_x[0], batch_y[0]).astype(BF)
+
+    grad_queries = jnp.concatenate([gq_a, gq_b], axis=1)
+    grad_keys = jnp.concatenate([gk_a, gk_b], axis=1)
+    grad_values = jnp.concatenate([gv_a, gv_b], axis=1)
+    part_all = (matmul_nt(grad_keys, w_keys) + matmul_nt(grad_values, w_values))
+    part_own = part_all[: 2 * chunk] + matmul_nt(grad_queries, w_queries)
+    part_own, part_other = part_own[:chunk], part_own[chunk:].astype(BF)
+    part_own, part_other, part_all, grad_queries, grad_keys, grad_values = event(
+        part_own, part_other, part_all[2 * chunk :], grad_queries, grad_keys, grad_values
+    )
+    part_other, other_partner_part = core_swap(part_other), core_swap(part_all[chunk:].astype(BF))
+
+    grad_out = matmul_tn(grad_branch_both, mixed).astype(BF)
+    grad_w_queries = matmul_tn(normed_own, grad_queries).astype(BF)
+    grad_w_keys = matmul_tn(normed_all, grad_keys).astype(BF)
+    grad_w_values = matmul_tn(normed_all, grad_values).astype(BF)
+    quarter_cols = grad_w_queries.shape[1] // 4
+
+    def attention_group(pieces):
+        cols = [g[:, k * quarter_cols : (k + 1) * quarter_cols] for k in pieces for g in (grad_w_queries, grad_w_keys, grad_w_values, grad_out)]
+        return jnp.split(jnp.concatenate(cols, axis=1), 4, axis=0)
+
+    half_cols = 4 * quarter_cols
+    own_e, x_e, y_e, d_e = attention_group((0, 1))
+    own_o, x_o, y_o, d_o = attention_group((2, 3))
+    own_e, own_o, x_e, y_e, d_e, x_o, y_o, d_o, d_0, d_1, x_1, y_0, part_other, other_partner_part = event(
+        own_e, own_o, x_e, y_e, d_e, x_o, y_o, d_o, d_0, d_1, x_1, y_0, part_other, other_partner_part
+    )
+    batch_x, batch_y = x_swap(jnp.stack([add(x_0, d_0), x_1])), y_swap(jnp.stack([y_0, add(y_1, d_1)]))
+    from_partner = z_swap((part_all[:chunk] + other_partner_part.astype(F32)).astype(BF), 1)
+    part_3, part_2 = event(part_3, part_2)
+    part_2 = z_swap(add(part_2, part_3), 2)
+    (from_partner,) = event(from_partner)
+    grad_normed_one = part_own + part_other.astype(F32) + from_partner.astype(F32)
+    scaled_one, inverse_one = norm_forward(rows)
+    grad_norm_one, grad_gain_one = norm_backward(grad_normed_one, scaled_one, inverse_one, gain_one)
+    grad_rows, gain_a, gain_b, batch_x, batch_y = event(
+        turn((grad_middle + grad_norm_one).astype(BF)), grad_gain_one, grad_gain_two, batch_x, batch_y
+    )
+    grad_inputs = home_swap(grad_rows)
+    part_0 = total_of(own_0, batch_x[0], batch_y[0])
+    part_1 = z_swap(total_of(own_1, batch_x[1], batch_y[1]).astype(BF), 1)
+    d_e, d_o = y_swap(d_e), x_swap(d_o)
+    d_e, d_o, y_e, x_o = event(d_e, d_o, y_e, x_o)
+    batch_x, batch_y = x_swap(jnp.stack([add(x_e, d_e), x_o])), y_swap(jnp.stack([y_e, add(y_o, d_o)]))
+    (grad_inputs,) = event(grad_inputs)
+    part_1, part_2, part_0 = event(part_1, part_2, part_0)
+    feed_total = part_0 + part_1.astype(F32) + part_2.astype(F32)
+    feed_keep, feed_give = pick(jnp.split(feed_total, 2, axis=1))
+    feed_give = core_swap(feed_give.astype(BF))
+
+    quarter = model // 4
+    a, b, c, d = jnp.split(jnp.stack([gain_a, gain_b], axis=0), 4, axis=1)
+    sent = x_swap(jnp.concatenate([b, d], axis=1))
+
+    batch_x, batch_y, sent = event(batch_x, batch_y, sent)
+    even, odd = total_of(own_e, batch_x[0], batch_y[0]), total_of(own_o, batch_x[1], batch_y[1])
+    att_3, att_1, att_2 = odd[:, half_cols:].astype(BF), even[:, half_cols:].astype(BF), odd[:, :half_cols].astype(BF)
+    att_3, att_1, a, c, sent = event(att_3, att_1, a, c, sent)
+    att_3, att_1 = z_swap(att_3, 1), z_swap(att_1, 1)
+    a, c = a + sent[:, :quarter], c + sent[:, quarter:]
+    sent = y_swap(c)
+    att_3, att_2, sent = event(att_3, att_2, sent)
+    att_2 = z_swap(add(att_2, att_3), 2)
+    a = a + sent
+    keep, give = pick(jnp.split(a, 2, axis=1))
+    sent = core_swap(give)
+    feed_give, sent = event(feed_give, sent)
+    a = keep + sent
+    size = a.shape[1] // 4
+    total = lax.dynamic_slice_in_dim(a, z * size, size, 1)
+    for k in range(1, 4):
+        total = total + z_swap(lax.dynamic_slice_in_dim(a, (z ^ k) * size, size, 1), k)
+    grad_gains = jnp.swapaxes(total, 0, 1)
+    grad_inputs = grad_inputs.astype(F32)
+    feed_out = sort_cores(feed_keep, feed_give.astype(F32), 2)
+    attention_total = even[:, :half_cols] + att_1.astype(F32) + att_2.astype(F32)
+    attention_total = jnp.stack([attention_total[:, n * quarter_cols : (n + 1) * quarter_cols] for n in range(4)])
+
+    def to_home(total):
+        keep, give = pick(jnp.split(total, 2, axis=1))
+        return sort_cores(keep, core_swap(give.astype(BF)).astype(F32), 2)
+
+    attention_out = to_home(attention_total)
+
+    return (
+        output,
+        grad_inputs,
+        jnp.swapaxes(attention_out[:3], 0, 1),
+        attention_out[3],
+        jnp.swapaxes(feed_out[:2], 0, 1),
+        feed_out[2],
+        grad_gains,
+    )
+
+
 def solution(mesh):
+    square = dict(mesh.shape) == {"dp": 8, "tensor": 4}
     return jax.shard_map(
-        on_device,
+        on_square if square else on_device,
         mesh=mesh,
         in_specs=(
             P(("dp", "tensor"), None),

time: 1240 us -> 534 us (0.43)
  waiting for transfers between devices: 832 us -> 175 us
  matrix products: 230 us -> 17.5 us
  Pallas kernels: 0 us -> 139 us
  starting transfers between devices: 1.83 us -> 115 us
  other arithmetic: 85.5 us -> 39.4 us
  blocking collectives: 22.4 us -> 0 us
    reduce_scatter x8 -> x0, waiting for transfers between devices: 355 us -> none  [the longest x1 77.2 us: on_device(): lax.psum_scatter(jnp.einsum('rcf,dcf->rd', piece, qkv_all, preferred_elem...]
    all_gather x7 -> x0, waiting for transfers between devices: 345 us -> none  [the longest x1 82.9 us: on_device(): gathered_one = lax.all_gather(normed_one, 'tensor', axis=0, tiled=True)]
    dot_general x102 -> x9, matrix products: 230 us -> 17.5 us  [the longest x4 8.98 us: matmul_nt(): return jnp.einsum('ab,cb->ac', a, b, preferred_element_type=F32)]
    ppermute x0 -> x72, waiting for transfers between devices: none -> 175 us  [shift(): return lax.ppermute(value, AXES, pairs)]
    pallas_call x0 -> x13, Pallas kernels: none -> 139 us  [the longest x2 46.8 us: feed_backward(): pl.pallas_call(lambda *refs: feed_backward_kernel(places, total is not No...]
    unnamed x17 -> x0, waiting for transfers between devices: 132 us -> none
    ppermute x0 -> x72, starting transfers between devices: none -> 115 us  [shift(): return lax.ppermute(value, AXES, pairs)]
    lt x41 -> x1, other arithmetic: 27.8 us -> 0.62 us  [on_square(): valid = (own_place + jnp.arange(chunk, dtype=jnp.int32) < length)[:, None]]
  transfers between devices with their start and end apart: 16 -> 72, of which waited for: 14 -> 31; matrix products, arithmetic and copies ran while one was open for 18% -> 11% of each run, Pallas kernels for 0% -> 26%
where the time goes in v2:
time: 534 us; the launch traced here: 530 us
  waiting for transfers between devices  175 us (33%)
  Pallas kernels  139 us (26%)
  starting transfers between devices  115 us (22%)
  local copies, waits for them, and re-layouts  39.6 us (7%)
  other arithmetic  39.4 us (7%)
  matrix products  17.5 us (3%)
    ppermute x72, waiting for transfers between devices, shift(): return lax.ppermute(value, AXES, pairs)  175 us
    ppermute x72, starting transfers between devices, shift(): return lax.ppermute(value, AXES, pairs)  115 us
    pallas_call x2, Pallas kernels, feed_backward(): pl.pallas_call(lambda *refs: feed_backward_kernel(places, total is not No...  46.8 us
    pallas_call x2, Pallas kernels, attend_backward(): pl.pallas_call(attend_backward_kernel, out_shape=(jax.ShapeDtypeStruct((r...  33.4 us
    unnamed x201, local copies, waits for them, and re-layouts  28.6 us
    pallas_call x4, Pallas kernels, attend_forward(): pl.pallas_call(attend_forward_kernel, out_shape=(jax.ShapeDtypeStruct((ro...  24.7 us
    pallas_call x4, Pallas kernels, feed_forward(): pl.pallas_call(lambda *refs: feed_forward_kernel(y is None, *refs), out_s...  21.1 us
    pallas_call x1, Pallas kernels, project(): pl.pallas_call(project_kernel, out_shape=(shape(4 * chunk, model), shape(...  13.5 us
  transfers between devices with their start and end apart: 72, of which 31 were waited for; matrix products, arithmetic and copies ran while one was open for 11% of the time, Pallas kernels for 26%

profile of v2, /device:TPU:0, one launch (start us, length us, event | category | flops | bytes accessed | tf_op | source)
XLA Modules:
  0.0 529.9 jit_solution(7764023384965590058)
XLA Ops:
  5.4 2.6 collective-permute-start.1
  11.6 2.4 collective-permute-done.3
  15.6 2.6 collective-permute-start.7
  19.5 5.6 %collective-permute-done.6 = bf16[256,512]{1,0:T(8,128)(2,1)S(1)} collective-permute-done((bf16[256,512]{1,0:T(8,128)(2,1)S(1)}, bf16[256,512]{1,0:T(8,128)(2,1)S(1)}, u32[]{:S(2)}, u32[]{:S(2)}) %collective-permute-start.6) | collective-permute-done | bytes 262176 | tf_op jit(solution)/shard_map/ppermute | solution.py:310
  25.1 11.8 %collective-permute-done.7 = bf16[256,512]{1,0:T(8,128)(2,1)S(1)} collective-permute-done((bf16[256,512]{1,0:T(8,128)(2,1)S(1)}, bf16[256,512]{1,0:T(8,128)(2,1)S(1)}, u32[]{:S(2)}, u32[]{:S(2)}) %collective-permute-start.7) | collective-permute-done | bytes 262176 | tf_op jit(solution)/shard_map/ppermute | solution.py:310
  39.0 5.7 %collective-permute-start.15 = (bf16[512,1024]{1,0:T(8,128)(2,1)S(1)}, bf16[512,1024]{1,0:T(8,128)(2,1)S(1)}, u32[]{:S(2)}, u32[]{:S(2)}) collective-permute-start(bf16[512,1024]{1,0:T(8,128)(2,1)S(1)} %pad_maximum_fusion.9), channel_id=1, source_target_pairs={{0,1},{1,0},{2,4},{4,2},{5,3},{6,7},{8,9},{9,8},{10,12},{12,10},{1... | collective-permute-start | bytes 3145736 | tf_op jit(solution)/shard_map/ppermute | solution.py:310
  44.8 2.4 collective-permute-done.10.refs_6_
  49.8 12.9 %collective-permute-start.14 = (bf16[512,1024]{1,0:T(8,128)(2,1)S(1)}, bf16[512,1024]{1,0:T(8,128)(2,1)S(1)}, u32[]{:S(2)}, u32[]{:S(2)}) collective-permute-start(bf16[512,1024]{1,0:T(8,128)(2,1)S(1)} %collective-permute-done.9.refs_0_), channel_id=1, source_target_pairs={{0,4},{1,5},{2,6},{3,7},{4,0},{5,1},{6,2},{7,3},{8,12},{9,13},{10,... | collective-permute-start | bytes 3145736 | tf_op jit(solution)/shard_map/ppermute | solution.py:310
  62.7 5.5 %collective-permute-done.15.refs_2_ = bf16[512,1024]{1,0:T(8,128)(2,1)S(1)} collective-permute-done((bf16[512,1024]{1,0:T(8,128)(2,1)S(1)}, bf16[512,1024]{1,0:T(8,128)(2,1)S(1)}, u32[]{:S(2)}, u32[]{:S(2)}) %collective-permute-start.15) | collective-permute-done | bytes 1048608 | tf_op jit(solution)/shard_map/ppermute | solution.py:310
  68.2 9.3 %collective-permute-start.16 = (bf16[512,1024]{1,0:T(8,128)(2,1)S(1)}, bf16[512,1024]{1,0:T(8,128)(2,1)S(1)}, u32[]{:S(2)}, u32[]{:S(2)}) collective-permute-start(bf16[512,1024]{1,0:T(8,128)(2,1)S(1)} %collective-permute-done.15.refs_2_), channel_id=1, source_target_pairs={{0,4},{1,5},{2,6},{3,7},{4,0},{5,1},{6,2},{7,3},{8,12},{9,13},{10,... | collective-permute-start | bytes 3145736 | tf_op jit(solution)/shard_map/ppermute | solution.py:310
  79.0 12.1 %collective-permute-start.20 = (bf16[3,256,512]{2,1,0:T(8,128)(2,1)S(1)}, bf16[3,256,512]{2,1,0:T(8,128)(2,1)S(1)}, u32[]{:S(2)}, u32[]{:S(2)}) collective-permute-start(bf16[3,256,512]{2,1,0:T(8,128)(2,1)S(1)} %maximum_select_fusion.1), channel_id=1, source_target_pairs={{0,1},{1,0},{2,3},{3,2},{4,5},{5,4},{6,7},{7,6},{8,9},{9,8},{10,11... | collective-permute-start | bytes 2359304 | tf_op jit(solution)/shard_map/ppermute | solution.py:310
  94.0 13.5 %project.1 = (bf16[2048,1024]{1,0:T(8,128)(2,1)}, bf16[1024,512]{1,0:T(8,128)(2,1)}, bf16[2048,512]{1,0:T(8,128)(2,1)}, bf16[2048,512]{1,0:T(8,128)(2,1)}, bf16[...) custom-call(bf16[512,1024]{1,0:T(8,128)(2,1)} %copy-done.47, ...), custom_call_target="tpu_custom_call" | custom-call | flops 1000 | bytes 1000 | tf_op jit(solution)/shard_map/project/pallas_call | solution.py:580
  110.5 3.8 collective-permute-start.23
  121.9 6.0 %attend_forward.4 = (bf16[1024,128]{1,0:T(8,128)(2,1)S(1)}, f32[1,8,1024]{2,1,0:T(8,128)S(1)}) custom-call(s32[1]{0:T(128)} %bitcast.12.outer_ref, s32[9]{0:T(128)S(1)} %stack.159.sc_ref, bf16[1024,512]{1,0:T(8,128)(2,1)S(1)} %copy-done.5, bf16[2048,512]{1,0:T(8,128)(2,1)S(1)} %copy-done.1, bf16[2048,512]{1,0:T(8,128)(2,1)S(1)} %copy-done.3), custom_call_target="tpu_custom_call" | custom-call | flops 1000 | bytes 1000 | tf_op jit(solution)/shard_map/attend_forward/pallas_call | solution.py:435
  128.0 6.4 %attend_forward.5 = (bf16[1024,128]{1,0:T(8,128)(2,1)S(1)}, f32[1,8,1024]{2,1,0:T(8,128)S(1)}) custom-call(s32[1]{0:T(128)} %bitcast.12.outer_ref, s32[9]{0:T(128)S(1)} %stack.159.sc_ref, bf16[1024,512]{1,0:T(8,128)(2,1)S(1)} %copy-done.5, bf16[2048,512]{1,0:T(8,128)(2,1)S(1)} %copy-done.1, bf16[2048,512]{1,0:T(8,128)(2,1)S(1)} %copy-done.3), custom_call_target="tpu_custom_call" | custom-call | flops 1000 | bytes 1000 | tf_op jit(solution)/shard_map/attend_forward/pallas_call | solution.py:435
  134.5 13.4 %collective-permute-done.23 = bf16[3,256,512]{2,1,0:T(8,128)(2,1)S(1)} collective-permute-done((bf16[3,256,512]{2,1,0:T(8,128)(2,1)S(1)}, bf16[3,256,512]{2,1,0:T(8,128)(2,1)S(1)}, u32[]{:S(2)}, u32[]{:S(2)}) %collective-permute-start.23) | collective-permute-done | bytes 786464 | tf_op jit(solution)/shard_map/ppermute | solution.py:310
  151.0 6.0 %attend_forward.6 = (bf16[1024,128]{1,0:T(8,128)(2,1)S(1)}, f32[1,8,1024]{2,1,0:T(8,128)S(1)}) custom-call(s32[1]{0:T(128)} %bitcast.12.outer_ref, s32[9]{0:T(128)S(1)} %stack.159.sc_ref, bf16[1024,512]{1,0:T(8,128)(2,1)S(1)} %copy-done.5, bf16[2048,512]{1,0:T(8,128)(2,1)S(1)} %copy-done.1, bf16[2048,512]{1,0:T(8,128)(2,1)S(1)} %copy-done.3), custom_call_target="tpu_custom_call" | custom-call | flops 1000 | bytes 1000 | tf_op jit(solution)/shard_map/attend_forward/pallas_call | solution.py:435
  157.0 6.2 %attend_forward.7 = (bf16[1024,128]{1,0:T(8,128)(2,1)S(1)}, f32[1,8,1024]{2,1,0:T(8,128)S(1)}) custom-call(s32[1]{0:T(128)} %bitcast.12.outer_ref, s32[9]{0:T(128)S(1)} %stack.159.sc_ref, bf16[1024,512]{1,0:T(8,128)(2,1)S(1)} %copy-done.5, bf16[2048,512]{1,0:T(8,128)(2,1)S(1)} %copy-done.1, bf16[2048,512]{1,0:T(8,128)(2,1)S(1)} %copy-done.3), custom_call_target="tpu_custom_call" | custom-call | flops 1000 | bytes 1000 | tf_op jit(solution)/shard_map/attend_forward/pallas_call | solution.py:435
  164.8 2.1 copy-done.51
  168.3 14.6 %collective-permute-done.26.refs_4_.refs_2_.refs_9_.refs_15_ = bf16[2,3,256,512]{3,2,1,0:T(8,128)(2,1)S(1)} collective-permute-done((bf16[2,3,256,512]{3,2,1,0:T(8,128)(2,1)S(1)}, bf16[2,3,256,512]{3,2,1,0:T(8,128)(2,1)S(1)}, u32[]{:S(2)}, u32[]{:S(2)}) %collective-permute-start.26) | collective-permute-done | bytes 1572896 | tf_op jit(solution)/shard_map/ppermute | solution.py:310
  184.3 2.2 collective-permute-start.31
  191.4 4.7 feed_forward.4
  197.1 6.6 %feed_forward.5 = (bf16[1024,512]{1,0:T(8,128)(2,1)S(1)}, bf16[1024,512]{1,0:T(8,128)(2,1)S(1)}, bf16[1024,512]{1,0:T(8,128)(2,1)S(1)}, f32[1024,1024]{1,0:T(8,128)S(1)}) custom-call(bf16[1024,1024]{1,0:T(8,128)(2,1)S(1)} %pad_maximum_fusion.refs_0_, bf16[1,3,256,512]{3,2,1,0:T(8,128)(2,1)S(1)} %bitcast.163, ...), custom_call_target="tpu_custom_call", output_to_operand_aliasing={{3}: (5, {})} | custom-call | flops 1000 | bytes 1000 | tf_op jit(solution)/shard_map/feed_forward/pallas_call | solution.py:644
  205.7 15.2 %collective-permute-done.31.refs_4_.refs_3_.refs_11_.refs_14_ = bf16[2,3,256,512]{3,2,1,0:T(8,128)(2,1)S(1)} collective-permute-done((bf16[2,3,256,512]{3,2,1,0:T(8,128)(2,1)S(1)}, bf16[2,3,256,512]{3,2,1,0:T(8,128)(2,1)S(1)}, u32[]{:S(2)}, u32[]{:S(2)}) %collective-permute-start.31) | collective-permute-done | bytes 1572896 | tf_op jit(solution)/shard_map/ppermute | solution.py:310
  220.9 1.6 collective-permute-start.34
  224.8 4.9 feed_forward.6
  229.7 9.2 %collective-permute-done.33 = bf16[3,256,512]{2,1,0:T(8,128)(2,1)S(1)} collective-permute-done((bf16[3,256,512]{2,1,0:T(8,128)(2,1)S(1)}, bf16[3,256,512]{2,1,0:T(8,128)(2,1)S(1)}, u32[]{:S(2)}, u32[]{:S(2)}) %collective-permute-start.33) | collective-permute-done | bytes 786464 | tf_op jit(solution)/shard_map/ppermute | solution.py:310
  240.0 4.9 feed_forward.7
  244.9 1.8 slice.247
  248.3 4.0 collective-permute-start.35
  254.9 2.8 fusion.38
  261.9 2.3 collective-permute-start.37
  264.2 22.8 %feed_backward.2 = (f32[1024,1024]{1,0:T(8,128)}, bf16[3,256,512]{2,1,0:T(8,128)(2,1)}, bf16[3,256,512]{2,1,0:T(8,128)(2,1)}, bf16[3,256,512]{2,1,0:T(8,128)(2,1...) custom-call(bf16[1024,1024]{1,0:T(8,128)(2,1)} %copy-done, ...), custom_call_target="tpu_custom_call" | custom-call | flops 1000 | bytes 1000 | tf_op jit(solution)/shard_map/feed_backward/pallas_call | solution.py:740
  287.0 1.8 collective-permute-start.38
  288.8 1.7 collective-permute-start.39
  290.7 24.0 %feed_backward.3 = (f32[512,1024]{1,0:T(8,128)}, bf16[512,1024]{1,0:T(8,128)(2,1)}, bf16[3,256,512]{2,1,0:T(8,128)(2,1)}, bf16[3,256,512]{2,1,0:T(8,128)(2,1)}, ...) custom-call(bf16[1024,1024]{1,0:T(8,128)(2,1)} %copy-done, ...), custom_call_target="tpu_custom_call" | custom-call | flops 1000 | bytes 1000 | tf_op jit(solution)/shard_map/feed_backward/pallas_call | solution.py:740
  314.7 1.9 fusion.44
  316.7 2.6 collective-permute-start.41
  322.5 3.0 fusion.39
  330.9 16.4 %shard_map.135 = (bf16[1024,256]{1,0:T(8,128)(2,1)S(1)}, bf16[2048,256]{1,0:T(8,128)(2,1)S(1)}, bf16[2048,256]{1,0:T(8,128)(2,1)S(1)}) custom-call(s32[9]{0:T(128)S(1)} %stack.159.sc_ref, bf16[1024,512]{1,0:T(8,128)(2,1)S(1)} %copy-done.6, bf16[2048,512]{1,0:T(8,128)(2,1)S(1)} %copy-done.2, bf16[2048,512]{1,0:T(8,128)(2,1)S(1)} %copy-done.4, ...), custom_call_target="tpu_custom_call" | custom-call | flops 1000 | bytes 1000 | tf_op jit(solution)/shard_map/pallas_call | solution.py:515
  347.4 17.0 %shard_map.136 = (bf16[1024,256]{1,0:T(8,128)(2,1)S(1)}, bf16[2048,256]{1,0:T(8,128)(2,1)S(1)}, bf16[2048,256]{1,0:T(8,128)(2,1)S(1)}) custom-call(s32[9]{0:T(128)S(1)} %stack.159.sc_ref, bf16[1024,512]{1,0:T(8,128)(2,1)S(1)} %copy-done.6, bf16[2048,512]{1,0:T(8,128)(2,1)S(1)} %copy-done.2, bf16[2048,512]{1,0:T(8,128)(2,1)S(1)} %copy-done.4, ...), custom_call_target="tpu_custom_call" | custom-call | flops 1000 | bytes 1000 | tf_op jit(solution)/shard_map/pallas_call | solution.py:515
  366.1 4.0 fusion.50
  371.3 2.4 convolution_add_fusion
  380.4 1.9 copy-done.85
  383.8 2.4 convolution_convert_fusion.3
  386.2 2.4 convolution_convert_fusion.2
  392.6 1.9 collective-permute-done.46
  397.9 13.5 %collective-permute-done.51 = bf16[3,256,512]{2,1,0:T(8,128)(2,1)S(1)} collective-permute-done((bf16[3,256,512]{2,1,0:T(8,128)(2,1)S(1)}, bf16[3,256,512]{2,1,0:T(8,128)(2,1)S(1)}, u32[]{:S(2)}, u32[]{:S(2)}) %collective-permute-start.51) | collective-permute-done | bytes 786464 | tf_op jit(solution)/shard_map/ppermute | solution.py:310
  417.2 15.1 %collective-permute-done.50 = bf16[512,1024]{1,0:T(8,128)(2,1)S(1)} collective-permute-done((bf16[512,1024]{1,0:T(8,128)(2,1)S(1)}, bf16[512,1024]{1,0:T(8,128)(2,1)S(1)}, u32[]{:S(2)}, u32[]{:S(2)}) %collective-permute-start.50) | collective-permute-done | bytes 1048608 | tf_op jit(solution)/shard_map/ppermute | solution.py:310
  436.0 10.3 %collective-permute-done.52 = bf16[2,3,256,512]{3,2,1,0:T(8,128)(2,1)S(1)} collective-permute-done((bf16[2,3,256,512]{3,2,1,0:T(8,128)(2,1)S(1)}, bf16[2,3,256,512]{3,2,1,0:T(8,128)(2,1)S(1)}, u32[]{:S(2)}, u32[]{:S(2)}) %collective-permute-start.52) | collective-permute-done | bytes 1572896 | tf_op jit(solution)/shard_map/ppermute | solution.py:310
  446.3 2.5 collective-permute-done.53
  448.8 9.5 %collective-permute-start.54 = (bf16[512,1024]{1,0:T(8,128)(2,1)}, bf16[512,1024]{1,0:T(8,128)(2,1)}, u32[]{:S(2)}, u32[]{:S(2)}) collective-permute-start(bf16[512,1024]{1,0:T(8,128)(2,1)} %pad_maximum_fusion.14), channel_id=1, source_target_pairs={{0,0},{1,1},{2,5},{3,4},{4,3},{5,2},{6,6},{7,7},{8,8},{9,9},{10,13... | collective-permute-start | bytes 3145736 | tf_op jit(solution)/shard_map/ppermute | solution.py:310
  460.4 1.6 convert_add_fusion.4
  465.9 13.7 %collective-permute-done.61 = bf16[3,256,512]{2,1,0:T(8,128)(2,1)S(1)} collective-permute-done((bf16[3,256,512]{2,1,0:T(8,128)(2,1)}, bf16[3,256,512]{2,1,0:T(8,128)(2,1)S(1)}, u32[]{:S(2)}, u32[]{:S(2)}) %collective-permute-start.61) | collective-permute-done | bytes 786464 | tf_op jit(solution)/shard_map/ppermute | solution.py:310
  479.6 16.9 %collective-permute-done.60 = bf16[3,256,512]{2,1,0:T(8,128)(2,1)} collective-permute-done((bf16[3,256,512]{2,1,0:T(8,128)(2,1)}, bf16[3,256,512]{2,1,0:T(8,128)(2,1)}, u32[]{:S(2)}, u32[]{:S(2)}) %collective-permute-start.60) | collective-permute-done | bytes 786464 | tf_op jit(solution)/shard_map/ppermute | solution.py:310
  497.9 2.1 fusion.20
  501.1 2.8 convert_element_type.344
  503.9 1.9 collective-permute-start.62
  505.9 3.5 collective-permute-done.63
  511.1 1.7 collective-permute-start.71
  513.9 1.7 collective-permute-start.69
  516.4 1.8 copy.23
  518.1 1.7 collective-permute-done.71
  519.8 5.1 collective-permute-done.70
  (416 shorter events, 108.7 us)
Async XLA Ops:
  0.6 4.7 collective-permute-start
  2.3 7.3 %collective-permute-start.4 = (bf16[4,128,128]{2,1,0:T(8,128)(2,1)S(1)}, bf16[4,128,128]{2,1,0:T(8,128)(2,1)S(1)}, u32[]{:S(2)}, u32[]{:S(2)}) collective-permute-start(bf16[4,128,128]{2,1,0:T(8,128)(2,1)S(1)} %get-tuple-element.438), channel_id=1, source_target_pairs={{0,4},{1,5},{2,6},{3,7},{4,0},{5,1},{6,2},{7,3},{8,12},{9,13},{10,... | collective-permute-start | bytes 393224 | tf_op jit(solution)/shard_map/ppermute | solution.py:310
  4.8 4.9 collective-permute-start.5
  5.4 4.7 collective-permute-start.1
  8.0 3.6 collective-permute-start.2
  9.5 4.5 collective-permute-start.3
  14.0 11.1 %collective-permute-start.6 = (bf16[256,512]{1,0:T(8,128)(2,1)S(1)}, bf16[256,512]{1,0:T(8,128)(2,1)S(1)}, u32[]{:S(2)}, u32[]{:S(2)}) collective-permute-start(bf16[256,512]{1,0:T(8,128)(2,1)S(1)} %pad_maximum_fusion.25), channel_id=1, source_target_pairs={{0,1},{1,0},{2,3},{3,2},{4,5},{5,4},{6,7},{7,6},{8,9},{9,8},{10,11... | collective-permute-start | bytes 786440 | tf_op jit(solution)/shard_map/ppermute | solution.py:310
  15.6 21.4 %collective-permute-start.7 = (bf16[256,512]{1,0:T(8,128)(2,1)S(1)}, bf16[256,512]{1,0:T(8,128)(2,1)S(1)}, u32[]{:S(2)}, u32[]{:S(2)}) collective-permute-start(bf16[256,512]{1,0:T(8,128)(2,1)S(1)} %pad_maximum_fusion.25), channel_id=1, source_target_pairs={{0,2},{1,3},{2,0},{3,1},{4,6},{5,7},{6,4},{7,5},{8,10},{9,11},{10,... | collective-permute-start | bytes 786440 | tf_op jit(solution)/shard_map/ppermute | solution.py:310
  18.2 18.8 %collective-permute-start.8 = (bf16[256,512]{1,0:T(8,128)(2,1)S(1)}, bf16[256,512]{1,0:T(8,128)(2,1)S(1)}, u32[]{:S(2)}, u32[]{:S(2)}) collective-permute-start(bf16[256,512]{1,0:T(8,128)(2,1)S(1)} %pad_maximum_fusion.25), channel_id=1, source_target_pairs={{0,3},{1,2},{2,1},{3,0},{4,7},{5,6},{6,5},{7,4},{8,11},{9,10},{10,... | collective-permute-start | bytes 786440 | tf_op jit(solution)/shard_map/ppermute | solution.py:310
  18.5 20.5 %collective-permute-start.12 = (bf16[3,256,512]{2,1,0:T(8,128)(2,1)S(1)}, bf16[3,256,512]{2,1,0:T(8,128)(2,1)S(1)}, u32[]{:S(2)}, u32[]{:S(2)}) collective-permute-start(bf16[3,256,512]{2,1,0:T(8,128)(2,1)S(1)} %maximum_select_fusion.1), channel_id=1, source_target_pairs={{0,8},{1,9},{2,10},{3,11},{4,12},{5,13},{6,14},{7,15},{8,0},{9,1},... | collective-permute-start | bytes 2359304 | tf_op jit(solution)/shard_map/ppermute | solution.py:310
  19.1 25.7 %collective-permute-start.13 = (bf16[3,256,512]{2,1,0:T(8,128)(2,1)S(1)}, bf16[3,256,512]{2,1,0:T(8,128)(2,1)S(1)}, u32[]{:S(2)}, u32[]{:S(2)}) collective-permute-start(bf16[3,256,512]{2,1,0:T(8,128)(2,1)S(1)} %maximum_select_fusion.1), channel_id=1, source_target_pairs={{0,16},{1,17},{2,18},{3,19},{4,20},{5,21},{6,22},{7,23},{8,24},{9,... | collective-permute-start | bytes 2359304 | tf_op jit(solution)/shard_map/ppermute | solution.py:310
  37.0 10.2 %collective-permute-start.10 = (bf16[2,256,512]{2,1,0:T(8,128)(2,1)S(1)}, bf16[2,256,512]{2,1,0:T(8,128)(2,1)S(1)}, u32[]{:S(2)}, u32[]{:S(2)}) collective-permute-start(bf16[2,256,512]{2,1,0:T(8,128)(2,1)S(1)} %pad_maximum_fusion.19.refs_5_), channel_id=1, source_target_pairs={{0,8},{1,9},{2,10},{3,11},{4,12},{5,13},{6,14},{7,15},{8,0},{9,1},... | collective-permute-start | bytes 1572872 | tf_op jit(solution)/shard_map/ppermute | solution.py:310
  37.7 9.7 %collective-permute-start.11 = (bf16[2,256,512]{2,1,0:T(8,128)(2,1)S(1)}, bf16[2,256,512]{2,1,0:T(8,128)(2,1)S(1)}, u32[]{:S(2)}, u32[]{:S(2)}) collective-permute-start(bf16[2,256,512]{2,1,0:T(8,128)(2,1)S(1)} %pad_maximum_fusion.20.refs_8_), channel_id=1, source_target_pairs={{0,16},{1,17},{2,18},{3,19},{4,20},{5,21},{6,22},{7,23},{8,24},{9,... | collective-permute-start | bytes 1572872 | tf_op jit(solution)/shard_map/ppermute | solution.py:310
  38.3 11.6 %collective-permute-start.9 = (bf16[512,1024]{1,0:T(8,128)(2,1)S(1)}, bf16[512,1024]{1,0:T(8,128)(2,1)S(1)}, u32[]{:S(2)}, u32[]{:S(2)}) collective-permute-start(bf16[512,1024]{1,0:T(8,128)(2,1)S(1)} %pad_maximum_fusion.9), channel_id=1, source_target_pairs={{0,0},{1,1},{2,5},{3,4},{4,3},{5,2},{6,6},{7,7},{8,8},{9,9},{10,13... | collective-permute-start | bytes 3145736 | tf_op jit(solution)/shard_map/ppermute | solution.py:310
  39.0 29.2 %collective-permute-start.15 = (bf16[512,1024]{1,0:T(8,128)(2,1)S(1)}, bf16[512,1024]{1,0:T(8,128)(2,1)S(1)}, u32[]{:S(2)}, u32[]{:S(2)}) collective-permute-start(bf16[512,1024]{1,0:T(8,128)(2,1)S(1)} %pad_maximum_fusion.9), channel_id=1, source_target_pairs={{0,1},{1,0},{2,4},{4,2},{5,3},{6,7},{8,9},{9,8},{10,12},{12,10},{1... | collective-permute-start | bytes 3145736 | tf_op jit(solution)/shard_map/ppermute | solution.py:310
  47.5 31.4 %collective-permute-start.17 = (bf16[4,256,512]{2,1,0:T(8,128)(2,1)S(1)}, bf16[4,256,512]{2,1,0:T(8,128)(2,1)S(1)}, u32[]{:S(2)}, u32[]{:S(2)}) collective-permute-start(bf16[4,256,512]{2,1,0:T(8,128)(2,1)S(1)} %pad_maximum_fusion.10), channel_id=1, source_target_pairs={{0,16},{1,17},{2,18},{3,19},{4,20},{5,21},{6,22},{7,23},{8,24},{9,... | collective-permute-start | bytes 3145736 | tf_op jit(solution)/shard_map/ppermute | solution.py:310
  48.3 43.4 %collective-permute-start.18 = (bf16[4,256,512]{2,1,0:T(8,128)(2,1)S(1)}, bf16[4,256,512]{2,1,0:T(8,128)(2,1)S(1)}, u32[]{:S(2)}, u32[]{:S(2)}) collective-permute-start(bf16[4,256,512]{2,1,0:T(8,128)(2,1)S(1)} %pad_maximum_fusion.11), channel_id=1, source_target_pairs={{0,8},{1,9},{2,10},{3,11},{4,12},{5,13},{6,14},{7,15},{8,0},{9,1},... | collective-permute-start | bytes 3145736 | tf_op jit(solution)/shard_map/ppermute | solution.py:310
  49.8 41.8 %collective-permute-start.14 = (bf16[512,1024]{1,0:T(8,128)(2,1)S(1)}, bf16[512,1024]{1,0:T(8,128)(2,1)S(1)}, u32[]{:S(2)}, u32[]{:S(2)}) collective-permute-start(bf16[512,1024]{1,0:T(8,128)(2,1)S(1)} %collective-permute-done.9.refs_0_), channel_id=1, source_target_pairs={{0,4},{1,5},{2,6},{3,7},{4,0},{5,1},{6,2},{7,3},{8,12},{9,13},{10,... | collective-permute-start | bytes 3145736 | tf_op jit(solution)/shard_map/ppermute | solution.py:310
  68.2 23.5 %collective-permute-start.16 = (bf16[512,1024]{1,0:T(8,128)(2,1)S(1)}, bf16[512,1024]{1,0:T(8,128)(2,1)S(1)}, u32[]{:S(2)}, u32[]{:S(2)}) collective-permute-start(bf16[512,1024]{1,0:T(8,128)(2,1)S(1)} %collective-permute-done.15.refs_2_), channel_id=1, source_target_pairs={{0,4},{1,5},{2,6},{3,7},{4,0},{5,1},{6,2},{7,3},{8,12},{9,13},{10,... | collective-permute-start | bytes 3145736 | tf_op jit(solution)/shard_map/ppermute | solution.py:310
  77.4 30.1 %collective-permute-start.19 = (bf16[3,256,512]{2,1,0:T(8,128)(2,1)S(1)}, bf16[3,256,512]{2,1,0:T(8,128)(2,1)S(1)}, u32[]{:S(2)}, u32[]{:S(2)}) collective-permute-start(bf16[3,256,512]{2,1,0:T(8,128)(2,1)S(1)} %collective-permute-done.12), channel_id=1, source_target_pairs={{0,16},{1,17},{2,18},{3,19},{4,20},{5,21},{6,22},{7,23},{8,24},{9,... | collective-permute-start | bytes 2359304 | tf_op jit(solution)/shard_map/ppermute | solution.py:310
  79.0 29.5 %collective-permute-start.20 = (bf16[3,256,512]{2,1,0:T(8,128)(2,1)S(1)}, bf16[3,256,512]{2,1,0:T(8,128)(2,1)S(1)}, u32[]{:S(2)}, u32[]{:S(2)}) collective-permute-start(bf16[3,256,512]{2,1,0:T(8,128)(2,1)S(1)} %maximum_select_fusion.1), channel_id=1, source_target_pairs={{0,1},{1,0},{2,3},{3,2},{4,5},{5,4},{6,7},{7,6},{8,9},{9,8},{10,11... | collective-permute-start | bytes 2359304 | tf_op jit(solution)/shard_map/ppermute | solution.py:310
  108.5 26.0 %collective-permute-start.21 = (bf16[3,256,512]{2,1,0:T(8,128)(2,1)S(1)}, bf16[3,256,512]{2,1,0:T(8,128)(2,1)}, u32[]{:S(2)}, u32[]{:S(2)}) collective-permute-start(bf16[3,256,512]{2,1,0:T(8,128)(2,1)S(1)} %collective-permute-done.20), channel_id=1, source_target_pairs={{0,8},{1,9},{2,10},{3,11},{4,12},{5,13},{6,14},{7,15},{8,0},{9,1},... | collective-permute-start | bytes 2359304 | tf_op jit(solution)/shard_map/ppermute | solution.py:310
  110.0 24.5 %collective-permute-start.22 = (bf16[3,256,512]{2,1,0:T(8,128)(2,1)S(1)}, bf16[3,256,512]{2,1,0:T(8,128)(2,1)S(1)}, u32[]{:S(2)}, u32[]{:S(2)}) collective-permute-start(bf16[3,256,512]{2,1,0:T(8,128)(2,1)S(1)} %collective-permute-done.20), channel_id=1, source_target_pairs={{0,16},{1,17},{2,18},{3,19},{4,20},{5,21},{6,22},{7,23},{8,24},{9,... | collective-permute-start | bytes 2359304 | tf_op jit(solution)/shard_map/ppermute | solution.py:310
  110.5 37.4 %collective-permute-start.23 = (bf16[3,256,512]{2,1,0:T(8,128)(2,1)S(1)}, bf16[3,256,512]{2,1,0:T(8,128)(2,1)S(1)}, u32[]{:S(2)}, u32[]{:S(2)}) collective-permute-start(bf16[3,256,512]{2,1,0:T(8,128)(2,1)S(1)} %maximum_select_fusion.1), channel_id=1, source_target_pairs={{0,2},{1,3},{2,0},{3,1},{4,6},{5,7},{6,4},{7,5},{8,10},{9,11},{10,... | collective-permute-start | bytes 2359304 | tf_op jit(solution)/shard_map/ppermute | solution.py:310
  148.0 34.8 %collective-permute-start.26 = (bf16[2,3,256,512]{3,2,1,0:T(8,128)(2,1)S(1)}, bf16[2,3,256,512]{3,2,1,0:T(8,128)(2,1)S(1)}, u32[]{:S(2)}, u32[]{:S(2)}) collective-permute-start(bf16[2,3,256,512]{3,2,1,0:T(8,128)(2,1)S(1)} %pad_maximum_fusion.3), channel_id=1, source_target_pairs={{0,8},{1,9},{2,10},{3,11},{4,12},{5,13},{6,14},{7,15},{8,0},{9,1},... | collective-permute-start | bytes 4718600 | tf_op jit(solution)/shard_map/ppermute | solution.py:310
  148.6 18.4 %collective-permute-start.24 = (bf16[3,256,512]{2,1,0:T(8,128)(2,1)S(1)}, bf16[3,256,512]{2,1,0:T(8,128)(2,1)S(1)}, u32[]{:S(2)}, u32[]{:S(2)}) collective-permute-start(bf16[3,256,512]{2,1,0:T(8,128)(2,1)S(1)} %collective-permute-done.23), channel_id=1, source_target_pairs={{0,1},{1,0},{2,3},{3,2},{4,5},{5,4},{6,7},{7,6},{8,9},{9,8},{10,11... | collective-permute-start | bytes 2359304 | tf_op jit(solution)/shard_map/ppermute | solution.py:310
  149.4 18.9 %collective-permute-start.25 = (bf16[3,256,512]{2,1,0:T(8,128)(2,1)S(1)}, bf16[3,256,512]{2,1,0:T(8,128)(2,1)S(1)}, u32[]{:S(2)}, u32[]{:S(2)}) collective-permute-start(bf16[3,256,512]{2,1,0:T(8,128)(2,1)S(1)} %collective-permute-done.23), channel_id=1, source_target_pairs={{0,16},{1,17},{2,18},{3,19},{4,20},{5,21},{6,22},{7,23},{8,24},{9,... | collective-permute-start | bytes 2359304 | tf_op jit(solution)/shard_map/ppermute | solution.py:310
  182.9 3.6 collective-permute-start.28
  183.0 3.5 collective-permute-start.27
  183.6 22.2 %collective-permute-start.32 = (bf16[3,256,512]{2,1,0:T(8,128)(2,1)S(1)}, bf16[3,256,512]{2,1,0:T(8,128)(2,1)S(1)}, u32[]{:S(2)}, u32[]{:S(2)}) collective-permute-start(bf16[3,256,512]{2,1,0:T(8,128)(2,1)S(1)} %collective-permute-done.24), channel_id=1, source_target_pairs={{0,8},{1,9},{2,10},{3,11},{4,12},{5,13},{6,14},{7,15},{8,0},{9,1},... | collective-permute-start | bytes 2359304 | tf_op jit(solution)/shard_map/ppermute | solution.py:310
  184.3 36.6 %collective-permute-start.31 = (bf16[2,3,256,512]{3,2,1,0:T(8,128)(2,1)S(1)}, bf16[2,3,256,512]{3,2,1,0:T(8,128)(2,1)S(1)}, u32[]{:S(2)}, u32[]{:S(2)}) collective-permute-start(bf16[2,3,256,512]{3,2,1,0:T(8,128)(2,1)S(1)} %pad_maximum_fusion.4), channel_id=1, source_target_pairs={{0,16},{1,17},{2,18},{3,19},{4,20},{5,21},{6,22},{7,23},{8,24},{9,... | collective-permute-start | bytes 4718600 | tf_op jit(solution)/shard_map/ppermute | solution.py:310
  220.9 27.3 %collective-permute-start.34 = (bf16[512,1024]{1,0:T(8,128)(2,1)S(1)}, bf16[512,1024]{1,0:T(8,128)(2,1)}, u32[]{:S(2)}, u32[]{:S(2)}) collective-permute-start(bf16[512,1024]{1,0:T(8,128)(2,1)S(1)} %pad_maximum_fusion.12), channel_id=1, source_target_pairs={{0,0},{1,1},{2,5},{3,4},{4,3},{5,2},{6,6},{7,7},{8,8},{9,9},{10,13... | collective-permute-start | bytes 3145736 | tf_op jit(solution)/shard_map/ppermute | solution.py:310
  222.6 16.3 %collective-permute-start.33 = (bf16[3,256,512]{2,1,0:T(8,128)(2,1)S(1)}, bf16[3,256,512]{2,1,0:T(8,128)(2,1)S(1)}, u32[]{:S(2)}, u32[]{:S(2)}) collective-permute-start(bf16[3,256,512]{2,1,0:T(8,128)(2,1)S(1)} %slice_bitcast_fusion.1), channel_id=1, source_target_pairs={{0,8},{1,9},{2,10},{3,11},{4,12},{5,13},{6,14},{7,15},{8,0},{9,1},... | collective-permute-start | bytes 2359304 | tf_op jit(solution)/shard_map/ppermute | solution.py:310
  248.3 6.6 %collective-permute-start.35 = (bf16[512,1024]{1,0:T(8,128)(2,1)}, bf16[512,1024]{1,0:T(8,128)(2,1)}, u32[]{:S(2)}, u32[]{:S(2)}) collective-permute-start(bf16[512,1024]{1,0:T(8,128)(2,1)} %slice.411), channel_id=1, source_target_pairs={{0,4},{1,5},{2,6},{3,7},{4,0},{5,1},{6,2},{7,3},{8,12},{9,13},{10,... | collective-permute-start | bytes 3145736 | tf_op jit(solution)/shard_map/ppermute | solution.py:310
  261.9 52.7 %collective-permute-start.37 = (bf16[512,1024]{1,0:T(8,128)(2,1)}, bf16[512,1024]{1,0:T(8,128)(2,1)S(1)}, u32[]{:S(2)}, u32[]{:S(2)}) collective-permute-start(bf16[512,1024]{1,0:T(8,128)(2,1)} %pad_maximum_fusion.13), channel_id=1, source_target_pairs={{0,0},{1,1},{2,5},{3,4},{4,3},{5,2},{6,6},{7,7},{8,8},{9,9},{10,13... | collective-permute-start | bytes 3145736 | tf_op jit(solution)/shard_map/ppermute | solution.py:310
  287.0 27.6 %collective-permute-start.38 = (bf16[3,256,512]{2,1,0:T(8,128)(2,1)}, bf16[3,256,512]{2,1,0:T(8,128)(2,1)}, u32[]{:S(2)}, u32[]{:S(2)}) collective-permute-start(bf16[3,256,512]{2,1,0:T(8,128)(2,1)} %get-tuple-element.258), channel_id=1, source_target_pairs={{0,16},{1,17},{2,18},{3,19},{4,20},{5,21},{6,22},{7,23},{8,24},{9,... | collective-permute-start | bytes 2359304 | tf_op jit(solution)/shard_map/ppermute | solution.py:310
  288.8 25.8 %collective-permute-start.39 = (bf16[3,256,512]{2,1,0:T(8,128)(2,1)}, bf16[3,256,512]{2,1,0:T(8,128)(2,1)S(1)}, u32[]{:S(2)}, u32[]{:S(2)}) collective-permute-start(bf16[3,256,512]{2,1,0:T(8,128)(2,1)} %get-tuple-element.259), channel_id=1, source_target_pairs={{0,8},{1,9},{2,10},{3,11},{4,12},{5,13},{6,14},{7,15},{8,0},{9,1},... | collective-permute-start | bytes 2359304 | tf_op jit(solution)/shard_map/ppermute | solution.py:310
  316.7 4.3 collective-permute-start.41
  326.8 51.8 %collective-permute-start.44 = (bf16[2,3,256,512]{3,2,1,0:T(8,128)(2,1)S(1)}, bf16[2,3,256,512]{3,2,1,0:T(8,128)(2,1)S(1)}, u32[]{:S(2)}, u32[]{:S(2)}) collective-permute-start(bf16[2,3,256,512]{3,2,1,0:T(8,128)(2,1)S(1)} %pad_maximum_fusion.5), channel_id=1, source_target_pairs={{0,8},{1,9},{2,10},{3,11},{4,12},{5,13},{6,14},{7,15},{8,0},{9,1},... | collective-permute-start | bytes 4718600 | tf_op jit(solution)/shard_map/ppermute | solution.py:310
  330.2 48.4 %collective-permute-start.45 = (bf16[2,3,256,512]{3,2,1,0:T(8,128)(2,1)S(1)}, bf16[2,3,256,512]{3,2,1,0:T(8,128)(2,1)S(1)}, u32[]{:S(2)}, u32[]{:S(2)}) collective-permute-start(bf16[2,3,256,512]{3,2,1,0:T(8,128)(2,1)S(1)} %pad_maximum_fusion.6), channel_id=1, source_target_pairs={{0,16},{1,17},{2,18},{3,19},{4,20},{5,21},{6,22},{7,23},{8,24},{9,... | collective-permute-start | bytes 4718600 | tf_op jit(solution)/shard_map/ppermute | solution.py:310
  374.3 20.2 %collective-permute-start.46 = (bf16[3,256,512]{2,1,0:T(8,128)(2,1)}, bf16[3,256,512]{2,1,0:T(8,128)(2,1)}, u32[]{:S(2)}, u32[]{:S(2)}) collective-permute-start(bf16[3,256,512]{2,1,0:T(8,128)(2,1)} %get-tuple-element.289), channel_id=1, source_target_pairs={{0,16},{1,17},{2,18},{3,19},{4,20},{5,21},{6,22},{7,23},{8,24},{9,... | collective-permute-start | bytes 2359304 | tf_op jit(solution)/shard_map/ppermute | solution.py:310
  375.8 19.4 %collective-permute-start.47 = (bf16[3,256,512]{2,1,0:T(8,128)(2,1)}, bf16[3,256,512]{2,1,0:T(8,128)(2,1)}, u32[]{:S(2)}, u32[]{:S(2)}) collective-permute-start(bf16[3,256,512]{2,1,0:T(8,128)(2,1)} %get-tuple-element.290), channel_id=1, source_target_pairs={{0,8},{1,9},{2,10},{3,11},{4,12},{5,13},{6,14},{7,15},{8,0},{9,1},... | collective-permute-start | bytes 2359304 | tf_op jit(solution)/shard_map/ppermute | solution.py:310
  388.6 6.6 %collective-permute-start.48 = (bf16[512,1024]{1,0:T(8,128)(2,1)S(1)}, bf16[512,1024]{1,0:T(8,128)(2,1)S(1)}, u32[]{:S(2)}, u32[]{:S(2)}) collective-permute-start(bf16[512,1024]{1,0:T(8,128)(2,1)S(1)} %slice.410), channel_id=1, source_target_pairs={{0,4},{1,5},{2,6},{3,7},{4,0},{5,1},{6,2},{7,3},{8,12},{9,13},{10,... | collective-permute-start | bytes 3145736 | tf_op jit(solution)/shard_map/ppermute | solution.py:310
  388.8 6.4 %collective-permute-start.49 = (bf16[512,1024]{1,0:T(8,128)(2,1)S(1)}, bf16[512,1024]{1,0:T(8,128)(2,1)S(1)}, u32[]{:S(2)}, u32[]{:S(2)}) collective-permute-start(bf16[512,1024]{1,0:T(8,128)(2,1)S(1)} %slice.409), channel_id=1, source_target_pairs={{0,4},{1,5},{2,6},{3,7},{4,0},{5,1},{6,2},{7,3},{8,12},{9,13},{10,... | collective-permute-start | bytes 3145736 | tf_op jit(solution)/shard_map/ppermute | solution.py:310
  390.8 20.5 %collective-permute-start.51 = (bf16[3,256,512]{2,1,0:T(8,128)(2,1)S(1)}, bf16[3,256,512]{2,1,0:T(8,128)(2,1)S(1)}, u32[]{:S(2)}, u32[]{:S(2)}) collective-permute-start(bf16[3,256,512]{2,1,0:T(8,128)(2,1)S(1)} %get-tuple-element.373), channel_id=1, source_target_pairs={{0,1},{1,0},{2,3},{3,2},{4,5},{5,4},{6,7},{7,6},{8,9},{9,8},{10,11... | collective-permute-start | bytes 2359304 | tf_op jit(solution)/shard_map/ppermute | solution.py:310
  395.6 36.7 %collective-permute-start.50 = (bf16[512,1024]{1,0:T(8,128)(2,1)S(1)}, bf16[512,1024]{1,0:T(8,128)(2,1)S(1)}, u32[]{:S(2)}, u32[]{:S(2)}) collective-permute-start(bf16[512,1024]{1,0:T(8,128)(2,1)S(1)} %add_convert_fusion), channel_id=1, source_target_pairs={{0,1},{1,0},{2,3},{3,2},{4,5},{5,4},{6,7},{7,6},{8,9},{9,8},{10,11... | collective-permute-start | bytes 3145736 | tf_op jit(solution)/shard_map/ppermute | solution.py:310
  395.6 62.6 %collective-permute-start.55 = (bf16[256,1024]{1,0:T(8,128)(2,1)S(1)}, bf16[256,1024]{1,0:T(8,128)(2,1)S(1)}, u32[]{:S(2)}, u32[]{:S(2)}) collective-permute-start(bf16[256,1024]{1,0:T(8,128)(2,1)S(1)} %get-tuple-element.312), channel_id=1, source_target_pairs={{0,16},{1,17},{2,18},{3,19},{4,20},{5,21},{6,22},{7,23},{8,24},{9,... | collective-permute-start | bytes 1572872 | tf_op jit(solution)/shard_map/ppermute | solution.py:310
  396.8 61.5 %collective-permute-start.56 = (bf16[256,1024]{1,0:T(8,128)(2,1)S(1)}, bf16[256,1024]{1,0:T(8,128)(2,1)S(1)}, u32[]{:S(2)}, u32[]{:S(2)}) collective-permute-start(bf16[256,1024]{1,0:T(8,128)(2,1)S(1)} %get-tuple-element.315), channel_id=1, source_target_pairs={{0,8},{1,9},{2,10},{3,11},{4,12},{5,13},{6,14},{7,15},{8,0},{9,1},... | collective-permute-start | bytes 1572872 | tf_op jit(solution)/shard_map/ppermute | solution.py:310
  412.9 33.4 %collective-permute-start.52 = (bf16[2,3,256,512]{3,2,1,0:T(8,128)(2,1)S(1)}, bf16[2,3,256,512]{3,2,1,0:T(8,128)(2,1)S(1)}, u32[]{:S(2)}, u32[]{:S(2)}) collective-permute-start(bf16[2,3,256,512]{3,2,1,0:T(8,128)(2,1)S(1)} %pad_maximum_fusion.7), channel_id=1, source_target_pairs={{0,8},{1,9},{2,10},{3,11},{4,12},{5,13},{6,14},{7,15},{8,0},{9,1},... | collective-permute-start | bytes 4718600 | tf_op jit(solution)/shard_map/ppermute | solution.py:310
  415.4 33.4 %collective-permute-start.53 = (bf16[2,3,256,512]{3,2,1,0:T(8,128)(2,1)S(1)}, bf16[2,3,256,512]{3,2,1,0:T(8,128)(2,1)S(1)}, u32[]{:S(2)}, u32[]{:S(2)}) collective-permute-start(bf16[2,3,256,512]{3,2,1,0:T(8,128)(2,1)S(1)} %pad_maximum_fusion.8), channel_id=1, source_target_pairs={{0,16},{1,17},{2,18},{3,19},{4,20},{5,21},{6,22},{7,23},{8,24},{9,... | collective-permute-start | bytes 4718600 | tf_op jit(solution)/shard_map/ppermute | solution.py:310
  432.3 47.3 %collective-permute-start.61 = (bf16[3,256,512]{2,1,0:T(8,128)(2,1)}, bf16[3,256,512]{2,1,0:T(8,128)(2,1)S(1)}, u32[]{:S(2)}, u32[]{:S(2)}) collective-permute-start(bf16[3,256,512]{2,1,0:T(8,128)(2,1)} %add_convert_fusion.1), channel_id=1, source_target_pairs={{0,2},{1,3},{2,0},{3,1},{4,6},{5,7},{6,4},{7,5},{8,10},{9,11},{10,... | collective-permute-start | bytes 2359304 | tf_op jit(solution)/shard_map/ppermute | solution.py:310
  448.8 16.2 %collective-permute-start.54 = (bf16[512,1024]{1,0:T(8,128)(2,1)}, bf16[512,1024]{1,0:T(8,128)(2,1)}, u32[]{:S(2)}, u32[]{:S(2)}) collective-permute-start(bf16[512,1024]{1,0:T(8,128)(2,1)} %pad_maximum_fusion.14), channel_id=1, source_target_pairs={{0,0},{1,1},{2,5},{3,4},{4,3},{5,2},{6,6},{7,7},{8,8},{9,9},{10,13... | collective-permute-start | bytes 3145736 | tf_op jit(solution)/shard_map/ppermute | solution.py:310
  459.5 38.4 %collective-permute-start.57 = (bf16[2,256,1024]{2,1,0:T(8,128)(2,1)}, bf16[2,256,1024]{2,1,0:T(8,128)(2,1)}, u32[]{:S(2)}, u32[]{:S(2)}) collective-permute-start(bf16[2,256,1024]{2,1,0:T(8,128)(2,1)} %pad_maximum_fusion.15), channel_id=1, source_target_pairs={{0,8},{1,9},{2,10},{3,11},{4,12},{5,13},{6,14},{7,15},{8,0},{9,1},... | collective-permute-start | bytes 3145736 | tf_op jit(solution)/shard_map/ppermute | solution.py:310
  462.0 34.4 %collective-permute-start.60 = (bf16[3,256,512]{2,1,0:T(8,128)(2,1)}, bf16[3,256,512]{2,1,0:T(8,128)(2,1)}, u32[]{:S(2)}, u32[]{:S(2)}) collective-permute-start(bf16[3,256,512]{2,1,0:T(8,128)(2,1)} %get-tuple-element.371), channel_id=1, source_target_pairs={{0,1},{1,0},{2,3},{3,2},{4,5},{5,4},{6,7},{7,6},{8,9},{9,8},{10,11... | collective-permute-start | bytes 2359304 | tf_op jit(solution)/shard_map/ppermute | solution.py:310
  463.9 34.0 %collective-permute-start.58 = (bf16[2,256,1024]{2,1,0:T(8,128)(2,1)}, bf16[2,256,1024]{2,1,0:T(8,128)(2,1)}, u32[]{:S(2)}, u32[]{:S(2)}) collective-permute-start(bf16[2,256,1024]{2,1,0:T(8,128)(2,1)} %pad_maximum_fusion.16), channel_id=1, source_target_pairs={{0,16},{1,17},{2,18},{3,19},{4,20},{5,21},{6,22},{7,23},{8,24},{9,... | collective-permute-start | bytes 3145736 | tf_op jit(solution)/shard_map/ppermute | solution.py:310
  465.0 32.9 %collective-permute-start.59 = (f32[2,512]{1,0:T(2,128)S(1)}, f32[2,512]{1,0:T(2,128)S(1)}, u32[]{:S(2)}, u32[]{:S(2)}) collective-permute-start(f32[2,512]{1,0:T(2,128)S(1)} %pad_maximum_fusion.30), channel_id=1, source_target_pairs={{0,8},{1,9},{2,10},{3,11},{4,12},{5,13},{6,14},{7,15},{8,0},{9,1},... | collective-permute-start | bytes 12296 | tf_op jit(solution)/shard_map/ppermute | solution.py:310
  500.1 9.2 %collective-permute-start.63 = (bf16[256,512]{1,0:T(8,128)(2,1)S(1)}, bf16[256,512]{1,0:T(8,128)(2,1)S(1)}, u32[]{:S(2)}, u32[]{:S(2)}) collective-permute-start(bf16[256,512]{1,0:T(8,128)(2,1)S(1)} %get-tuple-element.344), channel_id=1, source_target_pairs={{0,1},{1,0},{2,3},{3,2},{4,5},{5,4},{6,7},{7,6},{8,9},{9,8},{10,11... | collective-permute-start | bytes 786440 | tf_op jit(solution)/shard_map/ppermute | solution.py:310
  500.2 5.6 %collective-permute-start.64 = (f32[2,256]{1,0:T(2,128)S(1)}, f32[2,256]{1,0:T(2,128)S(1)}, u32[]{:S(2)}, u32[]{:S(2)}) collective-permute-start(f32[2,256]{1,0:T(2,128)S(1)} %slice_add_fusion.2), channel_id=1, source_target_pairs={{0,16},{1,17},{2,18},{3,19},{4,20},{5,21},{6,22},{7,23},{8,24},{9,... | collective-permute-start | bytes 6152 | tf_op jit(solution)/shard_map/ppermute | solution.py:310
  503.9 21.7 %collective-permute-start.62 = (bf16[256,512]{1,0:T(8,128)(2,1)S(1)}, bf16[256,512]{1,0:T(8,128)(2,1)S(1)}, u32[]{:S(2)}, u32[]{:S(2)}) collective-permute-start(bf16[256,512]{1,0:T(8,128)(2,1)S(1)} %slice.413), channel_id=1, source_target_pairs={{0,1},{1,0},{2,3},{3,2},{4,5},{5,4},{6,7},{7,6},{8,9},{9,8},{10,11... | collective-permute-start | bytes 786440 | tf_op jit(solution)/shard_map/ppermute | solution.py:310
  505.9 4.7 collective-permute-start.67
  509.5 16.1 %collective-permute-start.65 = (bf16[256,512]{1,0:T(8,128)(2,1)S(1)}, bf16[256,512]{1,0:T(8,128)(2,1)S(1)}, u32[]{:S(2)}, u32[]{:S(2)}) collective-permute-start(bf16[256,512]{1,0:T(8,128)(2,1)S(1)} %add_convert_fusion.8), channel_id=1, source_target_pairs={{0,2},{1,3},{2,0},{3,1},{4,6},{5,7},{6,4},{7,5},{8,10},{9,11},{10,... | collective-permute-start | bytes 786440 | tf_op jit(solution)/shard_map/ppermute | solution.py:310
  511.1 8.7 %collective-permute-start.71 = (f32[2,32]{1,0:T(2,128)S(1)}, f32[2,32]{1,0:T(2,128)S(1)}, u32[]{:S(2)}, u32[]{:S(2)}) collective-permute-start(f32[2,32]{1,0:T(2,128)S(1)} %get-tuple-element.447), channel_id=1, source_target_pairs={{0,3},{1,2},{2,1},{3,0},{4,7},{5,6},{6,5},{7,4},{8,11},{9,10},{10,... | collective-permute-start | bytes 776 | tf_op jit(solution)/shard_map/ppermute | solution.py:310
  512.8 12.1 %collective-permute-start.70 = (f32[2,32]{1,0:T(2,128)S(1)}, f32[2,32]{1,0:T(2,128)S(1)}, u32[]{:S(2)}, u32[]{:S(2)}) collective-permute-start(f32[2,32]{1,0:T(2,128)S(1)} %get-tuple-element.448), channel_id=1, source_target_pairs={{0,2},{1,3},{2,0},{3,1},{4,6},{5,7},{6,4},{7,5},{8,10},{9,11},{10,... | collective-permute-start | bytes 776 | tf_op jit(solution)/shard_map/ppermute | solution.py:310
  513.9 11.1 %collective-permute-start.69 = (f32[2,32]{1,0:T(2,128)S(1)}, f32[2,32]{1,0:T(2,128)S(1)}, u32[]{:S(2)}, u32[]{:S(2)}) collective-permute-start(f32[2,32]{1,0:T(2,128)S(1)} %get-tuple-element.446), channel_id=1, source_target_pairs={{0,1},{1,0},{2,3},{3,2},{4,5},{5,4},{6,7},{7,6},{8,9},{9,8},{10,11... | collective-permute-start | bytes 776 | tf_op jit(solution)/shard_map/ppermute | solution.py:310
  (101 other events, 964.3 us)

commit v3 on v2

--- a/solution.py
+++ b/solution.py
@@ -345,6 +345,10 @@
     return shift(value, home_of)
 
 
+def moved_home(value):
+    return shift(value, lambda *place: None if home_of(*place) == place else home_of(*place))
+
+
 def partner_of_home(y, x, c, z):
     y, x, c, z = home_of(y, x, c, z)
     z ^= 1
@@ -537,23 +541,20 @@
 
 
 def project_kernel(*refs):
-    rows_refs, gain_ref, (low_ref, low_x_ref, low_yd_ref, high_ref, high_y_ref, high_xd_ref) = refs[:4], refs[4], refs[5:11]
-    normed_ref, q_ref, k_ref, v_ref, wq_ref, wk_ref, wv_ref, wo_ref = refs[11:]
+    rows_refs, gain_ref, weight_refs = refs[:4], refs[4], (refs[5:9], refs[9:13])
+    normed_ref, q_ref, k_ref, v_ref, wq_ref, wk_ref, wv_ref, wo_ref = refs[13:]
     step = pl.program_id(0)
-    _, block, width = low_ref.shape
+    _, block, width = weight_refs[0][0].shape
     part = width // 4
     tile = rows_refs[0].shape[0] // 2
 
     @pl.when(step == 0)
     def _():
         for k in range(4):
-            if k < 2:
-                blocks = (low_ref.at[k], low_x_ref.at[k], low_yd_ref.at[k], low_yd_ref.at[k + 2])
-            else:
-                blocks = (high_ref.at[k - 2], high_xd_ref.at[k - 2], high_y_ref.at[k - 2], high_xd_ref.at[k])
             for r in range(4):
+                source = weight_refs[k // 2][r].at[k % 2]
                 for n, out in enumerate((wq_ref, wk_ref, wv_ref, wo_ref)):
-                    out[r * block : (r + 1) * block, k * part : (k + 1) * part] = blocks[r][:, n * part : (n + 1) * part]
+                    out[r * block : (r + 1) * block, k * part : (k + 1) * part] = source[:, n * part : (n + 1) * part]
 
     for n in range(4):
 
@@ -602,6 +603,140 @@
         cost_estimate=LIGHT,
         name="project",
     )(*rows_parts, gain, *weights)
+
+
+def rows_grads_kernel(dq_ref, dk_ref, dv_ref, wq_ref, wk_ref, wv_ref, own_ref, other_ref, partner_ref, partner_other_ref):
+    step = pl.program_id(0)
+    part = dot_nt(dk_ref[...], wk_ref[...]) + dot_nt(dv_ref[...], wv_ref[...])
+
+    @pl.when(step == 0)
+    def _():
+        own_ref[...] = part + dot_nt(dq_ref[...], wq_ref[...])
+
+    @pl.when(step == 1)
+    def _():
+        other_ref[...] = (part + dot_nt(dq_ref[...], wq_ref[...])).astype(BF)
+
+    @pl.when(step == 2)
+    def _():
+        partner_ref[...] = part
+
+    @pl.when(step == 3)
+    def _():
+        partner_other_ref[...] = part.astype(BF)
+
+
+def rows_grads(dq, dk, dv, wq, wk, wv):
+    slot, width = dk.shape
+    model = wq.shape[0]
+    chunk = slot // 4
+    whole = pl.BlockSpec((model, width), lambda i: (0, 0))
+    tiles = pl.BlockSpec((chunk, width), lambda i: (i, 0))
+    out = pl.BlockSpec((chunk, model), lambda i: (0, 0))
+    shape = lambda t: jax.ShapeDtypeStruct((chunk, model), t)
+    return pl.pallas_call(
+        rows_grads_kernel,
+        out_shape=(shape(F32), shape(BF), shape(F32), shape(BF)),
+        grid=(4,),
+        in_specs=[pl.BlockSpec((chunk, width), lambda i: (jnp.minimum(i, 1), 0)), tiles, tiles, whole, whole, whole],
+        out_specs=(out,) * 4,
+        compiler_params=pltpu.CompilerParams(vmem_limit_bytes=40 << 20),
+        cost_estimate=LIGHT,
+        name="rows_grads",
+    )(dq, dk, dv, wq, wk, wv)
+
+
+def attention_grads_kernel(x_ref, g_ref, dq_ref, dk_ref, dv_ref, mixed_ref, *out_refs):
+    rows = g_ref.shape[0]
+    x_turned = jnp.transpose(x_ref[...])
+    g_turned = jnp.transpose(g_ref[...])
+    grads = (
+        dot_nn(x_turned[:, :rows], dq_ref[...]),
+        dot_nn(x_turned, dk_ref[...]),
+        dot_nn(x_turned, dv_ref[...]),
+        dot_nn(g_turned, mixed_ref[...]),
+    )
+    part = dq_ref.shape[1] // 4
+    for r in range(4):
+
+        @pl.when(pl.program_id(0) == r)
+        def _():
+            for k in range(4):
+                for n in range(4):
+                    start = (k % 2 * 4 + n) * part
+                    out_refs[k // 2 * 4 + r][:, start : start + part] = grads[n][:, k * part : (k + 1) * part].astype(BF)
+
+
+def attention_grads(x, g, dq, dk, dv, mixed):
+    rows, model = g.shape
+    slot, width = dk.shape
+    block = model // 4
+    whole = lambda a: pl.BlockSpec(a.shape, lambda i: (0, 0))
+    out = pl.pallas_call(
+        attention_grads_kernel,
+        out_shape=(jax.ShapeDtypeStruct((block, 2 * width), BF),) * 8,
+        grid=(4,),
+        in_specs=[
+            pl.BlockSpec((slot, block), lambda i: (0, i)),
+            pl.BlockSpec((rows, block), lambda i: (0, i)),
+            whole(dq),
+            whole(dk),
+            whole(dv),
+            whole(mixed),
+        ],
+        out_specs=(pl.BlockSpec((block, 2 * width), lambda i: (0, 0)),) * 8,
+        compiler_params=pltpu.CompilerParams(vmem_limit_bytes=40 << 20),
+        cost_estimate=LIGHT,
+        name="attention_grads",
+    )(x, g, dq, dk, dv, mixed)
+    return out[:4], out[4:]
+
+
+def norm_grads_kernel(part_ref, first_ref, second_ref, values_ref, grad_ref, gain_ref, out_ref, low_ref, gain_grad_ref):
+    step = pl.program_id(0)
+    values = values_ref[...]
+    inverse = lax.rsqrt(jnp.mean(values * values, axis=-1, keepdims=True) + 1e-05)
+    scaled = values * inverse
+
+    @pl.when(step == 0)
+    def _():
+        gain_grad_ref[...] = jnp.zeros_like(gain_grad_ref)
+
+    received = jnp.where(step < 2, first_ref[...].astype(F32), second_ref[...].astype(F32))
+    grad_normed = part_ref[...] + received
+    grad_scaled = grad_normed * gain_ref[...]
+    grad = grad_ref[...] + inverse * (grad_scaled - scaled * jnp.mean(grad_scaled * scaled, axis=-1, keepdims=True))
+    out_ref[...] = grad
+    low_ref[...] = grad.astype(BF)
+    gain_grad_ref[...] += jnp.sum(grad_normed * scaled, axis=0, keepdims=True)
+
+
+def norm_grads(part, first, second, values, grad, gain):
+    rows, model = part.shape
+    tile = rows // 4
+    tiles = pl.BlockSpec((tile, model), lambda i: (i, 0))
+    row = pl.BlockSpec((1, model), lambda i: (0, 0))
+    return pl.pallas_call(
+        norm_grads_kernel,
+        out_shape=(
+            jax.ShapeDtypeStruct((rows, model), F32),
+            jax.ShapeDtypeStruct((rows, model), BF),
+            jax.ShapeDtypeStruct((1, model), F32),
+        ),
+        grid=(4,),
+        in_specs=[
+            tiles,
+            pl.BlockSpec((tile, model), lambda i: (jnp.minimum(i, 1), 0)),
+            pl.BlockSpec((tile, model), lambda i: (jnp.maximum(i - 2, 0), 0)),
+            tiles,
+            tiles,
+            row,
+        ],
+        out_specs=(tiles, tiles, row),
+        compiler_params=pltpu.CompilerParams(vmem_limit_bytes=24 << 20),
+        cost_estimate=LIGHT,
+        name="norm_grads",
+    )(part, first, second, values, grad, gain[None])
 
 
 def feed_forward_kernel(first_piece, *refs):
@@ -789,6 +924,7 @@
     odd_x = (dp // 2) % 2 == 1
     odd_y = dp // 4 == 1
     inner = jnp.where((z == 1) | (z == 2), 1, 0)
+    moves = (core == 1) == (z < 2)
     chunk_low, chunk_high = inner, 3 - inner
     length = lax.dynamic_index_in_dim(lengths, (dp // 2) * 2 + z // 2, 0, keepdims=False)
     count = jnp.sum(lengths).astype(F32)
@@ -851,22 +987,22 @@
     gains_x, gains_y, gains_d, attention_piece, feed_p[0] = event(gains_x, gains_y, gains_d, attention_piece, feed_piece)
     gains_all = jnp.concatenate([gains_pair, gains_x, gains_y, gains_d], axis=0)
 
+    inputs_rel, attention_piece = event(inputs_rel, attention_piece)
+    own_rows, partner_rows = home_swap(inputs_rel), shift(inputs_rel, partner_of_home)
     att_1, att_2, att_3 = z_swap(attention_piece, 1), z_swap(attention_piece, 2), z_swap(attention_piece, 3)
-    feed_x[0], feed_y[0] = x_swap(feed_p[0]), y_swap(feed_p[0])
-    att_1, att_2, att_3, inputs_rel = event(att_1, att_2, att_3, inputs_rel)
+    att_1, att_2, att_3, feed_piece = event(att_1, att_2, att_3, feed_p[0])
     att_low, att_high = jnp.stack([attention_piece, att_1]), jnp.stack([att_2, att_3])
-    own_rows, partner_rows = home_swap(inputs_rel), shift(inputs_rel, partner_of_home)
     att_low_x, att_high_y = x_swap(att_low), y_swap(att_high)
-    feed_x[0], feed_y[0] = event(feed_x[0], feed_y[0])
-    att_low_x, att_high_y, feed_piece = event(att_low_x, att_high_y, feed_p[0])
-    att_low_yd = y_swap(jnp.concatenate([att_low, att_low_x], axis=0))
-    att_high_xd = x_swap(jnp.concatenate([att_high, att_high_y], axis=0))
-    own_rows, feed_piece = event(own_rows, feed_piece)
-    partner_rows, feed_piece, feed_x[0] = event(partner_rows, feed_piece, feed_x[0])
-    other_rows, other_partner = core_swap(own_rows), core_swap(partner_rows)
+    att_low_y, att_high_x = y_swap(att_low), x_swap(att_high)
+    att_low_x, att_high_y = event(att_low_x, att_high_y)
+    att_low_d, att_high_d = y_swap(att_low_x), x_swap(att_high_y)
+    (own_rows,) = event(own_rows)
+    other_rows = core_swap(own_rows)
+    partner_rows, feed_piece = event(partner_rows, feed_piece)
+    other_partner = core_swap(partner_rows)
+    feed_x[0], feed_y[0] = x_swap(feed_piece), y_swap(feed_piece)
     feed_p[1] = z_swap(feed_piece, 1)
-    feed_d[0] = y_swap(feed_x[0])
-    att_low_yd, att_high_xd = event(att_low_yd, att_high_xd)
+    att_low_y, att_high_x, att_low_d, att_high_d = event(att_low_y, att_high_x, att_low_d, att_high_d)
     other_rows, other_partner, feed_piece = event(other_rows, other_partner, feed_piece)
     feed_p[2] = z_swap(feed_piece, 2)
     rows = own_rows.astype(F32)
@@ -874,7 +1010,7 @@
     gain_two = gains_all[:, 1].astype(F32)
 
     normed_all, queries, keys_all, values_all, w_queries, w_keys, w_values, w_out = project(
-        (own_rows, other_rows, partner_rows, other_partner), gain_one[None], [att_low, att_low_x, att_low_yd, att_high, att_high_y, att_high_xd]
+        (own_rows, other_rows, partner_rows, other_partner), gain_one[None], [att_low, att_low_x, att_low_y, att_low_d, att_high, att_high_x, att_high_y, att_high_d]
     )
     normed_own = normed_all[: 2 * chunk]
     outer_only = (1 - inner)[None].astype(jnp.int32)
@@ -883,25 +1019,31 @@
     def attend(n):
         return attend_forward(outer_only, scalars, queries, keys_all, values_all, n, 1)
 
-    queries, feed_d[0], feed_p[1] = event(queries, feed_d[0], feed_p[1])
+    queries, feed_x[0], feed_y[0] = event(queries, feed_x[0], feed_y[0])
+    feed_d[0] = y_swap(feed_x[0])
+    parts[0] = attend(0)
+    queries, feed_p[1], _ = event(queries, feed_p[1], parts[0][0])
     feed_x[1], feed_y[1] = x_swap(feed_p[1]), y_swap(feed_p[1])
-    parts[0] = attend(0)
     parts[1] = attend(1)
-    queries, feed_x[1], feed_y[1], feed_p[2], _, _ = event(queries, feed_x[1], feed_y[1], feed_p[2], parts[0][0], parts[1][0])
+    queries, feed_d[0], feed_p[2], _ = event(queries, feed_d[0], feed_p[2], parts[1][0])
+    feed_y[2] = y_swap(feed_p[2])
     feed_p[3] = z_swap(feed_p[2], 1)
+    parts[2] = attend(2)
+    queries, feed_x[1], feed_y[1], _ = event(queries, feed_x[1], feed_y[1], parts[2][0])
     batch_x = x_swap(jnp.stack([feed_y[1], feed_p[2]]))
-    feed_y[2] = y_swap(feed_p[2])
-    parts[2] = attend(2)
     parts[3] = attend(3)
     mixed = jnp.concatenate([p[0] for p in parts], axis=1)
     branch = matmul_nt(mixed, w_out)
-    branch_own, branch_other, feed_p[3], feed_y[2], batch_x, teacher = event(
-        branch[:chunk], branch[chunk:].astype(BF), feed_p[3], feed_y[2], batch_x, teacher
-    )
-    batch_y = y_swap(jnp.stack([feed_p[3], batch_x[1]]))
-    feed_x[3] = x_swap(feed_p[3])
+    branch_own, branch_other, feed_p[3], feed_y[2], teacher = event(
+        branch[:chunk], branch[chunk:].astype(BF), feed_p[3], feed_y[2], teacher
+    )
+    feed_y[3] = y_swap(feed_p[3])
+    branch_other, batch_x, feed_y[3] = event(core_swap(branch_other), batch_x, feed_y[3])
+    batch_x3, x_2 = event(jnp.stack([feed_p[3], feed_y[3]]), batch_x[1])
+    batch_x3 = x_swap(batch_x3)
+    feed_d[2] = y_swap(x_2)
     teacher_rel = turn(teacher)
-    middle = rows + branch_own + core_swap_halves(branch_other).astype(F32)
+    middle = rows + branch_own + branch_other.astype(F32)
 
     scaled_two, inverse_two = norm_forward(middle)
     normed_two = (scaled_two * gain_two).astype(BF)
@@ -913,23 +1055,24 @@
     ]
     for k in range(4):
         if k == 2:
-            feed, batch_y, feed_x[3], teacher_rel = event(feed, batch_y, feed_x[3], teacher_rel)
-            feed_d[3] = x_swap(batch_y[0])
-            teacher_rows = home_swap(teacher_rel)
-            pieces.append([alone(feed_p[2]), (batch_x, 1), alone(feed_y[2]), (batch_y, 1)])
+            feed, feed_d[2], teacher_rel = event(feed, feed_d[2], teacher_rel)
+            teacher_rows = moved_home(teacher_rel)
+            pieces.append([alone(feed_p[2]), (batch_x, 1), alone(feed_y[2]), alone(feed_d[2])])
         if k == 3:
-            feed, feed_d[3] = event(feed, feed_d[3])
-            pieces.append([alone(feed_p[3]), alone(feed_x[3]), (batch_y, 0), alone(feed_d[3])])
+            feed, batch_x3 = event(feed, batch_x3)
+            pieces.append([alone(feed_p[3]), (batch_x3, 0), alone(feed_y[3]), (batch_x3, 1)])
         silus[k], slopes[k], hiddens[k], feed = feed_forward(normed_two_all, pieces[k], feed)
     feed_own, feed_other, teacher_rows = event(feed[:chunk], feed[chunk:].astype(BF), teacher_rows)
     final = middle + feed_own + core_swap(feed_other).astype(F32)
 
     own_place = jnp.where(first, chunk_low, chunk_high) * chunk
     valid = (own_place + jnp.arange(chunk, dtype=jnp.int32) < length)[:, None]
+    teacher_rows = jnp.where(moves, teacher_rows, teacher_rel)
     grad_final = jnp.where(valid, final - teacher_rows.astype(F32), 0.0) * (total_rows / count)
     grad_feed = grad_final.astype(BF)
     grad_feed_all, output = event(jnp.concatenate([grad_feed, core_swap(grad_feed)], axis=0), turn(final.astype(BF)))
-    output = home_swap(output)
+    output_rel = output
+    output = moved_home(output)
 
     def add(a, b):
         return (a.astype(F32) + b.astype(F32)).astype(BF)
@@ -946,12 +1089,12 @@
     d_2, d_3 = y_swap(d_2), x_swap(d_3)
     (grad_x, grad_x_other), ((own_0, x_0, y_0, d_0), (own_1, x_1, y_1, d_1)) = feed_back(0, grad_x)
     grad_x, grad_x_other, output, d_2, d_3, d_0, d_1, y_2, x_3 = event(grad_x, grad_x_other, output, d_2, d_3, d_0, d_1, y_2, x_3)
-    batch_x, batch_y = x_swap(jnp.stack([add(x_2, d_2), x_3])), y_swap(jnp.stack([y_2, add(y_3, d_3)]))
-    grad_normed_two = grad_x + core_swap_halves(grad_x_other).astype(F32)
-
-    grad_norm_two, grad_gain_two = norm_backward(grad_normed_two, scaled_two, inverse_two, gain_two)
-    grad_middle = grad_final + grad_norm_two
-    grad_branch = grad_middle.astype(BF)
+    grad_x_other, batch_x, batch_y = event(grad_x_other, jnp.stack([add(x_2, d_2), x_3]), jnp.stack([y_2, add(y_3, d_3)]))
+    batch_x, batch_y = x_swap(batch_x), y_swap(batch_y)
+    tile = chunk // 2
+    first_rows, second_rows = core_swap(grad_x_other[:tile]), core_swap(grad_x_other[tile:])
+    grad_middle, grad_branch, grad_gain_two = norm_grads(grad_x, first_rows, second_rows, middle, grad_final, gain_two)
+    grad_gain_two = grad_gain_two[0]
     grad_branch_both = jnp.concatenate([grad_branch, core_swap_halves(grad_branch)], axis=0)
     grad_mixed = matmul(grad_branch_both, w_out).astype(BF)
     half_width = mixed.shape[1] // 2
@@ -965,55 +1108,40 @@
     d_0, d_1 = y_swap(d_0), x_swap(d_1)
     gq_b, gk_b, gv_b = attend_back(1)
 
-    gq_b, batch_x, batch_y = event(gq_b, batch_x, batch_y)
-    part_3 = z_swap(total_of(own_3, batch_x[1], batch_y[1]).astype(BF), 1)
-    part_2 = total_of(own_2, batch_x[0], batch_y[0]).astype(BF)
-
-    grad_queries = jnp.concatenate([gq_a, gq_b], axis=1)
+    gq_b, batch_x, batch_y, d_0, d_1, x_1, y_0 = event(gq_b, batch_x, batch_y, d_0, d_1, x_1, y_0)
+    grad_queries, batch_x, batch_y, part_3, part_2, gk_b, gv_b = event(
+        jnp.concatenate([gq_a, gq_b], axis=1),
+        jnp.stack([add(x_0, d_0), x_1]),
+        jnp.stack([y_0, add(y_1, d_1)]),
+        total_of(own_3, batch_x[1], batch_y[1]).astype(BF),
+        total_of(own_2, batch_x[0], batch_y[0]).astype(BF),
+        gk_b,
+        gv_b,
+    )
+    batch_x, batch_y, part_3 = x_swap(batch_x), y_swap(batch_y), z_swap(part_3, 1)
     grad_keys = jnp.concatenate([gk_a, gk_b], axis=1)
     grad_values = jnp.concatenate([gv_a, gv_b], axis=1)
-    part_all = (matmul_nt(grad_keys, w_keys) + matmul_nt(grad_values, w_values))
-    part_own = part_all[: 2 * chunk] + matmul_nt(grad_queries, w_queries)
-    part_own, part_other = part_own[:chunk], part_own[chunk:].astype(BF)
-    part_own, part_other, part_all, grad_queries, grad_keys, grad_values = event(
-        part_own, part_other, part_all[2 * chunk :], grad_queries, grad_keys, grad_values
-    )
-    part_other, other_partner_part = core_swap(part_other), core_swap(part_all[chunk:].astype(BF))
-
-    grad_out = matmul_tn(grad_branch_both, mixed).astype(BF)
-    grad_w_queries = matmul_tn(normed_own, grad_queries).astype(BF)
-    grad_w_keys = matmul_tn(normed_all, grad_keys).astype(BF)
-    grad_w_values = matmul_tn(normed_all, grad_values).astype(BF)
-    quarter_cols = grad_w_queries.shape[1] // 4
-
-    def attention_group(pieces):
-        cols = [g[:, k * quarter_cols : (k + 1) * quarter_cols] for k in pieces for g in (grad_w_queries, grad_w_keys, grad_w_values, grad_out)]
-        return jnp.split(jnp.concatenate(cols, axis=1), 4, axis=0)
-
+    part_own, part_other, partner_part, other_partner_part = rows_grads(grad_queries, grad_keys, grad_values, w_queries, w_keys, w_values)
+    part_other, other_partner_part, grad_queries = event(core_swap(part_other), core_swap(other_partner_part), grad_queries)
+    (from_partner,) = event((partner_part + other_partner_part.astype(F32)).astype(BF))
+    from_partner = z_swap(from_partner, 1)
+    (own_e, x_e, y_e, d_e), (own_o, x_o, y_o, d_o) = attention_grads(normed_all, grad_branch_both, grad_queries, grad_keys, grad_values, mixed)
+    quarter_cols = grad_queries.shape[1] // 4
     half_cols = 4 * quarter_cols
-    own_e, x_e, y_e, d_e = attention_group((0, 1))
-    own_o, x_o, y_o, d_o = attention_group((2, 3))
-    own_e, own_o, x_e, y_e, d_e, x_o, y_o, d_o, d_0, d_1, x_1, y_0, part_other, other_partner_part = event(
-        own_e, own_o, x_e, y_e, d_e, x_o, y_o, d_o, d_0, d_1, x_1, y_0, part_other, other_partner_part
-    )
-    batch_x, batch_y = x_swap(jnp.stack([add(x_0, d_0), x_1])), y_swap(jnp.stack([y_0, add(y_1, d_1)]))
-    from_partner = z_swap((part_all[:chunk] + other_partner_part.astype(F32)).astype(BF), 1)
-    part_3, part_2 = event(part_3, part_2)
-    part_2 = z_swap(add(part_2, part_3), 2)
+    d_e, d_o, x_e, y_e, x_o, y_o, part_3, part_2, batch_x, batch_y = event(d_e, d_o, x_e, y_e, x_o, y_o, part_3, part_2, batch_x, batch_y)
+    d_e, d_o = y_swap(d_e), x_swap(d_o)
+    part_2, part_1 = event(add(part_2, part_3), total_of(own_1, batch_x[1], batch_y[1]).astype(BF))
+    part_2, part_1 = z_swap(part_2, 2), z_swap(part_1, 1)
+    part_0 = total_of(own_0, batch_x[0], batch_y[0])
     (from_partner,) = event(from_partner)
     grad_normed_one = part_own + part_other.astype(F32) + from_partner.astype(F32)
     scaled_one, inverse_one = norm_forward(rows)
     grad_norm_one, grad_gain_one = norm_backward(grad_normed_one, scaled_one, inverse_one, gain_one)
-    grad_rows, gain_a, gain_b, batch_x, batch_y = event(
-        turn((grad_middle + grad_norm_one).astype(BF)), grad_gain_one, grad_gain_two, batch_x, batch_y
-    )
-    grad_inputs = home_swap(grad_rows)
-    part_0 = total_of(own_0, batch_x[0], batch_y[0])
-    part_1 = z_swap(total_of(own_1, batch_x[1], batch_y[1]).astype(BF), 1)
-    d_e, d_o = y_swap(d_e), x_swap(d_o)
-    d_e, d_o, y_e, x_o = event(d_e, d_o, y_e, x_o)
-    batch_x, batch_y = x_swap(jnp.stack([add(x_e, d_e), x_o])), y_swap(jnp.stack([y_e, add(y_o, d_o)]))
-    (grad_inputs,) = event(grad_inputs)
+    grad_rows, gain_a, gain_b = event(turn((grad_middle + grad_norm_one).astype(BF)), grad_gain_one, grad_gain_two)
+    grad_inputs = moved_home(grad_rows)
+    d_e, d_o = event(d_e, d_o)
+    batch_x, batch_y = event(jnp.stack([add(x_e, d_e), x_o]), jnp.stack([y_e, add(y_o, d_o)]))
+    batch_x, batch_y = x_swap(batch_x), y_swap(batch_y)
     part_1, part_2, part_0 = event(part_1, part_2, part_0)
     feed_total = part_0 + part_1.astype(F32) + part_2.astype(F32)
     feed_keep, feed_give = pick(jnp.split(feed_total, 2, axis=1))
@@ -1042,7 +1170,8 @@
     for k in range(1, 4):
         total = total + z_swap(lax.dynamic_slice_in_dim(a, (z ^ k) * size, size, 1), k)
     grad_gains = jnp.swapaxes(total, 0, 1)
-    grad_inputs = grad_inputs.astype(F32)
+    grad_inputs = jnp.where(moves, grad_inputs, grad_rows).astype(F32)
+    output = jnp.where(moves, output, output_rel)
     feed_out = sort_cores(feed_keep, feed_give.astype(F32), 2)
     attention_total = even[:, :half_cols] + att_1.astype(F32) + att_2.astype(F32)
     attention_total = jnp.stack([attention_total[:, n * quarter_cols : (n + 1) * quarter_cols] for n in range(4)])

time: 534 us -> 506 us (0.948)
  Pallas kernels: 139 us -> 161 us
  starting transfers between devices: 115 us -> 94.7 us
  waiting for transfers between devices: 175 us -> 157 us
  matrix products: 17.5 us -> 2.53 us
    pallas_call x0 -> x3, Pallas kernels: none -> 21.1 us  [the longest x1 9.81 us: attention_grads(): pl.pallas_call(attention_grads_kernel, out_shape=(jax.ShapeDtypeStruct((b...]
    ppermute x72 -> x73, starting transfers between devices: 115 us -> 94.7 us  [shift(): return lax.ppermute(value, AXES, pairs)]
    ppermute x72 -> x73, waiting for transfers between devices: 175 us -> 157 us  [shift(): return lax.ppermute(value, AXES, pairs)]
    dot_general x4 -> x1, matrix products: 8.98 us -> 1.28 us  [matmul_nt(): return jnp.einsum('ab,cb->ac', a, b, preferred_element_type=F32)]
    dot_general x4 -> x0, matrix products: 7.31 us -> none  [matmul_tn(): return jnp.einsum('ba,bc->ac', a, b, preferred_element_type=F32)]
    unnamed x201 -> x173, local copies, waits for them, and re-layouts: 28.6 us -> 32.8 us
  transfers between devices with their start and end apart: 72 -> 73, of which waited for: 31 -> 30; matrix products, arithmetic and copies ran while one was open for 11% -> 8% of each run, Pallas kernels for 26% -> 30%
where the time goes in v3:
time: 506 us; the launch traced here: 502 us
  Pallas kernels  161 us (32%)
  waiting for transfers between devices  157 us (31%)
  starting transfers between devices  94.7 us (19%)
  other arithmetic  41.4 us (8%)
  local copies, waits for them, and re-layouts  40.4 us (8%)
    ppermute x73, waiting for transfers between devices, shift(): return lax.ppermute(value, AXES, pairs)  157 us
    ppermute x73, starting transfers between devices, shift(): return lax.ppermute(value, AXES, pairs)  94.7 us
    pallas_call x2, Pallas kernels, feed_backward(): pl.pallas_call(lambda *refs: feed_backward_kernel(places, total is not No...  46.5 us
    pallas_call x2, Pallas kernels, attend_backward(): pl.pallas_call(attend_backward_kernel, out_shape=(jax.ShapeDtypeStruct((r...  33.1 us
    unnamed x173, local copies, waits for them, and re-layouts  32.8 us
    pallas_call x4, Pallas kernels, attend_forward(): pl.pallas_call(attend_forward_kernel, out_shape=(jax.ShapeDtypeStruct((ro...  24.8 us
    pallas_call x4, Pallas kernels, feed_forward(): pl.pallas_call(lambda *refs: feed_forward_kernel(y is None, *refs), out_s...  21.8 us
    pallas_call x1, Pallas kernels, project(): pl.pallas_call(project_kernel, out_shape=(shape(4 * chunk, model), shape(...  13.7 us
  transfers between devices with their start and end apart: 73, of which 30 were waited for; matrix products, arithmetic and copies ran while one was open for 8% of the time, Pallas kernels for 30%

profile of v3, /device:TPU:0, one launch (start us, length us, event | category | flops | bytes accessed | tf_op | source)
XLA Modules:
  0.0 501.7 jit_solution(5877997805510967912)
XLA Ops:
  5.9 2.6 collective-permute-start.1
  12.1 2.4 collective-permute-done.3
  14.5 1.6 collective-permute-start.7
  16.1 2.6 collective-permute-start.8
  18.9 1.6 collective-permute-start.6
  20.5 2.6 collective-permute-start.13
  23.1 2.5 collective-permute-done.7
  25.6 23.1 %collective-permute-done.8 = bf16[256,512]{1,0:T(8,128)(2,1)S(1)} collective-permute-done((bf16[256,512]{1,0:T(8,128)(2,1)S(1)}, bf16[256,512]{1,0:T(8,128)(2,1)S(1)}, u32[]{:S(2)}, u32[]{:S(2)}) %collective-permute-start.8) | collective-permute-done | bytes 262176 | tf_op jit(solution)/shard_map/ppermute | solution.py:310
  51.6 9.8 %collective-permute-done.10.refs_6_ = bf16[2,256,512]{2,1,0:T(8,128)(2,1)S(1)} collective-permute-done((bf16[2,256,512]{2,1,0:T(8,128)(2,1)S(1)}, bf16[2,256,512]{2,1,0:T(8,128)(2,1)S(1)}, u32[]{:S(2)}, u32[]{:S(2)}) %collective-permute-start.10) | collective-permute-done | bytes 524320 | tf_op jit(solution)/shard_map/ppermute | solution.py:310
  63.9 10.3 %collective-permute-start.12 = (bf16[512,1024]{1,0:T(8,128)(2,1)}, bf16[512,1024]{1,0:T(8,128)(2,1)}, u32[]{:S(2)}, u32[]{:S(2)}) collective-permute-start(bf16[512,1024]{1,0:T(8,128)(2,1)} %collective-permute-done.6.refs_0_), channel_id=1, source_target_pairs={{0,4},{1,5},{2,6},{3,7},{4,0},{5,1},{6,2},{7,3},{8,12},{9,13},{10,... | collective-permute-start | bytes 3145736 | tf_op jit(solution)/shard_map/ppermute | solution.py:310
  76.9 11.5 %collective-permute-start.21 = (bf16[3,256,512]{2,1,0:T(8,128)(2,1)S(1)}, bf16[3,256,512]{2,1,0:T(8,128)(2,1)}, u32[]{:S(2)}, u32[]{:S(2)}) collective-permute-start(bf16[3,256,512]{2,1,0:T(8,128)(2,1)S(1)} %maximum_select_fusion.1), channel_id=1, source_target_pairs={{0,1},{1,0},{2,3},{3,2},{4,5},{5,4},{6,7},{7,6},{8,9},{9,8},{10,11... | collective-permute-start | bytes 2359304 | tf_op jit(solution)/shard_map/ppermute | solution.py:310
  89.7 4.6 collective-permute-start.23
  94.3 13.7 %project.1 = (bf16[2048,1024]{1,0:T(8,128)(2,1)}, bf16[1024,512]{1,0:T(8,128)(2,1)}, bf16[2048,512]{1,0:T(8,128)(2,1)}, bf16[2048,512]{1,0:T(8,128)(2,1)}, bf16[...) custom-call(bf16[512,1024]{1,0:T(8,128)(2,1)} %collective-permute-done., ...), custom_call_target="tpu_custom_call" | custom-call | flops 1000 | bytes 1000 | tf_op jit(solution)/shard_map/project/pallas_call | solution.py:581
  111.3 1.6 copy-done.1
  112.9 1.6 copy-done.3
  115.7 6.0 %attend_forward.4 = (bf16[1024,128]{1,0:T(8,128)(2,1)S(1)}, f32[1,8,1024]{2,1,0:T(8,128)S(1)}) custom-call(s32[1]{0:T(128)} %bitcast.12.outer_ref, s32[9]{0:T(128)S(1)} %stack.162.sc_ref, bf16[1024,512]{1,0:T(8,128)(2,1)S(1)} %copy-done.5, bf16[2048,512]{1,0:T(8,128)(2,1)S(1)} %copy-done.1, bf16[2048,512]{1,0:T(8,128)(2,1)S(1)} %copy-done.3), custom_call_target="tpu_custom_call" | custom-call | flops 1000 | bytes 1000 | tf_op jit(solution)/shard_map/attend_forward/pallas_call | solution.py:439
  123.4 6.4 %attend_forward.5 = (bf16[1024,128]{1,0:T(8,128)(2,1)S(1)}, f32[1,8,1024]{2,1,0:T(8,128)S(1)}) custom-call(s32[1]{0:T(128)} %bitcast.12.outer_ref, s32[9]{0:T(128)S(1)} %stack.162.sc_ref, bf16[1024,512]{1,0:T(8,128)(2,1)S(1)} %copy-done.5, bf16[2048,512]{1,0:T(8,128)(2,1)S(1)} %copy-done.1, bf16[2048,512]{1,0:T(8,128)(2,1)S(1)} %copy-done.3), custom_call_target="tpu_custom_call" | custom-call | flops 1000 | bytes 1000 | tf_op jit(solution)/shard_map/attend_forward/pallas_call | solution.py:439
  130.0 1.6 collective-permute-start.26
  132.1 6.0 %attend_forward.6 = (bf16[1024,128]{1,0:T(8,128)(2,1)S(1)}, f32[1,8,1024]{2,1,0:T(8,128)S(1)}) custom-call(s32[1]{0:T(128)} %bitcast.12.outer_ref, s32[9]{0:T(128)S(1)} %stack.162.sc_ref, bf16[1024,512]{1,0:T(8,128)(2,1)S(1)} %copy-done.5, bf16[2048,512]{1,0:T(8,128)(2,1)S(1)} %copy-done.1, bf16[2048,512]{1,0:T(8,128)(2,1)S(1)} %copy-done.3), custom_call_target="tpu_custom_call" | custom-call | flops 1000 | bytes 1000 | tf_op jit(solution)/shard_map/attend_forward/pallas_call | solution.py:439
  139.3 4.2 collective-permute-done.25
  143.6 1.9 collective-permute-start.29
  145.6 6.2 %attend_forward.7 = (bf16[1024,128]{1,0:T(8,128)(2,1)S(1)}, f32[1,8,1024]{2,1,0:T(8,128)S(1)}) custom-call(s32[1]{0:T(128)} %bitcast.12.outer_ref, s32[9]{0:T(128)S(1)} %stack.162.sc_ref, bf16[1024,512]{1,0:T(8,128)(2,1)S(1)} %copy-done.5, bf16[2048,512]{1,0:T(8,128)(2,1)S(1)} %copy-done.1, bf16[2048,512]{1,0:T(8,128)(2,1)S(1)} %copy-done.3), custom_call_target="tpu_custom_call" | custom-call | flops 1000 | bytes 1000 | tf_op jit(solution)/shard_map/attend_forward/pallas_call | solution.py:439
  153.5 5.3 %collective-permute-done.27 = bf16[3,256,512]{2,1,0:T(8,128)(2,1)S(1)} collective-permute-done((bf16[3,256,512]{2,1,0:T(8,128)(2,1)S(1)}, bf16[3,256,512]{2,1,0:T(8,128)(2,1)S(1)}, u32[]{:S(2)}, u32[]{:S(2)}) %collective-permute-start.27) | collective-permute-done | bytes 786464 | tf_op jit(solution)/shard_map/ppermute | solution.py:310
  159.8 17.3 %collective-permute-done.29.refs_4_.refs_2_.refs_9_.refs_15_ = bf16[2,3,256,512]{3,2,1,0:T(8,128)(2,1)S(1)} collective-permute-done((bf16[2,3,256,512]{3,2,1,0:T(8,128)(2,1)S(1)}, bf16[2,3,256,512]{3,2,1,0:T(8,128)(2,1)S(1)}, u32[]{:S(2)}, u32[]{:S(2)}) %collective-permute-start.29) | collective-permute-done | bytes 1572896 | tf_op jit(solution)/shard_map/ppermute | solution.py:310
  177.1 1.6 collective-permute-done.30
  178.8 2.2 multiply_reduce_fusion
  187.3 6.0 %feed_forward.4 = (bf16[1024,512]{1,0:T(8,128)(2,1)S(1)}, bf16[1024,512]{1,0:T(8,128)(2,1)S(1)}, bf16[1024,512]{1,0:T(8,128)(2,1)S(1)}, f32[1024,1024]{1,0:T(8,128)S(1)}) custom-call(bf16[1024,1024]{1,0:T(8,128)(2,1)S(1)} %pad_maximum_fusion.refs_0_, bf16[1,3,256,512]{3,2,1,0:T(8,128)(2,1)S(1)} %bitcast.141, bf16[1,3,256,512]{3,2,1,0:T(8,128)(2,1)S(1)} %bitcast.150, ...), custom_call_target="tpu_custom_call" | custom-call | flops 1000 | bytes 1000 | tf_op jit(solution)/shard_map/feed_forward/pallas_call | solution.py:779
  196.4 6.0 %feed_forward.5 = (bf16[1024,512]{1,0:T(8,128)(2,1)S(1)}, bf16[1024,512]{1,0:T(8,128)(2,1)S(1)}, bf16[1024,512]{1,0:T(8,128)(2,1)S(1)}, f32[1024,1024]{1,0:T(8,128)S(1)}) custom-call(bf16[1024,1024]{1,0:T(8,128)(2,1)S(1)} %pad_maximum_fusion.refs_0_, bf16[1,3,256,512]{3,2,1,0:T(8,128)(2,1)} %bitcast.31.refs_1_.refs_12_, ...), custom_call_target="tpu_custom_call", output_to_operand_aliasing={{3}: (5, {})} | custom-call | flops 1000 | bytes 1000 | tf_op jit(solution)/shard_map/feed_forward/pallas_call | solution.py:779
  205.8 4.9 feed_forward.6
  213.7 6.0 %collective-permute-done.34.refs_2_.refs_4_.refs_13_.refs_15_ = bf16[2,3,256,512]{3,2,1,0:T(8,128)(2,1)S(1)} collective-permute-done((bf16[2,3,256,512]{3,2,1,0:T(8,128)(2,1)S(1)}, bf16[2,3,256,512]{3,2,1,0:T(8,128)(2,1)S(1)}, u32[]{:S(2)}, u32[]{:S(2)}) %collective-permute-start.34) | collective-permute-done | bytes 1572896 | tf_op jit(solution)/shard_map/ppermute | solution.py:310
  220.9 4.9 feed_forward.7
  225.8 1.8 slice.164
  233.3 4.7 fusion.32
  242.1 2.0 collective-permute-start.38
  244.2 22.6 %feed_backward.2 = (f32[1024,1024]{1,0:T(8,128)}, bf16[3,256,512]{2,1,0:T(8,128)(2,1)}, bf16[3,256,512]{2,1,0:T(8,128)(2,1)}, bf16[3,256,512]{2,1,0:T(8,128)(2,1...) custom-call(bf16[1024,1024]{1,0:T(8,128)(2,1)} %copy-done, ...), custom_call_target="tpu_custom_call" | custom-call | flops 1000 | bytes 1000 | tf_op jit(solution)/shard_map/feed_backward/pallas_call | solution.py:875
  267.8 1.6 collective-permute-start.40
  269.4 23.9 %feed_backward.3 = (f32[512,1024]{1,0:T(8,128)}, bf16[512,1024]{1,0:T(8,128)(2,1)}, bf16[3,256,512]{2,1,0:T(8,128)(2,1)}, bf16[3,256,512]{2,1,0:T(8,128)(2,1)}, ...) custom-call(bf16[1024,1024]{1,0:T(8,128)(2,1)} %copy-done, ...), custom_call_target="tpu_custom_call" | custom-call | flops 1000 | bytes 1000 | tf_op jit(solution)/shard_map/feed_backward/pallas_call | solution.py:875
  293.4 2.4 fusion.15
  297.4 1.6 collective-permute-start.41
  301.3 1.8 norm_grads.1
  310.1 16.4 %shard_map.135 = (bf16[1024,256]{1,0:T(8,128)(2,1)S(1)}, bf16[2048,256]{1,0:T(8,128)(2,1)S(1)}, bf16[2048,256]{1,0:T(8,128)(2,1)S(1)}) custom-call(s32[9]{0:T(128)S(1)} %stack.162.sc_ref, bf16[1024,512]{1,0:T(8,128)(2,1)S(1)} %copy-done.6, bf16[2048,512]{1,0:T(8,128)(2,1)S(1)} %copy-done.2, bf16[2048,512]{1,0:T(8,128)(2,1)S(1)} %copy-done.4, ...), custom_call_target="tpu_custom_call" | custom-call | flops 1000 | bytes 1000 | tf_op jit(solution)/shard_map/pallas_call | solution.py:519
  329.0 16.8 %shard_map.136 = (bf16[1024,256]{1,0:T(8,128)(2,1)S(1)}, bf16[2048,256]{1,0:T(8,128)(2,1)S(1)}, bf16[2048,256]{1,0:T(8,128)(2,1)S(1)}) custom-call(s32[9]{0:T(128)S(1)} %stack.162.sc_ref, bf16[1024,512]{1,0:T(8,128)(2,1)S(1)} %copy-done.6, bf16[2048,512]{1,0:T(8,128)(2,1)S(1)} %copy-done.2, bf16[2048,512]{1,0:T(8,128)(2,1)S(1)} %copy-done.4, ...), custom_call_target="tpu_custom_call" | custom-call | flops 1000 | bytes 1000 | tf_op jit(solution)/shard_map/pallas_call | solution.py:519
  346.0 11.8 %collective-permute-done.47 = bf16[3,256,512]{2,1,0:T(8,128)(2,1)S(1)} collective-permute-done((bf16[3,256,512]{2,1,0:T(8,128)(2,1)S(1)}, bf16[3,256,512]{2,1,0:T(8,128)(2,1)S(1)}, u32[]{:S(2)}, u32[]{:S(2)}) %collective-permute-start.47) | collective-permute-done | bytes 786464 | tf_op jit(solution)/shard_map/ppermute | solution.py:310
  362.5 1.9 fusion.12
  367.0 9.4 %rows_grads.1 = (f32[512,1024]{1,0:T(8,128)S(1)}, bf16[512,1024]{1,0:T(8,128)(2,1)}, f32[512,1024]{1,0:T(8,128)S(1)}, bf16[512,1024]{1,0:T(8,128)(2,1)}) custom-call(bf16[1024,512]{1,0:T(8,128)(2,1)S(1)} %pad_maximum_fusion.11.dq_ref, bf16[2048,512]{1,0:T(8,128)(2,1)S(1)} %constant_dynamic-update-slice_fusion.7.dk_ref, bf16[2048,512]{1,0:T(8,128)(2,1)} %copy-done.11, ...), custom_call_target="tpu_custom_call" | custom-call | flops 1000 | bytes 1000 | tf_op jit(solution)/shard_map/rows_grads/pallas_call | solution.py:637
  383.7 2.4 add_convert_fusion
  386.0 1.6 collective-permute-start.51
  387.6 2.3 broadcast_select_fusion
  390.0 9.8 %attention_grads.1 = (bf16[256,1024]{1,0:T(8,128)(2,1)S(1)}, bf16[256,1024]{1,0:T(8,128)(2,1)S(1)}, bf16[256,1024]{1,0:T(8,128)(2,1)S(1)}, bf16[256,1024]{1,0:T(...) custom-call(bf16[2048,1024]{1,0:T(8,128)(2,1)} %get-tuple-element.35, ...), custom_call_target="tpu_custom_call" | custom-call | flops 1000 | bytes 1000 | tf_op jit(solution)/shard_map/attention_grads/pallas_call | solution.py:675
  399.8 3.0 collective-permute-done.52
  402.8 13.4 %collective-permute-done.53 = bf16[2,3,256,512]{3,2,1,0:T(8,128)(2,1)} collective-permute-done((bf16[2,3,256,512]{3,2,1,0:T(8,128)(2,1)}, bf16[2,3,256,512]{3,2,1,0:T(8,128)(2,1)}, u32[]{:S(2)}, u32[]{:S(2)}) %collective-permute-start.53) | collective-permute-done | bytes 1572896 | tf_op jit(solution)/shard_map/ppermute | solution.py:310
  419.3 2.7 convert_add_fusion.3
  422.0 1.6 collective-permute-start.61
  424.9 2.6 fusion.8
  427.6 2.4 fusion.7
  434.2 23.1 %collective-permute-done.61 = bf16[3,256,512]{2,1,0:T(8,128)(2,1)S(1)} collective-permute-done((bf16[3,256,512]{2,1,0:T(8,128)(2,1)S(1)}, bf16[3,256,512]{2,1,0:T(8,128)(2,1)S(1)}, u32[]{:S(2)}, u32[]{:S(2)}) %collective-permute-start.61) | collective-permute-done | bytes 786464 | tf_op jit(solution)/shard_map/ppermute | solution.py:310
  458.1 12.0 %collective-permute-done.62 = bf16[3,256,512]{2,1,0:T(8,128)(2,1)S(1)} collective-permute-done((bf16[3,256,512]{2,1,0:T(8,128)(2,1)S(1)}, bf16[3,256,512]{2,1,0:T(8,128)(2,1)S(1)}, u32[]{:S(2)}, u32[]{:S(2)}) %collective-permute-start.62) | collective-permute-done | bytes 786464 | tf_op jit(solution)/shard_map/ppermute | solution.py:310
  471.4 2.8 collective-permute-start.64
  477.8 3.6 collective-permute-done.64
  481.5 3.4 collective-permute-start.66
  485.5 2.4 collective-permute-start.72
  490.8 1.8 copy.19
  492.5 2.8 collective-permute-done.72
  495.3 2.4 collective-permute-done.71
  (372 shorter events, 103.8 us)
Async XLA Ops:
  0.6 4.9 collective-permute-start
  2.3 7.8 %collective-permute-start.4 = (bf16[4,128,128]{2,1,0:T(8,128)(2,1)S(1)}, bf16[4,128,128]{2,1,0:T(8,128)(2,1)S(1)}, u32[]{:S(2)}, u32[]{:S(2)}) collective-permute-start(bf16[4,128,128]{2,1,0:T(8,128)(2,1)S(1)} %get-tuple-element.461), channel_id=1, source_target_pairs={{0,4},{1,5},{2,6},{3,7},{4,0},{5,1},{6,2},{7,3},{8,12},{9,13},{10,... | collective-permute-start | bytes 393224 | tf_op jit(solution)/shard_map/ppermute | solution.py:310
  4.8 5.4 %collective-permute-start.5 = (bf16[3,128,512]{2,1,0:T(8,128)(2,1)S(1)}, bf16[3,128,512]{2,1,0:T(8,128)(2,1)S(1)}, u32[]{:S(2)}, u32[]{:S(2)}) collective-permute-start(bf16[3,128,512]{2,1,0:T(8,128)(2,1)S(1)} %get-tuple-element.449), channel_id=1, source_target_pairs={{0,4},{1,5},{2,6},{3,7},{4,0},{5,1},{6,2},{7,3},{8,12},{9,13},{10,... | collective-permute-start | bytes 1179656 | tf_op jit(solution)/shard_map/ppermute | solution.py:310
  5.9 4.6 collective-permute-start.1
  8.5 3.6 collective-permute-start.2
  10.0 4.5 collective-permute-start.3
  14.5 11.1 %collective-permute-start.7 = (bf16[256,512]{1,0:T(8,128)(2,1)S(1)}, bf16[256,512]{1,0:T(8,128)(2,1)S(1)}, u32[]{:S(2)}, u32[]{:S(2)}) collective-permute-start(bf16[256,512]{1,0:T(8,128)(2,1)S(1)} %pad_maximum_fusion.21), channel_id=1, source_target_pairs={{0,1},{1,0},{2,3},{3,2},{4,5},{5,4},{6,7},{7,6},{8,9},{9,8},{10,11... | collective-permute-start | bytes 786440 | tf_op jit(solution)/shard_map/ppermute | solution.py:310
  16.1 32.7 %collective-permute-start.8 = (bf16[256,512]{1,0:T(8,128)(2,1)S(1)}, bf16[256,512]{1,0:T(8,128)(2,1)S(1)}, u32[]{:S(2)}, u32[]{:S(2)}) collective-permute-start(bf16[256,512]{1,0:T(8,128)(2,1)S(1)} %pad_maximum_fusion.21), channel_id=1, source_target_pairs={{0,2},{1,3},{2,0},{3,1},{4,6},{5,7},{6,4},{7,5},{8,10},{9,11},{10,... | collective-permute-start | bytes 786440 | tf_op jit(solution)/shard_map/ppermute | solution.py:310
  18.7 30.1 %collective-permute-start.9 = (bf16[256,512]{1,0:T(8,128)(2,1)S(1)}, bf16[256,512]{1,0:T(8,128)(2,1)S(1)}, u32[]{:S(2)}, u32[]{:S(2)}) collective-permute-start(bf16[256,512]{1,0:T(8,128)(2,1)S(1)} %pad_maximum_fusion.21), channel_id=1, source_target_pairs={{0,3},{1,2},{2,1},{3,0},{4,7},{5,6},{6,5},{7,4},{8,11},{9,10},{10,... | collective-permute-start | bytes 786440 | tf_op jit(solution)/shard_map/ppermute | solution.py:310
  18.9 43.5 %collective-permute-start.6 = (bf16[512,1024]{1,0:T(8,128)(2,1)S(1)}, bf16[512,1024]{1,0:T(8,128)(2,1)}, u32[]{:S(2)}, u32[]{:S(2)}) collective-permute-start(bf16[512,1024]{1,0:T(8,128)(2,1)S(1)} %pad_maximum_fusion.8), channel_id=1, source_target_pairs={{0,0},{1,1},{2,5},{3,4},{4,3},{5,2},{6,6},{7,7},{8,8},{9,9},{10,13... | collective-permute-start | bytes 3145736 | tf_op jit(solution)/shard_map/ppermute | solution.py:310
  20.5 43.4 %collective-permute-start.13 = (bf16[512,1024]{1,0:T(8,128)(2,1)S(1)}, bf16[512,1024]{1,0:T(8,128)(2,1)}, u32[]{:S(2)}, u32[]{:S(2)}) collective-permute-start(bf16[512,1024]{1,0:T(8,128)(2,1)S(1)} %pad_maximum_fusion.8), channel_id=1, source_target_pairs={{0,1},{1,0},{2,4},{4,2},{5,3},{6,7},{8,9},{9,8},{10,12},{12,10},{1... | collective-permute-start | bytes 3145736 | tf_op jit(solution)/shard_map/ppermute | solution.py:310
  48.8 12.5 %collective-permute-start.10 = (bf16[2,256,512]{2,1,0:T(8,128)(2,1)S(1)}, bf16[2,256,512]{2,1,0:T(8,128)(2,1)S(1)}, u32[]{:S(2)}, u32[]{:S(2)}) collective-permute-start(bf16[2,256,512]{2,1,0:T(8,128)(2,1)S(1)} %pad_maximum_fusion.15.refs_5_), channel_id=1, source_target_pairs={{0,8},{1,9},{2,10},{3,11},{4,12},{5,13},{6,14},{7,15},{8,0},{9,1},... | collective-permute-start | bytes 1572872 | tf_op jit(solution)/shard_map/ppermute | solution.py:310
  49.5 12.4 %collective-permute-start.11 = (bf16[2,256,512]{2,1,0:T(8,128)(2,1)S(1)}, bf16[2,256,512]{2,1,0:T(8,128)(2,1)S(1)}, u32[]{:S(2)}, u32[]{:S(2)}) collective-permute-start(bf16[2,256,512]{2,1,0:T(8,128)(2,1)S(1)} %pad_maximum_fusion.16.refs_9_), channel_id=1, source_target_pairs={{0,16},{1,17},{2,18},{3,19},{4,20},{5,21},{6,22},{7,23},{8,24},{9,... | collective-permute-start | bytes 1572872 | tf_op jit(solution)/shard_map/ppermute | solution.py:310
  50.0 24.2 %collective-permute-start.15 = (bf16[2,256,512]{2,1,0:T(8,128)(2,1)S(1)}, bf16[2,256,512]{2,1,0:T(8,128)(2,1)S(1)}, u32[]{:S(2)}, u32[]{:S(2)}) collective-permute-start(bf16[2,256,512]{2,1,0:T(8,128)(2,1)S(1)} %pad_maximum_fusion.15.refs_5_), channel_id=1, source_target_pairs={{0,16},{1,17},{2,18},{3,19},{4,20},{5,21},{6,22},{7,23},{8,24},{9,... | collective-permute-start | bytes 1572872 | tf_op jit(solution)/shard_map/ppermute | solution.py:310
  61.3 13.0 %collective-permute-start.16 = (bf16[2,256,512]{2,1,0:T(8,128)(2,1)S(1)}, bf16[2,256,512]{2,1,0:T(8,128)(2,1)S(1)}, u32[]{:S(2)}, u32[]{:S(2)}) collective-permute-start(bf16[2,256,512]{2,1,0:T(8,128)(2,1)S(1)} %pad_maximum_fusion.16.refs_9_), channel_id=1, source_target_pairs={{0,8},{1,9},{2,10},{3,11},{4,12},{5,13},{6,14},{7,15},{8,0},{9,1},... | collective-permute-start | bytes 1572872 | tf_op jit(solution)/shard_map/ppermute | solution.py:310
  61.9 13.0 %collective-permute-start.17 = (bf16[2,256,512]{2,1,0:T(8,128)(2,1)S(1)}, bf16[2,256,512]{2,1,0:T(8,128)(2,1)S(1)}, u32[]{:S(2)}, u32[]{:S(2)}) collective-permute-start(bf16[2,256,512]{2,1,0:T(8,128)(2,1)S(1)} %collective-permute-done.10.refs_6_), channel_id=1, source_target_pairs={{0,16},{1,17},{2,18},{3,19},{4,20},{5,21},{6,22},{7,23},{8,24},{9,... | collective-permute-start | bytes 1572872 | tf_op jit(solution)/shard_map/ppermute | solution.py:310
  62.4 13.8 %collective-permute-start.18 = (bf16[2,256,512]{2,1,0:T(8,128)(2,1)S(1)}, bf16[2,256,512]{2,1,0:T(8,128)(2,1)S(1)}, u32[]{:S(2)}, u32[]{:S(2)}) collective-permute-start(bf16[2,256,512]{2,1,0:T(8,128)(2,1)S(1)} %collective-permute-done.11.refs_11_), channel_id=1, source_target_pairs={{0,8},{1,9},{2,10},{3,11},{4,12},{5,13},{6,14},{7,15},{8,0},{9,1},... | collective-permute-start | bytes 1572872 | tf_op jit(solution)/shard_map/ppermute | solution.py:310
  63.9 25.8 %collective-permute-start.12 = (bf16[512,1024]{1,0:T(8,128)(2,1)}, bf16[512,1024]{1,0:T(8,128)(2,1)}, u32[]{:S(2)}, u32[]{:S(2)}) collective-permute-start(bf16[512,1024]{1,0:T(8,128)(2,1)} %collective-permute-done.6.refs_0_), channel_id=1, source_target_pairs={{0,4},{1,5},{2,6},{3,7},{4,0},{5,1},{6,2},{7,3},{8,12},{9,13},{10,... | collective-permute-start | bytes 3145736 | tf_op jit(solution)/shard_map/ppermute | solution.py:310
  74.2 15.5 %collective-permute-start.14 = (bf16[512,1024]{1,0:T(8,128)(2,1)}, bf16[512,1024]{1,0:T(8,128)(2,1)}, u32[]{:S(2)}, u32[]{:S(2)}) collective-permute-start(bf16[512,1024]{1,0:T(8,128)(2,1)} %collective-permute-done.13.refs_2_), channel_id=1, source_target_pairs={{0,4},{1,5},{2,6},{3,7},{4,0},{5,1},{6,2},{7,3},{8,12},{9,13},{10,... | collective-permute-start | bytes 3145736 | tf_op jit(solution)/shard_map/ppermute | solution.py:310
  74.3 33.7 %collective-permute-start.19 = (bf16[3,256,512]{2,1,0:T(8,128)(2,1)S(1)}, bf16[3,256,512]{2,1,0:T(8,128)(2,1)S(1)}, u32[]{:S(2)}, u32[]{:S(2)}) collective-permute-start(bf16[3,256,512]{2,1,0:T(8,128)(2,1)S(1)} %maximum_select_fusion.1), channel_id=1, source_target_pairs={{0,8},{1,9},{2,10},{3,11},{4,12},{5,13},{6,14},{7,15},{8,0},{9,1},... | collective-permute-start | bytes 2359304 | tf_op jit(solution)/shard_map/ppermute | solution.py:310
  74.8 33.2 %collective-permute-start.20 = (bf16[3,256,512]{2,1,0:T(8,128)(2,1)S(1)}, bf16[3,256,512]{2,1,0:T(8,128)(2,1)}, u32[]{:S(2)}, u32[]{:S(2)}) collective-permute-start(bf16[3,256,512]{2,1,0:T(8,128)(2,1)S(1)} %maximum_select_fusion.1), channel_id=1, source_target_pairs={{0,16},{1,17},{2,18},{3,19},{4,20},{5,21},{6,22},{7,23},{8,24},{9,... | collective-permute-start | bytes 2359304 | tf_op jit(solution)/shard_map/ppermute | solution.py:310
  76.9 44.8 %collective-permute-start.21 = (bf16[3,256,512]{2,1,0:T(8,128)(2,1)S(1)}, bf16[3,256,512]{2,1,0:T(8,128)(2,1)}, u32[]{:S(2)}, u32[]{:S(2)}) collective-permute-start(bf16[3,256,512]{2,1,0:T(8,128)(2,1)S(1)} %maximum_select_fusion.1), channel_id=1, source_target_pairs={{0,1},{1,0},{2,3},{3,2},{4,5},{5,4},{6,7},{7,6},{8,9},{9,8},{10,11... | collective-permute-start | bytes 2359304 | tf_op jit(solution)/shard_map/ppermute | solution.py:310
  89.7 40.2 %collective-permute-start.23 = (bf16[3,256,512]{2,1,0:T(8,128)(2,1)S(1)}, bf16[3,256,512]{2,1,0:T(8,128)(2,1)S(1)}, u32[]{:S(2)}, u32[]{:S(2)}) collective-permute-start(bf16[3,256,512]{2,1,0:T(8,128)(2,1)S(1)} %maximum_select_fusion.1), channel_id=1, source_target_pairs={{0,2},{1,3},{2,0},{3,1},{4,6},{5,7},{6,4},{7,5},{8,10},{9,11},{10,... | collective-permute-start | bytes 2359304 | tf_op jit(solution)/shard_map/ppermute | solution.py:310
  108.0 21.9 %collective-permute-start.22 = (bf16[3,256,512]{2,1,0:T(8,128)(2,1)S(1)}, bf16[3,256,512]{2,1,0:T(8,128)(2,1)}, u32[]{:S(2)}, u32[]{:S(2)}) collective-permute-start(bf16[3,256,512]{2,1,0:T(8,128)(2,1)S(1)} %collective-permute-done.19), channel_id=1, source_target_pairs={{0,16},{1,17},{2,18},{3,19},{4,20},{5,21},{6,22},{7,23},{8,24},{9,... | collective-permute-start | bytes 2359304 | tf_op jit(solution)/shard_map/ppermute | solution.py:310
  121.7 17.5 %collective-permute-start.24 = (bf16[3,256,512]{2,1,0:T(8,128)(2,1)}, bf16[3,256,512]{2,1,0:T(8,128)(2,1)S(1)}, u32[]{:S(2)}, u32[]{:S(2)}) collective-permute-start(bf16[3,256,512]{2,1,0:T(8,128)(2,1)} %collective-permute-done.21), channel_id=1, source_target_pairs={{0,8},{1,9},{2,10},{3,11},{4,12},{5,13},{6,14},{7,15},{8,0},{9,1},... | collective-permute-start | bytes 2359304 | tf_op jit(solution)/shard_map/ppermute | solution.py:310
  122.4 21.0 %collective-permute-start.25 = (bf16[3,256,512]{2,1,0:T(8,128)(2,1)}, bf16[3,256,512]{2,1,0:T(8,128)(2,1)S(1)}, u32[]{:S(2)}, u32[]{:S(2)}) collective-permute-start(bf16[3,256,512]{2,1,0:T(8,128)(2,1)} %collective-permute-done.21), channel_id=1, source_target_pairs={{0,16},{1,17},{2,18},{3,19},{4,20},{5,21},{6,22},{7,23},{8,24},{9,... | collective-permute-start | bytes 2359304 | tf_op jit(solution)/shard_map/ppermute | solution.py:310
  130.0 23.5 %collective-permute-start.26 = (bf16[3,256,512]{2,1,0:T(8,128)(2,1)S(1)}, bf16[3,256,512]{2,1,0:T(8,128)(2,1)S(1)}, u32[]{:S(2)}, u32[]{:S(2)}) collective-permute-start(bf16[3,256,512]{2,1,0:T(8,128)(2,1)S(1)} %collective-permute-done.23), channel_id=1, source_target_pairs={{0,1},{1,0},{2,3},{3,2},{4,5},{5,4},{6,7},{7,6},{8,9},{9,8},{10,11... | collective-permute-start | bytes 2359304 | tf_op jit(solution)/shard_map/ppermute | solution.py:310
  131.5 27.3 %collective-permute-start.27 = (bf16[3,256,512]{2,1,0:T(8,128)(2,1)S(1)}, bf16[3,256,512]{2,1,0:T(8,128)(2,1)S(1)}, u32[]{:S(2)}, u32[]{:S(2)}) collective-permute-start(bf16[3,256,512]{2,1,0:T(8,128)(2,1)S(1)} %collective-permute-done.23), channel_id=1, source_target_pairs={{0,16},{1,17},{2,18},{3,19},{4,20},{5,21},{6,22},{7,23},{8,24},{9,... | collective-permute-start | bytes 2359304 | tf_op jit(solution)/shard_map/ppermute | solution.py:310
  143.6 33.6 %collective-permute-start.29 = (bf16[2,3,256,512]{3,2,1,0:T(8,128)(2,1)S(1)}, bf16[2,3,256,512]{3,2,1,0:T(8,128)(2,1)S(1)}, u32[]{:S(2)}, u32[]{:S(2)}) collective-permute-start(bf16[2,3,256,512]{3,2,1,0:T(8,128)(2,1)S(1)} %pad_maximum_fusion.2), channel_id=1, source_target_pairs={{0,8},{1,9},{2,10},{3,11},{4,12},{5,13},{6,14},{7,15},{8,0},{9,1},... | collective-permute-start | bytes 4718600 | tf_op jit(solution)/shard_map/ppermute | solution.py:310
  158.8 20.0 %collective-permute-start.28 = (bf16[512,1024]{1,0:T(8,128)(2,1)S(1)}, bf16[512,1024]{1,0:T(8,128)(2,1)S(1)}, u32[]{:S(2)}, u32[]{:S(2)}) collective-permute-start(bf16[512,1024]{1,0:T(8,128)(2,1)S(1)} %slice.259), channel_id=1, source_target_pairs={{0,4},{1,5},{2,6},{3,7},{4,0},{5,1},{6,2},{7,3},{8,12},{9,13},{10,... | collective-permute-start | bytes 3145736 | tf_op jit(solution)/shard_map/ppermute | solution.py:310
  158.8 20.0 %collective-permute-start.30 = (bf16[3,256,512]{2,1,0:T(8,128)(2,1)S(1)}, bf16[3,256,512]{2,1,0:T(8,128)(2,1)S(1)}, u32[]{:S(2)}, u32[]{:S(2)}) collective-permute-start(bf16[3,256,512]{2,1,0:T(8,128)(2,1)S(1)} %collective-permute-done.26), channel_id=1, source_target_pairs={{0,16},{1,17},{2,18},{3,19},{4,20},{5,21},{6,22},{7,23},{8,24},{9,... | collective-permute-start | bytes 2359304 | tf_op jit(solution)/shard_map/ppermute | solution.py:310
  181.2 23.2 %collective-permute-start.33 = (bf16[3,256,512]{2,1,0:T(8,128)(2,1)S(1)}, bf16[3,256,512]{2,1,0:T(8,128)(2,1)S(1)}, u32[]{:S(2)}, u32[]{:S(2)}) collective-permute-start(bf16[3,256,512]{2,1,0:T(8,128)(2,1)S(1)} %slice_bitcast_fusion.1), channel_id=1, source_target_pairs={{0,16},{1,17},{2,18},{3,19},{4,20},{5,21},{6,22},{7,23},{8,24},{9,... | collective-permute-start | bytes 2359304 | tf_op jit(solution)/shard_map/ppermute | solution.py:310
  183.2 36.4 %collective-permute-start.34 = (bf16[2,3,256,512]{3,2,1,0:T(8,128)(2,1)S(1)}, bf16[2,3,256,512]{3,2,1,0:T(8,128)(2,1)S(1)}, u32[]{:S(2)}, u32[]{:S(2)}) collective-permute-start(bf16[2,3,256,512]{3,2,1,0:T(8,128)(2,1)S(1)} %pad_maximum_fusion.3), channel_id=1, source_target_pairs={{0,8},{1,9},{2,10},{3,11},{4,12},{5,13},{6,14},{7,15},{8,0},{9,1},... | collective-permute-start | bytes 4718600 | tf_op jit(solution)/shard_map/ppermute | solution.py:310
  204.4 24.9 %collective-permute-start.35 = (bf16[512,1024]{1,0:T(8,128)(2,1)S(1)}, bf16[512,1024]{1,0:T(8,128)(2,1)S(1)}, u32[]{:S(2)}, u32[]{:S(2)}) collective-permute-start(bf16[512,1024]{1,0:T(8,128)(2,1)S(1)} %pad_maximum_fusion.9), channel_id=1, source_target_pairs={{2,5},{3,4},{4,3},{5,2},{10,13},{11,12},{12,11},{13,10},{18,21},{1... | collective-permute-start | bytes 3145736 | tf_op jit(solution)/shard_map/ppermute | solution.py:310
  242.1 51.3 %collective-permute-start.38 = (bf16[512,1024]{1,0:T(8,128)(2,1)}, bf16[512,1024]{1,0:T(8,128)(2,1)}, u32[]{:S(2)}, u32[]{:S(2)}) collective-permute-start(bf16[512,1024]{1,0:T(8,128)(2,1)} %pad_maximum_fusion.10), channel_id=1, source_target_pairs={{2,5},{3,4},{4,3},{5,2},{10,13},{11,12},{12,11},{13,10},{18,21},{1... | collective-permute-start | bytes 3145736 | tf_op jit(solution)/shard_map/ppermute | solution.py:310
  266.8 26.6 %collective-permute-start.39 = (bf16[3,256,512]{2,1,0:T(8,128)(2,1)}, bf16[3,256,512]{2,1,0:T(8,128)(2,1)}, u32[]{:S(2)}, u32[]{:S(2)}) collective-permute-start(bf16[3,256,512]{2,1,0:T(8,128)(2,1)} %get-tuple-element.290), channel_id=1, source_target_pairs={{0,16},{1,17},{2,18},{3,19},{4,20},{5,21},{6,22},{7,23},{8,24},{9,... | collective-permute-start | bytes 2359304 | tf_op jit(solution)/shard_map/ppermute | solution.py:310
  267.8 25.6 %collective-permute-start.40 = (bf16[3,256,512]{2,1,0:T(8,128)(2,1)}, bf16[3,256,512]{2,1,0:T(8,128)(2,1)}, u32[]{:S(2)}, u32[]{:S(2)}) collective-permute-start(bf16[3,256,512]{2,1,0:T(8,128)(2,1)} %get-tuple-element.291), channel_id=1, source_target_pairs={{0,8},{1,9},{2,10},{3,11},{4,12},{5,13},{6,14},{7,15},{8,0},{9,1},... | collective-permute-start | bytes 2359304 | tf_op jit(solution)/shard_map/ppermute | solution.py:310
  303.9 42.1 %collective-permute-start.45 = (bf16[2,3,256,512]{3,2,1,0:T(8,128)(2,1)S(1)}, bf16[2,3,256,512]{3,2,1,0:T(8,128)(2,1)S(1)}, u32[]{:S(2)}, u32[]{:S(2)}) collective-permute-start(bf16[2,3,256,512]{3,2,1,0:T(8,128)(2,1)S(1)} %pad_maximum_fusion.4), channel_id=1, source_target_pairs={{0,8},{1,9},{2,10},{3,11},{4,12},{5,13},{6,14},{7,15},{8,0},{9,1},... | collective-permute-start | bytes 4718600 | tf_op jit(solution)/shard_map/ppermute | solution.py:310
  304.6 41.4 %collective-permute-start.46 = (bf16[2,3,256,512]{3,2,1,0:T(8,128)(2,1)S(1)}, bf16[2,3,256,512]{3,2,1,0:T(8,128)(2,1)S(1)}, u32[]{:S(2)}, u32[]{:S(2)}) collective-permute-start(bf16[2,3,256,512]{3,2,1,0:T(8,128)(2,1)S(1)} %pad_maximum_fusion.5), channel_id=1, source_target_pairs={{0,16},{1,17},{2,18},{3,19},{4,20},{5,21},{6,22},{7,23},{8,24},{9,... | collective-permute-start | bytes 4718600 | tf_op jit(solution)/shard_map/ppermute | solution.py:310
  326.4 31.4 %collective-permute-start.47 = (bf16[3,256,512]{2,1,0:T(8,128)(2,1)S(1)}, bf16[3,256,512]{2,1,0:T(8,128)(2,1)S(1)}, u32[]{:S(2)}, u32[]{:S(2)}) collective-permute-start(bf16[3,256,512]{2,1,0:T(8,128)(2,1)S(1)} %copy-done.78), channel_id=1, source_target_pairs={{0,16},{1,17},{2,18},{3,19},{4,20},{5,21},{6,22},{7,23},{8,24},{9,... | collective-permute-start | bytes 2359304 | tf_op jit(solution)/shard_map/ppermute | solution.py:310
  327.5 30.3 %collective-permute-start.48 = (bf16[3,256,512]{2,1,0:T(8,128)(2,1)S(1)}, bf16[3,256,512]{2,1,0:T(8,128)(2,1)S(1)}, u32[]{:S(2)}, u32[]{:S(2)}) collective-permute-start(bf16[3,256,512]{2,1,0:T(8,128)(2,1)S(1)} %copy-done.77), channel_id=1, source_target_pairs={{0,8},{1,9},{2,10},{3,11},{4,12},{5,13},{6,14},{7,15},{8,0},{9,1},... | collective-permute-start | bytes 2359304 | tf_op jit(solution)/shard_map/ppermute | solution.py:310
  379.2 3.6 collective-permute-start.49
  379.2 4.5 collective-permute-start.50
  379.7 36.6 %collective-permute-start.53 = (bf16[2,3,256,512]{3,2,1,0:T(8,128)(2,1)}, bf16[2,3,256,512]{3,2,1,0:T(8,128)(2,1)}, u32[]{:S(2)}, u32[]{:S(2)}) collective-permute-start(bf16[2,3,256,512]{3,2,1,0:T(8,128)(2,1)} %pad_maximum_fusion.6), channel_id=1, source_target_pairs={{0,8},{1,9},{2,10},{3,11},{4,12},{5,13},{6,14},{7,15},{8,0},{9,1},... | collective-permute-start | bytes 4718600 | tf_op jit(solution)/shard_map/ppermute | solution.py:310
  381.1 36.3 %collective-permute-start.54 = (bf16[2,3,256,512]{3,2,1,0:T(8,128)(2,1)}, bf16[2,3,256,512]{3,2,1,0:T(8,128)(2,1)}, u32[]{:S(2)}, u32[]{:S(2)}) collective-permute-start(bf16[2,3,256,512]{3,2,1,0:T(8,128)(2,1)} %pad_maximum_fusion.7), channel_id=1, source_target_pairs={{0,16},{1,17},{2,18},{3,19},{4,20},{5,21},{6,22},{7,23},{8,24},{9,... | collective-permute-start | bytes 4718600 | tf_op jit(solution)/shard_map/ppermute | solution.py:310
  382.2 20.7 %collective-permute-start.52 = (bf16[3,256,512]{2,1,0:T(8,128)(2,1)}, bf16[3,256,512]{2,1,0:T(8,128)(2,1)S(1)}, u32[]{:S(2)}, u32[]{:S(2)}) collective-permute-start(bf16[3,256,512]{2,1,0:T(8,128)(2,1)} %get-tuple-element.350), channel_id=1, source_target_pairs={{0,1},{1,0},{2,3},{3,2},{4,5},{5,4},{6,7},{7,6},{8,9},{9,8},{10,11... | collective-permute-start | bytes 2359304 | tf_op jit(solution)/shard_map/ppermute | solution.py:310
  386.0 38.9 %collective-permute-start.51 = (bf16[512,1024]{1,0:T(8,128)(2,1)S(1)}, bf16[512,1024]{1,0:T(8,128)(2,1)S(1)}, u32[]{:S(2)}, u32[]{:S(2)}) collective-permute-start(bf16[512,1024]{1,0:T(8,128)(2,1)S(1)} %add_convert_fusion), channel_id=1, source_target_pairs={{0,1},{1,0},{2,3},{3,2},{4,5},{5,4},{6,7},{7,6},{8,9},{9,8},{10,11... | collective-permute-start | bytes 3145736 | tf_op jit(solution)/shard_map/ppermute | solution.py:310
  417.4 13.6 %collective-permute-start.56 = (bf16[256,1024]{1,0:T(8,128)(2,1)S(1)}, bf16[256,1024]{1,0:T(8,128)(2,1)S(1)}, u32[]{:S(2)}, u32[]{:S(2)}) collective-permute-start(bf16[256,1024]{1,0:T(8,128)(2,1)S(1)} %get-tuple-element.369), channel_id=1, source_target_pairs={{0,16},{1,17},{2,18},{3,19},{4,20},{5,21},{6,22},{7,23},{8,24},{9,... | collective-permute-start | bytes 1572872 | tf_op jit(solution)/shard_map/ppermute | solution.py:310
  418.5 12.5 %collective-permute-start.57 = (bf16[256,1024]{1,0:T(8,128)(2,1)S(1)}, bf16[256,1024]{1,0:T(8,128)(2,1)S(1)}, u32[]{:S(2)}, u32[]{:S(2)}) collective-permute-start(bf16[256,1024]{1,0:T(8,128)(2,1)S(1)} %get-tuple-element.370), channel_id=1, source_target_pairs={{0,8},{1,9},{2,10},{3,11},{4,12},{5,13},{6,14},{7,15},{8,0},{9,1},... | collective-permute-start | bytes 1572872 | tf_op jit(solution)/shard_map/ppermute | solution.py:310
  422.0 35.4 %collective-permute-start.61 = (bf16[3,256,512]{2,1,0:T(8,128)(2,1)S(1)}, bf16[3,256,512]{2,1,0:T(8,128)(2,1)S(1)}, u32[]{:S(2)}, u32[]{:S(2)}) collective-permute-start(bf16[3,256,512]{2,1,0:T(8,128)(2,1)S(1)} %get-tuple-element.376), channel_id=1, source_target_pairs={{0,1},{1,0},{2,3},{3,2},{4,5},{5,4},{6,7},{7,6},{8,9},{9,8},{10,11... | collective-permute-start | bytes 2359304 | tf_op jit(solution)/shard_map/ppermute | solution.py:310
  423.6 46.5 %collective-permute-start.62 = (bf16[3,256,512]{2,1,0:T(8,128)(2,1)S(1)}, bf16[3,256,512]{2,1,0:T(8,128)(2,1)S(1)}, u32[]{:S(2)}, u32[]{:S(2)}) collective-permute-start(bf16[3,256,512]{2,1,0:T(8,128)(2,1)S(1)} %add_convert_fusion.1), channel_id=1, source_target_pairs={{0,2},{1,3},{2,0},{3,1},{4,6},{5,7},{6,4},{7,5},{8,10},{9,11},{10,... | collective-permute-start | bytes 2359304 | tf_op jit(solution)/shard_map/ppermute | solution.py:310
  430.3 45.0 %collective-permute-start.55 = (bf16[512,1024]{1,0:T(8,128)(2,1)S(1)}, bf16[512,1024]{1,0:T(8,128)(2,1)S(1)}, u32[]{:S(2)}, u32[]{:S(2)}) collective-permute-start(bf16[512,1024]{1,0:T(8,128)(2,1)S(1)} %pad_maximum_fusion.12), channel_id=1, source_target_pairs={{2,5},{3,4},{4,3},{5,2},{10,13},{11,12},{12,11},{13,10},{18,21},{1... | collective-permute-start | bytes 3145736 | tf_op jit(solution)/shard_map/ppermute | solution.py:310
  431.7 39.1 %collective-permute-start.58 = (bf16[2,256,1024]{2,1,0:T(8,128)(2,1)S(1)}, bf16[2,256,1024]{2,1,0:T(8,128)(2,1)S(1)}, u32[]{:S(2)}, u32[]{:S(2)}) collective-permute-start(bf16[2,256,1024]{2,1,0:T(8,128)(2,1)S(1)} %pad_maximum_fusion.13), channel_id=1, source_target_pairs={{0,8},{1,9},{2,10},{3,11},{4,12},{5,13},{6,14},{7,15},{8,0},{9,1},... | collective-permute-start | bytes 3145736 | tf_op jit(solution)/shard_map/ppermute | solution.py:310
  433.2 37.5 %collective-permute-start.59 = (bf16[2,256,1024]{2,1,0:T(8,128)(2,1)S(1)}, bf16[2,256,1024]{2,1,0:T(8,128)(2,1)S(1)}, u32[]{:S(2)}, u32[]{:S(2)}) collective-permute-start(bf16[2,256,1024]{2,1,0:T(8,128)(2,1)S(1)} %pad_maximum_fusion.14), channel_id=1, source_target_pairs={{0,16},{1,17},{2,18},{3,19},{4,20},{5,21},{6,22},{7,23},{8,24},{9,... | collective-permute-start | bytes 3145736 | tf_op jit(solution)/shard_map/ppermute | solution.py:310
  457.4 13.3 %collective-permute-start.60 = (f32[2,512]{1,0:T(2,128)S(1)}, f32[2,512]{1,0:T(2,128)S(1)}, u32[]{:S(2)}, u32[]{:S(2)}) collective-permute-start(f32[2,512]{1,0:T(2,128)S(1)} %pad_maximum_fusion.26), channel_id=1, source_target_pairs={{0,8},{1,9},{2,10},{3,11},{4,12},{5,13},{6,14},{7,15},{8,0},{9,1},... | collective-permute-start | bytes 12296 | tf_op jit(solution)/shard_map/ppermute | solution.py:310
  470.6 14.3 %collective-permute-start.68 = (bf16[3,128,512]{2,1,0:T(8,128)(2,1)S(1)}, bf16[3,128,512]{2,1,0:T(8,128)(2,1)S(1)}, u32[]{:S(2)}, u32[]{:S(2)}) collective-permute-start(bf16[3,128,512]{2,1,0:T(8,128)(2,1)S(1)} %select_convert_fusion.1), channel_id=1, source_target_pairs={{0,4},{1,5},{2,6},{3,7},{4,0},{5,1},{6,2},{7,3},{8,12},{9,13},{10,... | collective-permute-start | bytes 1179656 | tf_op jit(solution)/shard_map/ppermute | solution.py:310
  471.4 9.9 %collective-permute-start.64 = (bf16[256,512]{1,0:T(8,128)(2,1)S(1)}, bf16[256,512]{1,0:T(8,128)(2,1)S(1)}, u32[]{:S(2)}, u32[]{:S(2)}) collective-permute-start(bf16[256,512]{1,0:T(8,128)(2,1)S(1)} %get-tuple-element.396), channel_id=1, source_target_pairs={{0,1},{1,0},{2,3},{3,2},{4,5},{5,4},{6,7},{7,6},{8,9},{9,8},{10,11... | collective-permute-start | bytes 786440 | tf_op jit(solution)/shard_map/ppermute | solution.py:310
  474.2 3.6 collective-permute-start.65
  475.2 23.2 %collective-permute-start.63 = (bf16[256,512]{1,0:T(8,128)(2,1)S(1)}, bf16[256,512]{1,0:T(8,128)(2,1)S(1)}, u32[]{:S(2)}, u32[]{:S(2)}) collective-permute-start(bf16[256,512]{1,0:T(8,128)(2,1)S(1)} %slice.260), channel_id=1, source_target_pairs={{0,1},{1,0},{2,3},{3,2},{4,5},{5,4},{6,7},{7,6},{8,9},{9,8},{10,11... | collective-permute-start | bytes 786440 | tf_op jit(solution)/shard_map/ppermute | solution.py:310
  481.4 3.6 collective-permute-start.69
  481.5 16.8 %collective-permute-start.66 = (bf16[256,512]{1,0:T(8,128)(2,1)S(1)}, bf16[256,512]{1,0:T(8,128)(2,1)S(1)}, u32[]{:S(2)}, u32[]{:S(2)}) collective-permute-start(bf16[256,512]{1,0:T(8,128)(2,1)S(1)} %add_convert_fusion.8), channel_id=1, source_target_pairs={{0,2},{1,3},{2,0},{3,1},{4,6},{5,7},{6,4},{7,5},{8,10},{9,11},{10,... | collective-permute-start | bytes 786440 | tf_op jit(solution)/shard_map/ppermute | solution.py:310
  485.5 9.8 %collective-permute-start.72 = (f32[2,32]{1,0:T(2,128)S(1)}, f32[2,32]{1,0:T(2,128)S(1)}, u32[]{:S(2)}, u32[]{:S(2)}) collective-permute-start(f32[2,32]{1,0:T(2,128)S(1)} %get-tuple-element.471), channel_id=1, source_target_pairs={{0,3},{1,2},{2,1},{3,0},{4,7},{5,6},{6,5},{7,4},{8,11},{9,10},{10,... | collective-permute-start | bytes 776 | tf_op jit(solution)/shard_map/ppermute | solution.py:310
  487.9 9.8 %collective-permute-start.71 = (f32[2,32]{1,0:T(2,128)S(1)}, f32[2,32]{1,0:T(2,128)S(1)}, u32[]{:S(2)}, u32[]{:S(2)}) collective-permute-start(f32[2,32]{1,0:T(2,128)S(1)} %get-tuple-element.472), channel_id=1, source_target_pairs={{0,2},{1,3},{2,0},{3,1},{4,6},{5,7},{6,4},{7,5},{8,10},{9,11},{10,... | collective-permute-start | bytes 776 | tf_op jit(solution)/shard_map/ppermute | solution.py:310
  488.9 8.8 %collective-permute-start.70 = (f32[2,32]{1,0:T(2,128)S(1)}, f32[2,32]{1,0:T(2,128)S(1)}, u32[]{:S(2)}, u32[]{:S(2)}) collective-permute-start(f32[2,32]{1,0:T(2,128)S(1)} %get-tuple-element.470), channel_id=1, source_target_pairs={{0,1},{1,0},{2,3},{3,2},{4,5},{5,4},{6,7},{7,6},{8,9},{9,8},{10,11... | collective-permute-start | bytes 776 | tf_op jit(solution)/shard_map/ppermute | solution.py:310
  (90 other events, 1009.2 us)

commit v4 on v3

--- a/solution.py
+++ b/solution.py
@@ -692,9 +692,9 @@
     return out[:4], out[4:]
 
 
-def norm_grads_kernel(part_ref, first_ref, second_ref, values_ref, grad_ref, gain_ref, out_ref, low_ref, gain_grad_ref):
+def norm_grads_kernel(halves, part_ref, first_ref, second_ref, values_ref, grad_ref, gain_ref, out_ref, low_ref, gain_grad_ref):
     step = pl.program_id(0)
-    values = values_ref[...]
+    values = values_ref[...].astype(F32)
     inverse = lax.rsqrt(jnp.mean(values * values, axis=-1, keepdims=True) + 1e-05)
     scaled = values * inverse
 
@@ -702,7 +702,8 @@
     def _():
         gain_grad_ref[...] = jnp.zeros_like(gain_grad_ref)
 
-    received = jnp.where(step < 2, first_ref[...].astype(F32), second_ref[...].astype(F32))
+    first, second = first_ref[...].astype(F32), second_ref[...].astype(F32)
+    received = jnp.where(step < 2, first, second) if halves else first + second
     grad_normed = part_ref[...] + received
     grad_scaled = grad_normed * gain_ref[...]
     grad = grad_ref[...] + inverse * (grad_scaled - scaled * jnp.mean(grad_scaled * scaled, axis=-1, keepdims=True))
@@ -714,10 +715,11 @@
 def norm_grads(part, first, second, values, grad, gain):
     rows, model = part.shape
     tile = rows // 4
+    halves = first.shape[0] < rows
     tiles = pl.BlockSpec((tile, model), lambda i: (i, 0))
     row = pl.BlockSpec((1, model), lambda i: (0, 0))
     return pl.pallas_call(
-        norm_grads_kernel,
+        lambda *refs: norm_grads_kernel(halves, *refs),
         out_shape=(
             jax.ShapeDtypeStruct((rows, model), F32),
             jax.ShapeDtypeStruct((rows, model), BF),
@@ -726,8 +728,8 @@
         grid=(4,),
         in_specs=[
             tiles,
-            pl.BlockSpec((tile, model), lambda i: (jnp.minimum(i, 1), 0)),
-            pl.BlockSpec((tile, model), lambda i: (jnp.maximum(i - 2, 0), 0)),
+            pl.BlockSpec((tile, model), lambda i: (jnp.minimum(i, 1), 0)) if halves else tiles,
+            pl.BlockSpec((tile, model), lambda i: (jnp.maximum(i - 2, 0), 0)) if halves else tiles,
             tiles,
             tiles,
             row,
@@ -987,15 +989,19 @@
     gains_x, gains_y, gains_d, attention_piece, feed_p[0] = event(gains_x, gains_y, gains_d, attention_piece, feed_piece)
     gains_all = jnp.concatenate([gains_pair, gains_x, gains_y, gains_d], axis=0)
 
-    inputs_rel, attention_piece = event(inputs_rel, attention_piece)
     own_rows, partner_rows = home_swap(inputs_rel), shift(inputs_rel, partner_of_home)
-    att_1, att_2, att_3 = z_swap(attention_piece, 1), z_swap(attention_piece, 2), z_swap(attention_piece, 3)
-    att_1, att_2, att_3, feed_piece = event(att_1, att_2, att_3, feed_p[0])
-    att_low, att_high = jnp.stack([attention_piece, att_1]), jnp.stack([att_2, att_3])
-    att_low_x, att_high_y = x_swap(att_low), y_swap(att_high)
-    att_low_y, att_high_x = y_swap(att_low), x_swap(att_high)
-    att_low_x, att_high_y = event(att_low_x, att_high_y)
-    att_low_d, att_high_d = y_swap(att_low_x), x_swap(att_high_y)
+    att_1, att_2 = z_swap(attention_piece, 1), z_swap(attention_piece, 2)
+    att_1, feed_piece = event(att_1, feed_p[0])
+    att_low = jnp.stack([attention_piece, att_1])
+    att_low_x, att_low_y = x_swap(att_low), y_swap(att_low)
+    (att_2,) = event(att_2)
+    (att_3,) = event(z_swap(att_2, 1))
+    att_high = jnp.stack([att_2, att_3])
+    att_high_x, att_high_y = x_swap(att_high), y_swap(att_high)
+    (att_low_x,) = event(att_low_x)
+    att_low_d = y_swap(att_low_x)
+    (att_high_y,) = event(att_high_y)
+    att_high_d = x_swap(att_high_y)
     (own_rows,) = event(own_rows)
     other_rows = core_swap(own_rows)
     partner_rows, feed_piece = event(partner_rows, feed_piece)
@@ -1128,16 +1134,18 @@
     (own_e, x_e, y_e, d_e), (own_o, x_o, y_o, d_o) = attention_grads(normed_all, grad_branch_both, grad_queries, grad_keys, grad_values, mixed)
     quarter_cols = grad_queries.shape[1] // 4
     half_cols = 4 * quarter_cols
-    d_e, d_o, x_e, y_e, x_o, y_o, part_3, part_2, batch_x, batch_y = event(d_e, d_o, x_e, y_e, x_o, y_o, part_3, part_2, batch_x, batch_y)
+    d_e, d_o, x_e, y_e, x_o, y_o, part_3, part_2 = event(d_e, d_o, x_e, y_e, x_o, y_o, part_3, part_2)
+    (part_2,) = event(add(part_2, part_3))
+    part_2 = z_swap(part_2, 2)
+    batch_x, batch_y, d_e, d_o = event(batch_x, batch_y, d_e, d_o)
     d_e, d_o = y_swap(d_e), x_swap(d_o)
-    part_2, part_1 = event(add(part_2, part_3), total_of(own_1, batch_x[1], batch_y[1]).astype(BF))
-    part_2, part_1 = z_swap(part_2, 2), z_swap(part_1, 1)
+    (part_1,) = event(total_of(own_1, batch_x[1], batch_y[1]).astype(BF))
+    part_1 = z_swap(part_1, 1)
     part_0 = total_of(own_0, batch_x[0], batch_y[0])
     (from_partner,) = event(from_partner)
-    grad_normed_one = part_own + part_other.astype(F32) + from_partner.astype(F32)
-    scaled_one, inverse_one = norm_forward(rows)
-    grad_norm_one, grad_gain_one = norm_backward(grad_normed_one, scaled_one, inverse_one, gain_one)
-    grad_rows, gain_a, gain_b = event(turn((grad_middle + grad_norm_one).astype(BF)), grad_gain_one, grad_gain_two)
+    _, grad_rows, grad_gain_one = norm_grads(part_own, part_other, from_partner, own_rows, grad_middle, gain_one)
+    grad_rows, gain_a, gain_b, part_2 = event(grad_rows, grad_gain_one[0], grad_gain_two, part_2)
+    grad_rows = turn(grad_rows)
     grad_inputs = moved_home(grad_rows)
     d_e, d_o = event(d_e, d_o)
     batch_x, batch_y = event(jnp.stack([add(x_e, d_e), x_o]), jnp.stack([y_e, add(y_o, d_o)]))
@@ -1153,13 +1161,14 @@
 
     batch_x, batch_y, sent = event(batch_x, batch_y, sent)
     even, odd = total_of(own_e, batch_x[0], batch_y[0]), total_of(own_o, batch_x[1], batch_y[1])
-    att_3, att_1, att_2 = odd[:, half_cols:].astype(BF), even[:, half_cols:].astype(BF), odd[:, :half_cols].astype(BF)
-    att_3, att_1, a, c, sent = event(att_3, att_1, a, c, sent)
-    att_3, att_1 = z_swap(att_3, 1), z_swap(att_1, 1)
+    att_13, att_2 = jnp.stack([even[:, half_cols:], odd[:, half_cols:]]).astype(BF), odd[:, :half_cols].astype(BF)
+    att_13, att_2, a, c, sent = event(att_13, att_2, a, c, sent)
+    att_13 = z_swap(att_13, 1)
     a, c = a + sent[:, :quarter], c + sent[:, quarter:]
     sent = y_swap(c)
-    att_3, att_2, sent = event(att_3, att_2, sent)
-    att_2 = z_swap(add(att_2, att_3), 2)
+    att_13, att_2, sent = event(att_13, att_2, sent)
+    att_2 = z_swap(add(att_2, att_13[1]), 2)
+    att_1 = att_13[0]
     a = a + sent
     keep, give = pick(jnp.split(a, 2, axis=1))
     sent = core_swap(give)

time: 506 us -> 500 us (0.988)
  starting transfers between devices: 94.7 us -> 85.9 us
    ppermute x73 -> x72, starting transfers between devices: 94.7 us -> 85.9 us  [shift(): return lax.ppermute(value, AXES, pairs)]
    unnamed x173 -> x223, local copies, waits for them, and re-layouts: 32.8 us -> 34.7 us
    ppermute x73 -> x72, waiting for transfers between devices: 157 us -> 159 us  [shift(): return lax.ppermute(value, AXES, pairs)]
  transfers between devices with their start and end apart: 73 -> 72, of which waited for: 30 -> 35; matrix products, arithmetic and copies ran while one was open for 8% -> 7% of each run, Pallas kernels for 30% -> 31%
where the time goes in v4:
time: 500 us; the launch traced here: 496 us
  Pallas kernels  165 us (33%)
  waiting for transfers between devices  159 us (32%)
  starting transfers between devices  85.9 us (17%)
  local copies, waits for them, and re-layouts  42.5 us (8%)
  other arithmetic  36.5 us (7%)
    ppermute x72, waiting for transfers between devices, shift(): return lax.ppermute(value, AXES, pairs)  159 us
    ppermute x72, starting transfers between devices, shift(): return lax.ppermute(value, AXES, pairs)  85.9 us
    pallas_call x2, Pallas kernels, feed_backward(): pl.pallas_call(lambda *refs: feed_backward_kernel(places, total is not No...  46.6 us
    unnamed x223, local copies, waits for them, and re-layouts  34.7 us
    pallas_call x2, Pallas kernels, attend_backward(): pl.pallas_call(attend_backward_kernel, out_shape=(jax.ShapeDtypeStruct((r...  33.2 us
    pallas_call x4, Pallas kernels, attend_forward(): pl.pallas_call(attend_forward_kernel, out_shape=(jax.ShapeDtypeStruct((ro...  24.9 us
    pallas_call x4, Pallas kernels, feed_forward(): pl.pallas_call(lambda *refs: feed_forward_kernel(y is None, *refs), out_s...  22.4 us
    pallas_call x1, Pallas kernels, project(): pl.pallas_call(project_kernel, out_shape=(shape(4 * chunk, model), shape(...  13.8 us
  transfers between devices with their start and end apart: 72, of which 35 were waited for; matrix products, arithmetic and copies ran while one was open for 7% of the time, Pallas kernels for 31%

profile of v4, /device:TPU:0, one launch (start us, length us, event | category | flops | bytes accessed | tf_op | source)
XLA Modules:
  0.0 496.0 jit_solution(16941774870165877091)
XLA Ops:
  5.4 2.6 collective-permute-start.2
  8.0 1.5 collective-permute-start.3
  10.0 1.5 collective-permute-done.3
  12.1 2.0 collective-permute-done.4
  14.1 1.6 collective-permute-start.8
  15.6 2.6 collective-permute-start.7
  18.3 8.2 %collective-permute-done.8 = bf16[256,512]{1,0:T(8,128)(2,1)S(1)} collective-permute-done((bf16[256,512]{1,0:T(8,128)(2,1)S(1)}, bf16[256,512]{1,0:T(8,128)(2,1)S(1)}, u32[]{:S(2)}, u32[]{:S(2)}) %collective-permute-start.8) | collective-permute-done | bytes 262176 | tf_op jit(solution)/shard_map/ppermute | solution.py:310
  26.5 2.5 collective-permute-done.7
  30.4 3.6 collective-permute-start.13
  36.2 1.5 collective-permute-start.15
  37.7 10.7 %collective-permute-done.11.refs_6_ = bf16[2,256,512]{2,1,0:T(8,128)(2,1)S(1)} collective-permute-done((bf16[2,256,512]{2,1,0:T(8,128)(2,1)S(1)}, bf16[2,256,512]{2,1,0:T(8,128)(2,1)S(1)}, u32[]{:S(2)}, u32[]{:S(2)}) %collective-permute-start.11) | collective-permute-done | bytes 524320 | tf_op jit(solution)/shard_map/ppermute | solution.py:310
  51.5 6.9 %collective-permute-done.13.refs_2_ = bf16[512,1024]{1,0:T(8,128)(2,1)} collective-permute-done((bf16[512,1024]{1,0:T(8,128)(2,1)S(1)}, bf16[512,1024]{1,0:T(8,128)(2,1)}, u32[]{:S(2)}, u32[]{:S(2)}) %collective-permute-start.13) | collective-permute-done | bytes 1048608 | tf_op jit(solution)/shard_map/ppermute | solution.py:310
  58.4 11.0 %collective-permute-start.12 = (bf16[512,1024]{1,0:T(8,128)(2,1)S(1)}, bf16[512,1024]{1,0:T(8,128)(2,1)}, u32[]{:S(2)}, u32[]{:S(2)}) collective-permute-start(bf16[512,1024]{1,0:T(8,128)(2,1)S(1)} %collective-permute-done.refs_0_.refs_3_), channel_id=1, source_target_pairs={{0,4},{1,5},{2,6},{3,7},{4,0},{5,1},{6,2},{7,3},{8,12},{9,13},{10,... | collective-permute-start | bytes 3145736 | tf_op jit(solution)/shard_map/ppermute | solution.py:310
  70.1 1.9 collective-permute-done.17.refs_8_
  74.7 7.8 %collective-permute-start.21 = (bf16[3,256,512]{2,1,0:T(8,128)(2,1)S(1)}, bf16[3,256,512]{2,1,0:T(8,128)(2,1)}, u32[]{:S(2)}, u32[]{:S(2)}) collective-permute-start(bf16[3,256,512]{2,1,0:T(8,128)(2,1)S(1)} %maximum_select_fusion.1), channel_id=1, source_target_pairs={{0,1},{1,0},{2,3},{3,2},{4,5},{5,4},{6,7},{7,6},{8,9},{9,8},{10,11... | collective-permute-start | bytes 2359304 | tf_op jit(solution)/shard_map/ppermute | solution.py:310
  84.5 3.9 collective-permute-start.23
  88.4 13.8 %project.1 = (bf16[2048,1024]{1,0:T(8,128)(2,1)}, bf16[1024,512]{1,0:T(8,128)(2,1)}, bf16[2048,512]{1,0:T(8,128)(2,1)}, bf16[2048,512]{1,0:T(8,128)(2,1)}, bf16[...) custom-call(bf16[512,1024]{1,0:T(8,128)(2,1)} %copy-done.13, ...), custom_call_target="tpu_custom_call" | custom-call | flops 1000 | bytes 1000 | tf_op jit(solution)/shard_map/project/pallas_call | solution.py:581
  106.4 1.6 copy-done.1
  108.0 1.6 copy-done.3
  110.8 6.0 %attend_forward.4 = (bf16[1024,128]{1,0:T(8,128)(2,1)S(1)}, f32[1,8,1024]{2,1,0:T(8,128)S(1)}) custom-call(s32[1]{0:T(128)} %bitcast.12.outer_ref, s32[9]{0:T(128)S(1)} %stack.174.sc_ref, bf16[1024,512]{1,0:T(8,128)(2,1)S(1)} %copy-done.5, bf16[2048,512]{1,0:T(8,128)(2,1)S(1)} %copy-done.1, bf16[2048,512]{1,0:T(8,128)(2,1)S(1)} %copy-done.3), custom_call_target="tpu_custom_call" | custom-call | flops 1000 | bytes 1000 | tf_op jit(solution)/shard_map/attend_forward/pallas_call | solution.py:439
  116.8 1.6 collective-permute-start.24
  119.1 6.6 %attend_forward.5 = (bf16[1024,128]{1,0:T(8,128)(2,1)S(1)}, f32[1,8,1024]{2,1,0:T(8,128)S(1)}) custom-call(s32[1]{0:T(128)} %bitcast.12.outer_ref, s32[9]{0:T(128)S(1)} %stack.174.sc_ref, bf16[1024,512]{1,0:T(8,128)(2,1)S(1)} %copy-done.5, bf16[2048,512]{1,0:T(8,128)(2,1)S(1)} %copy-done.1, bf16[2048,512]{1,0:T(8,128)(2,1)S(1)} %copy-done.3), custom_call_target="tpu_custom_call" | custom-call | flops 1000 | bytes 1000 | tf_op jit(solution)/shard_map/attend_forward/pallas_call | solution.py:439
  127.4 6.0 %attend_forward.6 = (bf16[1024,128]{1,0:T(8,128)(2,1)S(1)}, f32[1,8,1024]{2,1,0:T(8,128)S(1)}) custom-call(s32[1]{0:T(128)} %bitcast.12.outer_ref, s32[9]{0:T(128)S(1)} %stack.174.sc_ref, bf16[1024,512]{1,0:T(8,128)(2,1)S(1)} %copy-done.5, bf16[2048,512]{1,0:T(8,128)(2,1)S(1)} %copy-done.1, bf16[2048,512]{1,0:T(8,128)(2,1)S(1)} %copy-done.3), custom_call_target="tpu_custom_call" | custom-call | flops 1000 | bytes 1000 | tf_op jit(solution)/shard_map/attend_forward/pallas_call | solution.py:439
  133.4 1.8 collective-permute-done.24
  135.2 4.3 collective-permute-done.25
  139.6 1.9 collective-permute-start.29
  141.6 6.2 %attend_forward.7 = (bf16[1024,128]{1,0:T(8,128)(2,1)S(1)}, f32[1,8,1024]{2,1,0:T(8,128)S(1)}) custom-call(s32[1]{0:T(128)} %bitcast.12.outer_ref, s32[9]{0:T(128)S(1)} %stack.174.sc_ref, bf16[1024,512]{1,0:T(8,128)(2,1)S(1)} %copy-done.5, bf16[2048,512]{1,0:T(8,128)(2,1)S(1)} %copy-done.1, bf16[2048,512]{1,0:T(8,128)(2,1)S(1)} %copy-done.3), custom_call_target="tpu_custom_call" | custom-call | flops 1000 | bytes 1000 | tf_op jit(solution)/shard_map/attend_forward/pallas_call | solution.py:439
  149.5 5.3 %collective-permute-done.27 = bf16[3,256,512]{2,1,0:T(8,128)(2,1)S(1)} collective-permute-done((bf16[3,256,512]{2,1,0:T(8,128)(2,1)S(1)}, bf16[3,256,512]{2,1,0:T(8,128)(2,1)S(1)}, u32[]{:S(2)}, u32[]{:S(2)}) %collective-permute-start.27) | collective-permute-done | bytes 786464 | tf_op jit(solution)/shard_map/ppermute | solution.py:310
  155.8 17.3 %collective-permute-done.29.refs_4_.refs_2_.refs_9_.refs_15_ = bf16[2,3,256,512]{3,2,1,0:T(8,128)(2,1)S(1)} collective-permute-done((bf16[2,3,256,512]{3,2,1,0:T(8,128)(2,1)S(1)}, bf16[2,3,256,512]{3,2,1,0:T(8,128)(2,1)S(1)}, u32[]{:S(2)}, u32[]{:S(2)}) %collective-permute-start.29) | collective-permute-done | bytes 1572896 | tf_op jit(solution)/shard_map/ppermute | solution.py:310
  173.2 1.7 collective-permute-done.30
  181.7 6.0 %feed_forward.4 = (bf16[1024,512]{1,0:T(8,128)(2,1)S(1)}, bf16[1024,512]{1,0:T(8,128)(2,1)S(1)}, bf16[1024,512]{1,0:T(8,128)(2,1)S(1)}, f32[1024,1024]{1,0:T(8,128)S(1)}) custom-call(bf16[1024,1024]{1,0:T(8,128)(2,1)S(1)} %pad_maximum_fusion.refs_0_, bf16[1,3,256,512]{3,2,1,0:T(8,128)(2,1)S(1)} %bitcast.154, ...), custom_call_target="tpu_custom_call" | custom-call | flops 1000 | bytes 1000 | tf_op jit(solution)/shard_map/feed_forward/pallas_call | solution.py:781
  188.7 6.6 %feed_forward.5 = (bf16[1024,512]{1,0:T(8,128)(2,1)S(1)}, bf16[1024,512]{1,0:T(8,128)(2,1)S(1)}, bf16[1024,512]{1,0:T(8,128)(2,1)S(1)}, f32[1024,1024]{1,0:T(8,128)S(1)}) custom-call(bf16[1024,1024]{1,0:T(8,128)(2,1)S(1)} %pad_maximum_fusion.refs_0_, bf16[1,3,256,512]{3,2,1,0:T(8,128)(2,1)} %bitcast.31.refs_1_.refs_12_, ...), custom_call_target="tpu_custom_call", output_to_operand_aliasing={{3}: (5, {})} | custom-call | flops 1000 | bytes 1000 | tf_op jit(solution)/shard_map/feed_forward/pallas_call | solution.py:781
  198.2 4.9 feed_forward.6
  206.0 8.0 %collective-permute-done.34.refs_2_.refs_4_.refs_13_.refs_15_ = bf16[2,3,256,512]{3,2,1,0:T(8,128)(2,1)S(1)} collective-permute-done((bf16[2,3,256,512]{3,2,1,0:T(8,128)(2,1)S(1)}, bf16[2,3,256,512]{3,2,1,0:T(8,128)(2,1)S(1)}, u32[]{:S(2)}, u32[]{:S(2)}) %collective-permute-start.34) | collective-permute-done | bytes 1572896 | tf_op jit(solution)/shard_map/ppermute | solution.py:310
  215.3 4.9 feed_forward.7
  220.2 1.8 slice.170
  227.6 4.7 fusion.23
  236.4 2.0 collective-permute-start.38
  238.4 22.6 %feed_backward.2 = (f32[1024,1024]{1,0:T(8,128)}, bf16[3,256,512]{2,1,0:T(8,128)(2,1)}, bf16[3,256,512]{2,1,0:T(8,128)(2,1)}, bf16[3,256,512]{2,1,0:T(8,128)(2,1...) custom-call(bf16[1024,1024]{1,0:T(8,128)(2,1)} %copy-done, ...), custom_call_target="tpu_custom_call" | custom-call | flops 1000 | bytes 1000 | tf_op jit(solution)/shard_map/feed_backward/pallas_call | solution.py:877
  262.1 1.7 collective-permute-start.40
  263.7 23.9 %feed_backward.3 = (f32[512,1024]{1,0:T(8,128)}, bf16[512,1024]{1,0:T(8,128)(2,1)}, bf16[3,256,512]{2,1,0:T(8,128)(2,1)}, bf16[3,256,512]{2,1,0:T(8,128)(2,1)}, ...) custom-call(bf16[1024,1024]{1,0:T(8,128)(2,1)} %copy-done, ...), custom_call_target="tpu_custom_call" | custom-call | flops 1000 | bytes 1000 | tf_op jit(solution)/shard_map/feed_backward/pallas_call | solution.py:877
  287.7 2.4 fusion.4
  294.9 1.8 norm_grads.2
  303.7 16.4 %shard_map.135 = (bf16[1024,256]{1,0:T(8,128)(2,1)S(1)}, bf16[2048,256]{1,0:T(8,128)(2,1)S(1)}, bf16[2048,256]{1,0:T(8,128)(2,1)S(1)}) custom-call(s32[9]{0:T(128)S(1)} %stack.174.sc_ref, bf16[1024,512]{1,0:T(8,128)(2,1)S(1)} %copy-done.6, bf16[2048,512]{1,0:T(8,128)(2,1)S(1)} %copy-done.2, bf16[2048,512]{1,0:T(8,128)(2,1)S(1)} %copy-done.4, ...), custom_call_target="tpu_custom_call" | custom-call | flops 1000 | bytes 1000 | tf_op jit(solution)/shard_map/pallas_call | solution.py:519
  322.6 16.8 %shard_map.136 = (bf16[1024,256]{1,0:T(8,128)(2,1)S(1)}, bf16[2048,256]{1,0:T(8,128)(2,1)S(1)}, bf16[2048,256]{1,0:T(8,128)(2,1)S(1)}) custom-call(s32[9]{0:T(128)S(1)} %stack.174.sc_ref, bf16[1024,512]{1,0:T(8,128)(2,1)S(1)} %copy-done.6, bf16[2048,512]{1,0:T(8,128)(2,1)S(1)} %copy-done.2, bf16[2048,512]{1,0:T(8,128)(2,1)S(1)} %copy-done.4, ...), custom_call_target="tpu_custom_call" | custom-call | flops 1000 | bytes 1000 | tf_op jit(solution)/shard_map/pallas_call | solution.py:519
  339.6 12.5 %collective-permute-done.47 = bf16[3,256,512]{2,1,0:T(8,128)(2,1)S(1)} collective-permute-done((bf16[3,256,512]{2,1,0:T(8,128)(2,1)S(1)}, bf16[3,256,512]{2,1,0:T(8,128)(2,1)S(1)}, u32[]{:S(2)}, u32[]{:S(2)}) %collective-permute-start.47) | collective-permute-done | bytes 786464 | tf_op jit(solution)/shard_map/ppermute | solution.py:310
  360.0 8.1 %rows_grads.1 = (f32[512,1024]{1,0:T(8,128)S(1)}, bf16[512,1024]{1,0:T(8,128)(2,1)S(1)}, f32[512,1024]{1,0:T(8,128)S(1)}, bf16[512,1024]{1,0:T(8,128)(2,1)S(1)}) custom-call(bf16[1024,512]{1,0:T(8,128)(2,1)S(1)} %pad_maximum_fusion.11.dq_ref, bf16[2048,512]{1,0:T(8,128)(2,1)S(1)} %constant_dynamic-update-slice_fusion.7.dk_ref, bf16[2048,512]{1,0:T(8,128)(2,1)} %copy-done.11, ...), custom_call_target="tpu_custom_call" | custom-call | flops 1000 | bytes 1000 | tf_op jit(solution)/shard_map/rows_grads/pallas_call | solution.py:637
  374.6 9.7 %attention_grads.1 = (bf16[256,1024]{1,0:T(8,128)(2,1)S(1)}, bf16[256,1024]{1,0:T(8,128)(2,1)S(1)}, bf16[256,1024]{1,0:T(8,128)(2,1)S(1)}, bf16[256,1024]{1,0:T(...) custom-call(bf16[2048,1024]{1,0:T(8,128)(2,1)} %get-tuple-element.35, ...), custom_call_target="tpu_custom_call" | custom-call | flops 1000 | bytes 1000 | tf_op jit(solution)/shard_map/attention_grads/pallas_call | solution.py:675
  392.8 2.0 collective-permute-start.55
  394.8 2.5 broadcast_select_fusion
  397.3 8.1 %collective-permute-done.52 = bf16[2,3,256,512]{3,2,1,0:T(8,128)(2,1)} collective-permute-done((bf16[2,3,256,512]{3,2,1,0:T(8,128)(2,1)}, bf16[2,3,256,512]{3,2,1,0:T(8,128)(2,1)}, u32[]{:S(2)}, u32[]{:S(2)}) %collective-permute-start.52) | collective-permute-done | bytes 1572896 | tf_op jit(solution)/shard_map/ppermute | solution.py:310
  408.3 2.6 convert_add_fusion.2
  411.3 19.8 %collective-permute-done.51.refs_2_ = bf16[512,1024]{1,0:T(8,128)(2,1)} collective-permute-done((bf16[512,1024]{1,0:T(8,128)(2,1)}, bf16[512,1024]{1,0:T(8,128)(2,1)}, u32[]{:S(2)}, u32[]{:S(2)}) %collective-permute-start.51) | collective-permute-done | bytes 1048608 | tf_op jit(solution)/shard_map/ppermute | solution.py:310
  431.1 4.4 norm_grads.3
  439.6 1.5 collective-permute-start.61
  441.1 5.2 %collective-permute-done.62 = bf16[3,256,512]{2,1,0:T(8,128)(2,1)S(1)} collective-permute-done((bf16[3,256,512]{2,1,0:T(8,128)(2,1)S(1)}, bf16[3,256,512]{2,1,0:T(8,128)(2,1)S(1)}, u32[]{:S(2)}, u32[]{:S(2)}) %collective-permute-start.62) | collective-permute-done | bytes 786464 | tf_op jit(solution)/shard_map/ppermute | solution.py:310
  448.1 12.5 %collective-permute-done.61 = f32[2,512]{1,0:T(2,128)S(1)} collective-permute-done((f32[2,512]{1,0:T(2,128)S(1)}, f32[2,512]{1,0:T(2,128)S(1)}, u32[]{:S(2)}, u32[]{:S(2)}) %collective-permute-start.61) | collective-permute-done | bytes 4128 | tf_op jit(solution)/shard_map/ppermute | solution.py:310
  463.8 1.6 select_convert_fusion
  466.5 8.5 %collective-permute-done.63 = bf16[2,256,512]{2,1,0:T(8,128)(2,1)S(1)} collective-permute-done((bf16[2,256,512]{2,1,0:T(8,128)(2,1)S(1)}, bf16[2,256,512]{2,1,0:T(8,128)(2,1)S(1)}, u32[]{:S(2)}, u32[]{:S(2)}) %collective-permute-start.63) | collective-permute-done | bytes 524320 | tf_op jit(solution)/shard_map/ppermute | solution.py:310
  475.0 2.0 collective-permute-start.68
  478.4 2.3 collective-permute-start.71
  480.7 2.1 collective-permute-start.69
  483.6 1.8 copy.19
  486.4 5.6 %collective-permute-done.70 = f32[2,32]{1,0:T(2,128)S(1)} collective-permute-done((f32[2,32]{1,0:T(2,128)S(1)}, f32[2,32]{1,0:T(2,128)S(1)}, u32[]{:S(2)}, u32[]{:S(2)}) %collective-permute-start.70) | collective-permute-done | bytes 288 | tf_op jit(solution)/shard_map/ppermute | solution.py:310
  (418 shorter events, 108.8 us)
Async XLA Ops:
  0.6 4.7 collective-permute-start.1
  2.3 7.2 %collective-permute-start.5 = (bf16[4,128,128]{2,1,0:T(8,128)(2,1)S(1)}, bf16[4,128,128]{2,1,0:T(8,128)(2,1)S(1)}, u32[]{:S(2)}, u32[]{:S(2)}) collective-permute-start(bf16[4,128,128]{2,1,0:T(8,128)(2,1)S(1)} %get-tuple-element.464), channel_id=1, source_target_pairs={{0,4},{1,5},{2,6},{3,7},{4,0},{5,1},{6,2},{7,3},{8,12},{9,13},{10,... | collective-permute-start | bytes 393224 | tf_op jit(solution)/shard_map/ppermute | solution.py:310
  4.8 4.8 collective-permute-start.6
  5.4 4.6 collective-permute-start.2
  8.0 3.6 collective-permute-start.3
  9.5 4.6 collective-permute-start.4
  14.1 12.5 %collective-permute-start.8 = (bf16[256,512]{1,0:T(8,128)(2,1)S(1)}, bf16[256,512]{1,0:T(8,128)(2,1)S(1)}, u32[]{:S(2)}, u32[]{:S(2)}) collective-permute-start(bf16[256,512]{1,0:T(8,128)(2,1)S(1)} %pad_maximum_fusion.22), channel_id=1, source_target_pairs={{0,1},{1,0},{2,3},{3,2},{4,5},{5,4},{6,7},{7,6},{8,9},{9,8},{10,11... | collective-permute-start | bytes 786440 | tf_op jit(solution)/shard_map/ppermute | solution.py:310
  15.6 13.4 %collective-permute-start.7 = (bf16[256,512]{1,0:T(8,128)(2,1)S(1)}, bf16[256,512]{1,0:T(8,128)(2,1)S(1)}, u32[]{:S(2)}, u32[]{:S(2)}) collective-permute-start(bf16[256,512]{1,0:T(8,128)(2,1)S(1)} %pad_maximum_fusion.22), channel_id=1, source_target_pairs={{0,2},{1,3},{2,0},{3,1},{4,6},{5,7},{6,4},{7,5},{8,10},{9,11},{10,... | collective-permute-start | bytes 786440 | tf_op jit(solution)/shard_map/ppermute | solution.py:310
  29.0 6.6 %collective-permute-start.9 = (bf16[256,512]{1,0:T(8,128)(2,1)S(1)}, bf16[256,512]{1,0:T(8,128)(2,1)S(1)}, u32[]{:S(2)}, u32[]{:S(2)}) collective-permute-start(bf16[256,512]{1,0:T(8,128)(2,1)S(1)} %collective-permute-done.7), channel_id=1, source_target_pairs={{0,1},{1,0},{2,3},{3,2},{4,5},{5,4},{6,7},{7,6},{8,9},{9,8},{10,11... | collective-permute-start | bytes 786440 | tf_op jit(solution)/shard_map/ppermute | solution.py:310
  29.5 20.5 %collective-permute-start = (bf16[512,1024]{1,0:T(8,128)(2,1)S(1)}, bf16[512,1024]{1,0:T(8,128)(2,1)S(1)}, u32[]{:S(2)}, u32[]{:S(2)}) collective-permute-start(bf16[512,1024]{1,0:T(8,128)(2,1)S(1)} %pad_maximum_fusion.8), channel_id=1, source_target_pairs={{0,0},{1,1},{2,5},{3,4},{4,3},{5,2},{6,6},{7,7},{8,8},{9,9},{10,13... | collective-permute-start | bytes 3145736 | tf_op jit(solution)/shard_map/ppermute | solution.py:310
  30.4 28.0 %collective-permute-start.13 = (bf16[512,1024]{1,0:T(8,128)(2,1)S(1)}, bf16[512,1024]{1,0:T(8,128)(2,1)}, u32[]{:S(2)}, u32[]{:S(2)}) collective-permute-start(bf16[512,1024]{1,0:T(8,128)(2,1)S(1)} %pad_maximum_fusion.8), channel_id=1, source_target_pairs={{0,1},{1,0},{2,4},{4,2},{5,3},{6,7},{8,9},{9,8},{10,12},{12,10},{1... | collective-permute-start | bytes 3145736 | tf_op jit(solution)/shard_map/ppermute | solution.py:310
  35.0 13.5 %collective-permute-start.11 = (bf16[2,256,512]{2,1,0:T(8,128)(2,1)S(1)}, bf16[2,256,512]{2,1,0:T(8,128)(2,1)S(1)}, u32[]{:S(2)}, u32[]{:S(2)}) collective-permute-start(bf16[2,256,512]{2,1,0:T(8,128)(2,1)S(1)} %pad_maximum_fusion.16.refs_5_), channel_id=1, source_target_pairs={{0,8},{1,9},{2,10},{3,11},{4,12},{5,13},{6,14},{7,15},{8,0},{9,1},... | collective-permute-start | bytes 1572872 | tf_op jit(solution)/shard_map/ppermute | solution.py:310
  35.7 13.8 %collective-permute-start.10 = (bf16[2,256,512]{2,1,0:T(8,128)(2,1)S(1)}, bf16[2,256,512]{2,1,0:T(8,128)(2,1)S(1)}, u32[]{:S(2)}, u32[]{:S(2)}) collective-permute-start(bf16[2,256,512]{2,1,0:T(8,128)(2,1)S(1)} %pad_maximum_fusion.15.refs_9_), channel_id=1, source_target_pairs={{0,16},{1,17},{2,18},{3,19},{4,20},{5,21},{6,22},{7,23},{8,24},{9,... | collective-permute-start | bytes 1572872 | tf_op jit(solution)/shard_map/ppermute | solution.py:310
  36.2 33.2 %collective-permute-start.15 = (bf16[2,256,512]{2,1,0:T(8,128)(2,1)S(1)}, bf16[2,256,512]{2,1,0:T(8,128)(2,1)S(1)}, u32[]{:S(2)}, u32[]{:S(2)}) collective-permute-start(bf16[2,256,512]{2,1,0:T(8,128)(2,1)S(1)} %pad_maximum_fusion.16.refs_5_), channel_id=1, source_target_pairs={{0,16},{1,17},{2,18},{3,19},{4,20},{5,21},{6,22},{7,23},{8,24},{9,... | collective-permute-start | bytes 1572872 | tf_op jit(solution)/shard_map/ppermute | solution.py:310
  48.5 21.0 %collective-permute-start.16 = (bf16[2,256,512]{2,1,0:T(8,128)(2,1)S(1)}, bf16[2,256,512]{2,1,0:T(8,128)(2,1)S(1)}, u32[]{:S(2)}, u32[]{:S(2)}) collective-permute-start(bf16[2,256,512]{2,1,0:T(8,128)(2,1)S(1)} %pad_maximum_fusion.15.refs_9_), channel_id=1, source_target_pairs={{0,8},{1,9},{2,10},{3,11},{4,12},{5,13},{6,14},{7,15},{8,0},{9,1},... | collective-permute-start | bytes 1572872 | tf_op jit(solution)/shard_map/ppermute | solution.py:310
  49.5 22.5 %collective-permute-start.17 = (bf16[2,256,512]{2,1,0:T(8,128)(2,1)S(1)}, bf16[2,256,512]{2,1,0:T(8,128)(2,1)S(1)}, u32[]{:S(2)}, u32[]{:S(2)}) collective-permute-start(bf16[2,256,512]{2,1,0:T(8,128)(2,1)S(1)} %collective-permute-done.11.refs_6_), channel_id=1, source_target_pairs={{0,16},{1,17},{2,18},{3,19},{4,20},{5,21},{6,22},{7,23},{8,24},{9,... | collective-permute-start | bytes 1572872 | tf_op jit(solution)/shard_map/ppermute | solution.py:310
  50.0 24.0 %collective-permute-start.18 = (bf16[2,256,512]{2,1,0:T(8,128)(2,1)S(1)}, bf16[2,256,512]{2,1,0:T(8,128)(2,1)S(1)}, u32[]{:S(2)}, u32[]{:S(2)}) collective-permute-start(bf16[2,256,512]{2,1,0:T(8,128)(2,1)S(1)} %collective-permute-done.10.refs_11_), channel_id=1, source_target_pairs={{0,8},{1,9},{2,10},{3,11},{4,12},{5,13},{6,14},{7,15},{8,0},{9,1},... | collective-permute-start | bytes 1572872 | tf_op jit(solution)/shard_map/ppermute | solution.py:310
  58.4 26.1 %collective-permute-start.12 = (bf16[512,1024]{1,0:T(8,128)(2,1)S(1)}, bf16[512,1024]{1,0:T(8,128)(2,1)}, u32[]{:S(2)}, u32[]{:S(2)}) collective-permute-start(bf16[512,1024]{1,0:T(8,128)(2,1)S(1)} %collective-permute-done.refs_0_.refs_3_), channel_id=1, source_target_pairs={{0,4},{1,5},{2,6},{3,7},{4,0},{5,1},{6,2},{7,3},{8,12},{9,13},{10,... | collective-permute-start | bytes 3145736 | tf_op jit(solution)/shard_map/ppermute | solution.py:310
  69.5 15.1 %collective-permute-start.14 = (bf16[512,1024]{1,0:T(8,128)(2,1)}, bf16[512,1024]{1,0:T(8,128)(2,1)}, u32[]{:S(2)}, u32[]{:S(2)}) collective-permute-start(bf16[512,1024]{1,0:T(8,128)(2,1)} %collective-permute-done.13.refs_2_), channel_id=1, source_target_pairs={{0,4},{1,5},{2,6},{3,7},{4,0},{5,1},{6,2},{7,3},{8,12},{9,13},{10,... | collective-permute-start | bytes 3145736 | tf_op jit(solution)/shard_map/ppermute | solution.py:310
  69.5 32.6 %collective-permute-start.19 = (bf16[3,256,512]{2,1,0:T(8,128)(2,1)S(1)}, bf16[3,256,512]{2,1,0:T(8,128)(2,1)}, u32[]{:S(2)}, u32[]{:S(2)}) collective-permute-start(bf16[3,256,512]{2,1,0:T(8,128)(2,1)S(1)} %maximum_select_fusion.1), channel_id=1, source_target_pairs={{0,8},{1,9},{2,10},{3,11},{4,12},{5,13},{6,14},{7,15},{8,0},{9,1},... | collective-permute-start | bytes 2359304 | tf_op jit(solution)/shard_map/ppermute | solution.py:310
  71.9 30.2 %collective-permute-start.20 = (bf16[3,256,512]{2,1,0:T(8,128)(2,1)S(1)}, bf16[3,256,512]{2,1,0:T(8,128)(2,1)}, u32[]{:S(2)}, u32[]{:S(2)}) collective-permute-start(bf16[3,256,512]{2,1,0:T(8,128)(2,1)S(1)} %maximum_select_fusion.1), channel_id=1, source_target_pairs={{0,16},{1,17},{2,18},{3,19},{4,20},{5,21},{6,22},{7,23},{8,24},{9,... | collective-permute-start | bytes 2359304 | tf_op jit(solution)/shard_map/ppermute | solution.py:310
  74.7 42.1 %collective-permute-start.21 = (bf16[3,256,512]{2,1,0:T(8,128)(2,1)S(1)}, bf16[3,256,512]{2,1,0:T(8,128)(2,1)}, u32[]{:S(2)}, u32[]{:S(2)}) collective-permute-start(bf16[3,256,512]{2,1,0:T(8,128)(2,1)S(1)} %maximum_select_fusion.1), channel_id=1, source_target_pairs={{0,1},{1,0},{2,3},{3,2},{4,5},{5,4},{6,7},{7,6},{8,9},{9,8},{10,11... | collective-permute-start | bytes 2359304 | tf_op jit(solution)/shard_map/ppermute | solution.py:310
  84.5 41.3 %collective-permute-start.23 = (bf16[3,256,512]{2,1,0:T(8,128)(2,1)S(1)}, bf16[3,256,512]{2,1,0:T(8,128)(2,1)S(1)}, u32[]{:S(2)}, u32[]{:S(2)}) collective-permute-start(bf16[3,256,512]{2,1,0:T(8,128)(2,1)S(1)} %maximum_select_fusion.1), channel_id=1, source_target_pairs={{0,2},{1,3},{2,0},{3,1},{4,6},{5,7},{6,4},{7,5},{8,10},{9,11},{10,... | collective-permute-start | bytes 2359304 | tf_op jit(solution)/shard_map/ppermute | solution.py:310
  102.2 23.6 %collective-permute-start.22 = (bf16[3,256,512]{2,1,0:T(8,128)(2,1)}, bf16[3,256,512]{2,1,0:T(8,128)(2,1)S(1)}, u32[]{:S(2)}, u32[]{:S(2)}) collective-permute-start(bf16[3,256,512]{2,1,0:T(8,128)(2,1)} %collective-permute-done.19), channel_id=1, source_target_pairs={{0,16},{1,17},{2,18},{3,19},{4,20},{5,21},{6,22},{7,23},{8,24},{9,... | collective-permute-start | bytes 2359304 | tf_op jit(solution)/shard_map/ppermute | solution.py:310
  116.8 18.4 %collective-permute-start.24 = (bf16[3,256,512]{2,1,0:T(8,128)(2,1)}, bf16[3,256,512]{2,1,0:T(8,128)(2,1)S(1)}, u32[]{:S(2)}, u32[]{:S(2)}) collective-permute-start(bf16[3,256,512]{2,1,0:T(8,128)(2,1)} %collective-permute-done.21), channel_id=1, source_target_pairs={{0,8},{1,9},{2,10},{3,11},{4,12},{5,13},{6,14},{7,15},{8,0},{9,1},... | collective-permute-start | bytes 2359304 | tf_op jit(solution)/shard_map/ppermute | solution.py:310
  118.4 21.1 %collective-permute-start.25 = (bf16[3,256,512]{2,1,0:T(8,128)(2,1)}, bf16[3,256,512]{2,1,0:T(8,128)(2,1)S(1)}, u32[]{:S(2)}, u32[]{:S(2)}) collective-permute-start(bf16[3,256,512]{2,1,0:T(8,128)(2,1)} %collective-permute-done.21), channel_id=1, source_target_pairs={{0,16},{1,17},{2,18},{3,19},{4,20},{5,21},{6,22},{7,23},{8,24},{9,... | collective-permute-start | bytes 2359304 | tf_op jit(solution)/shard_map/ppermute | solution.py:310
  125.9 23.6 %collective-permute-start.26 = (bf16[3,256,512]{2,1,0:T(8,128)(2,1)S(1)}, bf16[3,256,512]{2,1,0:T(8,128)(2,1)S(1)}, u32[]{:S(2)}, u32[]{:S(2)}) collective-permute-start(bf16[3,256,512]{2,1,0:T(8,128)(2,1)S(1)} %collective-permute-done.23), channel_id=1, source_target_pairs={{0,1},{1,0},{2,3},{3,2},{4,5},{5,4},{6,7},{7,6},{8,9},{9,8},{10,11... | collective-permute-start | bytes 2359304 | tf_op jit(solution)/shard_map/ppermute | solution.py:310
  126.0 28.9 %collective-permute-start.27 = (bf16[3,256,512]{2,1,0:T(8,128)(2,1)S(1)}, bf16[3,256,512]{2,1,0:T(8,128)(2,1)S(1)}, u32[]{:S(2)}, u32[]{:S(2)}) collective-permute-start(bf16[3,256,512]{2,1,0:T(8,128)(2,1)S(1)} %collective-permute-done.23), channel_id=1, source_target_pairs={{0,16},{1,17},{2,18},{3,19},{4,20},{5,21},{6,22},{7,23},{8,24},{9,... | collective-permute-start | bytes 2359304 | tf_op jit(solution)/shard_map/ppermute | solution.py:310
  139.6 33.5 %collective-permute-start.29 = (bf16[2,3,256,512]{3,2,1,0:T(8,128)(2,1)S(1)}, bf16[2,3,256,512]{3,2,1,0:T(8,128)(2,1)S(1)}, u32[]{:S(2)}, u32[]{:S(2)}) collective-permute-start(bf16[2,3,256,512]{3,2,1,0:T(8,128)(2,1)S(1)} %pad_maximum_fusion.2), channel_id=1, source_target_pairs={{0,8},{1,9},{2,10},{3,11},{4,12},{5,13},{6,14},{7,15},{8,0},{9,1},... | collective-permute-start | bytes 4718600 | tf_op jit(solution)/shard_map/ppermute | solution.py:310
  154.9 20.0 %collective-permute-start.28 = (bf16[512,1024]{1,0:T(8,128)(2,1)S(1)}, bf16[512,1024]{1,0:T(8,128)(2,1)S(1)}, u32[]{:S(2)}, u32[]{:S(2)}) collective-permute-start(bf16[512,1024]{1,0:T(8,128)(2,1)S(1)} %slice.272), channel_id=1, source_target_pairs={{0,4},{1,5},{2,6},{3,7},{4,0},{5,1},{6,2},{7,3},{8,12},{9,13},{10,... | collective-permute-start | bytes 3145736 | tf_op jit(solution)/shard_map/ppermute | solution.py:310
  154.9 20.0 %collective-permute-start.30 = (bf16[3,256,512]{2,1,0:T(8,128)(2,1)S(1)}, bf16[3,256,512]{2,1,0:T(8,128)(2,1)S(1)}, u32[]{:S(2)}, u32[]{:S(2)}) collective-permute-start(bf16[3,256,512]{2,1,0:T(8,128)(2,1)S(1)} %collective-permute-done.26), channel_id=1, source_target_pairs={{0,16},{1,17},{2,18},{3,19},{4,20},{5,21},{6,22},{7,23},{8,24},{9,... | collective-permute-start | bytes 2359304 | tf_op jit(solution)/shard_map/ppermute | solution.py:310
  175.6 20.8 %collective-permute-start.33 = (bf16[3,256,512]{2,1,0:T(8,128)(2,1)S(1)}, bf16[3,256,512]{2,1,0:T(8,128)(2,1)S(1)}, u32[]{:S(2)}, u32[]{:S(2)}) collective-permute-start(bf16[3,256,512]{2,1,0:T(8,128)(2,1)S(1)} %slice_bitcast_fusion.1), channel_id=1, source_target_pairs={{0,16},{1,17},{2,18},{3,19},{4,20},{5,21},{6,22},{7,23},{8,24},{9,... | collective-permute-start | bytes 2359304 | tf_op jit(solution)/shard_map/ppermute | solution.py:310
  177.6 36.4 %collective-permute-start.34 = (bf16[2,3,256,512]{3,2,1,0:T(8,128)(2,1)S(1)}, bf16[2,3,256,512]{3,2,1,0:T(8,128)(2,1)S(1)}, u32[]{:S(2)}, u32[]{:S(2)}) collective-permute-start(bf16[2,3,256,512]{3,2,1,0:T(8,128)(2,1)S(1)} %pad_maximum_fusion.3), channel_id=1, source_target_pairs={{0,8},{1,9},{2,10},{3,11},{4,12},{5,13},{6,14},{7,15},{8,0},{9,1},... | collective-permute-start | bytes 4718600 | tf_op jit(solution)/shard_map/ppermute | solution.py:310
  196.5 27.2 %collective-permute-start.35 = (bf16[512,1024]{1,0:T(8,128)(2,1)S(1)}, bf16[512,1024]{1,0:T(8,128)(2,1)S(1)}, u32[]{:S(2)}, u32[]{:S(2)}) collective-permute-start(bf16[512,1024]{1,0:T(8,128)(2,1)S(1)} %pad_maximum_fusion.9), channel_id=1, source_target_pairs={{2,5},{3,4},{4,3},{5,2},{10,13},{11,12},{12,11},{13,10},{18,21},{1... | collective-permute-start | bytes 3145736 | tf_op jit(solution)/shard_map/ppermute | solution.py:310
  224.6 3.0 collective-permute-start.36
  236.4 51.3 %collective-permute-start.38 = (bf16[512,1024]{1,0:T(8,128)(2,1)}, bf16[512,1024]{1,0:T(8,128)(2,1)}, u32[]{:S(2)}, u32[]{:S(2)}) collective-permute-start(bf16[512,1024]{1,0:T(8,128)(2,1)} %pad_maximum_fusion.10), channel_id=1, source_target_pairs={{2,5},{3,4},{4,3},{5,2},{10,13},{11,12},{12,11},{13,10},{18,21},{1... | collective-permute-start | bytes 3145736 | tf_op jit(solution)/shard_map/ppermute | solution.py:310
  261.0 26.7 %collective-permute-start.39 = (bf16[3,256,512]{2,1,0:T(8,128)(2,1)}, bf16[3,256,512]{2,1,0:T(8,128)(2,1)}, u32[]{:S(2)}, u32[]{:S(2)}) collective-permute-start(bf16[3,256,512]{2,1,0:T(8,128)(2,1)} %get-tuple-element.291), channel_id=1, source_target_pairs={{0,16},{1,17},{2,18},{3,19},{4,20},{5,21},{6,22},{7,23},{8,24},{9,... | collective-permute-start | bytes 2359304 | tf_op jit(solution)/shard_map/ppermute | solution.py:310
  262.1 25.6 %collective-permute-start.40 = (bf16[3,256,512]{2,1,0:T(8,128)(2,1)}, bf16[3,256,512]{2,1,0:T(8,128)(2,1)}, u32[]{:S(2)}, u32[]{:S(2)}) collective-permute-start(bf16[3,256,512]{2,1,0:T(8,128)(2,1)} %get-tuple-element.292), channel_id=1, source_target_pairs={{0,8},{1,9},{2,10},{3,11},{4,12},{5,13},{6,14},{7,15},{8,0},{9,1},... | collective-permute-start | bytes 2359304 | tf_op jit(solution)/shard_map/ppermute | solution.py:310
  296.8 3.2 collective-permute-start.43
  298.2 41.4 %collective-permute-start.45 = (bf16[2,3,256,512]{3,2,1,0:T(8,128)(2,1)S(1)}, bf16[2,3,256,512]{3,2,1,0:T(8,128)(2,1)S(1)}, u32[]{:S(2)}, u32[]{:S(2)}) collective-permute-start(bf16[2,3,256,512]{3,2,1,0:T(8,128)(2,1)S(1)} %pad_maximum_fusion.4), channel_id=1, source_target_pairs={{0,8},{1,9},{2,10},{3,11},{4,12},{5,13},{6,14},{7,15},{8,0},{9,1},... | collective-permute-start | bytes 4718600 | tf_op jit(solution)/shard_map/ppermute | solution.py:310
  298.8 40.7 %collective-permute-start.46 = (bf16[2,3,256,512]{3,2,1,0:T(8,128)(2,1)S(1)}, bf16[2,3,256,512]{3,2,1,0:T(8,128)(2,1)S(1)}, u32[]{:S(2)}, u32[]{:S(2)}) collective-permute-start(bf16[2,3,256,512]{3,2,1,0:T(8,128)(2,1)S(1)} %pad_maximum_fusion.5), channel_id=1, source_target_pairs={{0,16},{1,17},{2,18},{3,19},{4,20},{5,21},{6,22},{7,23},{8,24},{9,... | collective-permute-start | bytes 4718600 | tf_op jit(solution)/shard_map/ppermute | solution.py:310
  320.1 32.0 %collective-permute-start.47 = (bf16[3,256,512]{2,1,0:T(8,128)(2,1)S(1)}, bf16[3,256,512]{2,1,0:T(8,128)(2,1)S(1)}, u32[]{:S(2)}, u32[]{:S(2)}) collective-permute-start(bf16[3,256,512]{2,1,0:T(8,128)(2,1)S(1)} %copy-done.103), channel_id=1, source_target_pairs={{0,16},{1,17},{2,18},{3,19},{4,20},{5,21},{6,22},{7,23},{8,24},{9,... | collective-permute-start | bytes 2359304 | tf_op jit(solution)/shard_map/ppermute | solution.py:310
  321.1 31.0 %collective-permute-start.48 = (bf16[3,256,512]{2,1,0:T(8,128)(2,1)S(1)}, bf16[3,256,512]{2,1,0:T(8,128)(2,1)S(1)}, u32[]{:S(2)}, u32[]{:S(2)}) collective-permute-start(bf16[3,256,512]{2,1,0:T(8,128)(2,1)S(1)} %copy-done.102), channel_id=1, source_target_pairs={{0,8},{1,9},{2,10},{3,11},{4,12},{5,13},{6,14},{7,15},{8,0},{9,1},... | collective-permute-start | bytes 2359304 | tf_op jit(solution)/shard_map/ppermute | solution.py:310
  368.1 3.1 collective-permute-start.49
  368.2 4.1 collective-permute-start.50
  368.7 36.7 %collective-permute-start.52 = (bf16[2,3,256,512]{3,2,1,0:T(8,128)(2,1)}, bf16[2,3,256,512]{3,2,1,0:T(8,128)(2,1)}, u32[]{:S(2)}, u32[]{:S(2)}) collective-permute-start(bf16[2,3,256,512]{3,2,1,0:T(8,128)(2,1)} %pad_maximum_fusion.6), channel_id=1, source_target_pairs={{0,8},{1,9},{2,10},{3,11},{4,12},{5,13},{6,14},{7,15},{8,0},{9,1},... | collective-permute-start | bytes 4718600 | tf_op jit(solution)/shard_map/ppermute | solution.py:310
  370.1 36.4 %collective-permute-start.53 = (bf16[2,3,256,512]{3,2,1,0:T(8,128)(2,1)}, bf16[2,3,256,512]{3,2,1,0:T(8,128)(2,1)}, u32[]{:S(2)}, u32[]{:S(2)}) collective-permute-start(bf16[2,3,256,512]{3,2,1,0:T(8,128)(2,1)} %pad_maximum_fusion.7), channel_id=1, source_target_pairs={{0,16},{1,17},{2,18},{3,19},{4,20},{5,21},{6,22},{7,23},{8,24},{9,... | collective-permute-start | bytes 4718600 | tf_op jit(solution)/shard_map/ppermute | solution.py:310
  371.2 20.5 %collective-permute-start.54 = (bf16[3,256,512]{2,1,0:T(8,128)(2,1)S(1)}, bf16[3,256,512]{2,1,0:T(8,128)(2,1)S(1)}, u32[]{:S(2)}, u32[]{:S(2)}) collective-permute-start(bf16[3,256,512]{2,1,0:T(8,128)(2,1)S(1)} %get-tuple-element.350), channel_id=1, source_target_pairs={{0,1},{1,0},{2,3},{3,2},{4,5},{5,4},{6,7},{7,6},{8,9},{9,8},{10,11... | collective-permute-start | bytes 2359304 | tf_op jit(solution)/shard_map/ppermute | solution.py:310
  373.7 57.4 %collective-permute-start.51 = (bf16[512,1024]{1,0:T(8,128)(2,1)}, bf16[512,1024]{1,0:T(8,128)(2,1)}, u32[]{:S(2)}, u32[]{:S(2)}) collective-permute-start(bf16[512,1024]{1,0:T(8,128)(2,1)} %add_convert_fusion), channel_id=1, source_target_pairs={{0,1},{1,0},{2,3},{3,2},{4,5},{5,4},{6,7},{7,6},{8,9},{9,8},{10,11... | collective-permute-start | bytes 3145736 | tf_op jit(solution)/shard_map/ppermute | solution.py:310
  392.8 42.7 %collective-permute-start.55 = (bf16[3,256,512]{2,1,0:T(8,128)(2,1)}, bf16[3,256,512]{2,1,0:T(8,128)(2,1)}, u32[]{:S(2)}, u32[]{:S(2)}) collective-permute-start(bf16[3,256,512]{2,1,0:T(8,128)(2,1)} %add_convert_fusion.1), channel_id=1, source_target_pairs={{0,2},{1,3},{2,0},{3,1},{4,6},{5,7},{6,4},{7,5},{8,10},{9,11},{10,... | collective-permute-start | bytes 2359304 | tf_op jit(solution)/shard_map/ppermute | solution.py:310
  406.5 30.1 %collective-permute-start.57 = (bf16[256,1024]{1,0:T(8,128)(2,1)S(1)}, bf16[256,1024]{1,0:T(8,128)(2,1)S(1)}, u32[]{:S(2)}, u32[]{:S(2)}) collective-permute-start(bf16[256,1024]{1,0:T(8,128)(2,1)S(1)} %copy-done.72), channel_id=1, source_target_pairs={{0,16},{1,17},{2,18},{3,19},{4,20},{5,21},{6,22},{7,23},{8,24},{9,... | collective-permute-start | bytes 1572872 | tf_op jit(solution)/shard_map/ppermute | solution.py:310
  407.6 29.0 %collective-permute-start.58 = (bf16[256,1024]{1,0:T(8,128)(2,1)S(1)}, bf16[256,1024]{1,0:T(8,128)(2,1)S(1)}, u32[]{:S(2)}, u32[]{:S(2)}) collective-permute-start(bf16[256,1024]{1,0:T(8,128)(2,1)S(1)} %copy-done.70), channel_id=1, source_target_pairs={{0,8},{1,9},{2,10},{3,11},{4,12},{5,13},{6,14},{7,15},{8,0},{9,1},... | collective-permute-start | bytes 1572872 | tf_op jit(solution)/shard_map/ppermute | solution.py:310
  410.9 35.5 %collective-permute-start.62 = (bf16[3,256,512]{2,1,0:T(8,128)(2,1)S(1)}, bf16[3,256,512]{2,1,0:T(8,128)(2,1)S(1)}, u32[]{:S(2)}, u32[]{:S(2)}) collective-permute-start(bf16[3,256,512]{2,1,0:T(8,128)(2,1)S(1)} %get-tuple-element.378), channel_id=1, source_target_pairs={{0,1},{1,0},{2,3},{3,2},{4,5},{5,4},{6,7},{7,6},{8,9},{9,8},{10,11... | collective-permute-start | bytes 2359304 | tf_op jit(solution)/shard_map/ppermute | solution.py:310
  435.7 28.1 %collective-permute-start.56 = (bf16[512,1024]{1,0:T(8,128)(2,1)S(1)}, bf16[512,1024]{1,0:T(8,128)(2,1)S(1)}, u32[]{:S(2)}, u32[]{:S(2)}) collective-permute-start(bf16[512,1024]{1,0:T(8,128)(2,1)S(1)} %pad_maximum_fusion.12), channel_id=1, source_target_pairs={{2,5},{3,4},{4,3},{5,2},{10,13},{11,12},{12,11},{13,10},{18,21},{1... | collective-permute-start | bytes 3145736 | tf_op jit(solution)/shard_map/ppermute | solution.py:310
  438.0 22.7 %collective-permute-start.59 = (bf16[2,256,1024]{2,1,0:T(8,128)(2,1)S(1)}, bf16[2,256,1024]{2,1,0:T(8,128)(2,1)S(1)}, u32[]{:S(2)}, u32[]{:S(2)}) collective-permute-start(bf16[2,256,1024]{2,1,0:T(8,128)(2,1)S(1)} %pad_maximum_fusion.13), channel_id=1, source_target_pairs={{0,8},{1,9},{2,10},{3,11},{4,12},{5,13},{6,14},{7,15},{8,0},{9,1},... | collective-permute-start | bytes 3145736 | tf_op jit(solution)/shard_map/ppermute | solution.py:310
  438.7 22.8 %collective-permute-start.60 = (bf16[2,256,1024]{2,1,0:T(8,128)(2,1)S(1)}, bf16[2,256,1024]{2,1,0:T(8,128)(2,1)S(1)}, u32[]{:S(2)}, u32[]{:S(2)}) collective-permute-start(bf16[2,256,1024]{2,1,0:T(8,128)(2,1)S(1)} %pad_maximum_fusion.14), channel_id=1, source_target_pairs={{0,16},{1,17},{2,18},{3,19},{4,20},{5,21},{6,22},{7,23},{8,24},{9,... | collective-permute-start | bytes 3145736 | tf_op jit(solution)/shard_map/ppermute | solution.py:310
  439.6 21.0 %collective-permute-start.61 = (f32[2,512]{1,0:T(2,128)S(1)}, f32[2,512]{1,0:T(2,128)S(1)}, u32[]{:S(2)}, u32[]{:S(2)}) collective-permute-start(f32[2,512]{1,0:T(2,128)S(1)} %pad_maximum_fusion.27), channel_id=1, source_target_pairs={{0,8},{1,9},{2,10},{3,11},{4,12},{5,13},{6,14},{7,15},{8,0},{9,1},... | collective-permute-start | bytes 12296 | tf_op jit(solution)/shard_map/ppermute | solution.py:310
  448.1 29.1 %collective-permute-start.67 = (bf16[3,128,512]{2,1,0:T(8,128)(2,1)S(1)}, bf16[3,128,512]{2,1,0:T(8,128)(2,1)S(1)}, u32[]{:S(2)}, u32[]{:S(2)}) collective-permute-start(bf16[3,128,512]{2,1,0:T(8,128)(2,1)S(1)} %select_convert_fusion.1), channel_id=1, source_target_pairs={{0,4},{1,5},{2,6},{3,7},{4,0},{5,1},{6,2},{7,3},{8,12},{9,13},{10,... | collective-permute-start | bytes 1179656 | tf_op jit(solution)/shard_map/ppermute | solution.py:310
  462.3 12.8 %collective-permute-start.63 = (bf16[2,256,512]{2,1,0:T(8,128)(2,1)S(1)}, bf16[2,256,512]{2,1,0:T(8,128)(2,1)S(1)}, u32[]{:S(2)}, u32[]{:S(2)}) collective-permute-start(bf16[2,256,512]{2,1,0:T(8,128)(2,1)S(1)} %pad_maximum_fusion.19), channel_id=1, source_target_pairs={{0,1},{1,0},{2,3},{3,2},{4,5},{5,4},{6,7},{7,6},{8,9},{9,8},{10,11... | collective-permute-start | bytes 1572872 | tf_op jit(solution)/shard_map/ppermute | solution.py:310
  462.9 3.6 collective-permute-start.64
  477.1 15.6 %collective-permute-start.65 = (bf16[256,512]{1,0:T(8,128)(2,1)S(1)}, bf16[256,512]{1,0:T(8,128)(2,1)S(1)}, u32[]{:S(2)}, u32[]{:S(2)}) collective-permute-start(bf16[256,512]{1,0:T(8,128)(2,1)S(1)} %fusion.11), channel_id=1, source_target_pairs={{0,2},{1,3},{2,0},{3,1},{4,6},{5,7},{6,4},{7,5},{8,10},{9,11},{10,... | collective-permute-start | bytes 786440 | tf_op jit(solution)/shard_map/ppermute | solution.py:310
  478.4 8.0 %collective-permute-start.71 = (f32[2,32]{1,0:T(2,128)S(1)}, f32[2,32]{1,0:T(2,128)S(1)}, u32[]{:S(2)}, u32[]{:S(2)}) collective-permute-start(f32[2,32]{1,0:T(2,128)S(1)} %get-tuple-element.473), channel_id=1, source_target_pairs={{0,3},{1,2},{2,1},{3,0},{4,7},{5,6},{6,5},{7,4},{8,11},{9,10},{10,... | collective-permute-start | bytes 776 | tf_op jit(solution)/shard_map/ppermute | solution.py:310
  480.7 11.4 %collective-permute-start.70 = (f32[2,32]{1,0:T(2,128)S(1)}, f32[2,32]{1,0:T(2,128)S(1)}, u32[]{:S(2)}, u32[]{:S(2)}) collective-permute-start(f32[2,32]{1,0:T(2,128)S(1)} %get-tuple-element.474), channel_id=1, source_target_pairs={{0,2},{1,3},{2,0},{3,1},{4,6},{5,7},{6,4},{7,5},{8,10},{9,11},{10,... | collective-permute-start | bytes 776 | tf_op jit(solution)/shard_map/ppermute | solution.py:310
  480.7 11.3 %collective-permute-start.69 = (f32[2,32]{1,0:T(2,128)S(1)}, f32[2,32]{1,0:T(2,128)S(1)}, u32[]{:S(2)}, u32[]{:S(2)}) collective-permute-start(f32[2,32]{1,0:T(2,128)S(1)} %get-tuple-element.472), channel_id=1, source_target_pairs={{0,1},{1,0},{2,3},{3,2},{4,5},{5,4},{6,7},{7,6},{8,9},{9,8},{10,11... | collective-permute-start | bytes 776 | tf_op jit(solution)/shard_map/ppermute | solution.py:310
  (114 other events, 1145.5 us)

commit v5 on v4

--- a/solution.py
+++ b/solution.py
@@ -1161,14 +1161,13 @@
 
     batch_x, batch_y, sent = event(batch_x, batch_y, sent)
     even, odd = total_of(own_e, batch_x[0], batch_y[0]), total_of(own_o, batch_x[1], batch_y[1])
-    att_13, att_2 = jnp.stack([even[:, half_cols:], odd[:, half_cols:]]).astype(BF), odd[:, :half_cols].astype(BF)
-    att_13, att_2, a, c, sent = event(att_13, att_2, a, c, sent)
-    att_13 = z_swap(att_13, 1)
+    att_3, att_1, att_2 = odd[:, half_cols:].astype(BF), even[:, half_cols:].astype(BF), odd[:, :half_cols].astype(BF)
+    att_3, att_1, a, c, sent = event(att_3, att_1, a, c, sent)
+    att_3, att_1 = z_swap(att_3, 1), z_swap(att_1, 1)
     a, c = a + sent[:, :quarter], c + sent[:, quarter:]
     sent = y_swap(c)
-    att_13, att_2, sent = event(att_13, att_2, sent)
-    att_2 = z_swap(add(att_2, att_13[1]), 2)
-    att_1 = att_13[0]
+    att_3, att_2, sent = event(att_3, att_2, sent)
+    att_2 = z_swap(add(att_2, att_3), 2)
     a = a + sent
     keep, give = pick(jnp.split(a, 2, axis=1))
     sent = core_swap(give)

time: 500 us -> 497 us (level)
  waiting for transfers between devices: 159 us -> 152 us
    ppermute x72 -> x73, waiting for transfers between devices: 159 us -> 152 us  [shift(): return lax.ppermute(value, AXES, pairs)]
    ppermute x72 -> x73, starting transfers between devices: 85.9 us -> 89.8 us  [shift(): return lax.ppermute(value, AXES, pairs)]
  transfers between devices with their start and end apart: 72 -> 73, of which waited for: 35 -> 34; matrix products, arithmetic and copies ran while one was open for 7% -> 7% of each run, Pallas kernels for 31% -> 31%
where the time goes in v5:
time: 497 us; the launch traced here: 492 us
  Pallas kernels  165 us (33%)
  waiting for transfers between devices  152 us (31%)
  starting transfers between devices  89.8 us (18%)
  local copies, waits for them, and re-layouts  42.5 us (9%)
  other arithmetic  36.3 us (7%)
    ppermute x73, waiting for transfers between devices, shift(): return lax.ppermute(value, AXES, pairs)  152 us
    ppermute x73, starting transfers between devices, shift(): return lax.ppermute(value, AXES, pairs)  89.8 us
    pallas_call x2, Pallas kernels, feed_backward(): pl.pallas_call(lambda *refs: feed_backward_kernel(places, total is not No...  46.5 us
    unnamed x223, local copies, waits for them, and re-layouts  34.7 us
    pallas_call x2, Pallas kernels, attend_backward(): pl.pallas_call(attend_backward_kernel, out_shape=(jax.ShapeDtypeStruct((r...  33.2 us
    pallas_call x4, Pallas kernels, attend_forward(): pl.pallas_call(attend_forward_kernel, out_shape=(jax.ShapeDtypeStruct((ro...  24.9 us
    pallas_call x4, Pallas kernels, feed_forward(): pl.pallas_call(lambda *refs: feed_forward_kernel(y is None, *refs), out_s...  22.4 us
    pallas_call x1, Pallas kernels, project(): pl.pallas_call(project_kernel, out_shape=(shape(4 * chunk, model), shape(...  13.8 us
  transfers between devices with their start and end apart: 73, of which 34 were waited for; matrix products, arithmetic and copies ran while one was open for 7% of the time, Pallas kernels for 31%

profile of v5, /device:TPU:0, one launch (start us, length us, event | category | flops | bytes accessed | tf_op | source)
XLA Modules:
  0.0 492.5 jit_solution(16140552630747928690)
XLA Ops:
  5.4 2.6 collective-permute-start.2
  8.0 1.5 collective-permute-start.3
  10.0 1.5 collective-permute-done.3
  12.1 2.0 collective-permute-done.4
  14.1 1.6 collective-permute-start.8
  15.6 2.6 collective-permute-start.7
  18.3 8.2 %collective-permute-done.8 = bf16[256,512]{1,0:T(8,128)(2,1)S(1)} collective-permute-done((bf16[256,512]{1,0:T(8,128)(2,1)S(1)}, bf16[256,512]{1,0:T(8,128)(2,1)S(1)}, u32[]{:S(2)}, u32[]{:S(2)}) %collective-permute-start.8) | collective-permute-done | bytes 262176 | tf_op jit(solution)/shard_map/ppermute | solution.py:310
  26.5 2.5 collective-permute-done.7
  30.4 3.6 collective-permute-start.13
  36.2 1.5 collective-permute-start.15
  37.7 10.7 %collective-permute-done.11.refs_6_ = bf16[2,256,512]{2,1,0:T(8,128)(2,1)S(1)} collective-permute-done((bf16[2,256,512]{2,1,0:T(8,128)(2,1)S(1)}, bf16[2,256,512]{2,1,0:T(8,128)(2,1)S(1)}, u32[]{:S(2)}, u32[]{:S(2)}) %collective-permute-start.11) | collective-permute-done | bytes 524320 | tf_op jit(solution)/shard_map/ppermute | solution.py:310
  51.5 6.9 %collective-permute-done.13.refs_2_ = bf16[512,1024]{1,0:T(8,128)(2,1)} collective-permute-done((bf16[512,1024]{1,0:T(8,128)(2,1)S(1)}, bf16[512,1024]{1,0:T(8,128)(2,1)}, u32[]{:S(2)}, u32[]{:S(2)}) %collective-permute-start.13) | collective-permute-done | bytes 1048608 | tf_op jit(solution)/shard_map/ppermute | solution.py:310
  58.4 11.0 %collective-permute-start.12 = (bf16[512,1024]{1,0:T(8,128)(2,1)S(1)}, bf16[512,1024]{1,0:T(8,128)(2,1)}, u32[]{:S(2)}, u32[]{:S(2)}) collective-permute-start(bf16[512,1024]{1,0:T(8,128)(2,1)S(1)} %collective-permute-done.refs_0_.refs_3_), channel_id=1, source_target_pairs={{0,4},{1,5},{2,6},{3,7},{4,0},{5,1},{6,2},{7,3},{8,12},{9,13},{10,... | collective-permute-start | bytes 3145736 | tf_op jit(solution)/shard_map/ppermute | solution.py:310
  70.1 1.9 collective-permute-done.17.refs_8_
  74.7 7.8 %collective-permute-start.21 = (bf16[3,256,512]{2,1,0:T(8,128)(2,1)S(1)}, bf16[3,256,512]{2,1,0:T(8,128)(2,1)}, u32[]{:S(2)}, u32[]{:S(2)}) collective-permute-start(bf16[3,256,512]{2,1,0:T(8,128)(2,1)S(1)} %maximum_select_fusion.1), channel_id=1, source_target_pairs={{0,1},{1,0},{2,3},{3,2},{4,5},{5,4},{6,7},{7,6},{8,9},{9,8},{10,11... | collective-permute-start | bytes 2359304 | tf_op jit(solution)/shard_map/ppermute | solution.py:310
  84.5 3.9 collective-permute-start.23
  88.3 13.8 %project.1 = (bf16[2048,1024]{1,0:T(8,128)(2,1)}, bf16[1024,512]{1,0:T(8,128)(2,1)}, bf16[2048,512]{1,0:T(8,128)(2,1)}, bf16[2048,512]{1,0:T(8,128)(2,1)}, bf16[...) custom-call(bf16[512,1024]{1,0:T(8,128)(2,1)} %copy-done.13, ...), custom_call_target="tpu_custom_call" | custom-call | flops 1000 | bytes 1000 | tf_op jit(solution)/shard_map/project/pallas_call | solution.py:581
  106.3 1.6 copy-done.1
  107.9 1.6 copy-done.3
  110.7 6.0 %attend_forward.4 = (bf16[1024,128]{1,0:T(8,128)(2,1)S(1)}, f32[1,8,1024]{2,1,0:T(8,128)S(1)}) custom-call(s32[1]{0:T(128)} %bitcast.12.outer_ref, s32[9]{0:T(128)S(1)} %stack.162.sc_ref, bf16[1024,512]{1,0:T(8,128)(2,1)S(1)} %copy-done.5, bf16[2048,512]{1,0:T(8,128)(2,1)S(1)} %copy-done.1, bf16[2048,512]{1,0:T(8,128)(2,1)S(1)} %copy-done.3), custom_call_target="tpu_custom_call" | custom-call | flops 1000 | bytes 1000 | tf_op jit(solution)/shard_map/attend_forward/pallas_call | solution.py:439
  116.8 1.6 collective-permute-start.24
  119.1 6.6 %attend_forward.5 = (bf16[1024,128]{1,0:T(8,128)(2,1)S(1)}, f32[1,8,1024]{2,1,0:T(8,128)S(1)}) custom-call(s32[1]{0:T(128)} %bitcast.12.outer_ref, s32[9]{0:T(128)S(1)} %stack.162.sc_ref, bf16[1024,512]{1,0:T(8,128)(2,1)S(1)} %copy-done.5, bf16[2048,512]{1,0:T(8,128)(2,1)S(1)} %copy-done.1, bf16[2048,512]{1,0:T(8,128)(2,1)S(1)} %copy-done.3), custom_call_target="tpu_custom_call" | custom-call | flops 1000 | bytes 1000 | tf_op jit(solution)/shard_map/attend_forward/pallas_call | solution.py:439
  127.3 6.0 %attend_forward.6 = (bf16[1024,128]{1,0:T(8,128)(2,1)S(1)}, f32[1,8,1024]{2,1,0:T(8,128)S(1)}) custom-call(s32[1]{0:T(128)} %bitcast.12.outer_ref, s32[9]{0:T(128)S(1)} %stack.162.sc_ref, bf16[1024,512]{1,0:T(8,128)(2,1)S(1)} %copy-done.5, bf16[2048,512]{1,0:T(8,128)(2,1)S(1)} %copy-done.1, bf16[2048,512]{1,0:T(8,128)(2,1)S(1)} %copy-done.3), custom_call_target="tpu_custom_call" | custom-call | flops 1000 | bytes 1000 | tf_op jit(solution)/shard_map/attend_forward/pallas_call | solution.py:439
  133.4 1.8 collective-permute-done.24
  135.2 4.4 collective-permute-done.25
  139.7 1.8 collective-permute-start.29
  141.6 6.2 %attend_forward.7 = (bf16[1024,128]{1,0:T(8,128)(2,1)S(1)}, f32[1,8,1024]{2,1,0:T(8,128)S(1)}) custom-call(s32[1]{0:T(128)} %bitcast.12.outer_ref, s32[9]{0:T(128)S(1)} %stack.162.sc_ref, bf16[1024,512]{1,0:T(8,128)(2,1)S(1)} %copy-done.5, bf16[2048,512]{1,0:T(8,128)(2,1)S(1)} %copy-done.1, bf16[2048,512]{1,0:T(8,128)(2,1)S(1)} %copy-done.3), custom_call_target="tpu_custom_call" | custom-call | flops 1000 | bytes 1000 | tf_op jit(solution)/shard_map/attend_forward/pallas_call | solution.py:439
  149.5 5.3 %collective-permute-done.27 = bf16[3,256,512]{2,1,0:T(8,128)(2,1)S(1)} collective-permute-done((bf16[3,256,512]{2,1,0:T(8,128)(2,1)S(1)}, bf16[3,256,512]{2,1,0:T(8,128)(2,1)S(1)}, u32[]{:S(2)}, u32[]{:S(2)}) %collective-permute-start.27) | collective-permute-done | bytes 786464 | tf_op jit(solution)/shard_map/ppermute | solution.py:310
  155.9 17.2 %collective-permute-done.29.refs_4_.refs_2_.refs_9_.refs_15_ = bf16[2,3,256,512]{3,2,1,0:T(8,128)(2,1)S(1)} collective-permute-done((bf16[2,3,256,512]{3,2,1,0:T(8,128)(2,1)S(1)}, bf16[2,3,256,512]{3,2,1,0:T(8,128)(2,1)S(1)}, u32[]{:S(2)}, u32[]{:S(2)}) %collective-permute-start.29) | collective-permute-done | bytes 1572896 | tf_op jit(solution)/shard_map/ppermute | solution.py:310
  173.1 1.7 collective-permute-done.30
  177.6 1.5 collective-permute-start.34
  181.7 6.0 %feed_forward.4 = (bf16[1024,512]{1,0:T(8,128)(2,1)S(1)}, bf16[1024,512]{1,0:T(8,128)(2,1)S(1)}, bf16[1024,512]{1,0:T(8,128)(2,1)S(1)}, f32[1024,1024]{1,0:T(8,128)S(1)}) custom-call(bf16[1024,1024]{1,0:T(8,128)(2,1)S(1)} %pad_maximum_fusion.refs_0_, bf16[1,3,256,512]{3,2,1,0:T(8,128)(2,1)S(1)} %bitcast.144, ...), custom_call_target="tpu_custom_call" | custom-call | flops 1000 | bytes 1000 | tf_op jit(solution)/shard_map/feed_forward/pallas_call | solution.py:781
  188.8 6.6 %feed_forward.5 = (bf16[1024,512]{1,0:T(8,128)(2,1)S(1)}, bf16[1024,512]{1,0:T(8,128)(2,1)S(1)}, bf16[1024,512]{1,0:T(8,128)(2,1)S(1)}, f32[1024,1024]{1,0:T(8,128)S(1)}) custom-call(bf16[1024,1024]{1,0:T(8,128)(2,1)S(1)} %pad_maximum_fusion.refs_0_, bf16[1,3,256,512]{3,2,1,0:T(8,128)(2,1)} %bitcast.31.refs_1_.refs_12_, ...), custom_call_target="tpu_custom_call", output_to_operand_aliasing={{3}: (5, {})} | custom-call | flops 1000 | bytes 1000 | tf_op jit(solution)/shard_map/feed_forward/pallas_call | solution.py:781
  198.2 4.9 feed_forward.6
  206.0 8.0 %collective-permute-done.34.refs_2_.refs_4_.refs_13_.refs_15_ = bf16[2,3,256,512]{3,2,1,0:T(8,128)(2,1)S(1)} collective-permute-done((bf16[2,3,256,512]{3,2,1,0:T(8,128)(2,1)S(1)}, bf16[2,3,256,512]{3,2,1,0:T(8,128)(2,1)S(1)}, u32[]{:S(2)}, u32[]{:S(2)}) %collective-permute-start.34) | collective-permute-done | bytes 1572896 | tf_op jit(solution)/shard_map/ppermute | solution.py:310
  215.3 4.9 feed_forward.7
  220.2 1.8 slice.164
  227.6 4.6 fusion.21
  236.4 2.0 collective-permute-start.38
  238.4 22.6 %feed_backward.2 = (f32[1024,1024]{1,0:T(8,128)}, bf16[3,256,512]{2,1,0:T(8,128)(2,1)}, bf16[3,256,512]{2,1,0:T(8,128)(2,1)}, bf16[3,256,512]{2,1,0:T(8,128)(2,1...) custom-call(bf16[1024,1024]{1,0:T(8,128)(2,1)} %copy-done, ...), custom_call_target="tpu_custom_call" | custom-call | flops 1000 | bytes 1000 | tf_op jit(solution)/shard_map/feed_backward/pallas_call | solution.py:877
  262.1 1.6 collective-permute-start.40
  263.7 23.9 %feed_backward.3 = (f32[512,1024]{1,0:T(8,128)}, bf16[512,1024]{1,0:T(8,128)(2,1)}, bf16[3,256,512]{2,1,0:T(8,128)(2,1)}, bf16[3,256,512]{2,1,0:T(8,128)(2,1)}, ...) custom-call(bf16[1024,1024]{1,0:T(8,128)(2,1)} %copy-done, ...), custom_call_target="tpu_custom_call" | custom-call | flops 1000 | bytes 1000 | tf_op jit(solution)/shard_map/feed_backward/pallas_call | solution.py:877
  287.7 2.4 fusion.4
  294.8 1.8 norm_grads.2
  303.7 16.4 %shard_map.135 = (bf16[1024,256]{1,0:T(8,128)(2,1)S(1)}, bf16[2048,256]{1,0:T(8,128)(2,1)S(1)}, bf16[2048,256]{1,0:T(8,128)(2,1)S(1)}) custom-call(s32[9]{0:T(128)S(1)} %stack.162.sc_ref, bf16[1024,512]{1,0:T(8,128)(2,1)S(1)} %copy-done.6, bf16[2048,512]{1,0:T(8,128)(2,1)S(1)} %copy-done.2, bf16[2048,512]{1,0:T(8,128)(2,1)S(1)} %copy-done.4, ...), custom_call_target="tpu_custom_call" | custom-call | flops 1000 | bytes 1000 | tf_op jit(solution)/shard_map/pallas_call | solution.py:519
  322.6 16.8 %shard_map.136 = (bf16[1024,256]{1,0:T(8,128)(2,1)S(1)}, bf16[2048,256]{1,0:T(8,128)(2,1)S(1)}, bf16[2048,256]{1,0:T(8,128)(2,1)S(1)}) custom-call(s32[9]{0:T(128)S(1)} %stack.162.sc_ref, bf16[1024,512]{1,0:T(8,128)(2,1)S(1)} %copy-done.6, bf16[2048,512]{1,0:T(8,128)(2,1)S(1)} %copy-done.2, bf16[2048,512]{1,0:T(8,128)(2,1)S(1)} %copy-done.4, ...), custom_call_target="tpu_custom_call" | custom-call | flops 1000 | bytes 1000 | tf_op jit(solution)/shard_map/pallas_call | solution.py:519
  339.6 12.5 %collective-permute-done.47 = bf16[3,256,512]{2,1,0:T(8,128)(2,1)S(1)} collective-permute-done((bf16[3,256,512]{2,1,0:T(8,128)(2,1)S(1)}, bf16[3,256,512]{2,1,0:T(8,128)(2,1)S(1)}, u32[]{:S(2)}, u32[]{:S(2)}) %collective-permute-start.47) | collective-permute-done | bytes 786464 | tf_op jit(solution)/shard_map/ppermute | solution.py:310
  360.0 8.1 %rows_grads.1 = (f32[512,1024]{1,0:T(8,128)S(1)}, bf16[512,1024]{1,0:T(8,128)(2,1)S(1)}, f32[512,1024]{1,0:T(8,128)S(1)}, bf16[512,1024]{1,0:T(8,128)(2,1)S(1)}) custom-call(bf16[1024,512]{1,0:T(8,128)(2,1)S(1)} %pad_maximum_fusion.11.dq_ref, bf16[2048,512]{1,0:T(8,128)(2,1)S(1)} %constant_dynamic-update-slice_fusion.7.dk_ref, bf16[2048,512]{1,0:T(8,128)(2,1)} %copy-done.11, ...), custom_call_target="tpu_custom_call" | custom-call | flops 1000 | bytes 1000 | tf_op jit(solution)/shard_map/rows_grads/pallas_call | solution.py:637
  374.6 9.7 %attention_grads.1 = (bf16[256,1024]{1,0:T(8,128)(2,1)S(1)}, bf16[256,1024]{1,0:T(8,128)(2,1)S(1)}, bf16[256,1024]{1,0:T(8,128)(2,1)S(1)}, bf16[256,1024]{1,0:T(...) custom-call(bf16[2048,1024]{1,0:T(8,128)(2,1)} %get-tuple-element.35, ...), custom_call_target="tpu_custom_call" | custom-call | flops 1000 | bytes 1000 | tf_op jit(solution)/shard_map/attention_grads/pallas_call | solution.py:675
  392.8 2.0 collective-permute-start.55
  394.8 2.5 broadcast_select_fusion
  397.3 8.1 %collective-permute-done.52 = bf16[2,3,256,512]{3,2,1,0:T(8,128)(2,1)} collective-permute-done((bf16[2,3,256,512]{3,2,1,0:T(8,128)(2,1)}, bf16[2,3,256,512]{3,2,1,0:T(8,128)(2,1)}, u32[]{:S(2)}, u32[]{:S(2)}) %collective-permute-start.52) | collective-permute-done | bytes 1572896 | tf_op jit(solution)/shard_map/ppermute | solution.py:310
  408.2 2.6 convert_add_fusion.2
  411.2 19.9 %collective-permute-done.51.refs_2_ = bf16[512,1024]{1,0:T(8,128)(2,1)} collective-permute-done((bf16[512,1024]{1,0:T(8,128)(2,1)}, bf16[512,1024]{1,0:T(8,128)(2,1)}, u32[]{:S(2)}, u32[]{:S(2)}) %collective-permute-start.51) | collective-permute-done | bytes 1048608 | tf_op jit(solution)/shard_map/ppermute | solution.py:310
  431.1 4.4 norm_grads.3
  441.2 5.2 %collective-permute-done.62 = bf16[3,256,512]{2,1,0:T(8,128)(2,1)S(1)} collective-permute-done((bf16[3,256,512]{2,1,0:T(8,128)(2,1)S(1)}, bf16[3,256,512]{2,1,0:T(8,128)(2,1)S(1)}, u32[]{:S(2)}, u32[]{:S(2)}) %collective-permute-start.62) | collective-permute-done | bytes 786464 | tf_op jit(solution)/shard_map/ppermute | solution.py:310
  448.1 12.5 %collective-permute-done.61 = f32[2,512]{1,0:T(2,128)S(1)} collective-permute-done((f32[2,512]{1,0:T(2,128)S(1)}, f32[2,512]{1,0:T(2,128)S(1)}, u32[]{:S(2)}, u32[]{:S(2)}) %collective-permute-start.61) | collective-permute-done | bytes 4128 | tf_op jit(solution)/shard_map/ppermute | solution.py:310
  465.3 1.6 select_convert_fusion
  466.9 2.5 collective-permute-done.64
  469.4 4.4 collective-permute-start.69
  475.2 2.0 collective-permute-start.72
  477.5 2.1 collective-permute-start.70
  480.4 1.8 copy.19
  482.9 5.6 %collective-permute-done.71 = f32[2,32]{1,0:T(2,128)S(1)} collective-permute-done((f32[2,32]{1,0:T(2,128)S(1)}, f32[2,32]{1,0:T(2,128)S(1)}, u32[]{:S(2)}, u32[]{:S(2)}) %collective-permute-start.71) | collective-permute-done | bytes 288 | tf_op jit(solution)/shard_map/ppermute | solution.py:310
  (419 shorter events, 109.1 us)
Async XLA Ops:
  0.6 4.7 collective-permute-start.1
  2.3 7.2 %collective-permute-start.5 = (bf16[4,128,128]{2,1,0:T(8,128)(2,1)S(1)}, bf16[4,128,128]{2,1,0:T(8,128)(2,1)S(1)}, u32[]{:S(2)}, u32[]{:S(2)}) collective-permute-start(bf16[4,128,128]{2,1,0:T(8,128)(2,1)S(1)} %get-tuple-element.464), channel_id=1, source_target_pairs={{0,4},{1,5},{2,6},{3,7},{4,0},{5,1},{6,2},{7,3},{8,12},{9,13},{10,... | collective-permute-start | bytes 393224 | tf_op jit(solution)/shard_map/ppermute | solution.py:310
  4.8 4.8 collective-permute-start.6
  5.4 4.6 collective-permute-start.2
  8.0 3.6 collective-permute-start.3
  9.5 4.6 collective-permute-start.4
  14.1 12.5 %collective-permute-start.8 = (bf16[256,512]{1,0:T(8,128)(2,1)S(1)}, bf16[256,512]{1,0:T(8,128)(2,1)S(1)}, u32[]{:S(2)}, u32[]{:S(2)}) collective-permute-start(bf16[256,512]{1,0:T(8,128)(2,1)S(1)} %pad_maximum_fusion.21), channel_id=1, source_target_pairs={{0,1},{1,0},{2,3},{3,2},{4,5},{5,4},{6,7},{7,6},{8,9},{9,8},{10,11... | collective-permute-start | bytes 786440 | tf_op jit(solution)/shard_map/ppermute | solution.py:310
  15.6 13.4 %collective-permute-start.7 = (bf16[256,512]{1,0:T(8,128)(2,1)S(1)}, bf16[256,512]{1,0:T(8,128)(2,1)S(1)}, u32[]{:S(2)}, u32[]{:S(2)}) collective-permute-start(bf16[256,512]{1,0:T(8,128)(2,1)S(1)} %pad_maximum_fusion.21), channel_id=1, source_target_pairs={{0,2},{1,3},{2,0},{3,1},{4,6},{5,7},{6,4},{7,5},{8,10},{9,11},{10,... | collective-permute-start | bytes 786440 | tf_op jit(solution)/shard_map/ppermute | solution.py:310
  29.0 6.6 %collective-permute-start.9 = (bf16[256,512]{1,0:T(8,128)(2,1)S(1)}, bf16[256,512]{1,0:T(8,128)(2,1)S(1)}, u32[]{:S(2)}, u32[]{:S(2)}) collective-permute-start(bf16[256,512]{1,0:T(8,128)(2,1)S(1)} %collective-permute-done.7), channel_id=1, source_target_pairs={{0,1},{1,0},{2,3},{3,2},{4,5},{5,4},{6,7},{7,6},{8,9},{9,8},{10,11... | collective-permute-start | bytes 786440 | tf_op jit(solution)/shard_map/ppermute | solution.py:310
  29.5 20.5 %collective-permute-start = (bf16[512,1024]{1,0:T(8,128)(2,1)S(1)}, bf16[512,1024]{1,0:T(8,128)(2,1)S(1)}, u32[]{:S(2)}, u32[]{:S(2)}) collective-permute-start(bf16[512,1024]{1,0:T(8,128)(2,1)S(1)} %pad_maximum_fusion.8), channel_id=1, source_target_pairs={{0,0},{1,1},{2,5},{3,4},{4,3},{5,2},{6,6},{7,7},{8,8},{9,9},{10,13... | collective-permute-start | bytes 3145736 | tf_op jit(solution)/shard_map/ppermute | solution.py:310
  30.4 28.0 %collective-permute-start.13 = (bf16[512,1024]{1,0:T(8,128)(2,1)S(1)}, bf16[512,1024]{1,0:T(8,128)(2,1)}, u32[]{:S(2)}, u32[]{:S(2)}) collective-permute-start(bf16[512,1024]{1,0:T(8,128)(2,1)S(1)} %pad_maximum_fusion.8), channel_id=1, source_target_pairs={{0,1},{1,0},{2,4},{4,2},{5,3},{6,7},{8,9},{9,8},{10,12},{12,10},{1... | collective-permute-start | bytes 3145736 | tf_op jit(solution)/shard_map/ppermute | solution.py:310
  35.0 13.5 %collective-permute-start.11 = (bf16[2,256,512]{2,1,0:T(8,128)(2,1)S(1)}, bf16[2,256,512]{2,1,0:T(8,128)(2,1)S(1)}, u32[]{:S(2)}, u32[]{:S(2)}) collective-permute-start(bf16[2,256,512]{2,1,0:T(8,128)(2,1)S(1)} %pad_maximum_fusion.16.refs_5_), channel_id=1, source_target_pairs={{0,8},{1,9},{2,10},{3,11},{4,12},{5,13},{6,14},{7,15},{8,0},{9,1},... | collective-permute-start | bytes 1572872 | tf_op jit(solution)/shard_map/ppermute | solution.py:310
  35.7 13.8 %collective-permute-start.10 = (bf16[2,256,512]{2,1,0:T(8,128)(2,1)S(1)}, bf16[2,256,512]{2,1,0:T(8,128)(2,1)S(1)}, u32[]{:S(2)}, u32[]{:S(2)}) collective-permute-start(bf16[2,256,512]{2,1,0:T(8,128)(2,1)S(1)} %pad_maximum_fusion.15.refs_9_), channel_id=1, source_target_pairs={{0,16},{1,17},{2,18},{3,19},{4,20},{5,21},{6,22},{7,23},{8,24},{9,... | collective-permute-start | bytes 1572872 | tf_op jit(solution)/shard_map/ppermute | solution.py:310
  36.2 33.2 %collective-permute-start.15 = (bf16[2,256,512]{2,1,0:T(8,128)(2,1)S(1)}, bf16[2,256,512]{2,1,0:T(8,128)(2,1)S(1)}, u32[]{:S(2)}, u32[]{:S(2)}) collective-permute-start(bf16[2,256,512]{2,1,0:T(8,128)(2,1)S(1)} %pad_maximum_fusion.16.refs_5_), channel_id=1, source_target_pairs={{0,16},{1,17},{2,18},{3,19},{4,20},{5,21},{6,22},{7,23},{8,24},{9,... | collective-permute-start | bytes 1572872 | tf_op jit(solution)/shard_map/ppermute | solution.py:310
  48.5 21.0 %collective-permute-start.16 = (bf16[2,256,512]{2,1,0:T(8,128)(2,1)S(1)}, bf16[2,256,512]{2,1,0:T(8,128)(2,1)S(1)}, u32[]{:S(2)}, u32[]{:S(2)}) collective-permute-start(bf16[2,256,512]{2,1,0:T(8,128)(2,1)S(1)} %pad_maximum_fusion.15.refs_9_), channel_id=1, source_target_pairs={{0,8},{1,9},{2,10},{3,11},{4,12},{5,13},{6,14},{7,15},{8,0},{9,1},... | collective-permute-start | bytes 1572872 | tf_op jit(solution)/shard_map/ppermute | solution.py:310
  49.5 22.5 %collective-permute-start.17 = (bf16[2,256,512]{2,1,0:T(8,128)(2,1)S(1)}, bf16[2,256,512]{2,1,0:T(8,128)(2,1)S(1)}, u32[]{:S(2)}, u32[]{:S(2)}) collective-permute-start(bf16[2,256,512]{2,1,0:T(8,128)(2,1)S(1)} %collective-permute-done.11.refs_6_), channel_id=1, source_target_pairs={{0,16},{1,17},{2,18},{3,19},{4,20},{5,21},{6,22},{7,23},{8,24},{9,... | collective-permute-start | bytes 1572872 | tf_op jit(solution)/shard_map/ppermute | solution.py:310
  50.0 24.0 %collective-permute-start.18 = (bf16[2,256,512]{2,1,0:T(8,128)(2,1)S(1)}, bf16[2,256,512]{2,1,0:T(8,128)(2,1)S(1)}, u32[]{:S(2)}, u32[]{:S(2)}) collective-permute-start(bf16[2,256,512]{2,1,0:T(8,128)(2,1)S(1)} %collective-permute-done.10.refs_11_), channel_id=1, source_target_pairs={{0,8},{1,9},{2,10},{3,11},{4,12},{5,13},{6,14},{7,15},{8,0},{9,1},... | collective-permute-start | bytes 1572872 | tf_op jit(solution)/shard_map/ppermute | solution.py:310
  58.4 26.1 %collective-permute-start.12 = (bf16[512,1024]{1,0:T(8,128)(2,1)S(1)}, bf16[512,1024]{1,0:T(8,128)(2,1)}, u32[]{:S(2)}, u32[]{:S(2)}) collective-permute-start(bf16[512,1024]{1,0:T(8,128)(2,1)S(1)} %collective-permute-done.refs_0_.refs_3_), channel_id=1, source_target_pairs={{0,4},{1,5},{2,6},{3,7},{4,0},{5,1},{6,2},{7,3},{8,12},{9,13},{10,... | collective-permute-start | bytes 3145736 | tf_op jit(solution)/shard_map/ppermute | solution.py:310
  69.5 15.0 %collective-permute-start.14 = (bf16[512,1024]{1,0:T(8,128)(2,1)}, bf16[512,1024]{1,0:T(8,128)(2,1)}, u32[]{:S(2)}, u32[]{:S(2)}) collective-permute-start(bf16[512,1024]{1,0:T(8,128)(2,1)} %collective-permute-done.13.refs_2_), channel_id=1, source_target_pairs={{0,4},{1,5},{2,6},{3,7},{4,0},{5,1},{6,2},{7,3},{8,12},{9,13},{10,... | collective-permute-start | bytes 3145736 | tf_op jit(solution)/shard_map/ppermute | solution.py:310
  69.5 32.6 %collective-permute-start.19 = (bf16[3,256,512]{2,1,0:T(8,128)(2,1)S(1)}, bf16[3,256,512]{2,1,0:T(8,128)(2,1)}, u32[]{:S(2)}, u32[]{:S(2)}) collective-permute-start(bf16[3,256,512]{2,1,0:T(8,128)(2,1)S(1)} %maximum_select_fusion.1), channel_id=1, source_target_pairs={{0,8},{1,9},{2,10},{3,11},{4,12},{5,13},{6,14},{7,15},{8,0},{9,1},... | collective-permute-start | bytes 2359304 | tf_op jit(solution)/shard_map/ppermute | solution.py:310
  71.9 30.2 %collective-permute-start.20 = (bf16[3,256,512]{2,1,0:T(8,128)(2,1)S(1)}, bf16[3,256,512]{2,1,0:T(8,128)(2,1)}, u32[]{:S(2)}, u32[]{:S(2)}) collective-permute-start(bf16[3,256,512]{2,1,0:T(8,128)(2,1)S(1)} %maximum_select_fusion.1), channel_id=1, source_target_pairs={{0,16},{1,17},{2,18},{3,19},{4,20},{5,21},{6,22},{7,23},{8,24},{9,... | collective-permute-start | bytes 2359304 | tf_op jit(solution)/shard_map/ppermute | solution.py:310
  74.7 42.0 %collective-permute-start.21 = (bf16[3,256,512]{2,1,0:T(8,128)(2,1)S(1)}, bf16[3,256,512]{2,1,0:T(8,128)(2,1)}, u32[]{:S(2)}, u32[]{:S(2)}) collective-permute-start(bf16[3,256,512]{2,1,0:T(8,128)(2,1)S(1)} %maximum_select_fusion.1), channel_id=1, source_target_pairs={{0,1},{1,0},{2,3},{3,2},{4,5},{5,4},{6,7},{7,6},{8,9},{9,8},{10,11... | collective-permute-start | bytes 2359304 | tf_op jit(solution)/shard_map/ppermute | solution.py:310
  84.5 41.3 %collective-permute-start.23 = (bf16[3,256,512]{2,1,0:T(8,128)(2,1)S(1)}, bf16[3,256,512]{2,1,0:T(8,128)(2,1)S(1)}, u32[]{:S(2)}, u32[]{:S(2)}) collective-permute-start(bf16[3,256,512]{2,1,0:T(8,128)(2,1)S(1)} %maximum_select_fusion.1), channel_id=1, source_target_pairs={{0,2},{1,3},{2,0},{3,1},{4,6},{5,7},{6,4},{7,5},{8,10},{9,11},{10,... | collective-permute-start | bytes 2359304 | tf_op jit(solution)/shard_map/ppermute | solution.py:310
  102.2 23.6 %collective-permute-start.22 = (bf16[3,256,512]{2,1,0:T(8,128)(2,1)}, bf16[3,256,512]{2,1,0:T(8,128)(2,1)S(1)}, u32[]{:S(2)}, u32[]{:S(2)}) collective-permute-start(bf16[3,256,512]{2,1,0:T(8,128)(2,1)} %collective-permute-done.19), channel_id=1, source_target_pairs={{0,16},{1,17},{2,18},{3,19},{4,20},{5,21},{6,22},{7,23},{8,24},{9,... | collective-permute-start | bytes 2359304 | tf_op jit(solution)/shard_map/ppermute | solution.py:310
  116.8 18.4 %collective-permute-start.24 = (bf16[3,256,512]{2,1,0:T(8,128)(2,1)}, bf16[3,256,512]{2,1,0:T(8,128)(2,1)S(1)}, u32[]{:S(2)}, u32[]{:S(2)}) collective-permute-start(bf16[3,256,512]{2,1,0:T(8,128)(2,1)} %collective-permute-done.21), channel_id=1, source_target_pairs={{0,8},{1,9},{2,10},{3,11},{4,12},{5,13},{6,14},{7,15},{8,0},{9,1},... | collective-permute-start | bytes 2359304 | tf_op jit(solution)/shard_map/ppermute | solution.py:310
  118.3 21.2 %collective-permute-start.25 = (bf16[3,256,512]{2,1,0:T(8,128)(2,1)}, bf16[3,256,512]{2,1,0:T(8,128)(2,1)S(1)}, u32[]{:S(2)}, u32[]{:S(2)}) collective-permute-start(bf16[3,256,512]{2,1,0:T(8,128)(2,1)} %collective-permute-done.21), channel_id=1, source_target_pairs={{0,16},{1,17},{2,18},{3,19},{4,20},{5,21},{6,22},{7,23},{8,24},{9,... | collective-permute-start | bytes 2359304 | tf_op jit(solution)/shard_map/ppermute | solution.py:310
  125.8 23.7 %collective-permute-start.26 = (bf16[3,256,512]{2,1,0:T(8,128)(2,1)S(1)}, bf16[3,256,512]{2,1,0:T(8,128)(2,1)S(1)}, u32[]{:S(2)}, u32[]{:S(2)}) collective-permute-start(bf16[3,256,512]{2,1,0:T(8,128)(2,1)S(1)} %collective-permute-done.23), channel_id=1, source_target_pairs={{0,1},{1,0},{2,3},{3,2},{4,5},{5,4},{6,7},{7,6},{8,9},{9,8},{10,11... | collective-permute-start | bytes 2359304 | tf_op jit(solution)/shard_map/ppermute | solution.py:310
  125.9 29.0 %collective-permute-start.27 = (bf16[3,256,512]{2,1,0:T(8,128)(2,1)S(1)}, bf16[3,256,512]{2,1,0:T(8,128)(2,1)S(1)}, u32[]{:S(2)}, u32[]{:S(2)}) collective-permute-start(bf16[3,256,512]{2,1,0:T(8,128)(2,1)S(1)} %collective-permute-done.23), channel_id=1, source_target_pairs={{0,16},{1,17},{2,18},{3,19},{4,20},{5,21},{6,22},{7,23},{8,24},{9,... | collective-permute-start | bytes 2359304 | tf_op jit(solution)/shard_map/ppermute | solution.py:310
  139.7 33.4 %collective-permute-start.29 = (bf16[2,3,256,512]{3,2,1,0:T(8,128)(2,1)S(1)}, bf16[2,3,256,512]{3,2,1,0:T(8,128)(2,1)S(1)}, u32[]{:S(2)}, u32[]{:S(2)}) collective-permute-start(bf16[2,3,256,512]{3,2,1,0:T(8,128)(2,1)S(1)} %pad_maximum_fusion.2), channel_id=1, source_target_pairs={{0,8},{1,9},{2,10},{3,11},{4,12},{5,13},{6,14},{7,15},{8,0},{9,1},... | collective-permute-start | bytes 4718600 | tf_op jit(solution)/shard_map/ppermute | solution.py:310
  154.9 20.0 %collective-permute-start.28 = (bf16[512,1024]{1,0:T(8,128)(2,1)S(1)}, bf16[512,1024]{1,0:T(8,128)(2,1)S(1)}, u32[]{:S(2)}, u32[]{:S(2)}) collective-permute-start(bf16[512,1024]{1,0:T(8,128)(2,1)S(1)} %slice.259), channel_id=1, source_target_pairs={{0,4},{1,5},{2,6},{3,7},{4,0},{5,1},{6,2},{7,3},{8,12},{9,13},{10,... | collective-permute-start | bytes 3145736 | tf_op jit(solution)/shard_map/ppermute | solution.py:310
  154.9 20.0 %collective-permute-start.30 = (bf16[3,256,512]{2,1,0:T(8,128)(2,1)S(1)}, bf16[3,256,512]{2,1,0:T(8,128)(2,1)S(1)}, u32[]{:S(2)}, u32[]{:S(2)}) collective-permute-start(bf16[3,256,512]{2,1,0:T(8,128)(2,1)S(1)} %collective-permute-done.26), channel_id=1, source_target_pairs={{0,16},{1,17},{2,18},{3,19},{4,20},{5,21},{6,22},{7,23},{8,24},{9,... | collective-permute-start | bytes 2359304 | tf_op jit(solution)/shard_map/ppermute | solution.py:310
  175.6 20.9 %collective-permute-start.33 = (bf16[3,256,512]{2,1,0:T(8,128)(2,1)S(1)}, bf16[3,256,512]{2,1,0:T(8,128)(2,1)S(1)}, u32[]{:S(2)}, u32[]{:S(2)}) collective-permute-start(bf16[3,256,512]{2,1,0:T(8,128)(2,1)S(1)} %slice_bitcast_fusion.1), channel_id=1, source_target_pairs={{0,16},{1,17},{2,18},{3,19},{4,20},{5,21},{6,22},{7,23},{8,24},{9,... | collective-permute-start | bytes 2359304 | tf_op jit(solution)/shard_map/ppermute | solution.py:310
  177.6 36.4 %collective-permute-start.34 = (bf16[2,3,256,512]{3,2,1,0:T(8,128)(2,1)S(1)}, bf16[2,3,256,512]{3,2,1,0:T(8,128)(2,1)S(1)}, u32[]{:S(2)}, u32[]{:S(2)}) collective-permute-start(bf16[2,3,256,512]{3,2,1,0:T(8,128)(2,1)S(1)} %pad_maximum_fusion.3), channel_id=1, source_target_pairs={{0,8},{1,9},{2,10},{3,11},{4,12},{5,13},{6,14},{7,15},{8,0},{9,1},... | collective-permute-start | bytes 4718600 | tf_op jit(solution)/shard_map/ppermute | solution.py:310
  196.5 27.2 %collective-permute-start.35 = (bf16[512,1024]{1,0:T(8,128)(2,1)S(1)}, bf16[512,1024]{1,0:T(8,128)(2,1)S(1)}, u32[]{:S(2)}, u32[]{:S(2)}) collective-permute-start(bf16[512,1024]{1,0:T(8,128)(2,1)S(1)} %pad_maximum_fusion.9), channel_id=1, source_target_pairs={{2,5},{3,4},{4,3},{5,2},{10,13},{11,12},{12,11},{13,10},{18,21},{1... | collective-permute-start | bytes 3145736 | tf_op jit(solution)/shard_map/ppermute | solution.py:310
  236.4 51.3 %collective-permute-start.38 = (bf16[512,1024]{1,0:T(8,128)(2,1)}, bf16[512,1024]{1,0:T(8,128)(2,1)}, u32[]{:S(2)}, u32[]{:S(2)}) collective-permute-start(bf16[512,1024]{1,0:T(8,128)(2,1)} %pad_maximum_fusion.10), channel_id=1, source_target_pairs={{2,5},{3,4},{4,3},{5,2},{10,13},{11,12},{12,11},{13,10},{18,21},{1... | collective-permute-start | bytes 3145736 | tf_op jit(solution)/shard_map/ppermute | solution.py:310
  261.0 26.6 %collective-permute-start.39 = (bf16[3,256,512]{2,1,0:T(8,128)(2,1)}, bf16[3,256,512]{2,1,0:T(8,128)(2,1)}, u32[]{:S(2)}, u32[]{:S(2)}) collective-permute-start(bf16[3,256,512]{2,1,0:T(8,128)(2,1)} %get-tuple-element.291), channel_id=1, source_target_pairs={{0,16},{1,17},{2,18},{3,19},{4,20},{5,21},{6,22},{7,23},{8,24},{9,... | collective-permute-start | bytes 2359304 | tf_op jit(solution)/shard_map/ppermute | solution.py:310
  262.1 25.6 %collective-permute-start.40 = (bf16[3,256,512]{2,1,0:T(8,128)(2,1)}, bf16[3,256,512]{2,1,0:T(8,128)(2,1)}, u32[]{:S(2)}, u32[]{:S(2)}) collective-permute-start(bf16[3,256,512]{2,1,0:T(8,128)(2,1)} %get-tuple-element.292), channel_id=1, source_target_pairs={{0,8},{1,9},{2,10},{3,11},{4,12},{5,13},{6,14},{7,15},{8,0},{9,1},... | collective-permute-start | bytes 2359304 | tf_op jit(solution)/shard_map/ppermute | solution.py:310
  296.8 3.2 collective-permute-start.43
  298.2 41.4 %collective-permute-start.45 = (bf16[2,3,256,512]{3,2,1,0:T(8,128)(2,1)S(1)}, bf16[2,3,256,512]{3,2,1,0:T(8,128)(2,1)S(1)}, u32[]{:S(2)}, u32[]{:S(2)}) collective-permute-start(bf16[2,3,256,512]{3,2,1,0:T(8,128)(2,1)S(1)} %pad_maximum_fusion.4), channel_id=1, source_target_pairs={{0,8},{1,9},{2,10},{3,11},{4,12},{5,13},{6,14},{7,15},{8,0},{9,1},... | collective-permute-start | bytes 4718600 | tf_op jit(solution)/shard_map/ppermute | solution.py:310
  298.9 40.7 %collective-permute-start.46 = (bf16[2,3,256,512]{3,2,1,0:T(8,128)(2,1)S(1)}, bf16[2,3,256,512]{3,2,1,0:T(8,128)(2,1)S(1)}, u32[]{:S(2)}, u32[]{:S(2)}) collective-permute-start(bf16[2,3,256,512]{3,2,1,0:T(8,128)(2,1)S(1)} %pad_maximum_fusion.5), channel_id=1, source_target_pairs={{0,16},{1,17},{2,18},{3,19},{4,20},{5,21},{6,22},{7,23},{8,24},{9,... | collective-permute-start | bytes 4718600 | tf_op jit(solution)/shard_map/ppermute | solution.py:310
  320.1 32.0 %collective-permute-start.47 = (bf16[3,256,512]{2,1,0:T(8,128)(2,1)S(1)}, bf16[3,256,512]{2,1,0:T(8,128)(2,1)S(1)}, u32[]{:S(2)}, u32[]{:S(2)}) collective-permute-start(bf16[3,256,512]{2,1,0:T(8,128)(2,1)S(1)} %copy-done.103), channel_id=1, source_target_pairs={{0,16},{1,17},{2,18},{3,19},{4,20},{5,21},{6,22},{7,23},{8,24},{9,... | collective-permute-start | bytes 2359304 | tf_op jit(solution)/shard_map/ppermute | solution.py:310
  321.1 31.0 %collective-permute-start.48 = (bf16[3,256,512]{2,1,0:T(8,128)(2,1)S(1)}, bf16[3,256,512]{2,1,0:T(8,128)(2,1)S(1)}, u32[]{:S(2)}, u32[]{:S(2)}) collective-permute-start(bf16[3,256,512]{2,1,0:T(8,128)(2,1)S(1)} %copy-done.102), channel_id=1, source_target_pairs={{0,8},{1,9},{2,10},{3,11},{4,12},{5,13},{6,14},{7,15},{8,0},{9,1},... | collective-permute-start | bytes 2359304 | tf_op jit(solution)/shard_map/ppermute | solution.py:310
  368.2 4.1 collective-permute-start.50
  368.7 36.7 %collective-permute-start.52 = (bf16[2,3,256,512]{3,2,1,0:T(8,128)(2,1)}, bf16[2,3,256,512]{3,2,1,0:T(8,128)(2,1)}, u32[]{:S(2)}, u32[]{:S(2)}) collective-permute-start(bf16[2,3,256,512]{3,2,1,0:T(8,128)(2,1)} %pad_maximum_fusion.6), channel_id=1, source_target_pairs={{0,8},{1,9},{2,10},{3,11},{4,12},{5,13},{6,14},{7,15},{8,0},{9,1},... | collective-permute-start | bytes 4718600 | tf_op jit(solution)/shard_map/ppermute | solution.py:310
  370.1 36.4 %collective-permute-start.53 = (bf16[2,3,256,512]{3,2,1,0:T(8,128)(2,1)}, bf16[2,3,256,512]{3,2,1,0:T(8,128)(2,1)}, u32[]{:S(2)}, u32[]{:S(2)}) collective-permute-start(bf16[2,3,256,512]{3,2,1,0:T(8,128)(2,1)} %pad_maximum_fusion.7), channel_id=1, source_target_pairs={{0,16},{1,17},{2,18},{3,19},{4,20},{5,21},{6,22},{7,23},{8,24},{9,... | collective-permute-start | bytes 4718600 | tf_op jit(solution)/shard_map/ppermute | solution.py:310
  371.2 20.5 %collective-permute-start.54 = (bf16[3,256,512]{2,1,0:T(8,128)(2,1)S(1)}, bf16[3,256,512]{2,1,0:T(8,128)(2,1)S(1)}, u32[]{:S(2)}, u32[]{:S(2)}) collective-permute-start(bf16[3,256,512]{2,1,0:T(8,128)(2,1)S(1)} %get-tuple-element.350), channel_id=1, source_target_pairs={{0,1},{1,0},{2,3},{3,2},{4,5},{5,4},{6,7},{7,6},{8,9},{9,8},{10,11... | collective-permute-start | bytes 2359304 | tf_op jit(solution)/shard_map/ppermute | solution.py:310
  373.7 57.4 %collective-permute-start.51 = (bf16[512,1024]{1,0:T(8,128)(2,1)}, bf16[512,1024]{1,0:T(8,128)(2,1)}, u32[]{:S(2)}, u32[]{:S(2)}) collective-permute-start(bf16[512,1024]{1,0:T(8,128)(2,1)} %add_convert_fusion), channel_id=1, source_target_pairs={{0,1},{1,0},{2,3},{3,2},{4,5},{5,4},{6,7},{7,6},{8,9},{9,8},{10,11... | collective-permute-start | bytes 3145736 | tf_op jit(solution)/shard_map/ppermute | solution.py:310
  392.8 42.7 %collective-permute-start.55 = (bf16[3,256,512]{2,1,0:T(8,128)(2,1)}, bf16[3,256,512]{2,1,0:T(8,128)(2,1)}, u32[]{:S(2)}, u32[]{:S(2)}) collective-permute-start(bf16[3,256,512]{2,1,0:T(8,128)(2,1)} %add_convert_fusion.1), channel_id=1, source_target_pairs={{0,2},{1,3},{2,0},{3,1},{4,6},{5,7},{6,4},{7,5},{8,10},{9,11},{10,... | collective-permute-start | bytes 2359304 | tf_op jit(solution)/shard_map/ppermute | solution.py:310
  406.5 30.1 %collective-permute-start.57 = (bf16[256,1024]{1,0:T(8,128)(2,1)S(1)}, bf16[256,1024]{1,0:T(8,128)(2,1)S(1)}, u32[]{:S(2)}, u32[]{:S(2)}) collective-permute-start(bf16[256,1024]{1,0:T(8,128)(2,1)S(1)} %copy-done.72), channel_id=1, source_target_pairs={{0,16},{1,17},{2,18},{3,19},{4,20},{5,21},{6,22},{7,23},{8,24},{9,... | collective-permute-start | bytes 1572872 | tf_op jit(solution)/shard_map/ppermute | solution.py:310
  407.6 29.0 %collective-permute-start.58 = (bf16[256,1024]{1,0:T(8,128)(2,1)S(1)}, bf16[256,1024]{1,0:T(8,128)(2,1)S(1)}, u32[]{:S(2)}, u32[]{:S(2)}) collective-permute-start(bf16[256,1024]{1,0:T(8,128)(2,1)S(1)} %copy-done.70), channel_id=1, source_target_pairs={{0,8},{1,9},{2,10},{3,11},{4,12},{5,13},{6,14},{7,15},{8,0},{9,1},... | collective-permute-start | bytes 1572872 | tf_op jit(solution)/shard_map/ppermute | solution.py:310
  410.9 35.5 %collective-permute-start.62 = (bf16[3,256,512]{2,1,0:T(8,128)(2,1)S(1)}, bf16[3,256,512]{2,1,0:T(8,128)(2,1)S(1)}, u32[]{:S(2)}, u32[]{:S(2)}) collective-permute-start(bf16[3,256,512]{2,1,0:T(8,128)(2,1)S(1)} %get-tuple-element.378), channel_id=1, source_target_pairs={{0,1},{1,0},{2,3},{3,2},{4,5},{5,4},{6,7},{7,6},{8,9},{9,8},{10,11... | collective-permute-start | bytes 2359304 | tf_op jit(solution)/shard_map/ppermute | solution.py:310
  435.8 29.5 %collective-permute-start.56 = (bf16[512,1024]{1,0:T(8,128)(2,1)S(1)}, bf16[512,1024]{1,0:T(8,128)(2,1)S(1)}, u32[]{:S(2)}, u32[]{:S(2)}) collective-permute-start(bf16[512,1024]{1,0:T(8,128)(2,1)S(1)} %pad_maximum_fusion.12), channel_id=1, source_target_pairs={{2,5},{3,4},{4,3},{5,2},{10,13},{11,12},{12,11},{13,10},{18,21},{1... | collective-permute-start | bytes 3145736 | tf_op jit(solution)/shard_map/ppermute | solution.py:310
  438.0 22.6 %collective-permute-start.59 = (bf16[2,256,1024]{2,1,0:T(8,128)(2,1)S(1)}, bf16[2,256,1024]{2,1,0:T(8,128)(2,1)S(1)}, u32[]{:S(2)}, u32[]{:S(2)}) collective-permute-start(bf16[2,256,1024]{2,1,0:T(8,128)(2,1)S(1)} %pad_maximum_fusion.13), channel_id=1, source_target_pairs={{0,8},{1,9},{2,10},{3,11},{4,12},{5,13},{6,14},{7,15},{8,0},{9,1},... | collective-permute-start | bytes 3145736 | tf_op jit(solution)/shard_map/ppermute | solution.py:310
  438.7 22.8 %collective-permute-start.60 = (bf16[2,256,1024]{2,1,0:T(8,128)(2,1)S(1)}, bf16[2,256,1024]{2,1,0:T(8,128)(2,1)S(1)}, u32[]{:S(2)}, u32[]{:S(2)}) collective-permute-start(bf16[2,256,1024]{2,1,0:T(8,128)(2,1)S(1)} %pad_maximum_fusion.14), channel_id=1, source_target_pairs={{0,16},{1,17},{2,18},{3,19},{4,20},{5,21},{6,22},{7,23},{8,24},{9,... | collective-permute-start | bytes 3145736 | tf_op jit(solution)/shard_map/ppermute | solution.py:310
  439.7 21.0 %collective-permute-start.61 = (f32[2,512]{1,0:T(2,128)S(1)}, f32[2,512]{1,0:T(2,128)S(1)}, u32[]{:S(2)}, u32[]{:S(2)}) collective-permute-start(f32[2,512]{1,0:T(2,128)S(1)} %pad_maximum_fusion.26), channel_id=1, source_target_pairs={{0,8},{1,9},{2,10},{3,11},{4,12},{5,13},{6,14},{7,15},{8,0},{9,1},... | collective-permute-start | bytes 12296 | tf_op jit(solution)/shard_map/ppermute | solution.py:310
  448.1 25.9 %collective-permute-start.68 = (bf16[3,128,512]{2,1,0:T(8,128)(2,1)S(1)}, bf16[3,128,512]{2,1,0:T(8,128)(2,1)S(1)}, u32[]{:S(2)}, u32[]{:S(2)}) collective-permute-start(bf16[3,128,512]{2,1,0:T(8,128)(2,1)S(1)} %select_convert_fusion.1), channel_id=1, source_target_pairs={{0,4},{1,5},{2,6},{3,7},{4,0},{5,1},{6,2},{7,3},{8,12},{9,13},{10,... | collective-permute-start | bytes 1179656 | tf_op jit(solution)/shard_map/ppermute | solution.py:310
  462.2 7.1 %collective-permute-start.64 = (bf16[256,512]{1,0:T(8,128)(2,1)S(1)}, bf16[256,512]{1,0:T(8,128)(2,1)S(1)}, u32[]{:S(2)}, u32[]{:S(2)}) collective-permute-start(bf16[256,512]{1,0:T(8,128)(2,1)S(1)} %get-tuple-element.402), channel_id=1, source_target_pairs={{0,1},{1,0},{2,3},{3,2},{4,5},{5,4},{6,7},{7,6},{8,9},{9,8},{10,11... | collective-permute-start | bytes 786440 | tf_op jit(solution)/shard_map/ppermute | solution.py:310
  462.9 4.0 collective-permute-start.65
  463.8 25.3 %collective-permute-start.63 = (bf16[256,512]{1,0:T(8,128)(2,1)S(1)}, bf16[256,512]{1,0:T(8,128)(2,1)S(1)}, u32[]{:S(2)}, u32[]{:S(2)}) collective-permute-start(bf16[256,512]{1,0:T(8,128)(2,1)S(1)} %slice.260), channel_id=1, source_target_pairs={{0,1},{1,0},{2,3},{3,2},{4,5},{5,4},{6,7},{7,6},{8,9},{9,8},{10,11... | collective-permute-start | bytes 786440 | tf_op jit(solution)/shard_map/ppermute | solution.py:310
  469.4 5.2 %collective-permute-start.69 = (f32[2,128]{1,0:T(2,128)S(1)}, f32[2,128]{1,0:T(2,128)S(1)}, u32[]{:S(2)}, u32[]{:S(2)}) collective-permute-start(f32[2,128]{1,0:T(2,128)S(1)} %broadcast_select_fusion.38), channel_id=1, source_target_pairs={{0,4},{1,5},{2,6},{3,7},{4,0},{5,1},{6,2},{7,3},{8,12},{9,13},{10,... | collective-permute-start | bytes 3080 | tf_op jit(solution)/shard_map/ppermute | solution.py:310
  473.8 15.3 %collective-permute-start.66 = (bf16[256,512]{1,0:T(8,128)(2,1)S(1)}, bf16[256,512]{1,0:T(8,128)(2,1)S(1)}, u32[]{:S(2)}, u32[]{:S(2)}) collective-permute-start(bf16[256,512]{1,0:T(8,128)(2,1)S(1)} %add_convert_fusion.8), channel_id=1, source_target_pairs={{0,2},{1,3},{2,0},{3,1},{4,6},{5,7},{6,4},{7,5},{8,10},{9,11},{10,... | collective-permute-start | bytes 786440 | tf_op jit(solution)/shard_map/ppermute | solution.py:310
  475.2 7.7 %collective-permute-start.72 = (f32[2,32]{1,0:T(2,128)S(1)}, f32[2,32]{1,0:T(2,128)S(1)}, u32[]{:S(2)}, u32[]{:S(2)}) collective-permute-start(f32[2,32]{1,0:T(2,128)S(1)} %get-tuple-element.473), channel_id=1, source_target_pairs={{0,3},{1,2},{2,1},{3,0},{4,7},{5,6},{6,5},{7,4},{8,11},{9,10},{10,... | collective-permute-start | bytes 776 | tf_op jit(solution)/shard_map/ppermute | solution.py:310
  477.1 11.4 %collective-permute-start.71 = (f32[2,32]{1,0:T(2,128)S(1)}, f32[2,32]{1,0:T(2,128)S(1)}, u32[]{:S(2)}, u32[]{:S(2)}) collective-permute-start(f32[2,32]{1,0:T(2,128)S(1)} %get-tuple-element.474), channel_id=1, source_target_pairs={{0,2},{1,3},{2,0},{3,1},{4,6},{5,7},{6,4},{7,5},{8,10},{9,11},{10,... | collective-permute-start | bytes 776 | tf_op jit(solution)/shard_map/ppermute | solution.py:310
  477.5 11.0 %collective-permute-start.70 = (f32[2,32]{1,0:T(2,128)S(1)}, f32[2,32]{1,0:T(2,128)S(1)}, u32[]{:S(2)}, u32[]{:S(2)}) collective-permute-start(f32[2,32]{1,0:T(2,128)S(1)} %get-tuple-element.472), channel_id=1, source_target_pairs={{0,1},{1,0},{2,3},{3,2},{4,5},{5,4},{6,7},{7,6},{8,9},{9,8},{10,11... | collective-permute-start | bytes 776 | tf_op jit(solution)/shard_map/ppermute | solution.py:310
  (115 other events, 1149.1 us)

commit v6 on v5

--- a/solution.py
+++ b/solution.py
@@ -1115,14 +1115,9 @@
     gq_b, gk_b, gv_b = attend_back(1)
 
     gq_b, batch_x, batch_y, d_0, d_1, x_1, y_0 = event(gq_b, batch_x, batch_y, d_0, d_1, x_1, y_0)
-    grad_queries, batch_x, batch_y, part_3, part_2, gk_b, gv_b = event(
-        jnp.concatenate([gq_a, gq_b], axis=1),
-        jnp.stack([add(x_0, d_0), x_1]),
-        jnp.stack([y_0, add(y_1, d_1)]),
-        total_of(own_3, batch_x[1], batch_y[1]).astype(BF),
-        total_of(own_2, batch_x[0], batch_y[0]).astype(BF),
-        gk_b,
-        gv_b,
+    part_3, part_2 = total_of(own_3, batch_x[1], batch_y[1]).astype(BF), total_of(own_2, batch_x[0], batch_y[0]).astype(BF)
+    grad_queries, batch_x, batch_y, gk_b, gv_b = event(
+        jnp.concatenate([gq_a, gq_b], axis=1), jnp.stack([add(x_0, d_0), x_1]), jnp.stack([y_0, add(y_1, d_1)]), gk_b, gv_b
     )
     batch_x, batch_y, part_3 = x_swap(batch_x), y_swap(batch_y), z_swap(part_3, 1)
     grad_keys = jnp.concatenate([gk_a, gk_b], axis=1)

time: 497 us -> 496 us (level)
  no operation moved by 1% of the time
where the time goes in v6:
time: 496 us; the launch traced here: 492 us
  Pallas kernels  165 us (33%)
  waiting for transfers between devices  152 us (31%)
  starting transfers between devices  90.2 us (18%)
  local copies, waits for them, and re-layouts  41.8 us (8%)
  other arithmetic  36.3 us (7%)
    ppermute x73, waiting for transfers between devices, shift(): return lax.ppermute(value, AXES, pairs)  152 us
    ppermute x73, starting transfers between devices, shift(): return lax.ppermute(value, AXES, pairs)  90.2 us
    pallas_call x2, Pallas kernels, feed_backward(): pl.pallas_call(lambda *refs: feed_backward_kernel(places, total is not No...  46.6 us
    unnamed x223, local copies, waits for them, and re-layouts  34 us
    pallas_call x2, Pallas kernels, attend_backward(): pl.pallas_call(attend_backward_kernel, out_shape=(jax.ShapeDtypeStruct((r...  33.2 us
    pallas_call x4, Pallas kernels, attend_forward(): pl.pallas_call(attend_forward_kernel, out_shape=(jax.ShapeDtypeStruct((ro...  24.7 us
    pallas_call x4, Pallas kernels, feed_forward(): pl.pallas_call(lambda *refs: feed_forward_kernel(y is None, *refs), out_s...  22.4 us
    pallas_call x1, Pallas kernels, project(): pl.pallas_call(project_kernel, out_shape=(shape(4 * chunk, model), shape(...  13.7 us
  transfers between devices with their start and end apart: 73, of which 34 were waited for; matrix products, arithmetic and copies ran while one was open for 7% of the time, Pallas kernels for 31%

profile of v6, /device:TPU:0, one launch (start us, length us, event | category | flops | bytes accessed | tf_op | source)
XLA Modules:
  0.0 492.0 jit_solution(15300876044037719103)
XLA Ops:
  5.4 2.6 collective-permute-start.2
  8.0 1.5 collective-permute-start.3
  12.1 2.0 collective-permute-done.4
  14.1 1.6 collective-permute-start.8
  15.6 2.6 collective-permute-start.7
  18.3 8.2 %collective-permute-done.8 = bf16[256,512]{1,0:T(8,128)(2,1)S(1)} collective-permute-done((bf16[256,512]{1,0:T(8,128)(2,1)S(1)}, bf16[256,512]{1,0:T(8,128)(2,1)S(1)}, u32[]{:S(2)}, u32[]{:S(2)}) %collective-permute-start.8) | collective-permute-done | bytes 262176 | tf_op jit(solution)/shard_map/ppermute | solution.py:310
  26.5 2.5 collective-permute-done.7
  30.4 3.6 collective-permute-start.13
  36.2 1.5 collective-permute-start.15
  37.7 10.7 %collective-permute-done.11.refs_6_ = bf16[2,256,512]{2,1,0:T(8,128)(2,1)S(1)} collective-permute-done((bf16[2,256,512]{2,1,0:T(8,128)(2,1)S(1)}, bf16[2,256,512]{2,1,0:T(8,128)(2,1)S(1)}, u32[]{:S(2)}, u32[]{:S(2)}) %collective-permute-start.11) | collective-permute-done | bytes 524320 | tf_op jit(solution)/shard_map/ppermute | solution.py:310
  51.5 6.9 %collective-permute-done.13.refs_2_ = bf16[512,1024]{1,0:T(8,128)(2,1)} collective-permute-done((bf16[512,1024]{1,0:T(8,128)(2,1)S(1)}, bf16[512,1024]{1,0:T(8,128)(2,1)}, u32[]{:S(2)}, u32[]{:S(2)}) %collective-permute-start.13) | collective-permute-done | bytes 1048608 | tf_op jit(solution)/shard_map/ppermute | solution.py:310
  58.4 11.0 %collective-permute-start.12 = (bf16[512,1024]{1,0:T(8,128)(2,1)S(1)}, bf16[512,1024]{1,0:T(8,128)(2,1)}, u32[]{:S(2)}, u32[]{:S(2)}) collective-permute-start(bf16[512,1024]{1,0:T(8,128)(2,1)S(1)} %collective-permute-done.refs_0_.refs_3_), channel_id=1, source_target_pairs={{0,4},{1,5},{2,6},{3,7},{4,0},{5,1},{6,2},{7,3},{8,12},{9,13},{10,... | collective-permute-start | bytes 3145736 | tf_op jit(solution)/shard_map/ppermute | solution.py:310
  70.1 1.9 collective-permute-done.17.refs_8_
  74.7 7.8 %collective-permute-start.21 = (bf16[3,256,512]{2,1,0:T(8,128)(2,1)S(1)}, bf16[3,256,512]{2,1,0:T(8,128)(2,1)}, u32[]{:S(2)}, u32[]{:S(2)}) collective-permute-start(bf16[3,256,512]{2,1,0:T(8,128)(2,1)S(1)} %maximum_select_fusion.1), channel_id=1, source_target_pairs={{0,1},{1,0},{2,3},{3,2},{4,5},{5,4},{6,7},{7,6},{8,9},{9,8},{10,11... | collective-permute-start | bytes 2359304 | tf_op jit(solution)/shard_map/ppermute | solution.py:310
  84.5 3.9 collective-permute-start.23
  88.3 13.7 %project.1 = (bf16[2048,1024]{1,0:T(8,128)(2,1)}, bf16[1024,512]{1,0:T(8,128)(2,1)}, bf16[2048,512]{1,0:T(8,128)(2,1)}, bf16[2048,512]{1,0:T(8,128)(2,1)}, bf16[...) custom-call(bf16[512,1024]{1,0:T(8,128)(2,1)} %copy-done.13, ...), custom_call_target="tpu_custom_call" | custom-call | flops 1000 | bytes 1000 | tf_op jit(solution)/shard_map/project/pallas_call | solution.py:581
  106.2 1.6 copy-done.1
  107.8 1.6 copy-done.3
  110.6 6.0 %attend_forward.4 = (bf16[1024,128]{1,0:T(8,128)(2,1)S(1)}, f32[1,8,1024]{2,1,0:T(8,128)S(1)}) custom-call(s32[1]{0:T(128)} %bitcast.12.outer_ref, s32[9]{0:T(128)S(1)} %stack.162.sc_ref, bf16[1024,512]{1,0:T(8,128)(2,1)S(1)} %copy-done.5, bf16[2048,512]{1,0:T(8,128)(2,1)S(1)} %copy-done.1, bf16[2048,512]{1,0:T(8,128)(2,1)S(1)} %copy-done.3), custom_call_target="tpu_custom_call" | custom-call | flops 1000 | bytes 1000 | tf_op jit(solution)/shard_map/attend_forward/pallas_call | solution.py:439
  116.6 1.6 collective-permute-start.24
  118.9 6.4 %attend_forward.5 = (bf16[1024,128]{1,0:T(8,128)(2,1)S(1)}, f32[1,8,1024]{2,1,0:T(8,128)S(1)}) custom-call(s32[1]{0:T(128)} %bitcast.12.outer_ref, s32[9]{0:T(128)S(1)} %stack.162.sc_ref, bf16[1024,512]{1,0:T(8,128)(2,1)S(1)} %copy-done.5, bf16[2048,512]{1,0:T(8,128)(2,1)S(1)} %copy-done.1, bf16[2048,512]{1,0:T(8,128)(2,1)S(1)} %copy-done.3), custom_call_target="tpu_custom_call" | custom-call | flops 1000 | bytes 1000 | tf_op jit(solution)/shard_map/attend_forward/pallas_call | solution.py:439
  127.0 6.0 %attend_forward.6 = (bf16[1024,128]{1,0:T(8,128)(2,1)S(1)}, f32[1,8,1024]{2,1,0:T(8,128)S(1)}) custom-call(s32[1]{0:T(128)} %bitcast.12.outer_ref, s32[9]{0:T(128)S(1)} %stack.162.sc_ref, bf16[1024,512]{1,0:T(8,128)(2,1)S(1)} %copy-done.5, bf16[2048,512]{1,0:T(8,128)(2,1)S(1)} %copy-done.1, bf16[2048,512]{1,0:T(8,128)(2,1)S(1)} %copy-done.3), custom_call_target="tpu_custom_call" | custom-call | flops 1000 | bytes 1000 | tf_op jit(solution)/shard_map/attend_forward/pallas_call | solution.py:439
  133.1 2.0 collective-permute-done.24
  135.1 4.4 collective-permute-done.25
  139.6 1.8 collective-permute-start.29
  141.4 6.2 %attend_forward.7 = (bf16[1024,128]{1,0:T(8,128)(2,1)S(1)}, f32[1,8,1024]{2,1,0:T(8,128)S(1)}) custom-call(s32[1]{0:T(128)} %bitcast.12.outer_ref, s32[9]{0:T(128)S(1)} %stack.162.sc_ref, bf16[1024,512]{1,0:T(8,128)(2,1)S(1)} %copy-done.5, bf16[2048,512]{1,0:T(8,128)(2,1)S(1)} %copy-done.1, bf16[2048,512]{1,0:T(8,128)(2,1)S(1)} %copy-done.3), custom_call_target="tpu_custom_call" | custom-call | flops 1000 | bytes 1000 | tf_op jit(solution)/shard_map/attend_forward/pallas_call | solution.py:439
  149.4 5.3 %collective-permute-done.27 = bf16[3,256,512]{2,1,0:T(8,128)(2,1)S(1)} collective-permute-done((bf16[3,256,512]{2,1,0:T(8,128)(2,1)S(1)}, bf16[3,256,512]{2,1,0:T(8,128)(2,1)S(1)}, u32[]{:S(2)}, u32[]{:S(2)}) %collective-permute-start.27) | collective-permute-done | bytes 786464 | tf_op jit(solution)/shard_map/ppermute | solution.py:310
  155.8 17.2 %collective-permute-done.29.refs_4_.refs_2_.refs_9_.refs_15_ = bf16[2,3,256,512]{3,2,1,0:T(8,128)(2,1)S(1)} collective-permute-done((bf16[2,3,256,512]{3,2,1,0:T(8,128)(2,1)S(1)}, bf16[2,3,256,512]{3,2,1,0:T(8,128)(2,1)S(1)}, u32[]{:S(2)}, u32[]{:S(2)}) %collective-permute-start.29) | collective-permute-done | bytes 1572896 | tf_op jit(solution)/shard_map/ppermute | solution.py:310
  173.0 1.7 collective-permute-done.30
  181.5 6.0 %feed_forward.4 = (bf16[1024,512]{1,0:T(8,128)(2,1)S(1)}, bf16[1024,512]{1,0:T(8,128)(2,1)S(1)}, bf16[1024,512]{1,0:T(8,128)(2,1)S(1)}, f32[1024,1024]{1,0:T(8,128)S(1)}) custom-call(bf16[1024,1024]{1,0:T(8,128)(2,1)S(1)} %pad_maximum_fusion.refs_0_, bf16[1,3,256,512]{3,2,1,0:T(8,128)(2,1)S(1)} %bitcast.144, ...), custom_call_target="tpu_custom_call" | custom-call | flops 1000 | bytes 1000 | tf_op jit(solution)/shard_map/feed_forward/pallas_call | solution.py:781
  188.6 6.6 %feed_forward.5 = (bf16[1024,512]{1,0:T(8,128)(2,1)S(1)}, bf16[1024,512]{1,0:T(8,128)(2,1)S(1)}, bf16[1024,512]{1,0:T(8,128)(2,1)S(1)}, f32[1024,1024]{1,0:T(8,128)S(1)}) custom-call(bf16[1024,1024]{1,0:T(8,128)(2,1)S(1)} %pad_maximum_fusion.refs_0_, bf16[1,3,256,512]{3,2,1,0:T(8,128)(2,1)} %bitcast.31.refs_1_.refs_12_, ...), custom_call_target="tpu_custom_call", output_to_operand_aliasing={{3}: (5, {})} | custom-call | flops 1000 | bytes 1000 | tf_op jit(solution)/shard_map/feed_forward/pallas_call | solution.py:781
  197.9 4.9 feed_forward.6
  205.8 8.0 %collective-permute-done.34.refs_2_.refs_4_.refs_13_.refs_15_ = bf16[2,3,256,512]{3,2,1,0:T(8,128)(2,1)S(1)} collective-permute-done((bf16[2,3,256,512]{3,2,1,0:T(8,128)(2,1)S(1)}, bf16[2,3,256,512]{3,2,1,0:T(8,128)(2,1)S(1)}, u32[]{:S(2)}, u32[]{:S(2)}) %collective-permute-start.34) | collective-permute-done | bytes 1572896 | tf_op jit(solution)/shard_map/ppermute | solution.py:310
  215.1 4.9 feed_forward.7
  220.0 1.8 slice.164
  227.4 4.6 fusion.21
  236.2 2.0 collective-permute-start.38
  238.2 22.6 %feed_backward.2 = (f32[1024,1024]{1,0:T(8,128)}, bf16[3,256,512]{2,1,0:T(8,128)(2,1)}, bf16[3,256,512]{2,1,0:T(8,128)(2,1)}, bf16[3,256,512]{2,1,0:T(8,128)(2,1...) custom-call(bf16[1024,1024]{1,0:T(8,128)(2,1)} %copy-done, ...), custom_call_target="tpu_custom_call" | custom-call | flops 1000 | bytes 1000 | tf_op jit(solution)/shard_map/feed_backward/pallas_call | solution.py:877
  261.9 1.7 collective-permute-start.40
  263.5 24.0 %feed_backward.3 = (f32[512,1024]{1,0:T(8,128)}, bf16[512,1024]{1,0:T(8,128)(2,1)}, bf16[3,256,512]{2,1,0:T(8,128)(2,1)}, bf16[3,256,512]{2,1,0:T(8,128)(2,1)}, ...) custom-call(bf16[1024,1024]{1,0:T(8,128)(2,1)} %copy-done, ...), custom_call_target="tpu_custom_call" | custom-call | flops 1000 | bytes 1000 | tf_op jit(solution)/shard_map/feed_backward/pallas_call | solution.py:877
  287.6 2.4 fusion.4
  294.8 1.8 norm_grads.2
  303.6 16.4 %shard_map.135 = (bf16[1024,256]{1,0:T(8,128)(2,1)S(1)}, bf16[2048,256]{1,0:T(8,128)(2,1)S(1)}, bf16[2048,256]{1,0:T(8,128)(2,1)S(1)}) custom-call(s32[9]{0:T(128)S(1)} %stack.162.sc_ref, bf16[1024,512]{1,0:T(8,128)(2,1)S(1)} %copy-done.6, bf16[2048,512]{1,0:T(8,128)(2,1)S(1)} %copy-done.2, bf16[2048,512]{1,0:T(8,128)(2,1)S(1)} %copy-done.4, ...), custom_call_target="tpu_custom_call" | custom-call | flops 1000 | bytes 1000 | tf_op jit(solution)/shard_map/pallas_call | solution.py:519
  322.6 16.8 %shard_map.136 = (bf16[1024,256]{1,0:T(8,128)(2,1)S(1)}, bf16[2048,256]{1,0:T(8,128)(2,1)S(1)}, bf16[2048,256]{1,0:T(8,128)(2,1)S(1)}) custom-call(s32[9]{0:T(128)S(1)} %stack.162.sc_ref, bf16[1024,512]{1,0:T(8,128)(2,1)S(1)} %copy-done.6, bf16[2048,512]{1,0:T(8,128)(2,1)S(1)} %copy-done.2, bf16[2048,512]{1,0:T(8,128)(2,1)S(1)} %copy-done.4, ...), custom_call_target="tpu_custom_call" | custom-call | flops 1000 | bytes 1000 | tf_op jit(solution)/shard_map/pallas_call | solution.py:519
  339.6 12.5 %collective-permute-done.47 = bf16[3,256,512]{2,1,0:T(8,128)(2,1)S(1)} collective-permute-done((bf16[3,256,512]{2,1,0:T(8,128)(2,1)S(1)}, bf16[3,256,512]{2,1,0:T(8,128)(2,1)S(1)}, u32[]{:S(2)}, u32[]{:S(2)}) %collective-permute-start.47) | collective-permute-done | bytes 786464 | tf_op jit(solution)/shard_map/ppermute | solution.py:310
  358.7 8.3 %rows_grads.1 = (f32[512,1024]{1,0:T(8,128)S(1)}, bf16[512,1024]{1,0:T(8,128)(2,1)S(1)}, f32[512,1024]{1,0:T(8,128)S(1)}, bf16[512,1024]{1,0:T(8,128)(2,1)S(1)}) custom-call(bf16[1024,512]{1,0:T(8,128)(2,1)S(1)} %pad_maximum_fusion.11.dq_ref, bf16[2048,512]{1,0:T(8,128)(2,1)S(1)} %constant_dynamic-update-slice_fusion.7.dk_ref, bf16[2048,512]{1,0:T(8,128)(2,1)} %copy-done.11, ...), custom_call_target="tpu_custom_call" | custom-call | flops 1000 | bytes 1000 | tf_op jit(solution)/shard_map/rows_grads/pallas_call | solution.py:637
  372.6 1.6 collective-permute-start.51
  374.2 9.7 %attention_grads.1 = (bf16[256,1024]{1,0:T(8,128)(2,1)S(1)}, bf16[256,1024]{1,0:T(8,128)(2,1)S(1)}, bf16[256,1024]{1,0:T(8,128)(2,1)S(1)}, bf16[256,1024]{1,0:T(...) custom-call(bf16[2048,1024]{1,0:T(8,128)(2,1)} %get-tuple-element.35, ...), custom_call_target="tpu_custom_call" | custom-call | flops 1000 | bytes 1000 | tf_op jit(solution)/shard_map/attention_grads/pallas_call | solution.py:675
  392.3 1.9 collective-permute-start.55
  394.3 2.5 broadcast_select_fusion
  396.7 7.5 %collective-permute-done.52 = bf16[2,3,256,512]{3,2,1,0:T(8,128)(2,1)} collective-permute-done((bf16[2,3,256,512]{3,2,1,0:T(8,128)(2,1)}, bf16[2,3,256,512]{3,2,1,0:T(8,128)(2,1)}, u32[]{:S(2)}, u32[]{:S(2)}) %collective-permute-start.52) | collective-permute-done | bytes 1572896 | tf_op jit(solution)/shard_map/ppermute | solution.py:310
  407.0 2.6 convert_add_fusion.2
  409.9 20.8 %collective-permute-done.51.refs_2_ = bf16[512,1024]{1,0:T(8,128)(2,1)} collective-permute-done((bf16[512,1024]{1,0:T(8,128)(2,1)}, bf16[512,1024]{1,0:T(8,128)(2,1)}, u32[]{:S(2)}, u32[]{:S(2)}) %collective-permute-start.51) | collective-permute-done | bytes 1048608 | tf_op jit(solution)/shard_map/ppermute | solution.py:310
  430.6 4.4 norm_grads.3
  440.8 5.1 %collective-permute-done.62 = bf16[3,256,512]{2,1,0:T(8,128)(2,1)S(1)} collective-permute-done((bf16[3,256,512]{2,1,0:T(8,128)(2,1)S(1)}, bf16[3,256,512]{2,1,0:T(8,128)(2,1)S(1)}, u32[]{:S(2)}, u32[]{:S(2)}) %collective-permute-start.62) | collective-permute-done | bytes 786464 | tf_op jit(solution)/shard_map/ppermute | solution.py:310
  447.7 12.7 %collective-permute-done.61 = f32[2,512]{1,0:T(2,128)S(1)} collective-permute-done((f32[2,512]{1,0:T(2,128)S(1)}, f32[2,512]{1,0:T(2,128)S(1)}, u32[]{:S(2)}, u32[]{:S(2)}) %collective-permute-start.61) | collective-permute-done | bytes 4128 | tf_op jit(solution)/shard_map/ppermute | solution.py:310
  463.4 1.6 collective-permute-start.63
  465.0 1.6 select_convert_fusion
  466.6 2.5 collective-permute-done.64
  469.2 4.1 collective-permute-start.69
  474.7 2.0 collective-permute-start.72
  477.0 2.1 collective-permute-start.70
  479.9 1.8 copy.19
  482.4 5.6 %collective-permute-done.71 = f32[2,32]{1,0:T(2,128)S(1)} collective-permute-done((f32[2,32]{1,0:T(2,128)S(1)}, f32[2,32]{1,0:T(2,128)S(1)}, u32[]{:S(2)}, u32[]{:S(2)}) %collective-permute-start.71) | collective-permute-done | bytes 288 | tf_op jit(solution)/shard_map/ppermute | solution.py:310
  (419 shorter events, 108.4 us)
Async XLA Ops:
  0.6 4.7 collective-permute-start.1
  2.3 7.2 %collective-permute-start.5 = (bf16[4,128,128]{2,1,0:T(8,128)(2,1)S(1)}, bf16[4,128,128]{2,1,0:T(8,128)(2,1)S(1)}, u32[]{:S(2)}, u32[]{:S(2)}) collective-permute-start(bf16[4,128,128]{2,1,0:T(8,128)(2,1)S(1)} %get-tuple-element.460), channel_id=1, source_target_pairs={{0,4},{1,5},{2,6},{3,7},{4,0},{5,1},{6,2},{7,3},{8,12},{9,13},{10,... | collective-permute-start | bytes 393224 | tf_op jit(solution)/shard_map/ppermute | solution.py:310
  4.8 4.8 collective-permute-start.6
  5.4 4.6 collective-permute-start.2
  8.0 3.6 collective-permute-start.3
  9.5 4.6 collective-permute-start.4
  14.1 12.5 %collective-permute-start.8 = (bf16[256,512]{1,0:T(8,128)(2,1)S(1)}, bf16[256,512]{1,0:T(8,128)(2,1)S(1)}, u32[]{:S(2)}, u32[]{:S(2)}) collective-permute-start(bf16[256,512]{1,0:T(8,128)(2,1)S(1)} %pad_maximum_fusion.21), channel_id=1, source_target_pairs={{0,1},{1,0},{2,3},{3,2},{4,5},{5,4},{6,7},{7,6},{8,9},{9,8},{10,11... | collective-permute-start | bytes 786440 | tf_op jit(solution)/shard_map/ppermute | solution.py:310
  15.6 13.4 %collective-permute-start.7 = (bf16[256,512]{1,0:T(8,128)(2,1)S(1)}, bf16[256,512]{1,0:T(8,128)(2,1)S(1)}, u32[]{:S(2)}, u32[]{:S(2)}) collective-permute-start(bf16[256,512]{1,0:T(8,128)(2,1)S(1)} %pad_maximum_fusion.21), channel_id=1, source_target_pairs={{0,2},{1,3},{2,0},{3,1},{4,6},{5,7},{6,4},{7,5},{8,10},{9,11},{10,... | collective-permute-start | bytes 786440 | tf_op jit(solution)/shard_map/ppermute | solution.py:310
  29.0 6.6 %collective-permute-start.9 = (bf16[256,512]{1,0:T(8,128)(2,1)S(1)}, bf16[256,512]{1,0:T(8,128)(2,1)S(1)}, u32[]{:S(2)}, u32[]{:S(2)}) collective-permute-start(bf16[256,512]{1,0:T(8,128)(2,1)S(1)} %collective-permute-done.7), channel_id=1, source_target_pairs={{0,1},{1,0},{2,3},{3,2},{4,5},{5,4},{6,7},{7,6},{8,9},{9,8},{10,11... | collective-permute-start | bytes 786440 | tf_op jit(solution)/shard_map/ppermute | solution.py:310
  29.5 20.5 %collective-permute-start = (bf16[512,1024]{1,0:T(8,128)(2,1)S(1)}, bf16[512,1024]{1,0:T(8,128)(2,1)S(1)}, u32[]{:S(2)}, u32[]{:S(2)}) collective-permute-start(bf16[512,1024]{1,0:T(8,128)(2,1)S(1)} %pad_maximum_fusion.8), channel_id=1, source_target_pairs={{0,0},{1,1},{2,5},{3,4},{4,3},{5,2},{6,6},{7,7},{8,8},{9,9},{10,13... | collective-permute-start | bytes 3145736 | tf_op jit(solution)/shard_map/ppermute | solution.py:310
  30.4 28.0 %collective-permute-start.13 = (bf16[512,1024]{1,0:T(8,128)(2,1)S(1)}, bf16[512,1024]{1,0:T(8,128)(2,1)}, u32[]{:S(2)}, u32[]{:S(2)}) collective-permute-start(bf16[512,1024]{1,0:T(8,128)(2,1)S(1)} %pad_maximum_fusion.8), channel_id=1, source_target_pairs={{0,1},{1,0},{2,4},{4,2},{5,3},{6,7},{8,9},{9,8},{10,12},{12,10},{1... | collective-permute-start | bytes 3145736 | tf_op jit(solution)/shard_map/ppermute | solution.py:310
  35.0 13.5 %collective-permute-start.11 = (bf16[2,256,512]{2,1,0:T(8,128)(2,1)S(1)}, bf16[2,256,512]{2,1,0:T(8,128)(2,1)S(1)}, u32[]{:S(2)}, u32[]{:S(2)}) collective-permute-start(bf16[2,256,512]{2,1,0:T(8,128)(2,1)S(1)} %pad_maximum_fusion.16.refs_5_), channel_id=1, source_target_pairs={{0,8},{1,9},{2,10},{3,11},{4,12},{5,13},{6,14},{7,15},{8,0},{9,1},... | collective-permute-start | bytes 1572872 | tf_op jit(solution)/shard_map/ppermute | solution.py:310
  35.7 13.8 %collective-permute-start.10 = (bf16[2,256,512]{2,1,0:T(8,128)(2,1)S(1)}, bf16[2,256,512]{2,1,0:T(8,128)(2,1)S(1)}, u32[]{:S(2)}, u32[]{:S(2)}) collective-permute-start(bf16[2,256,512]{2,1,0:T(8,128)(2,1)S(1)} %pad_maximum_fusion.15.refs_9_), channel_id=1, source_target_pairs={{0,16},{1,17},{2,18},{3,19},{4,20},{5,21},{6,22},{7,23},{8,24},{9,... | collective-permute-start | bytes 1572872 | tf_op jit(solution)/shard_map/ppermute | solution.py:310
  36.2 33.2 %collective-permute-start.15 = (bf16[2,256,512]{2,1,0:T(8,128)(2,1)S(1)}, bf16[2,256,512]{2,1,0:T(8,128)(2,1)S(1)}, u32[]{:S(2)}, u32[]{:S(2)}) collective-permute-start(bf16[2,256,512]{2,1,0:T(8,128)(2,1)S(1)} %pad_maximum_fusion.16.refs_5_), channel_id=1, source_target_pairs={{0,16},{1,17},{2,18},{3,19},{4,20},{5,21},{6,22},{7,23},{8,24},{9,... | collective-permute-start | bytes 1572872 | tf_op jit(solution)/shard_map/ppermute | solution.py:310
  48.5 21.0 %collective-permute-start.16 = (bf16[2,256,512]{2,1,0:T(8,128)(2,1)S(1)}, bf16[2,256,512]{2,1,0:T(8,128)(2,1)S(1)}, u32[]{:S(2)}, u32[]{:S(2)}) collective-permute-start(bf16[2,256,512]{2,1,0:T(8,128)(2,1)S(1)} %pad_maximum_fusion.15.refs_9_), channel_id=1, source_target_pairs={{0,8},{1,9},{2,10},{3,11},{4,12},{5,13},{6,14},{7,15},{8,0},{9,1},... | collective-permute-start | bytes 1572872 | tf_op jit(solution)/shard_map/ppermute | solution.py:310
  49.5 22.5 %collective-permute-start.17 = (bf16[2,256,512]{2,1,0:T(8,128)(2,1)S(1)}, bf16[2,256,512]{2,1,0:T(8,128)(2,1)S(1)}, u32[]{:S(2)}, u32[]{:S(2)}) collective-permute-start(bf16[2,256,512]{2,1,0:T(8,128)(2,1)S(1)} %collective-permute-done.11.refs_6_), channel_id=1, source_target_pairs={{0,16},{1,17},{2,18},{3,19},{4,20},{5,21},{6,22},{7,23},{8,24},{9,... | collective-permute-start | bytes 1572872 | tf_op jit(solution)/shard_map/ppermute | solution.py:310
  50.0 24.0 %collective-permute-start.18 = (bf16[2,256,512]{2,1,0:T(8,128)(2,1)S(1)}, bf16[2,256,512]{2,1,0:T(8,128)(2,1)S(1)}, u32[]{:S(2)}, u32[]{:S(2)}) collective-permute-start(bf16[2,256,512]{2,1,0:T(8,128)(2,1)S(1)} %collective-permute-done.10.refs_11_), channel_id=1, source_target_pairs={{0,8},{1,9},{2,10},{3,11},{4,12},{5,13},{6,14},{7,15},{8,0},{9,1},... | collective-permute-start | bytes 1572872 | tf_op jit(solution)/shard_map/ppermute | solution.py:310
  58.4 26.1 %collective-permute-start.12 = (bf16[512,1024]{1,0:T(8,128)(2,1)S(1)}, bf16[512,1024]{1,0:T(8,128)(2,1)}, u32[]{:S(2)}, u32[]{:S(2)}) collective-permute-start(bf16[512,1024]{1,0:T(8,128)(2,1)S(1)} %collective-permute-done.refs_0_.refs_3_), channel_id=1, source_target_pairs={{0,4},{1,5},{2,6},{3,7},{4,0},{5,1},{6,2},{7,3},{8,12},{9,13},{10,... | collective-permute-start | bytes 3145736 | tf_op jit(solution)/shard_map/ppermute | solution.py:310
  69.5 15.0 %collective-permute-start.14 = (bf16[512,1024]{1,0:T(8,128)(2,1)}, bf16[512,1024]{1,0:T(8,128)(2,1)}, u32[]{:S(2)}, u32[]{:S(2)}) collective-permute-start(bf16[512,1024]{1,0:T(8,128)(2,1)} %collective-permute-done.13.refs_2_), channel_id=1, source_target_pairs={{0,4},{1,5},{2,6},{3,7},{4,0},{5,1},{6,2},{7,3},{8,12},{9,13},{10,... | collective-permute-start | bytes 3145736 | tf_op jit(solution)/shard_map/ppermute | solution.py:310
  69.5 32.5 %collective-permute-start.19 = (bf16[3,256,512]{2,1,0:T(8,128)(2,1)S(1)}, bf16[3,256,512]{2,1,0:T(8,128)(2,1)}, u32[]{:S(2)}, u32[]{:S(2)}) collective-permute-start(bf16[3,256,512]{2,1,0:T(8,128)(2,1)S(1)} %maximum_select_fusion.1), channel_id=1, source_target_pairs={{0,8},{1,9},{2,10},{3,11},{4,12},{5,13},{6,14},{7,15},{8,0},{9,1},... | collective-permute-start | bytes 2359304 | tf_op jit(solution)/shard_map/ppermute | solution.py:310
  71.9 30.1 %collective-permute-start.20 = (bf16[3,256,512]{2,1,0:T(8,128)(2,1)S(1)}, bf16[3,256,512]{2,1,0:T(8,128)(2,1)}, u32[]{:S(2)}, u32[]{:S(2)}) collective-permute-start(bf16[3,256,512]{2,1,0:T(8,128)(2,1)S(1)} %maximum_select_fusion.1), channel_id=1, source_target_pairs={{0,16},{1,17},{2,18},{3,19},{4,20},{5,21},{6,22},{7,23},{8,24},{9,... | collective-permute-start | bytes 2359304 | tf_op jit(solution)/shard_map/ppermute | solution.py:310
  74.7 41.9 %collective-permute-start.21 = (bf16[3,256,512]{2,1,0:T(8,128)(2,1)S(1)}, bf16[3,256,512]{2,1,0:T(8,128)(2,1)}, u32[]{:S(2)}, u32[]{:S(2)}) collective-permute-start(bf16[3,256,512]{2,1,0:T(8,128)(2,1)S(1)} %maximum_select_fusion.1), channel_id=1, source_target_pairs={{0,1},{1,0},{2,3},{3,2},{4,5},{5,4},{6,7},{7,6},{8,9},{9,8},{10,11... | collective-permute-start | bytes 2359304 | tf_op jit(solution)/shard_map/ppermute | solution.py:310
  84.5 41.0 %collective-permute-start.23 = (bf16[3,256,512]{2,1,0:T(8,128)(2,1)S(1)}, bf16[3,256,512]{2,1,0:T(8,128)(2,1)S(1)}, u32[]{:S(2)}, u32[]{:S(2)}) collective-permute-start(bf16[3,256,512]{2,1,0:T(8,128)(2,1)S(1)} %maximum_select_fusion.1), channel_id=1, source_target_pairs={{0,2},{1,3},{2,0},{3,1},{4,6},{5,7},{6,4},{7,5},{8,10},{9,11},{10,... | collective-permute-start | bytes 2359304 | tf_op jit(solution)/shard_map/ppermute | solution.py:310
  102.1 23.4 %collective-permute-start.22 = (bf16[3,256,512]{2,1,0:T(8,128)(2,1)}, bf16[3,256,512]{2,1,0:T(8,128)(2,1)S(1)}, u32[]{:S(2)}, u32[]{:S(2)}) collective-permute-start(bf16[3,256,512]{2,1,0:T(8,128)(2,1)} %collective-permute-done.19), channel_id=1, source_target_pairs={{0,16},{1,17},{2,18},{3,19},{4,20},{5,21},{6,22},{7,23},{8,24},{9,... | collective-permute-start | bytes 2359304 | tf_op jit(solution)/shard_map/ppermute | solution.py:310
  116.6 18.4 %collective-permute-start.24 = (bf16[3,256,512]{2,1,0:T(8,128)(2,1)}, bf16[3,256,512]{2,1,0:T(8,128)(2,1)S(1)}, u32[]{:S(2)}, u32[]{:S(2)}) collective-permute-start(bf16[3,256,512]{2,1,0:T(8,128)(2,1)} %collective-permute-done.21), channel_id=1, source_target_pairs={{0,8},{1,9},{2,10},{3,11},{4,12},{5,13},{6,14},{7,15},{8,0},{9,1},... | collective-permute-start | bytes 2359304 | tf_op jit(solution)/shard_map/ppermute | solution.py:310
  118.2 21.2 %collective-permute-start.25 = (bf16[3,256,512]{2,1,0:T(8,128)(2,1)}, bf16[3,256,512]{2,1,0:T(8,128)(2,1)S(1)}, u32[]{:S(2)}, u32[]{:S(2)}) collective-permute-start(bf16[3,256,512]{2,1,0:T(8,128)(2,1)} %collective-permute-done.21), channel_id=1, source_target_pairs={{0,16},{1,17},{2,18},{3,19},{4,20},{5,21},{6,22},{7,23},{8,24},{9,... | collective-permute-start | bytes 2359304 | tf_op jit(solution)/shard_map/ppermute | solution.py:310
  125.5 23.9 %collective-permute-start.26 = (bf16[3,256,512]{2,1,0:T(8,128)(2,1)S(1)}, bf16[3,256,512]{2,1,0:T(8,128)(2,1)S(1)}, u32[]{:S(2)}, u32[]{:S(2)}) collective-permute-start(bf16[3,256,512]{2,1,0:T(8,128)(2,1)S(1)} %collective-permute-done.23), channel_id=1, source_target_pairs={{0,1},{1,0},{2,3},{3,2},{4,5},{5,4},{6,7},{7,6},{8,9},{9,8},{10,11... | collective-permute-start | bytes 2359304 | tf_op jit(solution)/shard_map/ppermute | solution.py:310
  125.6 29.2 %collective-permute-start.27 = (bf16[3,256,512]{2,1,0:T(8,128)(2,1)S(1)}, bf16[3,256,512]{2,1,0:T(8,128)(2,1)S(1)}, u32[]{:S(2)}, u32[]{:S(2)}) collective-permute-start(bf16[3,256,512]{2,1,0:T(8,128)(2,1)S(1)} %collective-permute-done.23), channel_id=1, source_target_pairs={{0,16},{1,17},{2,18},{3,19},{4,20},{5,21},{6,22},{7,23},{8,24},{9,... | collective-permute-start | bytes 2359304 | tf_op jit(solution)/shard_map/ppermute | solution.py:310
  139.6 33.4 %collective-permute-start.29 = (bf16[2,3,256,512]{3,2,1,0:T(8,128)(2,1)S(1)}, bf16[2,3,256,512]{3,2,1,0:T(8,128)(2,1)S(1)}, u32[]{:S(2)}, u32[]{:S(2)}) collective-permute-start(bf16[2,3,256,512]{3,2,1,0:T(8,128)(2,1)S(1)} %pad_maximum_fusion.2), channel_id=1, source_target_pairs={{0,8},{1,9},{2,10},{3,11},{4,12},{5,13},{6,14},{7,15},{8,0},{9,1},... | collective-permute-start | bytes 4718600 | tf_op jit(solution)/shard_map/ppermute | solution.py:310
  154.7 20.0 %collective-permute-start.28 = (bf16[512,1024]{1,0:T(8,128)(2,1)S(1)}, bf16[512,1024]{1,0:T(8,128)(2,1)S(1)}, u32[]{:S(2)}, u32[]{:S(2)}) collective-permute-start(bf16[512,1024]{1,0:T(8,128)(2,1)S(1)} %slice.259), channel_id=1, source_target_pairs={{0,4},{1,5},{2,6},{3,7},{4,0},{5,1},{6,2},{7,3},{8,12},{9,13},{10,... | collective-permute-start | bytes 3145736 | tf_op jit(solution)/shard_map/ppermute | solution.py:310
  154.7 20.0 %collective-permute-start.30 = (bf16[3,256,512]{2,1,0:T(8,128)(2,1)S(1)}, bf16[3,256,512]{2,1,0:T(8,128)(2,1)S(1)}, u32[]{:S(2)}, u32[]{:S(2)}) collective-permute-start(bf16[3,256,512]{2,1,0:T(8,128)(2,1)S(1)} %collective-permute-done.26), channel_id=1, source_target_pairs={{0,16},{1,17},{2,18},{3,19},{4,20},{5,21},{6,22},{7,23},{8,24},{9,... | collective-permute-start | bytes 2359304 | tf_op jit(solution)/shard_map/ppermute | solution.py:310
  175.5 20.7 %collective-permute-start.33 = (bf16[3,256,512]{2,1,0:T(8,128)(2,1)S(1)}, bf16[3,256,512]{2,1,0:T(8,128)(2,1)S(1)}, u32[]{:S(2)}, u32[]{:S(2)}) collective-permute-start(bf16[3,256,512]{2,1,0:T(8,128)(2,1)S(1)} %slice_bitcast_fusion.1), channel_id=1, source_target_pairs={{0,16},{1,17},{2,18},{3,19},{4,20},{5,21},{6,22},{7,23},{8,24},{9,... | collective-permute-start | bytes 2359304 | tf_op jit(solution)/shard_map/ppermute | solution.py:310
  177.4 36.4 %collective-permute-start.34 = (bf16[2,3,256,512]{3,2,1,0:T(8,128)(2,1)S(1)}, bf16[2,3,256,512]{3,2,1,0:T(8,128)(2,1)S(1)}, u32[]{:S(2)}, u32[]{:S(2)}) collective-permute-start(bf16[2,3,256,512]{3,2,1,0:T(8,128)(2,1)S(1)} %pad_maximum_fusion.3), channel_id=1, source_target_pairs={{0,8},{1,9},{2,10},{3,11},{4,12},{5,13},{6,14},{7,15},{8,0},{9,1},... | collective-permute-start | bytes 4718600 | tf_op jit(solution)/shard_map/ppermute | solution.py:310
  196.2 27.2 %collective-permute-start.35 = (bf16[512,1024]{1,0:T(8,128)(2,1)S(1)}, bf16[512,1024]{1,0:T(8,128)(2,1)S(1)}, u32[]{:S(2)}, u32[]{:S(2)}) collective-permute-start(bf16[512,1024]{1,0:T(8,128)(2,1)S(1)} %pad_maximum_fusion.9), channel_id=1, source_target_pairs={{2,5},{3,4},{4,3},{5,2},{10,13},{11,12},{12,11},{13,10},{18,21},{1... | collective-permute-start | bytes 3145736 | tf_op jit(solution)/shard_map/ppermute | solution.py:310
  236.2 51.4 %collective-permute-start.38 = (bf16[512,1024]{1,0:T(8,128)(2,1)}, bf16[512,1024]{1,0:T(8,128)(2,1)}, u32[]{:S(2)}, u32[]{:S(2)}) collective-permute-start(bf16[512,1024]{1,0:T(8,128)(2,1)} %pad_maximum_fusion.10), channel_id=1, source_target_pairs={{2,5},{3,4},{4,3},{5,2},{10,13},{11,12},{12,11},{13,10},{18,21},{1... | collective-permute-start | bytes 3145736 | tf_op jit(solution)/shard_map/ppermute | solution.py:310
  260.8 26.7 %collective-permute-start.39 = (bf16[3,256,512]{2,1,0:T(8,128)(2,1)}, bf16[3,256,512]{2,1,0:T(8,128)(2,1)}, u32[]{:S(2)}, u32[]{:S(2)}) collective-permute-start(bf16[3,256,512]{2,1,0:T(8,128)(2,1)} %get-tuple-element.289), channel_id=1, source_target_pairs={{0,16},{1,17},{2,18},{3,19},{4,20},{5,21},{6,22},{7,23},{8,24},{9,... | collective-permute-start | bytes 2359304 | tf_op jit(solution)/shard_map/ppermute | solution.py:310
  261.9 25.6 %collective-permute-start.40 = (bf16[3,256,512]{2,1,0:T(8,128)(2,1)}, bf16[3,256,512]{2,1,0:T(8,128)(2,1)}, u32[]{:S(2)}, u32[]{:S(2)}) collective-permute-start(bf16[3,256,512]{2,1,0:T(8,128)(2,1)} %get-tuple-element.290), channel_id=1, source_target_pairs={{0,8},{1,9},{2,10},{3,11},{4,12},{5,13},{6,14},{7,15},{8,0},{9,1},... | collective-permute-start | bytes 2359304 | tf_op jit(solution)/shard_map/ppermute | solution.py:310
  298.2 41.4 %collective-permute-start.45 = (bf16[2,3,256,512]{3,2,1,0:T(8,128)(2,1)S(1)}, bf16[2,3,256,512]{3,2,1,0:T(8,128)(2,1)S(1)}, u32[]{:S(2)}, u32[]{:S(2)}) collective-permute-start(bf16[2,3,256,512]{3,2,1,0:T(8,128)(2,1)S(1)} %pad_maximum_fusion.4), channel_id=1, source_target_pairs={{0,8},{1,9},{2,10},{3,11},{4,12},{5,13},{6,14},{7,15},{8,0},{9,1},... | collective-permute-start | bytes 4718600 | tf_op jit(solution)/shard_map/ppermute | solution.py:310
  298.8 40.8 %collective-permute-start.46 = (bf16[2,3,256,512]{3,2,1,0:T(8,128)(2,1)S(1)}, bf16[2,3,256,512]{3,2,1,0:T(8,128)(2,1)S(1)}, u32[]{:S(2)}, u32[]{:S(2)}) collective-permute-start(bf16[2,3,256,512]{3,2,1,0:T(8,128)(2,1)S(1)} %pad_maximum_fusion.5), channel_id=1, source_target_pairs={{0,16},{1,17},{2,18},{3,19},{4,20},{5,21},{6,22},{7,23},{8,24},{9,... | collective-permute-start | bytes 4718600 | tf_op jit(solution)/shard_map/ppermute | solution.py:310
  320.0 32.1 %collective-permute-start.47 = (bf16[3,256,512]{2,1,0:T(8,128)(2,1)S(1)}, bf16[3,256,512]{2,1,0:T(8,128)(2,1)S(1)}, u32[]{:S(2)}, u32[]{:S(2)}) collective-permute-start(bf16[3,256,512]{2,1,0:T(8,128)(2,1)S(1)} %copy-done.103), channel_id=1, source_target_pairs={{0,16},{1,17},{2,18},{3,19},{4,20},{5,21},{6,22},{7,23},{8,24},{9,... | collective-permute-start | bytes 2359304 | tf_op jit(solution)/shard_map/ppermute | solution.py:310
  321.1 31.0 %collective-permute-start.48 = (bf16[3,256,512]{2,1,0:T(8,128)(2,1)S(1)}, bf16[3,256,512]{2,1,0:T(8,128)(2,1)S(1)}, u32[]{:S(2)}, u32[]{:S(2)}) collective-permute-start(bf16[3,256,512]{2,1,0:T(8,128)(2,1)S(1)} %copy-done.102), channel_id=1, source_target_pairs={{0,8},{1,9},{2,10},{3,11},{4,12},{5,13},{6,14},{7,15},{8,0},{9,1},... | collective-permute-start | bytes 2359304 | tf_op jit(solution)/shard_map/ppermute | solution.py:310
  367.0 3.8 collective-permute-start.49
  367.0 4.1 collective-permute-start.50
  367.5 36.7 %collective-permute-start.52 = (bf16[2,3,256,512]{3,2,1,0:T(8,128)(2,1)}, bf16[2,3,256,512]{3,2,1,0:T(8,128)(2,1)}, u32[]{:S(2)}, u32[]{:S(2)}) collective-permute-start(bf16[2,3,256,512]{3,2,1,0:T(8,128)(2,1)} %pad_maximum_fusion.6), channel_id=1, source_target_pairs={{0,8},{1,9},{2,10},{3,11},{4,12},{5,13},{6,14},{7,15},{8,0},{9,1},... | collective-permute-start | bytes 4718600 | tf_op jit(solution)/shard_map/ppermute | solution.py:310
  369.0 36.4 %collective-permute-start.53 = (bf16[2,3,256,512]{3,2,1,0:T(8,128)(2,1)}, bf16[2,3,256,512]{3,2,1,0:T(8,128)(2,1)}, u32[]{:S(2)}, u32[]{:S(2)}) collective-permute-start(bf16[2,3,256,512]{3,2,1,0:T(8,128)(2,1)} %pad_maximum_fusion.7), channel_id=1, source_target_pairs={{0,16},{1,17},{2,18},{3,19},{4,20},{5,21},{6,22},{7,23},{8,24},{9,... | collective-permute-start | bytes 4718600 | tf_op jit(solution)/shard_map/ppermute | solution.py:310
  370.7 20.5 %collective-permute-start.54 = (bf16[3,256,512]{2,1,0:T(8,128)(2,1)S(1)}, bf16[3,256,512]{2,1,0:T(8,128)(2,1)S(1)}, u32[]{:S(2)}, u32[]{:S(2)}) collective-permute-start(bf16[3,256,512]{2,1,0:T(8,128)(2,1)S(1)} %get-tuple-element.422), channel_id=1, source_target_pairs={{0,1},{1,0},{2,3},{3,2},{4,5},{5,4},{6,7},{7,6},{8,9},{9,8},{10,11... | collective-permute-start | bytes 2359304 | tf_op jit(solution)/shard_map/ppermute | solution.py:310
  372.6 58.1 %collective-permute-start.51 = (bf16[512,1024]{1,0:T(8,128)(2,1)}, bf16[512,1024]{1,0:T(8,128)(2,1)}, u32[]{:S(2)}, u32[]{:S(2)}) collective-permute-start(bf16[512,1024]{1,0:T(8,128)(2,1)} %add_convert_fusion), channel_id=1, source_target_pairs={{0,1},{1,0},{2,3},{3,2},{4,5},{5,4},{6,7},{7,6},{8,9},{9,8},{10,11... | collective-permute-start | bytes 3145736 | tf_op jit(solution)/shard_map/ppermute | solution.py:310
  392.3 42.7 %collective-permute-start.55 = (bf16[3,256,512]{2,1,0:T(8,128)(2,1)}, bf16[3,256,512]{2,1,0:T(8,128)(2,1)}, u32[]{:S(2)}, u32[]{:S(2)}) collective-permute-start(bf16[3,256,512]{2,1,0:T(8,128)(2,1)} %add_convert_fusion.1), channel_id=1, source_target_pairs={{0,2},{1,3},{2,0},{3,1},{4,6},{5,7},{6,4},{7,5},{8,10},{9,11},{10,... | collective-permute-start | bytes 2359304 | tf_op jit(solution)/shard_map/ppermute | solution.py:310
  405.4 30.8 %collective-permute-start.57 = (bf16[256,1024]{1,0:T(8,128)(2,1)S(1)}, bf16[256,1024]{1,0:T(8,128)(2,1)S(1)}, u32[]{:S(2)}, u32[]{:S(2)}) collective-permute-start(bf16[256,1024]{1,0:T(8,128)(2,1)S(1)} %copy-done.72), channel_id=1, source_target_pairs={{0,16},{1,17},{2,18},{3,19},{4,20},{5,21},{6,22},{7,23},{8,24},{9,... | collective-permute-start | bytes 1572872 | tf_op jit(solution)/shard_map/ppermute | solution.py:310
  406.4 29.8 %collective-permute-start.58 = (bf16[256,1024]{1,0:T(8,128)(2,1)S(1)}, bf16[256,1024]{1,0:T(8,128)(2,1)S(1)}, u32[]{:S(2)}, u32[]{:S(2)}) collective-permute-start(bf16[256,1024]{1,0:T(8,128)(2,1)S(1)} %copy-done.70), channel_id=1, source_target_pairs={{0,8},{1,9},{2,10},{3,11},{4,12},{5,13},{6,14},{7,15},{8,0},{9,1},... | collective-permute-start | bytes 1572872 | tf_op jit(solution)/shard_map/ppermute | solution.py:310
  409.6 36.2 %collective-permute-start.62 = (bf16[3,256,512]{2,1,0:T(8,128)(2,1)S(1)}, bf16[3,256,512]{2,1,0:T(8,128)(2,1)S(1)}, u32[]{:S(2)}, u32[]{:S(2)}) collective-permute-start(bf16[3,256,512]{2,1,0:T(8,128)(2,1)S(1)} %get-tuple-element.374), channel_id=1, source_target_pairs={{0,1},{1,0},{2,3},{3,2},{4,5},{5,4},{6,7},{7,6},{8,9},{9,8},{10,11... | collective-permute-start | bytes 2359304 | tf_op jit(solution)/shard_map/ppermute | solution.py:310
  435.3 29.7 %collective-permute-start.56 = (bf16[512,1024]{1,0:T(8,128)(2,1)S(1)}, bf16[512,1024]{1,0:T(8,128)(2,1)S(1)}, u32[]{:S(2)}, u32[]{:S(2)}) collective-permute-start(bf16[512,1024]{1,0:T(8,128)(2,1)S(1)} %pad_maximum_fusion.12), channel_id=1, source_target_pairs={{2,5},{3,4},{4,3},{5,2},{10,13},{11,12},{12,11},{13,10},{18,21},{1... | collective-permute-start | bytes 3145736 | tf_op jit(solution)/shard_map/ppermute | solution.py:310
  437.6 22.8 %collective-permute-start.59 = (bf16[2,256,1024]{2,1,0:T(8,128)(2,1)S(1)}, bf16[2,256,1024]{2,1,0:T(8,128)(2,1)S(1)}, u32[]{:S(2)}, u32[]{:S(2)}) collective-permute-start(bf16[2,256,1024]{2,1,0:T(8,128)(2,1)S(1)} %pad_maximum_fusion.13), channel_id=1, source_target_pairs={{0,8},{1,9},{2,10},{3,11},{4,12},{5,13},{6,14},{7,15},{8,0},{9,1},... | collective-permute-start | bytes 3145736 | tf_op jit(solution)/shard_map/ppermute | solution.py:310
  438.2 23.0 %collective-permute-start.60 = (bf16[2,256,1024]{2,1,0:T(8,128)(2,1)S(1)}, bf16[2,256,1024]{2,1,0:T(8,128)(2,1)S(1)}, u32[]{:S(2)}, u32[]{:S(2)}) collective-permute-start(bf16[2,256,1024]{2,1,0:T(8,128)(2,1)S(1)} %pad_maximum_fusion.14), channel_id=1, source_target_pairs={{0,16},{1,17},{2,18},{3,19},{4,20},{5,21},{6,22},{7,23},{8,24},{9,... | collective-permute-start | bytes 3145736 | tf_op jit(solution)/shard_map/ppermute | solution.py:310
  439.3 21.1 %collective-permute-start.61 = (f32[2,512]{1,0:T(2,128)S(1)}, f32[2,512]{1,0:T(2,128)S(1)}, u32[]{:S(2)}, u32[]{:S(2)}) collective-permute-start(f32[2,512]{1,0:T(2,128)S(1)} %pad_maximum_fusion.26), channel_id=1, source_target_pairs={{0,8},{1,9},{2,10},{3,11},{4,12},{5,13},{6,14},{7,15},{8,0},{9,1},... | collective-permute-start | bytes 12296 | tf_op jit(solution)/shard_map/ppermute | solution.py:310
  447.6 25.9 %collective-permute-start.68 = (bf16[3,128,512]{2,1,0:T(8,128)(2,1)S(1)}, bf16[3,128,512]{2,1,0:T(8,128)(2,1)S(1)}, u32[]{:S(2)}, u32[]{:S(2)}) collective-permute-start(bf16[3,128,512]{2,1,0:T(8,128)(2,1)S(1)} %select_convert_fusion.1), channel_id=1, source_target_pairs={{0,4},{1,5},{2,6},{3,7},{4,0},{5,1},{6,2},{7,3},{8,12},{9,13},{10,... | collective-permute-start | bytes 1179656 | tf_op jit(solution)/shard_map/ppermute | solution.py:310
  461.9 7.3 %collective-permute-start.64 = (bf16[256,512]{1,0:T(8,128)(2,1)S(1)}, bf16[256,512]{1,0:T(8,128)(2,1)S(1)}, u32[]{:S(2)}, u32[]{:S(2)}) collective-permute-start(bf16[256,512]{1,0:T(8,128)(2,1)S(1)} %get-tuple-element.398), channel_id=1, source_target_pairs={{0,1},{1,0},{2,3},{3,2},{4,5},{5,4},{6,7},{7,6},{8,9},{9,8},{10,11... | collective-permute-start | bytes 786440 | tf_op jit(solution)/shard_map/ppermute | solution.py:310
  462.4 4.2 collective-permute-start.65
  463.4 25.3 %collective-permute-start.63 = (bf16[256,512]{1,0:T(8,128)(2,1)S(1)}, bf16[256,512]{1,0:T(8,128)(2,1)S(1)}, u32[]{:S(2)}, u32[]{:S(2)}) collective-permute-start(bf16[256,512]{1,0:T(8,128)(2,1)S(1)} %slice.260), channel_id=1, source_target_pairs={{0,1},{1,0},{2,3},{3,2},{4,5},{5,4},{6,7},{7,6},{8,9},{9,8},{10,11... | collective-permute-start | bytes 786440 | tf_op jit(solution)/shard_map/ppermute | solution.py:310
  469.2 4.9 %collective-permute-start.69 = (f32[2,128]{1,0:T(2,128)S(1)}, f32[2,128]{1,0:T(2,128)S(1)}, u32[]{:S(2)}, u32[]{:S(2)}) collective-permute-start(f32[2,128]{1,0:T(2,128)S(1)} %broadcast_select_fusion.38), channel_id=1, source_target_pairs={{0,4},{1,5},{2,6},{3,7},{4,0},{5,1},{6,2},{7,3},{8,12},{9,13},{10,... | collective-permute-start | bytes 3080 | tf_op jit(solution)/shard_map/ppermute | solution.py:310
  473.4 15.3 %collective-permute-start.66 = (bf16[256,512]{1,0:T(8,128)(2,1)S(1)}, bf16[256,512]{1,0:T(8,128)(2,1)S(1)}, u32[]{:S(2)}, u32[]{:S(2)}) collective-permute-start(bf16[256,512]{1,0:T(8,128)(2,1)S(1)} %add_convert_fusion.8), channel_id=1, source_target_pairs={{0,2},{1,3},{2,0},{3,1},{4,6},{5,7},{6,4},{7,5},{8,10},{9,11},{10,... | collective-permute-start | bytes 786440 | tf_op jit(solution)/shard_map/ppermute | solution.py:310
  474.7 7.7 %collective-permute-start.72 = (f32[2,32]{1,0:T(2,128)S(1)}, f32[2,32]{1,0:T(2,128)S(1)}, u32[]{:S(2)}, u32[]{:S(2)}) collective-permute-start(f32[2,32]{1,0:T(2,128)S(1)} %get-tuple-element.469), channel_id=1, source_target_pairs={{0,3},{1,2},{2,1},{3,0},{4,7},{5,6},{6,5},{7,4},{8,11},{9,10},{10,... | collective-permute-start | bytes 776 | tf_op jit(solution)/shard_map/ppermute | solution.py:310
  476.7 11.4 %collective-permute-start.71 = (f32[2,32]{1,0:T(2,128)S(1)}, f32[2,32]{1,0:T(2,128)S(1)}, u32[]{:S(2)}, u32[]{:S(2)}) collective-permute-start(f32[2,32]{1,0:T(2,128)S(1)} %get-tuple-element.470), channel_id=1, source_target_pairs={{0,2},{1,3},{2,0},{3,1},{4,6},{5,7},{6,4},{7,5},{8,10},{9,11},{10,... | collective-permute-start | bytes 776 | tf_op jit(solution)/shard_map/ppermute | solution.py:310
  477.0 11.0 %collective-permute-start.70 = (f32[2,32]{1,0:T(2,128)S(1)}, f32[2,32]{1,0:T(2,128)S(1)}, u32[]{:S(2)}, u32[]{:S(2)}) collective-permute-start(f32[2,32]{1,0:T(2,128)S(1)} %get-tuple-element.468), channel_id=1, source_target_pairs={{0,1},{1,0},{2,3},{3,2},{4,5},{5,4},{6,7},{7,6},{8,9},{9,8},{10,11... | collective-permute-start | bytes 776 | tf_op jit(solution)/shard_map/ppermute | solution.py:310
  (115 other events, 1168.6 us)
